TPU v7x, 256 devices: a whole 4x4x8 slice. The times are simulated.
256 devices in a mesh: dp: 8 (over x, core), ulysses: 32 (over z, y).
Axes of the slice: x: 4, y: 4, z: 8, core: 2. Of those that a mesh axis runs over, the one named last changes fastest.
Arguments:
- normalized_input: bfloat16 [8, 4096, 4096], P('dp', 'ulysses'), may hold values from -6 to 6
- frozen_queries: bfloat16 [8, 4096, 4096], P('dp', 'ulysses'), may hold values from -40 to 40
- frozen_keys: bfloat16 [8, 4096, 4096], P('dp', 'ulysses'), may hold values from -8 to 8
- frozen_values: bfloat16 [8, 4096, 4096], P('dp', 'ulysses'), may hold values from -6 to 6
- output_gradient: bfloat16 [8, 4096, 4096], P('dp', 'ulysses'), may hold values from -0.125 to 0.125
- adapter_down_maps: bfloat16 [2, 4096, 64], replicated, may hold values from -0.09375 to 0.09375
- adapter_up_maps: bfloat16 [2, 64, 4096], replicated, may hold values from -0.75 to 0.75
- shifted: int32 [32], replicated, may hold values from 0 to 1, as said below
Outputs:
- grad_down: float32 [2, 4096, 64], P(None, 'ulysses')
- grad_up: float32 [2, 64, 4096], P(None, None, 'ulysses')
Inputs may be any that keep to these rules, and one draw needn't show every extreme that they name: `shifted`: exactly half of the 32 heads are marked 1, the others 0.
All inputs are finite; a program needn't handle non-finite values.
Results may differ from a plain program's by a relative error of at most 0.0067.
Values may be sent and summed in bfloat16 or wider, within the bound.
No kernel may reach another device: no remote copies, remote signals or barrier semaphores. Data moves between devices by JAX's collectives and lax.ppermute only.
A program may use at most 64 MiB of HBM per device.

v0:
```python
import math

import jax
import jax.numpy as jnp
from jax import lax
from jax.sharding import PartitionSpec as P

HEADS = 32
HD = 128
GROUP = 1024
SHIFT = 512


adapter_scale = 0.5


def group_backward(query_matrix, key_rows, value_matrix, upstream):
    factor = 1.0 / math.sqrt(query_matrix.shape[-1])
    scores = jnp.dot(query_matrix, key_rows.T, preferred_element_type=jnp.float32) * factor
    row_ids = lax.broadcasted_iota(jnp.int32, scores.shape, 0)
    column_ids = lax.broadcasted_iota(jnp.int32, scores.shape, 1)
    scores = jnp.where(column_ids <= row_ids, scores, -jnp.inf)
    row_top = jnp.max(scores, axis=1, keepdims=True)
    weights = jnp.exp(scores - row_top)
    row_total = jnp.sum(weights, axis=1, keepdims=True)
    attention = (weights / row_total).astype(jnp.bfloat16)
    output = jnp.dot(attention, value_matrix, preferred_element_type=jnp.float32)
    group_values = jnp.dot(attention.T, upstream, preferred_element_type=jnp.float32).astype(
        jnp.bfloat16
    )
    grad_attention = jnp.dot(upstream, value_matrix.T, preferred_element_type=jnp.float32)
    center = jnp.sum(upstream.astype(jnp.float32) * output, axis=1, keepdims=True)
    grad_scores = (attention.astype(jnp.float32) * (grad_attention - center)).astype(jnp.bfloat16)
    group_queries = (
        jnp.dot(grad_scores, key_rows, preferred_element_type=jnp.float32) * factor
    ).astype(jnp.bfloat16)
    return (group_queries, group_values)


def run_group(bundle):
    return group_backward(*bundle)


def head_backward(query_matrix, key_rows, value_matrix, upstream, flag):
    offset = flag * SHIFT
    head_width = query_matrix.shape[-1]
    blocks = tuple(
        (
            jnp.roll(member, -offset, axis=0).reshape(-1, GROUP, head_width)
            for member in (query_matrix, key_rows, value_matrix, upstream)
        )
    )
    grad_query, grad_value = lax.map(run_group, blocks)
    grad_query = jnp.roll(grad_query.reshape(-1, head_width), offset, axis=0)
    grad_value = jnp.roll(grad_value.reshape(-1, head_width), offset, axis=0)
    return (grad_query, grad_value)


def run_head(bundle):
    return head_backward(*bundle)


def per_device(
    normalized_input,
    frozen_queries,
    frozen_keys,
    frozen_values,
    output_gradient,
    adapter_down_maps,
    adapter_up_maps,
    shifted,
):
    seq_dev = normalized_input.shape[1]
    token_rows = normalized_input[0]
    rank_projection = jnp.einsum(
        "jp,kpi->kji", token_rows, adapter_down_maps, preferred_element_type=jnp.float32
    ).astype(jnp.bfloat16)
    raised_rows = jnp.einsum(
        "hgo,how->hgw", rank_projection, adapter_up_maps, preferred_element_type=jnp.float32
    )
    query_matrix = (frozen_queries[0].astype(jnp.float32) + adapter_scale * raised_rows[0]).astype(
        jnp.bfloat16
    )
    value_matrix = (frozen_values[0].astype(jnp.float32) + adapter_scale * raised_rows[1]).astype(
        jnp.bfloat16
    )
    rank_count = lax.axis_size("ulysses")
    local_heads = HEADS // rank_count
    local_width = local_heads * HD
    seq_total = seq_dev * rank_count

    def split_heads(member):
        return member.reshape(seq_dev, rank_count, local_width)

    arrived = (
        lax.all_to_all(
            split_heads(query_matrix), "ulysses", split_axis=1, concat_axis=0, tiled=True
        ),
        lax.all_to_all(
            split_heads(frozen_keys[0]), "ulysses", split_axis=1, concat_axis=0, tiled=True
        ),
        lax.all_to_all(
            split_heads(value_matrix), "ulysses", split_axis=1, concat_axis=0, tiled=True
        ),
        lax.all_to_all(
            split_heads(output_gradient[0]), "ulysses", split_axis=1, concat_axis=0, tiled=True
        ),
    )

    def per_head(member):
        return member.transpose(1, 0, 2)

    first_head = lax.axis_index("ulysses") * local_heads
    head_flags = lax.dynamic_slice_in_dim(shifted, first_head, local_heads)
    grad_query, grad_value = lax.map(
        run_head, tuple((per_head(member) for member in arrived)) + (head_flags,)
    )
    head_grads = (
        jnp.stack([grad_query, grad_value]).transpose(0, 2, 1, 3).reshape(2, seq_total, local_width)
    )
    returned = lax.all_to_all(
        head_grads.reshape(2, seq_total, 1, local_width),
        "ulysses",
        split_axis=1,
        concat_axis=2,
        tiled=True,
    )
    token_gradient = returned.reshape(2, seq_dev, rank_count * local_width)
    up_portion = adapter_scale * jnp.einsum(
        "vbw,vbe->vwe", rank_projection, token_gradient, preferred_element_type=jnp.float32
    )
    rank_backprop = jnp.einsum(
        "cne,cke->cnk", token_gradient, adapter_up_maps, preferred_element_type=jnp.float32
    ).astype(jnp.bfloat16)
    down_portion = adapter_scale * jnp.einsum(
        "yt,cyu->ctu", token_rows, rank_backprop, preferred_element_type=jnp.float32
    )
    down_share, up_share = (
        lax.psum_scatter(down_portion, "ulysses", scatter_dimension=1, tiled=True),
        lax.psum_scatter(up_portion, "ulysses", scatter_dimension=2, tiled=True),
    )
    grad_down, grad_up = lax.psum((down_share, up_share), "dp")
    return (grad_down, grad_up)


def solution(mesh):
    in_specs = (
        P("dp", "ulysses", None),
        P("dp", "ulysses", None),
        P("dp", "ulysses", None),
        P("dp", "ulysses", None),
        P("dp", "ulysses", None),
        P(),
        P(),
        P(),
    )
    out_specs = (P(None, "ulysses", None), P(None, None, "ulysses"))
    return jax.shard_map(
        per_device, mesh=mesh, in_specs=in_specs, out_specs=out_specs, check_vma=False
    )
```

profile of v0, /device:TPU:1, one launch (start us, length us, event | category | flops | bytes accessed | tf_op | source)
XLA Modules:
  0.0 789.7 jit_solution(1102728348083496166)
XLA Ops:
  13.2 12.0 %all-to-all-start = ((bf16[128,32,128]{2,0,1:T(8,128)(2,1)}), bf16[128,32,128]{2,0,1:T(8,128)(2,1)S(1)}, u32[]{:S(2)}, u32[]{:S(2)}) async-start(bf16[128,32,128]{2,0,1:T(8,128)(2,1)} %copy.23), calls=%async_computation | async-start | bytes 2097152 | tf_op jit(solution)/shard_map/all_to_all | solution.py:96
  26.8 24.6 %all-to-all-done = bf16[128,32,128]{2,0,1:T(8,128)(2,1)S(1)} async-done(((bf16[128,32,128]{2,0,1:T(8,128)(2,1)}), bf16[128,32,128]{2,0,1:T(8,128)(2,1)S(1)}, u32[]{:S(2)}, u32[]{:S(2)}) %all-to-all-start) | async-done | bytes 1048608 | tf_op jit(solution)/shard_map/all_to_all | solution.py:96
  51.4 6.4 all-to-all-start.3
  57.8 2.3 copy.24
  62.3 20.7 %all-to-all-done.3 = bf16[128,32,128]{2,0,1:T(8,128)(2,1)S(1)} async-done(((bf16[128,32,128]{2,0,1:T(8,128)(2,1)}), bf16[128,32,128]{2,0,1:T(8,128)(2,1)S(1)}, u32[]{:S(2)}, u32[]{:S(2)}) %all-to-all-start.3) | async-done | bytes 1048608 | tf_op jit(solution)/shard_map/all_to_all | solution.py:102
  83.1 7.0 all-to-all-start.1
  92.3 2.3 copy.27
  94.6 19.8 %all-to-all-done.1 = bf16[128,32,128]{2,0,1:T(8,128)(2,1)} async-done(((bf16[128,32,128]{2,0,1:T(8,128)(2,1)}), bf16[128,32,128]{2,0,1:T(8,128)(2,1)}, u32[]{:S(2)}, u32[]{:S(2)}) %all-to-all-start.1) | async-done | bytes 1048608 | tf_op jit(solution)/shard_map/all_to_all | solution.py:99
  114.4 7.5 all-to-all-start.2
  123.5 4.6 fusion.42
  128.1 4.6 fusion.39
  132.7 2.9 fusion.41
  135.7 10.7 %all-to-all-done.2 = bf16[128,32,128]{2,0,1:T(8,128)(2,1)} async-done(((bf16[128,32,128]{2,0,1:T(8,128)(2,1)}), bf16[128,32,128]{2,0,1:T(8,128)(2,1)}, u32[]{:S(2)}, u32[]{:S(2)}) %all-to-all-start.2) | async-done | bytes 1048608 | tf_op jit(solution)/shard_map/all_to_all | solution.py:105
  146.4 2.9 fusion.40
  149.3 49.9 %while.21 = (s32[]{:T(128)}, bf16[4,1024,128]{2,1,0:T(8,128)(2,1)}, bf16[4,1024,128]{2,1,0:T(8,128)(2,1)}, bf16[4,1024,128]{2,1,0:T(8,128)(2,1)}, bf16[4,1024,12...) while((s32[]{:T(128)}, bf16[4,1024,128]{2,1,0:T(8,128)(2,1)}, ...), condition=%wide.region_4.6_spmd, body=%wide.region_0.5_spmd.sunk | while | flops 1362883584 | bytes 24674904 | solution.py:53
  155.5 3.9 fusion.79
  159.4 2.4 fusion.80
  168.0 3.9 fusion.79
  171.9 2.4 fusion.80
  180.5 3.9 fusion.79
  184.4 2.4 fusion.80
  193.0 3.9 fusion.79
  196.8 2.4 fusion.80
  199.2 2.6 fusion.36
  202.0 17.8 %copy.30 = bf16[2,4096,1,128]{3,0,2,1:T(2,128)(2,1)S(1)} copy(bf16[2,4096,1,128]{3,1,0,2:T(8,128)(2,1)S(1)} %maximum_bitcast_fusion) | data formatting | bytes 4194304 | tf_op jit(solution)/shard_map/transpose | solution.py:119
  219.8 53.4 %all_to_all.75 = bf16[2,4096,1,128]{3,0,2,1:T(2,128)(2,1)S(1)} all-to-all(bf16[2,4096,1,128]{3,0,2,1:T(2,128)(2,1)S(1)} %copy.30), channel_id=1, replica_groups=mesh['dp'=8,'ulysses'=32] {'ulysses'}, dimensions={1} | all-to-all | bytes 4194304 | tf_op jit(solution)/shard_map/all_to_all | solution.py:121
  273.5 2.7 copy.32
  276.2 2.8 reshape.69
  280.9 3.8 fusion.30
  284.8 208.5 %reduce-scatter.5.cloned.1.call-done = f32[2,64,128]{2,1,0:T(8,128)} async-done(((f32[2,64,4096]{2,1,0:T(8,128)}), f32[2,64,128]{2,1,0:T(8,128)}) %reduce-scatter.5.cloned.1.call-update) | async-done | bytes 65552 | tf_op jit(solution)/shard_map/reduce_scatter | solution.py:140
  493.3 218.9 %reduce-scatter.3.cloned.1.call-done = f32[2,128,64]{1,2,0:T(8,128)} async-done(((f32[2,4096,64]{1,2,0:T(8,128)}), f32[2,128,64]{1,2,0:T(8,128)}) %reduce-scatter.3.cloned.1.call-update) | async-done | bytes 65552 | tf_op jit(solution)/shard_map/reduce_scatter | solution.py:139
  712.2 68.1 %all-reduce.3.cloned.1.call-done = (f32[2,128,64]{1,2,0:T(8,128)}, f32[2,64,128]{2,1,0:T(8,128)}) async-done(((f32[2,128,64]{1,2,0:T(8,128)}, f32[2,64,128]{2,1,0:T(8,128)}), (f32[2,128,64]{1,2,0:T(8,128)}, f32[2,64,128]{2,1,0:T(8,128)})) %all-reduce.3.cloned.1.call-update) | async-done | bytes 131088 | tf_op jit(solution)/shard_map/psum | solution.py:142
  (55 shorter events, 43.0 us)
Async XLA Ops:
  7.2 2.1 copy-start
  9.3 1.2 copy-start.1
  9.3 1.5 copy-start.2
  13.2 38.2 %all-to-all-start = ((bf16[128,32,128]{2,0,1:T(8,128)(2,1)}), bf16[128,32,128]{2,0,1:T(8,128)(2,1)S(1)}, u32[]{:S(2)}, u32[]{:S(2)}) async-start(bf16[128,32,128]{2,0,1:T(8,128)(2,1)} %copy.23), calls=%async_computation | async-start | bytes 2097152 | tf_op jit(solution)/shard_map/all_to_all | solution.py:96
  51.4 31.6 %all-to-all-start.3 = ((bf16[128,32,128]{2,0,1:T(8,128)(2,1)}), bf16[128,32,128]{2,0,1:T(8,128)(2,1)S(1)}, u32[]{:S(2)}, u32[]{:S(2)}) async-start(bf16[128,32,128]{2,0,1:T(8,128)(2,1)} %copy.28), calls=%async_computation.3 | async-start | bytes 2097152 | tf_op jit(solution)/shard_map/all_to_all | solution.py:102
  83.1 31.3 %all-to-all-start.1 = ((bf16[128,32,128]{2,0,1:T(8,128)(2,1)}), bf16[128,32,128]{2,0,1:T(8,128)(2,1)}, u32[]{:S(2)}, u32[]{:S(2)}) async-start(bf16[128,32,128]{2,0,1:T(8,128)(2,1)} %copy.25), calls=%async_computation.1 | async-start | bytes 2097152 | tf_op jit(solution)/shard_map/all_to_all | solution.py:99
  92.3 29.9 %copy-start.3 = (s32[32]{0:T(128)S(1)}, s32[32]{0:T(128)}, u32[]{:S(2)}) copy-start(s32[32]{0:T(128)} %param.19) | copy-start | bytes 388
  114.4 32.0 %all-to-all-start.2 = ((bf16[128,32,128]{2,0,1:T(8,128)(2,1)}), bf16[128,32,128]{2,0,1:T(8,128)(2,1)}, u32[]{:S(2)}, u32[]{:S(2)}) async-start(bf16[128,32,128]{2,0,1:T(8,128)(2,1)} %copy.27), calls=%async_computation.2 | async-start | bytes 2097152 | tf_op jit(solution)/shard_map/all_to_all | solution.py:105
  122.0 371.3 %reduce-scatter.5.cloned.1.call-start = ((), (), s32[]{:S(2)}) async-start(), calls=%async_computation.8 | async-start | bytes 2162688 | tf_op jit(solution)/shard_map/reduce_scatter | solution.py:140
  280.9 431.3 %reduce-scatter.3.cloned.1.call-start = ((), (), s32[]{:S(2)}) async-start(), calls=%async_computation.7 | async-start | bytes 2162688 | tf_op jit(solution)/shard_map/reduce_scatter | solution.py:139
  284.7 495.5 %all-reduce.3.cloned.1.call-start = ((), (), s32[]{:S(2)}) async-start(), calls=%async_computation.9 | async-start | bytes 262144 | tf_op jit(solution)/shard_map/psum | solution.py:142
Sparse Core Ops, SparseCore 0:
  281.0 212.2 reduce-scatter.4
  497.6 214.5 reduce-scatter.2
  714.5 65.6 all-reduce.2
where the time goes:
time: 792 us; the launch traced here: 790 us
  waiting for transfers between devices  571 us (72%)
  blocking collectives  53.4 us (7%)
  local copies, waits for them, and re-layouts  47.6 us (6%)
  matrix products  46.5 us (6%)
  starting transfers between devices  33.2 us (4%)
  other arithmetic  23 us (3%)
  between operations  14.6 us (2%)
    reduce_scatter x1, waiting for transfers between devices, per_device(): lax.psum_scatter(down_portion, 'ulysses', scatter_dimension=1, tiled=True)  219 us
    reduce_scatter x1, waiting for transfers between devices, per_device(): lax.psum_scatter(up_portion, 'ulysses', scatter_dimension=2, tiled=True)  208 us
    psum x1, waiting for transfers between devices, per_device(): grad_down, grad_up = lax.psum((down_share, up_share), 'dp')  68.1 us
    all_to_all x1, blocking collectives, per_device(): lax.all_to_all(head_grads.reshape(2, seq_total, 1, local_width), 'ulysses...  53.4 us
    all_to_all x1, waiting for transfers between devices, per_device(): lax.all_to_all(split_heads(query_matrix), 'ulysses', split_axis=1, concat...  24.6 us
    all_to_all x1, waiting for transfers between devices, per_device(): lax.all_to_all(split_heads(value_matrix), 'ulysses', split_axis=1, concat...  20.7 us
    all_to_all x1, waiting for transfers between devices, per_device(): lax.all_to_all(split_heads(frozen_keys[0]), 'ulysses', split_axis=1, conc...  19.8 us
    transpose x1, local copies, waits for them, and re-layouts, per_device(): jnp.stack([grad_query, grad_value]).transpose(0, 2, 1, 3)  17.8 us
  transfers between devices with their start and end apart: 7, of which 7 were waited for; matrix products, arithmetic and copies ran while one was open for 3% of the time, Pallas kernels for 0%

commit v1 on v0

v1 whole, which is shorter than its diff:
```python
import math

import jax
import jax.numpy as jnp
from jax import lax
from jax.experimental import pallas as pl
from jax.experimental.pallas import tpu as pltpu
from jax.sharding import PartitionSpec as P

HEADS = 32
HD = 128
GROUP = 1024
SHIFT = 512
RANK = 64
ROWS = 128
ZS, YS = 8, 4
MEMBERS = 8
RB = 256
BF16, F32 = jnp.bfloat16, jnp.float32

adapter_scale = 0.5

PLAIN_GROUPS = [[MEMBERS * g + i for i in range(MEMBERS)] for g in range(4)]
SHIFT_GROUPS = [[(MEMBERS * g + 4 + i) % HEADS for i in range(MEMBERS)] for g in range(4)]
Y_GROUPS = [[YS * z + y for y in range(YS)] for z in range(ZS)]


def z_shift(dz):
    return [(z * YS + y, ((z + dz) % ZS) * YS + y) for z in range(ZS) for y in range(YS)]


def exchange(member, axis, groups=None):
    return lax.all_to_all(member, axis, 0, 0, tiled=True, axis_index_groups=groups)


def prepare_kernel(heads, low_ref, fq_ref, fk_ref, fv_ref, go_ref, up_ref, out_ref, qb, vb, ub, sems):
    copies = []
    for j in range(MEMBERS):
        cols = pl.ds(pl.multiple_of(heads[j] * HD, HD), HD)
        row = [
            pltpu.make_async_copy(fq_ref.at[:, cols], qb.at[j], sems.at[j, 0]),
            pltpu.make_async_copy(fv_ref.at[:, cols], vb.at[j], sems.at[j, 1]),
            pltpu.make_async_copy(up_ref.at[:, cols], ub.at[j], sems.at[j, 2]),
            pltpu.make_async_copy(fk_ref.at[:, cols], out_ref.at[j, :, pl.ds(HD, HD)], sems.at[j, 3]),
            pltpu.make_async_copy(go_ref.at[:, cols], out_ref.at[j, :, pl.ds(3 * HD, HD)], sems.at[j, 4]),
        ]
        for copy in row:
            copy.start()
        copies.append(row)
    low = low_ref[...]
    for j in range(MEMBERS):
        for copy in copies[j][:3]:
            copy.wait()
        up = ub[j]
        raised_q = jnp.dot(low[:, :RANK], up[:RANK], preferred_element_type=F32)
        raised_v = jnp.dot(low[:, RANK:], up[RANK:], preferred_element_type=F32)
        out_ref[j, :, pl.ds(0, HD)] = (qb[j].astype(F32) + adapter_scale * raised_q).astype(BF16)
        out_ref[j, :, pl.ds(2 * HD, HD)] = (vb[j].astype(F32) + adapter_scale * raised_v).astype(BF16)
    for j in range(MEMBERS):
        for copy in copies[j][3:]:
            copy.wait()


def prepare(heads, low, fq, fk, fv, go, up):
    anywhere = pl.BlockSpec(memory_space=pl.ANY)
    return pl.pallas_call(
        prepare_kernel,
        out_shape=jax.ShapeDtypeStruct((MEMBERS, ROWS, 4 * HD), BF16),
        grid_spec=pltpu.PrefetchScalarGridSpec(
            num_scalar_prefetch=1,
            grid=(1,),
            in_specs=[pl.BlockSpec((ROWS, 2 * RANK), lambda i, h: (0, 0))] + [anywhere] * 5,
            out_specs=pl.BlockSpec((MEMBERS, ROWS, 4 * HD), lambda i, h: (0, 0, 0)),
            scratch_shapes=[pltpu.VMEM((MEMBERS, ROWS, HD), BF16)] * 3
            + [pltpu.SemaphoreType.DMA((MEMBERS, 5))],
        ),
        cost_estimate=pl.CostEstimate(flops=4 * 10**7, bytes_accessed=2 * 10**6, transcendentals=0),
    )(heads, low, fq, fk, fv, go, up)


def dot_t(a, b):
    return lax.dot_general(a, b, (((1,), (1,)), ((), ())), preferred_element_type=F32)


def dot_0(a, b):
    return lax.dot_general(a, b, (((0,), (0,)), ((), ())), preferred_element_type=F32)


def attention_kernel(first, head, x_ref, low_ref, up_ref, *refs):
    if first:
        back_ref, upgrad_ref, dv_acc, dq_buf = refs
    else:
        before_ref, back_ref, upgrad_ref, dv_acc, dq_buf = refs
    factor = 1.0 / math.sqrt(HD)
    bend = factor * math.log2(math.e)
    row_ids = lax.broadcasted_iota(jnp.int32, (RB, RB), 0)
    column_ids = lax.broadcasted_iota(jnp.int32, (RB, RB), 1)
    keep = column_ids <= row_ids
    for i in range(GROUP // RB):
        n = (i + 1) * RB
        rows = pl.ds(i * RB, RB)
        q = x_ref[rows, pl.ds(0, HD)]
        g = x_ref[rows, pl.ds(3 * HD, HD)]
        k = x_ref[pl.ds(0, n), pl.ds(HD, HD)]
        v = x_ref[pl.ds(0, n), pl.ds(2 * HD, HD)]
        scores = dot_t(q, k)
        last = jnp.where(keep, scores[:, i * RB :], -1e30)
        scores = last if i == 0 else jnp.concatenate([scores[:, : i * RB], last], axis=1)
        top = jnp.max(scores, axis=1, keepdims=True)
        weights = jnp.exp2((scores - top) * bend)
        total = jnp.sum(weights, axis=1, keepdims=True)
        attention = (weights * (1.0 / total)).astype(BF16)
        output = jnp.dot(attention, v, preferred_element_type=F32)
        grad_attention = dot_t(g, v)
        center = jnp.sum(g.astype(F32) * output, axis=1, keepdims=True)
        grad_scores = (attention.astype(F32) * (grad_attention - center)).astype(BF16)
        dq = jnp.dot(grad_scores, k, preferred_element_type=F32) * factor
        dq_buf[rows, :] = dq.astype(BF16)
        dv = dot_0(attention, g)
        if i:
            dv_acc[pl.ds(0, i * RB), :] += dv[: i * RB]
        dv_acc[rows, :] = dv[i * RB :]
    dq = dq_buf[...]
    dv = dv_acc[...].astype(BF16)
    low = low_ref[...]
    up = up_ref[...]
    upgrad_ref[pl.ds(0, RANK), :] = adapter_scale * dot_0(low[:, :RANK], dq)
    upgrad_ref[pl.ds(RANK, RANK), :] = adapter_scale * dot_0(low[:, RANK:], dv)
    lanes = lax.broadcasted_iota(jnp.int32, (GROUP, 2 * RANK), 1)
    back = jnp.where(lanes < RANK, dot_t(dq, up), dot_t(dv, up))
    if first:
        back_ref[...] = back
    else:
        back_ref[...] = (back + before_ref[...]).astype(BF16)


def attention_chunk(head, arrived, low, up, before=None):
    first = before is None
    whole = lambda shape: pl.BlockSpec(shape, lambda i, h: (0, 0))

    def body(*refs):
        attention_kernel(first, *refs)

    more = [] if first else [before]
    return pl.pallas_call(
        body,
        name="attention_first" if first else "attention_second",
        out_shape=(
            jax.ShapeDtypeStruct((GROUP, 2 * RANK), F32 if first else BF16),
            jax.ShapeDtypeStruct((2 * RANK, HD), F32),
        ),
        grid_spec=pltpu.PrefetchScalarGridSpec(
            num_scalar_prefetch=1,
            grid=(1,),
            in_specs=[
                whole((GROUP, 4 * HD)),
                whole((GROUP, 2 * RANK)),
                pl.BlockSpec((2 * RANK, HD), lambda i, h: (0, h[0])),
            ]
            + [whole((GROUP, 2 * RANK))] * len(more),
            out_specs=[whole((GROUP, 2 * RANK)), whole((2 * RANK, HD))],
            scratch_shapes=[pltpu.VMEM((GROUP, HD), F32), pltpu.VMEM((GROUP, HD), BF16)],
        ),
        compiler_params=pltpu.CompilerParams(vmem_limit_bytes=48 * 2**20),
        cost_estimate=pl.CostEstimate(flops=3 * 10**9, bytes_accessed=2 * 10**6, transcendentals=10**6),
    )(head, arrived.reshape(GROUP, 4 * HD), low, up, *more)


def per_device(
    normalized_input,
    frozen_queries,
    frozen_keys,
    frozen_values,
    output_gradient,
    adapter_down_maps,
    adapter_up_maps,
    shifted,
):
    token_rows = normalized_input[0]
    me = lax.axis_index("ulysses")
    z = me // YS
    even = z % 2 == 0
    up = adapter_up_maps.reshape(2 * RANK, HEADS * HD)

    flags = shifted.astype(jnp.int32)
    index = jnp.arange(HEADS, dtype=jnp.int32)
    before = jnp.sum(jnp.where(index[None, :] < index[:, None], flags[None, :], 0), axis=1)
    place = jnp.where(flags > 0, HEADS // 2 + before, index - before)
    order = jnp.sum(jnp.where(place[None, :] == index[:, None], index[None, :], 0), axis=1)

    low = jnp.einsum("jp,kpi->jki", token_rows, adapter_down_maps, preferred_element_type=F32)
    low = low.astype(BF16).reshape(ROWS, 2 * RANK)

    own = exchange(jnp.broadcast_to(low[None], (YS, ROWS, 2 * RANK)), "ulysses", Y_GROUPS)
    own = own.reshape(YS * ROWS, 2 * RANK)
    later = lax.ppermute(own, "ulysses", z_shift(-1))
    earlier = lax.ppermute(own, "ulysses", z_shift(1))
    leading = jnp.concatenate([own, later], axis=0)
    trailing = jnp.concatenate([earlier, own], axis=0)
    low_plain = jnp.where(even, leading, trailing)
    low_shift = jnp.where(even, trailing, leading)

    seats = (me % MEMBERS, (me + 4) % MEMBERS)
    back, upgrads, held = [], [], []
    for part in range(2):
        groups = (PLAIN_GROUPS, SHIFT_GROUPS)[part]
        lows = (low_plain, low_shift)[part]
        partial = None
        for c in (2 * part, 2 * part + 1):
            heads = order[c * MEMBERS : (c + 1) * MEMBERS]
            sent = prepare(
                heads, low, frozen_queries[0], frozen_keys[0], frozen_values[0], output_gradient[0], up
            )
            arrived = exchange(sent, "ulysses", groups)
            head = lax.dynamic_slice_in_dim(heads, seats[part], 1)
            partial, upgrad = attention_chunk(head, arrived, lows, up, partial)
            upgrads.append(upgrad)
            held.append(head)
        summed = exchange(partial.reshape(MEMBERS, ROWS, 2 * RANK), "ulysses", groups)
        back.append(jnp.sum(summed.astype(F32), axis=0))
    back_rank = (back[0] + back[1]).astype(BF16)

    down = adapter_scale * jnp.einsum("tc,tk->ck", token_rows, back_rank, preferred_element_type=F32)
    down = down.astype(BF16).reshape(HEADS, 8, 16, 2 * RANK).transpose(1, 0, 2, 3)
    ups = jnp.stack(upgrads).astype(BF16).reshape(4, 8, 16, HD).transpose(1, 0, 2, 3)
    both = jnp.concatenate([down, ups], axis=1)
    both = jnp.sum(exchange(both, "dp").astype(F32), axis=0)
    heads = jnp.concatenate(held)
    slots = jnp.sum(
        jnp.where((heads[None, :] == index[:, None])[:, :, None, None], both[None, HEADS:], 0.0), axis=1
    )
    both = jnp.concatenate([both[:HEADS], slots], axis=1).astype(BF16)
    both = jnp.sum(exchange(both, "ulysses").astype(F32), axis=0)
    both = exchange(jnp.broadcast_to(both[None], (8, 32, HD)), "dp")
    grad_down = both[:, :16].reshape(HD, 2, RANK).transpose(1, 0, 2)
    grad_up = both[:, 16:].reshape(2, RANK, HD)
    return (grad_down, grad_up)


def solution(mesh):
    rows = P("dp", "ulysses", None)
    in_specs = (rows, rows, rows, rows, rows, P(), P(), P())
    out_specs = (P(None, "ulysses", None), P(None, None, "ulysses"))
    return jax.shard_map(
        per_device, mesh=mesh, in_specs=in_specs, out_specs=out_specs, check_vma=False
    )
```

time: 792 us -> 196 us (0.25)
  waiting for transfers between devices: 571 us -> 58.4 us
  matrix products: 46.5 us -> 2.13 us
  Pallas kernels: 0 us -> 41.9 us
  local copies, waits for them, and re-layouts: 47.6 us -> 9.18 us
  blocking collectives: 53.4 us -> 26.9 us
  other arithmetic: 23 us -> 5.65 us
  starting transfers between devices: 33.2 us -> 49.7 us
  between operations: 14.6 us -> 0.96 us
    reduce_scatter x2 -> x0, waiting for transfers between devices: 427 us -> none  [the longest x1 219 us: per_device(): lax.psum_scatter(down_portion, 'ulysses', scatter_dimension=1, tiled=True)]
    psum x1 -> x0, waiting for transfers between devices: 68.1 us -> none  [per_device(): grad_down, grad_up = lax.psum((down_share, up_share), 'dp')]
    dot_general x20 -> x1, matrix products: 46.5 us -> 0.46 us  [per_device(): jnp.einsum('tc,tk->ck', token_rows, back_rank, preferred_element_type=F32)]
    pallas_call x0 -> x8, Pallas kernels: none -> 41.9 us  [the longest x4 22.4 us: attention_chunk(): pl.pallas_call(body, name='attention_first' if first else 'attention_seco...]
    all_to_all x4 -> x8, waiting for transfers between devices: 75.8 us -> 48.4 us  [exchange(): lax.all_to_all(member, axis, 0, 0, tiled=True, axis_index_groups=groups)]
    all_to_all x1 -> x2, blocking collectives: 53.4 us -> 26.9 us  [exchange(): lax.all_to_all(member, axis, 0, 0, tiled=True, axis_index_groups=groups)]
    transpose x1 -> x0, local copies, waits for them, and re-layouts: 17.8 us -> none  [per_device(): jnp.stack([grad_query, grad_value]).transpose(0, 2, 1, 3)]
    all_to_all x4 -> x8, starting transfers between devices: 32.9 us -> 47 us  [exchange(): lax.all_to_all(member, axis, 0, 0, tiled=True, axis_index_groups=groups)]
  transfers between devices with their start and end apart: 7 -> 10, of which waited for: 7 -> 7; matrix products, arithmetic and copies ran while one was open for 3% -> 4% of each run, Pallas kernels for 0% -> 22%
where the time goes in v1:
time: 196 us; the launch traced here: 195 us
  waiting for transfers between devices  58.4 us (30%)
  starting transfers between devices  49.7 us (25%)
  Pallas kernels  41.9 us (21%)
  blocking collectives  26.9 us (14%)
  local copies, waits for them, and re-layouts  9.18 us (5%)
  other arithmetic  5.65 us (3%)
  matrix products  2.13 us (1%)
    all_to_all x8, waiting for transfers between devices, exchange(): lax.all_to_all(member, axis, 0, 0, tiled=True, axis_index_groups=groups)  48.4 us
    all_to_all x8, starting transfers between devices, exchange(): lax.all_to_all(member, axis, 0, 0, tiled=True, axis_index_groups=groups)  47 us
    all_to_all x2, blocking collectives, exchange(): lax.all_to_all(member, axis, 0, 0, tiled=True, axis_index_groups=groups)  26.9 us
    pallas_call x4, Pallas kernels, attention_chunk(): pl.pallas_call(body, name='attention_first' if first else 'attention_seco...  22.4 us
    pallas_call x4, Pallas kernels, prepare(): pl.pallas_call(prepare_kernel, out_shape=jax.ShapeDtypeStruct((MEMBERS, R...  19.5 us
    ppermute x1, waiting for transfers between devices, per_device(): earlier = lax.ppermute(own, 'ulysses', z_shift(1))  8.6 us
  transfers between devices with their start and end apart: 10, of which 7 were waited for; matrix products, arithmetic and copies ran while one was open for 4% of the time, Pallas kernels for 22%

profile of v1, /device:TPU:1, one launch (start us, length us, event | category | flops | bytes accessed | tf_op | source)
XLA Modules:
  0.0 194.8 jit_solution(17122870946450326180)
XLA Ops:
  0.6 1.2 copy-done
  1.9 1.7 fusion.3
  4.4 5.0 %all-to-all-start.1 = ((bf16[4,128,128]{2,1,0:T(8,128)(2,1)}), bf16[4,128,128]{2,1,0:T(8,128)(2,1)S(1)}, u32[]{:S(2)}, u32[]{:S(2)}) async-start(bf16[4,128,128]{2,1,0:T(8,128)(2,1)} %broadcast_in_dim.59), calls=%async_computation.1 | async-start | bytes 262144 | tf_op jit(solution)/shard_map/all_to_all | solution.py:33
  10.3 4.9 %shard_map.98 = bf16[8,128,512]{2,1,0:T(8,128)(2,1)} custom-call(s32[8]{0:T(128)} %get-tuple-element.29.heads, bf16[128,128]{1,0:T(8,128)(2,1)} %copy-done.5, bf16[128,4096]{1,0:T(8,128)(2,1)} %bitcast.47, bf16[128,4096]{1,0:T(8,128)(2,1)} %bitcast.51, bf16[128,4096]{1,0:T(8,128)(2,1)} %bitcast.55, bf16[128,4096]{1,0:T(8,128)(2,1)} %bitcast.59, ...), custom_call_target="tpu_custom_call" | custom-call | flops 40000000 | bytes 2000000 | tf_op jit(solution)/shard_map/pallas_call | solution.py:66
  15.2 9.8 %all-to-all-start.5 = ((bf16[8,128,512]{2,1,0:T(8,128)(2,1)}), bf16[8,128,512]{2,1,0:T(8,128)(2,1)S(1)}, u32[]{:S(2)}, u32[]{:S(2)}) async-start(bf16[8,128,512]{2,1,0:T(8,128)(2,1)} %shard_map.98), calls=%async_computation.5 | async-start | bytes 2097152 | tf_op jit(solution)/shard_map/all_to_all | solution.py:33
  25.0 4.8 %shard_map.97 = bf16[8,128,512]{2,1,0:T(8,128)(2,1)} custom-call(s32[8]{0:T(128)} %get-tuple-element.30.heads, bf16[128,128]{1,0:T(8,128)(2,1)} %copy-done.5, bf16[128,4096]{1,0:T(8,128)(2,1)} %bitcast.48, bf16[128,4096]{1,0:T(8,128)(2,1)} %bitcast.52, bf16[128,4096]{1,0:T(8,128)(2,1)} %bitcast.56, bf16[128,4096]{1,0:T(8,128)(2,1)} %bitcast.60, ...), custom_call_target="tpu_custom_call" | custom-call | flops 40000000 | bytes 2000000 | tf_op jit(solution)/shard_map/pallas_call | solution.py:66
  29.8 9.7 %all-to-all-done.5 = bf16[8,128,512]{2,1,0:T(8,128)(2,1)S(1)} async-done(((bf16[8,128,512]{2,1,0:T(8,128)(2,1)}), bf16[8,128,512]{2,1,0:T(8,128)(2,1)S(1)}, u32[]{:S(2)}, u32[]{:S(2)}) %all-to-all-start.5) | async-done | bytes 1048608 | tf_op jit(solution)/shard_map/all_to_all | solution.py:33
  39.6 5.2 %all-to-all-start.4 = ((bf16[8,128,512]{2,1,0:T(8,128)(2,1)}), bf16[8,128,512]{2,1,0:T(8,128)(2,1)S(1)}, u32[]{:S(2)}, u32[]{:S(2)}) async-start(bf16[8,128,512]{2,1,0:T(8,128)(2,1)} %shard_map.97), calls=%async_computation.4 | async-start | bytes 2097152 | tf_op jit(solution)/shard_map/all_to_all | solution.py:33
  44.8 4.9 %shard_map.96 = bf16[8,128,512]{2,1,0:T(8,128)(2,1)} custom-call(s32[8]{0:T(128)} %get-tuple-element.28.heads, bf16[128,128]{1,0:T(8,128)(2,1)} %copy-done.5, bf16[128,4096]{1,0:T(8,128)(2,1)} %bitcast.49, bf16[128,4096]{1,0:T(8,128)(2,1)} %bitcast.53, bf16[128,4096]{1,0:T(8,128)(2,1)} %bitcast.57, bf16[128,4096]{1,0:T(8,128)(2,1)} %bitcast.61, ...), custom_call_target="tpu_custom_call" | custom-call | flops 40000000 | bytes 2000000 | tf_op jit(solution)/shard_map/pallas_call | solution.py:66
  49.7 9.8 %all-to-all-done.4 = bf16[8,128,512]{2,1,0:T(8,128)(2,1)S(1)} async-done(((bf16[8,128,512]{2,1,0:T(8,128)(2,1)}), bf16[8,128,512]{2,1,0:T(8,128)(2,1)S(1)}, u32[]{:S(2)}, u32[]{:S(2)}) %all-to-all-start.4) | async-done | bytes 1048608 | tf_op jit(solution)/shard_map/all_to_all | solution.py:33
  59.5 4.2 %all-to-all-start.2 = ((bf16[8,128,512]{2,1,0:T(8,128)(2,1)}), bf16[8,128,512]{2,1,0:T(8,128)(2,1)}, u32[]{:S(2)}, u32[]{:S(2)}) async-start(bf16[8,128,512]{2,1,0:T(8,128)(2,1)} %shard_map.96), calls=%async_computation.2 | async-start | bytes 2097152 | tf_op jit(solution)/shard_map/all_to_all | solution.py:33
  63.7 4.9 %shard_map.95 = bf16[8,128,512]{2,1,0:T(8,128)(2,1)} custom-call(s32[8]{0:T(128)} %get-tuple-element.31.heads, bf16[128,128]{1,0:T(8,128)(2,1)} %copy-done.5, bf16[128,4096]{1,0:T(8,128)(2,1)} %bitcast.50, bf16[128,4096]{1,0:T(8,128)(2,1)} %bitcast.54, bf16[128,4096]{1,0:T(8,128)(2,1)} %bitcast.58, bf16[128,4096]{1,0:T(8,128)(2,1)} %bitcast.62, ...), custom_call_target="tpu_custom_call" | custom-call | flops 40000000 | bytes 2000000 | tf_op jit(solution)/shard_map/pallas_call | solution.py:66
  68.7 9.9 %all-to-all-done.2 = bf16[8,128,512]{2,1,0:T(8,128)(2,1)} async-done(((bf16[8,128,512]{2,1,0:T(8,128)(2,1)}), bf16[8,128,512]{2,1,0:T(8,128)(2,1)}, u32[]{:S(2)}, u32[]{:S(2)}) %all-to-all-start.2) | async-done | bytes 1048608 | tf_op jit(solution)/shard_map/all_to_all | solution.py:33
  78.7 4.2 %all-to-all-start = ((bf16[8,128,512]{2,1,0:T(8,128)(2,1)}), bf16[8,128,512]{2,1,0:T(8,128)(2,1)}, u32[]{:S(2)}, u32[]{:S(2)}) async-start(bf16[8,128,512]{2,1,0:T(8,128)(2,1)} %shard_map.95), calls=%async_computation | async-start | bytes 2097152 | tf_op jit(solution)/shard_map/all_to_all | solution.py:33
  82.9 1.4 collective-permute-start.1
  84.3 1.4 collective-permute-start
  88.0 8.6 %collective-permute-done.1 = bf16[512,128]{1,0:T(8,128)(2,1)S(1)} collective-permute-done((bf16[512,128]{1,0:T(8,128)(2,1)S(1)}, bf16[512,128]{1,0:T(8,128)(2,1)S(1)}, u32[]{:S(2)}, u32[]{:S(2)}) %collective-permute-start.1) | collective-permute-done | bytes 131104 | tf_op jit(solution)/shard_map/ppermute | solution.py:197
  97.3 1.4 collective-permute-done
  98.7 1.2 broadcast_select_fusion.1
  99.9 4.6 %attention_first.3 = (f32[1024,128]{1,0:T(8,128)S(1)}, f32[128,128]{1,0:T(8,128)S(1)}) custom-call(s32[1]{0:T(128)} %dynamic_slice.15.refs_0_, bf16[1024,512]{1,0:T(8,128)(2,1)S(1)} %bitcast.45, bf16[1024,128]{1,0:T(8,128)(2,1)S(1)} %get-tuple-element.25.refs_2_, bf16[128,4096]{1,0:T(8,128)(2,1)S(1)} %bitcast.41), custom_call_target="tpu_custom_call" | custom-call | flops 3000000000 | bytes 2000000 | tf_op jit(solution)/shard_map/attention_first/pallas_call | solution.py:145
  104.5 5.4 %attention_second.3 = (bf16[1024,128]{1,0:T(8,128)(2,1)}, f32[128,128]{1,0:T(8,128)S(1)}) custom-call(s32[1]{0:T(128)} %dynamic_slice.14.refs_0_, bf16[1024,512]{1,0:T(8,128)(2,1)S(1)} %bitcast.46, bf16[1024,128]{1,0:T(8,128)(2,1)S(1)} %get-tuple-element.25.refs_2_, bf16[128,4096]{1,0:T(8,128)(2,1)S(1)} %bitcast.42, f32[1024,128]{1,0:T(8,128)S(1)} %get-tuple-element.12.refs_4_), custom_call_target="tpu_custom_call" | custom-call | flops 3000000000 | bytes 2000000 | tf_op jit(solution)/shard_map/attention_second/pallas_call | solution.py:145
  109.9 6.4 %all-to-all-start.6 = ((bf16[8,128,128]{2,1,0:T(8,128)(2,1)}), bf16[8,128,128]{2,1,0:T(8,128)(2,1)}, u32[]{:S(2)}, u32[]{:S(2)}) async-start(bf16[8,128,128]{2,1,0:T(8,128)(2,1)} %bitcast.16), calls=%async_computation.6 | async-start | bytes 524288 | tf_op jit(solution)/shard_map/all_to_all | solution.py:33
  116.3 5.9 %attention_first.2 = (f32[1024,128]{1,0:T(8,128)S(1)}, f32[128,128]{1,0:T(8,128)S(1)}) custom-call(s32[1]{0:T(128)} %dynamic_slice.13.refs_0_, bf16[1024,512]{1,0:T(8,128)(2,1)} %bitcast.12.refs_1_, bf16[1024,128]{1,0:T(8,128)(2,1)S(1)} %get-tuple-element.24.refs_2_, bf16[128,4096]{1,0:T(8,128)(2,1)S(1)} %bitcast.43), custom_call_target="tpu_custom_call" | custom-call | flops 3000000000 | bytes 2000000 | tf_op jit(solution)/shard_map/attention_first/pallas_call | solution.py:145
  122.1 6.6 %attention_second.2 = (bf16[1024,128]{1,0:T(8,128)(2,1)}, f32[128,128]{1,0:T(8,128)S(1)}) custom-call(s32[1]{0:T(128)} %dynamic_slice.12.refs_0_, bf16[1024,512]{1,0:T(8,128)(2,1)} %bitcast.10.refs_1_, bf16[1024,128]{1,0:T(8,128)(2,1)S(1)} %get-tuple-element.24.refs_2_, bf16[128,4096]{1,0:T(8,128)(2,1)S(1)} %bitcast.44, ...), custom_call_target="tpu_custom_call" | custom-call | flops 3000000000 | bytes 2000000 | tf_op jit(solution)/shard_map/attention_second/pallas_call | solution.py:145
  128.7 4.1 %all-to-all-start.3 = ((bf16[8,128,128]{2,1,0:T(8,128)(2,1)}), bf16[8,128,128]{2,1,0:T(8,128)(2,1)S(1)}, u32[]{:S(2)}, u32[]{:S(2)}) async-start(bf16[8,128,128]{2,1,0:T(8,128)(2,1)} %bitcast.13), calls=%async_computation.3 | async-start | bytes 524288 | tf_op jit(solution)/shard_map/all_to_all | solution.py:33
  133.9 5.0 %all-to-all-done.3 = bf16[8,128,128]{2,1,0:T(8,128)(2,1)S(1)} async-done(((bf16[8,128,128]{2,1,0:T(8,128)(2,1)}), bf16[8,128,128]{2,1,0:T(8,128)(2,1)S(1)}, u32[]{:S(2)}, u32[]{:S(2)}) %all-to-all-start.3) | async-done | bytes 262176 | tf_op jit(solution)/shard_map/all_to_all | solution.py:33
  140.2 1.3 copy.34
  141.4 8.0 %all-to-all-start.7 = ((bf16[8,36,16,128]{3,2,1,0:T(8,128)(2,1)}), bf16[8,36,16,128]{3,2,1,0:T(8,128)(2,1)S(1)}, u32[]{:S(2)}, u32[]{:S(2)}) async-start(bf16[8,36,16,128]{3,2,1,0:T(8,128)(2,1)} %copy.34), calls=%async_computation.7 | async-start | bytes 2359296 | tf_op jit(solution)/shard_map/all_to_all | solution.py:33
  149.4 2.6 %pad_add_fusion = s32[4]{0:T(128)S(1)} fusion(s32[1]{0:T(128)} %dynamic_slice.14.refs_0_, s32[1]{0:T(128)} %dynamic_slice.15.refs_0_, s32[1]{0:T(128)} %dynamic_slice.12.refs_0_, s32[1]{0:T(128)} %dynamic_slice.13.refs_0_), kind=kLoop, calls=%fused_computation.26 | loop fusion | flops 12 | bytes 32 | tf_op jit(solution)/shard_map/concatenate | solution.py:228
  152.0 13.9 %all-to-all-done.7 = bf16[8,36,16,128]{3,2,1,0:T(8,128)(2,1)S(1)} async-done(((bf16[8,36,16,128]{3,2,1,0:T(8,128)(2,1)}), bf16[8,36,16,128]{3,2,1,0:T(8,128)(2,1)S(1)}, u32[]{:S(2)}, u32[]{:S(2)}) %all-to-all-start.7) | async-done | bytes 1179680 | tf_op jit(solution)/shard_map/all_to_all | solution.py:33
  166.3 16.6 %all_to_all.50 = bf16[32,32,128]{2,1,0:T(8,128)(2,1)S(1)} all-to-all(bf16[32,32,128]{2,1,0:T(8,128)(2,1)S(1)} %pad_maximum_fusion.3), channel_id=1, replica_groups=mesh['dp'=8,'ulysses'=32] {'ulysses'}, dimensions={0} | all-to-all | bytes 524288 | tf_op jit(solution)/shard_map/all_to_all | solution.py:33
  183.0 10.2 %all_to_all.51 = f32[8,32,128]{2,1,0:T(8,128)S(1)} all-to-all(f32[8,32,128]{2,1,0:T(8,128)S(1)} %broadcast_in_dim.63), channel_id=1, replica_groups=mesh['dp'=8,'ulysses'=32] {'dp'}, dimensions={0} | all-to-all | bytes 262144 | tf_op jit(solution)/shard_map/all_to_all | solution.py:33
  (60 shorter events, 9.0 us)
Async XLA Ops:
  0.6 1.2 copy-start
  1.9 7.5 %copy-start.12 = (s32[32]{0:T(128)S(1)}, s32[32]{0:T(128)}, u32[]{:S(2)}) copy-start(s32[32]{0:T(128)} %param.15) | copy-start | bytes 388
  3.7 6.6 %copy-start.5 = (bf16[128,128]{1,0:T(8,128)(2,1)}, bf16[128,128]{1,0:T(8,128)(2,1)S(1)}, u32[]{:S(2)}) copy-start(bf16[128,128]{1,0:T(8,128)(2,1)S(1)} %copy.28.low_ref) | copy-start | bytes 98308
  4.4 10.8 %all-to-all-start.1 = ((bf16[4,128,128]{2,1,0:T(8,128)(2,1)}), bf16[4,128,128]{2,1,0:T(8,128)(2,1)S(1)}, u32[]{:S(2)}, u32[]{:S(2)}) async-start(bf16[4,128,128]{2,1,0:T(8,128)(2,1)} %broadcast_in_dim.59), calls=%async_computation.1 | async-start | bytes 262144 | tf_op jit(solution)/shard_map/all_to_all | solution.py:33
  15.2 69.1 %copy-start.6 = (bf16[4,128,128]{2,1,0:T(8,128)(2,1)}, bf16[4,128,128]{2,1,0:T(8,128)(2,1)S(1)}, u32[]{:S(2)}) copy-start(bf16[4,128,128]{2,1,0:T(8,128)(2,1)S(1)} %all-to-all-done.1) | copy-start | bytes 393220
  15.2 24.4 %all-to-all-start.5 = ((bf16[8,128,512]{2,1,0:T(8,128)(2,1)}), bf16[8,128,512]{2,1,0:T(8,128)(2,1)S(1)}, u32[]{:S(2)}, u32[]{:S(2)}) async-start(bf16[8,128,512]{2,1,0:T(8,128)(2,1)} %shard_map.98), calls=%async_computation.5 | async-start | bytes 2097152 | tf_op jit(solution)/shard_map/all_to_all | solution.py:33
  39.6 19.9 %all-to-all-start.4 = ((bf16[8,128,512]{2,1,0:T(8,128)(2,1)}), bf16[8,128,512]{2,1,0:T(8,128)(2,1)S(1)}, u32[]{:S(2)}, u32[]{:S(2)}) async-start(bf16[8,128,512]{2,1,0:T(8,128)(2,1)} %shard_map.97), calls=%async_computation.4 | async-start | bytes 2097152 | tf_op jit(solution)/shard_map/all_to_all | solution.py:33
  59.5 4.3 %copy-start.2 = (bf16[8,128,512]{2,1,0:T(8,128)(2,1)}, bf16[8,128,512]{2,1,0:T(8,128)(2,1)S(1)}, u32[]{:S(2)}) copy-start(bf16[8,128,512]{2,1,0:T(8,128)(2,1)S(1)} %all-to-all-done.4) | copy-start | bytes 3145732
  59.5 19.2 %all-to-all-start.2 = ((bf16[8,128,512]{2,1,0:T(8,128)(2,1)}), bf16[8,128,512]{2,1,0:T(8,128)(2,1)}, u32[]{:S(2)}, u32[]{:S(2)}) async-start(bf16[8,128,512]{2,1,0:T(8,128)(2,1)} %shard_map.96), calls=%async_computation.2 | async-start | bytes 2097152 | tf_op jit(solution)/shard_map/all_to_all | solution.py:33
  68.7 17.0 %copy-start.11 = (s32[8]{0:T(128)S(1)}, s32[8]{0:T(128)}, u32[]{:S(2)}) copy-start(s32[8]{0:T(128)} %get-tuple-element.30.heads) | copy-start | bytes 100
  68.7 17.6 %copy-start.10 = (s32[8]{0:T(128)S(1)}, s32[8]{0:T(128)}, u32[]{:S(2)}) copy-start(s32[8]{0:T(128)} %get-tuple-element.29.heads) | copy-start | bytes 100
  68.7 18.1 %copy-start.9 = (s32[8]{0:T(128)S(1)}, s32[8]{0:T(128)}, u32[]{:S(2)}) copy-start(s32[8]{0:T(128)} %get-tuple-element.31.heads) | copy-start | bytes 100
  68.7 18.8 %copy-start.8 = (s32[8]{0:T(128)S(1)}, s32[8]{0:T(128)}, u32[]{:S(2)}) copy-start(s32[8]{0:T(128)} %get-tuple-element.28.heads) | copy-start | bytes 100
  68.7 31.2 %copy-start.1 = (bf16[2,64,4096]{2,1,0:T(8,128)(2,1)S(1)}, bf16[2,64,4096]{2,1,0:T(8,128)(2,1)}, u32[]{:S(2)}) copy-start(bf16[2,64,4096]{2,1,0:T(8,128)(2,1)} %param.14) | copy-start | bytes 3145732
  78.7 31.2 %all-to-all-start = ((bf16[8,128,512]{2,1,0:T(8,128)(2,1)}), bf16[8,128,512]{2,1,0:T(8,128)(2,1)}, u32[]{:S(2)}, u32[]{:S(2)}) async-start(bf16[8,128,512]{2,1,0:T(8,128)(2,1)} %shard_map.95), calls=%async_computation | async-start | bytes 2097152 | tf_op jit(solution)/shard_map/all_to_all | solution.py:33
  82.9 13.7 %collective-permute-start.1 = (bf16[512,128]{1,0:T(8,128)(2,1)S(1)}, bf16[512,128]{1,0:T(8,128)(2,1)S(1)}, u32[]{:S(2)}, u32[]{:S(2)}) collective-permute-start(bf16[512,128]{1,0:T(8,128)(2,1)S(1)} %bitcast.64), channel_id=1, source_target_pairs={{0,4},{1,5},{2,6},{3,7},{4,8},{5,9},{6,10},{7,11},{8,12},{9,13},{1... | collective-permute-start | bytes 393224 | tf_op jit(solution)/shard_map/ppermute | solution.py:197
  84.3 14.4 %collective-permute-start = (bf16[512,128]{1,0:T(8,128)(2,1)S(1)}, bf16[512,128]{1,0:T(8,128)(2,1)}, u32[]{:S(2)}, u32[]{:S(2)}) collective-permute-start(bf16[512,128]{1,0:T(8,128)(2,1)S(1)} %bitcast.65), channel_id=1, source_target_pairs={{0,28},{1,29},{2,30},{3,31},{4,0},{5,1},{6,2},{7,3},{8,4},{9,5},{1... | collective-permute-start | bytes 393224 | tf_op jit(solution)/shard_map/ppermute | solution.py:196
  96.6 0.7 copy-start.7
  99.9 4.6 %copy-start.3 = (bf16[8,128,512]{2,1,0:T(8,128)(2,1)S(1)}, bf16[8,128,512]{2,1,0:T(8,128)(2,1)}, u32[]{:S(2)}) copy-start(bf16[8,128,512]{2,1,0:T(8,128)(2,1)} %copy-done.2) | copy-start | bytes 3145732
  109.9 18.8 %all-to-all-start.6 = ((bf16[8,128,128]{2,1,0:T(8,128)(2,1)}), bf16[8,128,128]{2,1,0:T(8,128)(2,1)}, u32[]{:S(2)}, u32[]{:S(2)}) async-start(bf16[8,128,128]{2,1,0:T(8,128)(2,1)} %bitcast.16), calls=%async_computation.6 | async-start | bytes 524288 | tf_op jit(solution)/shard_map/all_to_all | solution.py:33
  128.7 10.2 %copy-start.4 = (bf16[1,128,4096]{2,1,0:T(8,128)(2,1)S(1)}, bf16[1,128,4096]{2,1,0:T(8,128)(2,1)}, u32[]{:S(2)}) copy-start(bf16[1,128,4096]{2,1,0:T(8,128)(2,1)} %param.8) | copy-start | bytes 3145732
  128.7 10.2 %all-to-all-start.3 = ((bf16[8,128,128]{2,1,0:T(8,128)(2,1)}), bf16[8,128,128]{2,1,0:T(8,128)(2,1)S(1)}, u32[]{:S(2)}, u32[]{:S(2)}) async-start(bf16[8,128,128]{2,1,0:T(8,128)(2,1)} %bitcast.13), calls=%async_computation.3 | async-start | bytes 524288 | tf_op jit(solution)/shard_map/all_to_all | solution.py:33
  141.4 24.5 %all-to-all-start.7 = ((bf16[8,36,16,128]{3,2,1,0:T(8,128)(2,1)}), bf16[8,36,16,128]{3,2,1,0:T(8,128)(2,1)S(1)}, u32[]{:S(2)}, u32[]{:S(2)}) async-start(bf16[8,36,16,128]{3,2,1,0:T(8,128)(2,1)} %copy.34), calls=%async_computation.7 | async-start | bytes 2359296 | tf_op jit(solution)/shard_map/all_to_all | solution.py:33

commit v2 on v1

v2 whole, which is shorter than its diff:
```python
import math

import jax
import jax.numpy as jnp
import numpy as np
from jax import lax
from jax.experimental import pallas as pl
from jax.experimental.pallas import tpu as pltpu
from jax.sharding import PartitionSpec as P

HEADS = 32
HD = 128
WIDTH = HEADS * HD
GROUP = 1024
PLANE = 512
RANK = 64
BOTH = 2 * RANK
ROWS = 128
ZS, YS = 8, 4
XS, CS = 4, 2
SLICES = XS * CS
MEMBERS = 8
PIECE = 16
RB = 256
BF16, F32 = jnp.bfloat16, jnp.float32

adapter_scale = 0.5

PLAIN_GROUPS = [[MEMBERS * g + i for i in range(MEMBERS)] for g in range(4)]
SHIFT_GROUPS = [[(MEMBERS * g + 4 + i) % HEADS for i in range(MEMBERS)] for g in range(4)]
PLAIN_SWAP = [(u, u ^ 4) for u in range(HEADS)]
CORE_SWAP = [(d, d ^ 1) for d in range(SLICES)]
ANYWHERE = pl.BlockSpec(memory_space=pl.ANY)
SCALARS = pl.BlockSpec(memory_space=pltpu.SMEM)

SPOTS = np.array(
    [[u % 4, u % 8, (u + 4) % 8, PLANE * (u // 4 % 2), PLANE * (1 - u // 4 % 2), 0, 0, 0] for u in range(HEADS)],
    np.int32,
)
SPOT_Y, SPOT_PLAIN, SPOT_SHIFT, SPOT_OWN_PLAIN, SPOT_OWN_SHIFT = range(5)


def z_shift(dz):
    return [(z * YS + y, ((z + dz) % ZS) * YS + y) for z in range(ZS) for y in range(YS)]


def y_shift(dy):
    return [(z * YS + y, z * YS + (y + dy) % YS) for z in range(ZS) for y in range(YS)]


def x_shift(dx):
    return [(x * CS + c, ((x + dx) % XS) * CS + c) for x in range(XS) for c in range(CS)]


def exchange(member, axis, groups=None):
    return lax.all_to_all(member, axis, 0, 0, tiled=True, axis_index_groups=groups)


def after(values, *others):
    return lax.optimization_barrier((values, others))[0]


def block(shape):
    return pl.BlockSpec(shape, lambda i, *s: (0,) * len(shape))


def dot_t(a, b):
    return lax.dot_general(a, b, (((1,), (1,)), ((), ())), preferred_element_type=F32)


def dot_0(a, b):
    return lax.dot_general(a, b, (((0,), (0,)), ((), ())), preferred_element_type=F32)


def call(kernel, name, scalars, in_specs, out_specs, out_shape, scratch, cost, vmem=40):
    return pl.pallas_call(
        kernel,
        name=name,
        out_shape=out_shape,
        grid_spec=pltpu.PrefetchScalarGridSpec(
            num_scalar_prefetch=scalars,
            grid=(1,),
            in_specs=in_specs,
            out_specs=out_specs,
            scratch_shapes=scratch,
        ),
        compiler_params=pltpu.CompilerParams(vmem_limit_bytes=vmem * 2**20),
        cost_estimate=pl.CostEstimate(flops=cost[0], bytes_accessed=cost[1], transcendentals=0),
    )


def prepare_first_kernel(flags, fk_ref, go_ref, out_ref, order, sems):
    def place(h, ones):
        flag = flags[h]
        order[jnp.where(flag > 0, HEADS // 2 + ones, h - ones)] = h
        return ones + jnp.where(flag > 0, 1, 0)

    lax.fori_loop(0, HEADS, place, 0, unroll=True)
    copies = []
    for p in range(2 * MEMBERS):
        item, seat = divmod(p, MEMBERS)
        cols = pl.ds(pl.multiple_of(order[p] * HD, HD), HD)
        for t, ref in enumerate((fk_ref, go_ref)):
            spot = out_ref.at[seat, :, pl.ds((2 * item + t) * HD, HD)]
            copies.append(pltpu.make_async_copy(ref.at[:, cols], spot, sems.at[p, t]))
            copies[-1].start()
    for copy in copies:
        copy.wait()


def prepare_first(flags, fk, go):
    return call(
        prepare_first_kernel,
        "prepare_first",
        1,
        [ANYWHERE] * 2,
        [block((MEMBERS, ROWS, 4 * HD)), SCALARS],
        (jax.ShapeDtypeStruct((MEMBERS, ROWS, 4 * HD), BF16), jax.ShapeDtypeStruct((HEADS,), jnp.int32)),
        [pltpu.SemaphoreType.DMA((2 * MEMBERS, 2))],
        (0, 2 * 10**6),
    )(flags, fk, go)


def prepare_rest_kernel(order, x_ref, down_ref, fq_ref, fv_ref, up_ref, fk_ref, go_ref, *refs):
    a_ref, b_ref, c_ref, low_ref, sems = refs
    copies = []
    for p in range(2 * MEMBERS):
        item, seat = divmod(p, MEMBERS)
        cols = pl.ds(pl.multiple_of(order[2 * MEMBERS + p] * HD, HD), HD)
        for t, ref in ((1, fk_ref), (3, go_ref)):
            spot = (b_ref, c_ref)[item].at[seat, :, pl.ds(t * HD, HD)]
            copies.append(pltpu.make_async_copy(ref.at[:, cols], spot, sems.at[p, t // 2]))
            copies[-1].start()
    low = dot_t(x_ref[...], down_ref[...]).astype(BF16)
    low_ref[...] = low
    for p in range(4 * MEMBERS):
        item, seat = divmod(p, MEMBERS)
        cols = pl.ds(pl.multiple_of(order[p] * HD, HD), HD)
        raised_q = jnp.dot(low[:, :RANK], up_ref[pl.ds(0, RANK), cols], preferred_element_type=F32)
        raised_v = jnp.dot(low[:, RANK:], up_ref[pl.ds(RANK, RANK), cols], preferred_element_type=F32)
        q = (fq_ref[:, cols].astype(F32) + adapter_scale * raised_q).astype(BF16)
        v = (fv_ref[:, cols].astype(F32) + adapter_scale * raised_v).astype(BF16)
        if item < 2:
            a_ref[seat, :, pl.ds(2 * item * HD, HD)] = q
            a_ref[seat, :, pl.ds((2 * item + 1) * HD, HD)] = v
        else:
            out = (b_ref, c_ref)[item - 2]
            out[seat, :, pl.ds(0, HD)] = q
            out[seat, :, pl.ds(2 * HD, HD)] = v
    for copy in copies:
        copy.wait()


def prepare_rest(order, x, down, fq, fv, up, fk, go):
    chunk = jax.ShapeDtypeStruct((MEMBERS, ROWS, 4 * HD), BF16)
    return call(
        prepare_rest_kernel,
        "prepare_rest",
        1,
        [block((ROWS, WIDTH)), block((BOTH, WIDTH))]
        + [block((ROWS, WIDTH))] * 2
        + [block((BOTH, WIDTH))]
        + [ANYWHERE] * 2,
        [block((MEMBERS, ROWS, 4 * HD))] * 3 + [block((ROWS, BOTH))],
        (chunk,) * 3 + (jax.ShapeDtypeStruct((ROWS, BOTH), BF16),),
        [pltpu.SemaphoreType.DMA((2 * MEMBERS, 2))],
        (4 * 10**9, 10 * 10**6),
    )(order, x, down, fq, fv, up, fk, go)


def turn_kernel(spot, x_ref, out_ref):
    x, core = spot[0] // CS, spot[0] % CS
    for u in range(HEADS):
        turned = x_ref[:, pl.ds(u * HD, HD)].T
        for d in range(SLICES):
            other = (core + d) % CS
            step = (d // CS - x + XS) % XS
            out_ref[other, step, pl.ds(u * PIECE, PIECE), :] = turned[d * PIECE : (d + 1) * PIECE]


def turn(spot, x):
    shape = (CS, XS, HEADS * PIECE, ROWS)
    return call(
        turn_kernel,
        "turn_input",
        1,
        [block(x.shape)],
        block(shape),
        jax.ShapeDtypeStruct(shape, BF16),
        [],
        (10**9, 2 * 10**6),
    )(spot, x)


def attention_kernel(kind, order, spot, q_ref, k_ref, v_ref, g_ref, up_ref, *refs):
    if kind == "first":
        back_ref, grads_ref, dv_acc = refs
    elif kind == "plain":
        before_ref, mine_ref, theirs_ref, grads_ref, dv_acc, sum_ref = refs
    else:
        before_ref, mine_ref, theirs_ref, back_ref, grads_ref, dv_acc, sum_ref = refs
    factor = 1.0 / math.sqrt(HD)
    bend = factor * math.log2(math.e)
    row_ids = lax.broadcasted_iota(jnp.int32, (RB, RB), 0)
    column_ids = lax.broadcasted_iota(jnp.int32, (RB, RB), 1)
    keep = column_ids <= row_ids
    for i in range(GROUP // RB):
        n = (i + 1) * RB
        rows = pl.ds(i * RB, RB)
        q = q_ref[rows, :]
        g = g_ref[rows, :]
        k = k_ref[pl.ds(0, n), :]
        v = v_ref[pl.ds(0, n), :]
        scores = dot_t(q, k)
        last = jnp.where(keep, scores[:, i * RB :], -1e30)
        scores = last if i == 0 else jnp.concatenate([scores[:, : i * RB], last], axis=1)
        top = jnp.max(scores, axis=1, keepdims=True)
        weights = jnp.exp2((scores - top) * bend)
        total = jnp.sum(weights, axis=1, keepdims=True)
        attention = (weights * (1.0 / total)).astype(BF16)
        output = jnp.dot(attention, v, preferred_element_type=F32)
        grad_attention = dot_t(g, v)
        center = jnp.sum(g.astype(F32) * output, axis=1, keepdims=True)
        grad_scores = (attention.astype(F32) * (grad_attention - center)).astype(BF16)
        dq = jnp.dot(grad_scores, k, preferred_element_type=F32) * factor
        grads_ref[rows, pl.ds(0, HD)] = dq.astype(BF16)
        dv = dot_0(attention, g)
        if i:
            dv_acc[pl.ds(0, i * RB), :] += dv[: i * RB]
        dv_acc[rows, :] = dv[i * RB :]
    dq = grads_ref[:, pl.ds(0, HD)]
    dv = dv_acc[...].astype(BF16)
    grads_ref[:, pl.ds(HD, HD)] = dv
    up = up_ref[...]
    lanes = lax.broadcasted_iota(jnp.int32, (GROUP, BOTH), 1)
    back = jnp.where(lanes < RANK, dot_t(dq, up), dot_t(dv, up))
    if kind == "first":
        back_ref[...] = back
        return
    sum_ref[...] = back + before_ref[...]
    if kind == "plain":
        own = pl.multiple_of(spot[SPOT_OWN_PLAIN], PLANE)
        mine_ref[...] = sum_ref[pl.ds(own, PLANE), :]
        theirs_ref[...] = sum_ref[pl.ds(PLANE - own, PLANE), :].astype(BF16)
    else:
        own = pl.multiple_of(spot[SPOT_OWN_SHIFT], PLANE)
        sum_ref[pl.ds(own, PLANE), :] += mine_ref[...] + theirs_ref[...].astype(F32)
        back_ref[...] = sum_ref[...].astype(BF16)


def attention_item(kind, item, order, spot, members, up, *more):
    arrays = [array.reshape(GROUP, 4 * HD) for array, _ in members]
    columns = [pl.BlockSpec((GROUP, HD), lambda i, *s, column=column: (0, column)) for _, column in members]
    seat = SPOT_PLAIN if item < 2 else SPOT_SHIFT
    shapes = {
        "first": [((GROUP, BOTH), F32)],
        "plain": [((PLANE, BOTH), F32), ((PLANE, BOTH), BF16)],
        "shifted": [((GROUP, BOTH), BF16)],
    }[kind] + [((GROUP, 2 * HD), BF16)]
    scratch = [pltpu.VMEM((GROUP, HD), F32)]
    if kind != "first":
        scratch.append(pltpu.VMEM((GROUP, BOTH), F32))

    def body(*refs):
        attention_kernel(kind, *refs)

    return call(
        body,
        "attention_" + kind,
        2,
        columns
        + [pl.BlockSpec((BOTH, HD), lambda i, order, spot: (0, order[item * MEMBERS + spot[seat]]))]
        + [block(array.shape) for array in more],
        [block(shape) for shape, _ in shapes],
        [jax.ShapeDtypeStruct(*shape) for shape in shapes],
        scratch,
        (4 * 10**9, 3 * 10**6),
    )(order, spot, *arrays, up, *more)


def up_gradient_kernel(spot, own_ref, later_ref, earlier_ref, *refs):
    out_ref, low_a, low_b = refs[-3:]
    y = spot[SPOT_Y]

    def fill(low, first, second):
        for half, ref in enumerate((first, second)):
            for s in range(YS):
                low[pl.ds(half * PLANE + s * ROWS, ROWS), :] = ref[(y - s + YS) % YS]

    @pl.when(spot[SPOT_OWN_PLAIN] == 0)
    def _():
        fill(low_a, own_ref, later_ref)
        fill(low_b, earlier_ref, own_ref)

    @pl.when(spot[SPOT_OWN_PLAIN] != 0)
    def _():
        fill(low_a, earlier_ref, own_ref)
        fill(low_b, own_ref, later_ref)

    for item, grads in enumerate(refs[:4]):
        low = (low_a, low_b)[item // 2][...]
        for m in range(2):
            part = adapter_scale * dot_0(low[:, m * RANK : (m + 1) * RANK], grads[:, pl.ds(m * HD, HD)])
            part = part.astype(BF16)
            for e in range(RANK // PIECE):
                d = m * (RANK // PIECE) + e
                out_ref[d, pl.ds(item * PIECE, PIECE), :] = part[e * PIECE : (e + 1) * PIECE]


def up_gradients(spot, own, later, earlier, grads):
    shape = (SLICES, 4 * PIECE, HD)
    return call(
        up_gradient_kernel,
        "up_gradients",
        1,
        [block((YS, ROWS, BOTH))] * 3 + [block((GROUP, 2 * HD))] * 4,
        block(shape),
        jax.ShapeDtypeStruct(shape, BF16),
        [pltpu.VMEM((GROUP, BOTH), BF16)] * 2,
        (2 * 10**9, 3 * 10**6),
    )(spot, own, later, earlier, *grads)


def gather_kernel(summed_ref, ups_ref, out_ref):
    back = jnp.sum(summed_ref[...].astype(F32), axis=0).astype(BF16)
    for d in range(SLICES):
        out_ref[d, pl.ds(0, ROWS), :] = back
    out_ref[:, pl.ds(ROWS, 4 * PIECE), :] = ups_ref[...]


def gather_parts(summed, ups):
    shape = (SLICES, ROWS + 4 * PIECE, HD)
    return call(
        gather_kernel,
        "gather_parts",
        0,
        [block(summed.shape), block(ups.shape)],
        block(shape),
        jax.ShapeDtypeStruct(shape, BF16),
        [],
        (10**7, 10**6),
    )(summed, ups)


def merge_kernel(order, spot, place, both_ref, *refs):
    x_refs, out_ref = refs[:-1], refs[-1]
    x, core = place[0] // CS, place[0] % CS
    total = jnp.zeros((HEADS * PIECE, BOTH), F32)
    for dx in range(XS):
        for other in range(CS):
            s = (x - dx + XS) % XS * CS + (core + other) % CS
            back = both_ref[s, pl.ds(0, ROWS), :]
            total += jnp.dot(x_refs[dx][other], back, preferred_element_type=F32)
    total = (adapter_scale * total).astype(BF16)
    for u in range(HEADS):
        out_ref[u, pl.ds(0, PIECE), :] = total[u * PIECE : (u + 1) * PIECE]
        out_ref[u, pl.ds(PIECE, PIECE), :] = jnp.zeros((PIECE, HD), BF16)
    ups = jnp.sum(both_ref[:, pl.ds(ROWS, 4 * PIECE), :].astype(F32), axis=0).astype(BF16)
    for item in range(4):
        seat = spot[SPOT_PLAIN if item < 2 else SPOT_SHIFT]
        head = order[item * MEMBERS + seat]
        out_ref[head, pl.ds(PIECE, PIECE), :] = ups[item * PIECE : (item + 1) * PIECE]


def merge(order, spot, place, both, pieces):
    shape = (HEADS, 2 * PIECE, HD)
    return call(
        merge_kernel,
        "merge_gradients",
        3,
        [block(both.shape)] + [block(piece.shape) for piece in pieces],
        block(shape),
        jax.ShapeDtypeStruct(shape, BF16),
        [],
        (2 * 10**8, 2 * 10**6),
    )(order, spot, place, both, *pieces)


def spread_kernel(in_ref, out_ref):
    total = jnp.sum(in_ref[...].astype(F32), axis=0)
    for d in range(SLICES):
        out_ref[d] = total


def spread(both):
    shape = (SLICES, 2 * PIECE, HD)
    return call(
        spread_kernel,
        "spread_sums",
        0,
        [block(both.shape)],
        block(shape),
        jax.ShapeDtypeStruct(shape, F32),
        [],
        (10**6, 10**6),
    )(both)


def finish_kernel(in_ref, down_ref, up_ref):
    down = in_ref[:, pl.ds(0, PIECE), :].reshape(HD, BOTH).T
    up = in_ref[:, pl.ds(PIECE, PIECE), :].reshape(BOTH, HD)
    for m in range(2):
        down_ref[m] = down[m * RANK : (m + 1) * RANK]
        up_ref[m] = up[m * RANK : (m + 1) * RANK]


def finish(both):
    shape = (2, RANK, HD)
    return call(
        finish_kernel,
        "finish",
        0,
        [block(both.shape)],
        [block(shape)] * 2,
        [jax.ShapeDtypeStruct(shape, F32)] * 2,
        [],
        (10**6, 10**6),
    )(both)


def per_device(
    normalized_input,
    frozen_queries,
    frozen_keys,
    frozen_values,
    output_gradient,
    adapter_down_maps,
    adapter_up_maps,
    shifted,
):
    tokens = normalized_input[0]
    spot = lax.dynamic_slice(jnp.asarray(SPOTS), (lax.axis_index("ulysses"), 0), (1, 8)).reshape(8)
    place = lax.axis_index("dp").reshape(1)
    up = adapter_up_maps.reshape(BOTH, WIDTH)
    down = adapter_down_maps.transpose(0, 2, 1).reshape(BOTH, WIDTH)

    sent_a, order = prepare_first(shifted.astype(jnp.int32), frozen_keys[0], output_gradient[0])
    keys_a = exchange(sent_a, "ulysses", PLAIN_GROUPS)
    sent_b, sent_c, sent_d, low = prepare_rest(
        order, tokens, down, frozen_queries[0], frozen_values[0], up, frozen_keys[0], output_gradient[0]
    )

    sent_b, keys_a, low, tokens = after((sent_b, keys_a, low, tokens))
    queries_b = exchange(sent_b, "ulysses", PLAIN_GROUPS)
    own = jnp.stack([low] + [lax.ppermute(low, "ulysses", y_shift(dy)) for dy in (1, 2, 3)])
    turned = turn(place, tokens)
    other = lax.ppermute(turned[1], "dp", CORE_SWAP)

    sent_c, keys_a, queries_b, own, turned, other = after((sent_c, keys_a, queries_b, own, turned, other))
    arrived_c = exchange(sent_c, "ulysses", SHIFT_GROUPS)
    later = lax.ppermute(own, "ulysses", z_shift(-1))
    earlier = lax.ppermute(own, "ulysses", z_shift(1))
    partial, grads_0 = attention_item(
        "first", 0, order, spot, [(queries_b, 0), (keys_a, 0), (queries_b, 1), (keys_a, 1)], up
    )
    mine, theirs, grads_1 = attention_item(
        "plain", 1, order, spot, [(queries_b, 2), (keys_a, 2), (queries_b, 3), (keys_a, 3)], up, partial
    )

    sent_d, arrived_c, later, earlier, theirs, turned, other = after(
        (sent_d, arrived_c, later, earlier, theirs, turned, other)
    )
    arrived_d = exchange(sent_d, "ulysses", SHIFT_GROUPS)
    theirs = lax.ppermute(theirs, "ulysses", PLAIN_SWAP)
    pieces = [jnp.stack([turned[0, dx], other[dx]]) for dx in range(XS)]
    pieces = pieces[:1] + [lax.ppermute(pieces[dx], "dp", x_shift(dx)) for dx in (1, 2, 3)]
    partial, grads_2 = attention_item("first", 2, order, spot, [(arrived_c, t) for t in range(4)], up)

    arrived_d, theirs, pieces = after((arrived_d, theirs, pieces), partial)
    partial, grads_3 = attention_item(
        "shifted", 3, order, spot, [(arrived_d, t) for t in range(4)], up, partial, mine, theirs
    )
    summed = exchange(partial.reshape(MEMBERS, ROWS, BOTH), "ulysses", SHIFT_GROUPS)
    ups = up_gradients(spot, own, later, earlier, (grads_0, grads_1, grads_2, grads_3))
    both = exchange(gather_parts(summed, ups), "dp")
    both = exchange(merge(order, spot, place, both, pieces), "ulysses")
    both = exchange(spread(both), "dp")
    grad_down, grad_up = finish(both)
    return (grad_down.transpose(0, 2, 1), grad_up)


def solution(mesh):
    rows = P("dp", "ulysses", None)
    in_specs = (rows, rows, rows, rows, rows, P(), P(), P())
    out_specs = (P(None, "ulysses", None), P(None, None, "ulysses"))
    return jax.shard_map(
        per_device, mesh=mesh, in_specs=in_specs, out_specs=out_specs, check_vma=False
    )
```

time: 196 us -> 163 us (0.83)
  waiting for transfers between devices: 58.4 us -> 19.8 us
  local copies, waits for them, and re-layouts: 9.18 us -> 30.6 us
  Pallas kernels: 41.9 us -> 28.3 us
  blocking collectives: 26.9 us -> 39.3 us
  starting transfers between devices: 49.7 us -> 43.2 us
  other arithmetic: 5.65 us -> 0.12 us
  matrix products: 2.13 us -> 0 us
    all_to_all x8 -> x5, waiting for transfers between devices: 48.4 us -> 5.56 us  [exchange(): lax.all_to_all(member, axis, 0, 0, tiled=True, axis_index_groups=groups)]
    unnamed x27 -> x84, local copies, waits for them, and re-layouts: 2.65 us -> 28.7 us
    all_to_all x8 -> x5, starting transfers between devices: 47 us -> 31.7 us  [exchange(): lax.all_to_all(member, axis, 0, 0, tiled=True, axis_index_groups=groups)]
    ppermute x0 -> x8, waiting for transfers between devices: none -> 14.3 us  [the longest x3 8.2 us: per_device(): lax.ppermute(low, 'ulysses', y_shift(dy))]
    pallas_call x8 -> x12, Pallas kernels: 41.9 us -> 28.3 us  [the longest x4 18.1 us: attention_item(): call(body, 'attention_' + kind, 2, columns + [pl.BlockSpec((BOTH, HD), la...]
    all_to_all x2 -> x3, blocking collectives: 26.9 us -> 39.3 us  [exchange(): lax.all_to_all(member, axis, 0, 0, tiled=True, axis_index_groups=groups)]
    ppermute x0 -> x8, starting transfers between devices: none -> 10 us  [the longest x3 5.33 us: per_device(): lax.ppermute(low, 'ulysses', y_shift(dy))]
    ppermute x1, waiting for transfers between devices: 8.6 us -> 0.01 us  [per_device(): earlier = lax.ppermute(own, 'ulysses', z_shift(1))]
  transfers between devices with their start and end apart: 10 -> 15, of which waited for: 7 -> 4; matrix products, arithmetic and copies ran while one was open for 4% -> 1% of each run, Pallas kernels for 22% -> 12%
where the time goes in v2:
time: 163 us; the launch traced here: 162 us
  starting transfers between devices  43.2 us (27%)
  blocking collectives  39.3 us (24%)
  local copies, waits for them, and re-layouts  30.6 us (19%)
  Pallas kernels  28.3 us (17%)
  waiting for transfers between devices  19.8 us (12%)
    all_to_all x3, blocking collectives, exchange(): lax.all_to_all(member, axis, 0, 0, tiled=True, axis_index_groups=groups)  39.3 us
    all_to_all x5, starting transfers between devices, exchange(): lax.all_to_all(member, axis, 0, 0, tiled=True, axis_index_groups=groups)  31.7 us
    unnamed x84, local copies, waits for them, and re-layouts  28.7 us
    pallas_call x4, Pallas kernels, attention_item(): call(body, 'attention_' + kind, 2, columns + [pl.BlockSpec((BOTH, HD), la...  18.1 us
    ppermute x3, waiting for transfers between devices, per_device(): lax.ppermute(low, 'ulysses', y_shift(dy))  8.2 us
    ppermute x3, waiting for transfers between devices, per_device(): lax.ppermute(pieces[dx], 'dp', x_shift(dx))  6.05 us
    all_to_all x5, waiting for transfers between devices, exchange(): lax.all_to_all(member, axis, 0, 0, tiled=True, axis_index_groups=groups)  5.56 us
    ppermute x3, starting transfers between devices, per_device(): lax.ppermute(low, 'ulysses', y_shift(dy))  5.33 us
  transfers between devices with their start and end apart: 15, of which 4 were waited for; matrix products, arithmetic and copies ran while one was open for 1% of the time, Pallas kernels for 12%

profile of v2, /device:TPU:1, one launch (start us, length us, event | category | flops | bytes accessed | tf_op | source)
XLA Modules:
  0.0 162.3 jit_solution(1631208890707621947)
XLA Ops:
  1.3 1.2 copy-done
  2.5 1.2 copy-done.2
  3.7 1.9 %prepare_first.1 = (bf16[8,128,512]{2,1,0:T(8,128)(2,1)S(1)}, s32[32]{0:T(128)S(1)}) custom-call(s32[32]{0:T(128)S(1)} %copy-done.12, bf16[128,4096]{1,0:T(8,128)(2,1)S(1)} %bitcast.32, bf16[128,4096]{1,0:T(8,128)(2,1)S(1)} %bitcast.34), custom_call_target="tpu_custom_call" | custom-call | bytes 2000000 | tf_op jit(solution)/shard_map/prepare_first/pallas_call | solution.py:112
  6.7 6.5 %all-to-all-start = ((bf16[8,128,512]{2,1,0:T(8,128)(2,1)}), bf16[8,128,512]{2,1,0:T(8,128)(2,1)S(1)}, u32[]{:S(2)}, u32[]{:S(2)}) async-start(bf16[8,128,512]{2,1,0:T(8,128)(2,1)} %copy-done.7), calls=%async_computation | async-start | bytes 2097152 | tf_op jit(solution)/shard_map/all_to_all | solution.py:56
  14.4 1.2 copy-done.14
  15.7 1.2 copy-done.15
  16.9 1.2 copy-done.16
  18.1 1.2 copy-done.18
  19.3 4.4 %prepare_rest.1 = (bf16[8,128,512]{2,1,0:T(8,128)(2,1)S(1)}, bf16[8,128,512]{2,1,0:T(8,128)(2,1)}, bf16[8,128,512]{2,1,0:T(8,128)(2,1)}, bf16[128,128]{1,0:T(8,128)(2,1)S(1)}) custom-call(s32[32]{0:T(128)S(1)} %get-tuple-element.42.order.refs_0_, bf16[128,4096]{1,0:T(8,128)(2,1)S(1)} %bitcast.56, bf16[128,4096]{1,0:T(8,128)(2,1)S(1)} %bitcast.53, ...), custom_call_target="tpu_custom_call" | custom-call | flops 4000000000 | bytes 10000000 | tf_op jit(solution)/shard_map/prepare_rest/pallas_call | solution.py:156
  24.7 3.4 %all-to-all-done = bf16[8,128,512]{2,1,0:T(8,128)(2,1)S(1)} async-done(((bf16[8,128,512]{2,1,0:T(8,128)(2,1)}), bf16[8,128,512]{2,1,0:T(8,128)(2,1)S(1)}, u32[]{:S(2)}, u32[]{:S(2)}) %all-to-all-start) | async-done | bytes 1048608 | tf_op jit(solution)/shard_map/all_to_all | solution.py:56
  28.1 3.7 %all-to-all-start.1 = ((bf16[8,128,512]{2,1,0:T(8,128)(2,1)}), bf16[8,128,512]{2,1,0:T(8,128)(2,1)S(1)}, u32[]{:S(2)}, u32[]{:S(2)}) async-start(bf16[8,128,512]{2,1,0:T(8,128)(2,1)} %copy-done.6), calls=%async_computation.1 | async-start | bytes 2097152 | tf_op jit(solution)/shard_map/all_to_all | solution.py:56
  34.3 1.8 %collective-permute-start = (bf16[128,128]{1,0:T(8,128)(2,1)S(1)}, bf16[128,128]{1,0:T(8,128)(2,1)S(1)}, u32[]{:S(2)}, u32[]{:S(2)}) collective-permute-start(bf16[128,128]{1,0:T(8,128)(2,1)S(1)} %get-tuple-element.50), channel_id=1, source_target_pairs={{0,1},{1,2},{2,3},{3,0},{4,5},{5,6},{6,7},{7,4},{8,9},{9,10},{10,1... | collective-permute-start | bytes 98312 | tf_op jit(solution)/shard_map/ppermute | solution.py:445
  36.0 2.4 %collective-permute-start.1 = (bf16[128,128]{1,0:T(8,128)(2,1)S(1)}, bf16[128,128]{1,0:T(8,128)(2,1)S(1)}, u32[]{:S(2)}, u32[]{:S(2)}) collective-permute-start(bf16[128,128]{1,0:T(8,128)(2,1)S(1)} %get-tuple-element.50), channel_id=1, source_target_pairs={{0,2},{1,3},{2,0},{3,1},{4,6},{5,7},{6,4},{7,5},{8,10},{9,11},{10,... | collective-permute-start | bytes 98312 | tf_op jit(solution)/shard_map/ppermute | solution.py:445
  39.6 8.2 %collective-permute-done = bf16[128,128]{1,0:T(8,128)(2,1)S(1)} collective-permute-done((bf16[128,128]{1,0:T(8,128)(2,1)S(1)}, bf16[128,128]{1,0:T(8,128)(2,1)S(1)}, u32[]{:S(2)}, u32[]{:S(2)}) %collective-permute-start) | collective-permute-done | bytes 32800 | tf_op jit(solution)/shard_map/ppermute | solution.py:445
  48.8 8.6 %all-to-all-start.2 = ((bf16[8,128,512]{2,1,0:T(8,128)(2,1)}), bf16[8,128,512]{2,1,0:T(8,128)(2,1)S(1)}, u32[]{:S(2)}, u32[]{:S(2)}) async-start(bf16[8,128,512]{2,1,0:T(8,128)(2,1)} %get-tuple-element.52), calls=%async_computation.2 | async-start | bytes 2097152 | tf_op jit(solution)/shard_map/all_to_all | solution.py:56
  58.2 1.4 collective-permute-start.5
  59.6 1.2 copy-done.5
  60.8 1.2 copy-done.19
  62.0 4.3 %attention_first.2 = (f32[1024,128]{1,0:T(8,128)S(1)}, bf16[1024,256]{1,0:T(8,128)(2,1)S(1)}) custom-call(s32[32]{0:T(128)S(1)} %get-tuple-element.42.order.refs_0_, s32[8]{0:T(128)S(1)} %dynamic-slice_bitcast_fusion.refs_1_.spot, bf16[1024,512]{1,0:T(8,128)(2,1)S(1)} %bitcast.44, bf16[1024,512]{1,0:T(8,128)(2,1)S(1)} %bitcast.36, ...), custom_call_target="tpu_custom_call" | custom-call | flops 4000000000 | bytes 3000000 | tf_op jit(solution)/shard_map/attention_first/pallas_call | solution.py:267
  67.2 4.4 %attention_plain.1 = (f32[512,128]{1,0:T(8,128)S(1)}, bf16[512,128]{1,0:T(8,128)(2,1)S(1)}, bf16[1024,256]{1,0:T(8,128)(2,1)S(1)}) custom-call(s32[32]{0:T(128)S(1)} %get-tuple-element.42.order.refs_0_, s32[8]{0:T(128)S(1)} %dynamic-slice_bitcast_fusion.refs_1_.spot, bf16[1024,512]{1,0:T(8,128)(2,1)S(1)} %bitcast.46, bf16[1024,512]{1,0:T(8,128)(2,1)S(1)} %bitcast.38, ...), custom_call_target="tpu_custom_call" | custom-call | flops 4000000000 | bytes 3000000 | tf_op jit(solution)/shard_map/attention_plain/pallas_call | solution.py:267
  74.4 6.4 %all-to-all-start.3 = ((bf16[8,128,512]{2,1,0:T(8,128)(2,1)}), bf16[8,128,512]{2,1,0:T(8,128)(2,1)S(1)}, u32[]{:S(2)}, u32[]{:S(2)}) async-start(bf16[8,128,512]{2,1,0:T(8,128)(2,1)} %get-tuple-element.60), calls=%async_computation.3 | async-start | bytes 2097152 | tf_op jit(solution)/shard_map/all_to_all | solution.py:56
  82.0 2.6 %collective-permute-start.9 = (bf16[2,512,128]{2,1,0:T(8,128)(2,1)S(1)}, bf16[2,512,128]{2,1,0:T(8,128)(2,1)S(1)}, u32[]{:S(2)}, u32[]{:S(2)}) collective-permute-start(bf16[2,512,128]{2,1,0:T(8,128)(2,1)S(1)} %pad_maximum_fusion.3), channel_id=1, source_target_pairs={{0,192},{32,224},{64,0},{96,32},{128,64},{160,96},{192,128},{224,1... | collective-permute-start | bytes 786440 | tf_op jit(solution)/shard_map/ppermute | solution.py:466
  86.1 4.3 %attention_first.3 = (f32[1024,128]{1,0:T(8,128)S(1)}, bf16[1024,256]{1,0:T(8,128)(2,1)S(1)}) custom-call(s32[32]{0:T(128)S(1)} %get-tuple-element.42.order.refs_0_, s32[8]{0:T(128)S(1)} %dynamic-slice_bitcast_fusion.refs_1_.spot, bf16[1024,512]{1,0:T(8,128)(2,1)S(1)} %bitcast.40, bf16[1024,512]{1,0:T(8,128)(2,1)S(1)} %bitcast.41, ...), custom_call_target="tpu_custom_call" | custom-call | flops 4000000000 | bytes 3000000 | tf_op jit(solution)/shard_map/attention_first/pallas_call | solution.py:267
  92.9 6.0 %collective-permute-done.7.refs_1_ = bf16[2,512,128]{2,1,0:T(8,128)(2,1)S(1)} collective-permute-done((bf16[2,512,128]{2,1,0:T(8,128)(2,1)S(1)}, bf16[2,512,128]{2,1,0:T(8,128)(2,1)S(1)}, u32[]{:S(2)}, u32[]{:S(2)}) %collective-permute-start.7) | collective-permute-done | bytes 262176 | tf_op jit(solution)/shard_map/ppermute | solution.py:466
  99.6 1.2 copy-done.21
  103.8 5.1 %attention_shifted.1 = (bf16[1024,128]{1,0:T(8,128)(2,1)}, bf16[1024,256]{1,0:T(8,128)(2,1)S(1)}) custom-call(s32[32]{0:T(128)S(1)} %get-tuple-element.42.order.refs_0_, s32[8]{0:T(128)S(1)} %dynamic-slice_bitcast_fusion.refs_1_.spot, bf16[1024,512]{1,0:T(8,128)(2,1)S(1)} %bitcast.48, bf16[1024,512]{1,0:T(8,128)(2,1)S(1)} %bitcast.49, ...), custom_call_target="tpu_custom_call" | custom-call | flops 4000000000 | bytes 3000000 | tf_op jit(solution)/shard_map/attention_shifted/pallas_call | solution.py:267
  109.7 6.5 %all-to-all-start.4 = ((bf16[8,128,128]{2,1,0:T(8,128)(2,1)}), bf16[8,128,128]{2,1,0:T(8,128)(2,1)S(1)}, u32[]{:S(2)}, u32[]{:S(2)}) async-start(bf16[8,128,128]{2,1,0:T(8,128)(2,1)} %bitcast.23), calls=%async_computation.4 | async-start | bytes 524288 | tf_op jit(solution)/shard_map/all_to_all | solution.py:56
  117.2 1.7 %up_gradients.1.ups_ref = bf16[8,64,128]{2,1,0:T(8,128)(2,1)S(1)} custom-call(s32[8]{0:T(128)S(1)} %dynamic-slice_bitcast_fusion.refs_1_.spot, bf16[4,128,128]{2,1,0:T(8,128)(2,1)S(1)} %pad_maximum_fusion.4.own_ref, bf16[4,128,128]{2,1,0:T(8,128)(2,1)S(1)} %copy-done.23, bf16[4,128,128]{2,1,0:T(8,128)(2,1)S(1)} %copy-done.25, ...), custom_call_target="tpu_custom_call" | custom-call | flops 2000000000 | bytes 3000000 | tf_op jit(solution)/shard_map/up_gradients/pallas_call | solution.py:312
  118.9 2.2 %all-to-all-done.4.summed_ref = bf16[8,128,128]{2,1,0:T(8,128)(2,1)S(1)} async-done(((bf16[8,128,128]{2,1,0:T(8,128)(2,1)}), bf16[8,128,128]{2,1,0:T(8,128)(2,1)S(1)}, u32[]{:S(2)}, u32[]{:S(2)}) %all-to-all-start.4) | async-done | bytes 262176 | tf_op jit(solution)/shard_map/all_to_all | solution.py:56
  121.2 13.7 %all_to_all.40.both_ref = bf16[8,192,128]{2,1,0:T(8,128)(2,1)S(1)} all-to-all(bf16[8,192,128]{2,1,0:T(8,128)(2,1)S(1)} %gather_parts.1), channel_id=1, replica_groups=mesh['dp'=8,'ulysses'=32] {'dp'}, dimensions={0} | all-to-all | bytes 786432 | tf_op jit(solution)/shard_map/all_to_all | solution.py:56
  135.8 15.4 %all_to_all.41.in_ref = bf16[32,32,128]{2,1,0:T(8,128)(2,1)S(1)} all-to-all(bf16[32,32,128]{2,1,0:T(8,128)(2,1)S(1)} %merge_gradients.1), channel_id=1, replica_groups=mesh['dp'=8,'ulysses'=32] {'ulysses'}, dimensions={0} | all-to-all | bytes 524288 | tf_op jit(solution)/shard_map/all_to_all | solution.py:56
  151.3 10.2 %all_to_all.42.in_ref = f32[8,32,128]{2,1,0:T(8,128)S(1)} all-to-all(f32[8,32,128]{2,1,0:T(8,128)S(1)} %spread_sums.1), channel_id=1, replica_groups=mesh['dp'=8,'ulysses'=32] {'dp'}, dimensions={0} | all-to-all | bytes 262144 | tf_op jit(solution)/shard_map/all_to_all | solution.py:56
  (106 shorter events, 25.3 us)
Async XLA Ops:
  1.3 1.2 copy-start
  2.5 1.2 copy-start.2
  6.7 6.5 %copy-start.1 = (bf16[1,128,4096]{2,1,0:T(8,128)(2,1)S(1)}, bf16[1,128,4096]{2,1,0:T(8,128)(2,1)}, u32[]{:S(2)}) copy-start(bf16[1,128,4096]{2,1,0:T(8,128)(2,1)} %param.11) | copy-start | bytes 3145732
  6.7 6.5 %copy-start.3 = (bf16[1,128,4096]{2,1,0:T(8,128)(2,1)S(1)}, bf16[1,128,4096]{2,1,0:T(8,128)(2,1)}, u32[]{:S(2)}) copy-start(bf16[1,128,4096]{2,1,0:T(8,128)(2,1)} %param.13) | copy-start | bytes 3145732
  6.7 21.4 %all-to-all-start = ((bf16[8,128,512]{2,1,0:T(8,128)(2,1)}), bf16[8,128,512]{2,1,0:T(8,128)(2,1)S(1)}, u32[]{:S(2)}, u32[]{:S(2)}) async-start(bf16[8,128,512]{2,1,0:T(8,128)(2,1)} %copy-done.7), calls=%async_computation | async-start | bytes 2097152 | tf_op jit(solution)/shard_map/all_to_all | solution.py:56
  13.2 1.2 copy-start.13
  14.4 1.2 copy-start.14
  15.7 1.2 copy-start.15
  16.9 1.2 copy-start.16
  28.1 19.7 %all-to-all-start.1 = ((bf16[8,128,512]{2,1,0:T(8,128)(2,1)}), bf16[8,128,512]{2,1,0:T(8,128)(2,1)S(1)}, u32[]{:S(2)}, u32[]{:S(2)}) async-start(bf16[8,128,512]{2,1,0:T(8,128)(2,1)} %copy-done.6), calls=%async_computation.1 | async-start | bytes 2097152 | tf_op jit(solution)/shard_map/all_to_all | solution.py:56
  33.4 14.4 %collective-permute-start.3 = (bf16[4,512,128]{2,1,0:T(8,128)(2,1)S(1)}, bf16[4,512,128]{2,1,0:T(8,128)(2,1)}, u32[]{:S(2)}, u32[]{:S(2)}) collective-permute-start(bf16[4,512,128]{2,1,0:T(8,128)(2,1)S(1)} %slice_bitcast_fusion), channel_id=1, source_target_pairs={{0,32},{32,0},{64,96},{96,64},{128,160},{160,128},{192,224},{224,1... | collective-permute-start | bytes 1572872 | tf_op jit(solution)/shard_map/ppermute | solution.py:447
  34.3 13.5 %collective-permute-start = (bf16[128,128]{1,0:T(8,128)(2,1)S(1)}, bf16[128,128]{1,0:T(8,128)(2,1)S(1)}, u32[]{:S(2)}, u32[]{:S(2)}) collective-permute-start(bf16[128,128]{1,0:T(8,128)(2,1)S(1)} %get-tuple-element.50), channel_id=1, source_target_pairs={{0,1},{1,2},{2,3},{3,0},{4,5},{5,6},{6,7},{7,4},{8,9},{9,10},{10,1... | collective-permute-start | bytes 98312 | tf_op jit(solution)/shard_map/ppermute | solution.py:445
  36.0 11.8 %collective-permute-start.1 = (bf16[128,128]{1,0:T(8,128)(2,1)S(1)}, bf16[128,128]{1,0:T(8,128)(2,1)S(1)}, u32[]{:S(2)}, u32[]{:S(2)}) collective-permute-start(bf16[128,128]{1,0:T(8,128)(2,1)S(1)} %get-tuple-element.50), channel_id=1, source_target_pairs={{0,2},{1,3},{2,0},{3,1},{4,6},{5,7},{6,4},{7,5},{8,10},{9,11},{10,... | collective-permute-start | bytes 98312 | tf_op jit(solution)/shard_map/ppermute | solution.py:445
  38.4 9.4 %collective-permute-start.2 = (bf16[128,128]{1,0:T(8,128)(2,1)S(1)}, bf16[128,128]{1,0:T(8,128)(2,1)S(1)}, u32[]{:S(2)}, u32[]{:S(2)}) collective-permute-start(bf16[128,128]{1,0:T(8,128)(2,1)S(1)} %get-tuple-element.50), channel_id=1, source_target_pairs={{0,3},{1,0},{2,1},{3,2},{4,7},{5,4},{6,5},{7,6},{8,11},{9,8},{10,9... | collective-permute-start | bytes 98312 | tf_op jit(solution)/shard_map/ppermute | solution.py:445
  48.8 24.9 %all-to-all-start.2 = ((bf16[8,128,512]{2,1,0:T(8,128)(2,1)}), bf16[8,128,512]{2,1,0:T(8,128)(2,1)S(1)}, u32[]{:S(2)}, u32[]{:S(2)}) async-start(bf16[8,128,512]{2,1,0:T(8,128)(2,1)} %get-tuple-element.52), calls=%async_computation.2 | async-start | bytes 2097152 | tf_op jit(solution)/shard_map/all_to_all | solution.py:56
  58.1 15.6 %collective-permute-start.4 = (bf16[4,128,128]{2,1,0:T(8,128)(2,1)S(1)}, bf16[4,128,128]{2,1,0:T(8,128)(2,1)S(1)}, u32[]{:S(2)}, u32[]{:S(2)}) collective-permute-start(bf16[4,128,128]{2,1,0:T(8,128)(2,1)S(1)} %pad_maximum_fusion.4.own_ref), channel_id=1, source_target_pairs={{0,28},{1,29},{2,30},{3,31},{4,0},{5,1},{6,2},{7,3},{8,4},{9,5},{1... | collective-permute-start | bytes 393224 | tf_op jit(solution)/shard_map/ppermute | solution.py:451
  58.2 15.5 %collective-permute-start.5 = (bf16[4,128,128]{2,1,0:T(8,128)(2,1)S(1)}, bf16[4,128,128]{2,1,0:T(8,128)(2,1)S(1)}, u32[]{:S(2)}, u32[]{:S(2)}) collective-permute-start(bf16[4,128,128]{2,1,0:T(8,128)(2,1)S(1)} %pad_maximum_fusion.4.own_ref), channel_id=1, source_target_pairs={{0,4},{1,5},{2,6},{3,7},{4,8},{5,9},{6,10},{7,11},{8,12},{9,13},{1... | collective-permute-start | bytes 393224 | tf_op jit(solution)/shard_map/ppermute | solution.py:452
  74.4 25.2 %all-to-all-start.3 = ((bf16[8,128,512]{2,1,0:T(8,128)(2,1)}), bf16[8,128,512]{2,1,0:T(8,128)(2,1)S(1)}, u32[]{:S(2)}, u32[]{:S(2)}) async-start(bf16[8,128,512]{2,1,0:T(8,128)(2,1)} %get-tuple-element.60), calls=%async_computation.3 | async-start | bytes 2097152 | tf_op jit(solution)/shard_map/all_to_all | solution.py:56
  82.0 4.1 %copy-start.20 = (bf16[2,64,4096]{2,1,0:T(8,128)(2,1)S(1)}, bf16[2,64,4096]{2,1,0:T(8,128)(2,1)}, u32[]{:S(2)}) copy-start(bf16[2,64,4096]{2,1,0:T(8,128)(2,1)} %param.15) | copy-start | bytes 3145732
  82.0 10.0 %collective-permute-start.9 = (bf16[2,512,128]{2,1,0:T(8,128)(2,1)S(1)}, bf16[2,512,128]{2,1,0:T(8,128)(2,1)S(1)}, u32[]{:S(2)}, u32[]{:S(2)}) collective-permute-start(bf16[2,512,128]{2,1,0:T(8,128)(2,1)S(1)} %pad_maximum_fusion.3), channel_id=1, source_target_pairs={{0,192},{32,224},{64,0},{96,32},{128,64},{160,96},{192,128},{224,1... | collective-permute-start | bytes 786440 | tf_op jit(solution)/shard_map/ppermute | solution.py:466
  84.6 7.4 %collective-permute-start.8 = (bf16[2,512,128]{2,1,0:T(8,128)(2,1)S(1)}, bf16[2,512,128]{2,1,0:T(8,128)(2,1)S(1)}, u32[]{:S(2)}, u32[]{:S(2)}) collective-permute-start(bf16[2,512,128]{2,1,0:T(8,128)(2,1)S(1)} %pad_maximum_fusion.2), channel_id=1, source_target_pairs={{0,128},{32,160},{64,192},{96,224},{128,0},{160,32},{192,64},{224,... | collective-permute-start | bytes 786440 | tf_op jit(solution)/shard_map/ppermute | solution.py:466
  85.2 13.7 %collective-permute-start.7 = (bf16[2,512,128]{2,1,0:T(8,128)(2,1)S(1)}, bf16[2,512,128]{2,1,0:T(8,128)(2,1)S(1)}, u32[]{:S(2)}, u32[]{:S(2)}) collective-permute-start(bf16[2,512,128]{2,1,0:T(8,128)(2,1)S(1)} %pad_maximum_fusion.1), channel_id=1, source_target_pairs={{0,64},{32,96},{64,128},{96,160},{128,192},{160,224},{192,0},{224,... | collective-permute-start | bytes 786440 | tf_op jit(solution)/shard_map/ppermute | solution.py:466
  86.1 5.2 %collective-permute-start.6 = (bf16[512,128]{1,0:T(8,128)(2,1)S(1)}, bf16[512,128]{1,0:T(8,128)(2,1)S(1)}, u32[]{:S(2)}, u32[]{:S(2)}) collective-permute-start(bf16[512,128]{1,0:T(8,128)(2,1)S(1)} %copy-done.27), channel_id=1, source_target_pairs={{0,4},{1,5},{2,6},{3,7},{4,0},{5,1},{6,2},{7,3},{8,12},{9,13},{10,... | collective-permute-start | bytes 393224 | tf_op jit(solution)/shard_map/ppermute | solution.py:464
  99.6 1.2 copy-start.21
  103.7 12.4 %copy-start.31 = (bf16[1024,256]{1,0:T(8,128)(2,1)S(1)}, bf16[1024,256]{1,0:T(8,128)(2,1)}, u32[]{:S(2)}) copy-start(bf16[1024,256]{1,0:T(8,128)(2,1)} %copy-done.30) | copy-start | bytes 1572868
  103.7 12.4 %copy-start.33 = (bf16[1024,256]{1,0:T(8,128)(2,1)S(1)}, bf16[1024,256]{1,0:T(8,128)(2,1)}, u32[]{:S(2)}) copy-start(bf16[1024,256]{1,0:T(8,128)(2,1)} %copy-done.32) | copy-start | bytes 1572868
  103.8 12.4 %copy-start.35 = (bf16[1024,256]{1,0:T(8,128)(2,1)S(1)}, bf16[1024,256]{1,0:T(8,128)(2,1)}, u32[]{:S(2)}) copy-start(bf16[1024,256]{1,0:T(8,128)(2,1)} %copy-done.34) | copy-start | bytes 1572868
  109.7 6.5 %copy-start.23 = (bf16[4,128,128]{2,1,0:T(8,128)(2,1)S(1)}, bf16[4,128,128]{2,1,0:T(8,128)(2,1)}, u32[]{:S(2)}) copy-start(bf16[4,128,128]{2,1,0:T(8,128)(2,1)} %copy-done.22) | copy-start | bytes 393220
  109.7 6.5 %copy-start.25 = (bf16[4,128,128]{2,1,0:T(8,128)(2,1)S(1)}, bf16[4,128,128]{2,1,0:T(8,128)(2,1)}, u32[]{:S(2)}) copy-start(bf16[4,128,128]{2,1,0:T(8,128)(2,1)} %copy-done.24) | copy-start | bytes 393220
  109.7 11.4 %all-to-all-start.4 = ((bf16[8,128,128]{2,1,0:T(8,128)(2,1)}), bf16[8,128,128]{2,1,0:T(8,128)(2,1)S(1)}, u32[]{:S(2)}, u32[]{:S(2)}) async-start(bf16[8,128,128]{2,1,0:T(8,128)(2,1)} %bitcast.23), calls=%async_computation.4 | async-start | bytes 524288 | tf_op jit(solution)/shard_map/all_to_all | solution.py:56
  121.2 13.7 %copy-start.9 = (bf16[2,512,128]{2,1,0:T(8,128)(2,1)S(1)}, bf16[2,512,128]{2,1,0:T(8,128)(2,1)}, u32[]{:S(2)}) copy-start(bf16[2,512,128]{2,1,0:T(8,128)(2,1)} %copy-done.8) | copy-start | bytes 786436
  121.2 13.7 %copy-start.11 = (bf16[2,512,128]{2,1,0:T(8,128)(2,1)S(1)}, bf16[2,512,128]{2,1,0:T(8,128)(2,1)}, u32[]{:S(2)}) copy-start(bf16[2,512,128]{2,1,0:T(8,128)(2,1)} %copy-done.10) | copy-start | bytes 786436
  (25 other events, 22.3 us)

commit v3 on v2

--- a/solution.py
+++ b/solution.py
@@ -30,7 +30,7 @@
 SHIFT_GROUPS = [[(MEMBERS * g + 4 + i) % HEADS for i in range(MEMBERS)] for g in range(4)]
 PLAIN_SWAP = [(u, u ^ 4) for u in range(HEADS)]
 CORE_SWAP = [(d, d ^ 1) for d in range(SLICES)]
-ANYWHERE = pl.BlockSpec(memory_space=pl.ANY)
+ANYWHERE = pl.BlockSpec(memory_space=pltpu.HBM)
 SCALARS = pl.BlockSpec(memory_space=pltpu.SMEM)
 
 SPOTS = np.array(
@@ -72,7 +72,7 @@
     return lax.dot_general(a, b, (((0,), (0,)), ((), ())), preferred_element_type=F32)
 
 
-def call(kernel, name, scalars, in_specs, out_specs, out_shape, scratch, cost, vmem=40):
+def call(kernel, name, scalars, in_specs, out_specs, out_shape, scratch, cost):
     return pl.pallas_call(
         kernel,
         name=name,
@@ -84,88 +84,114 @@
             out_specs=out_specs,
             scratch_shapes=scratch,
         ),
-        compiler_params=pltpu.CompilerParams(vmem_limit_bytes=vmem * 2**20),
         cost_estimate=pl.CostEstimate(flops=cost[0], bytes_accessed=cost[1], transcendentals=0),
     )
 
 
-def prepare_first_kernel(flags, fk_ref, go_ref, out_ref, order, sems):
+def order_heads(flags, order):
     def place(h, ones):
         flag = flags[h]
         order[jnp.where(flag > 0, HEADS // 2 + ones, h - ones)] = h
         return ones + jnp.where(flag > 0, 1, 0)
 
     lax.fori_loop(0, HEADS, place, 0, unroll=True)
+
+
+def fetch_heads(first, order, fq_ref, fk_ref, fv_ref, go_ref, out_ref, q_in, v_in, sems):
     copies = []
     for p in range(2 * MEMBERS):
         item, seat = divmod(p, MEMBERS)
-        cols = pl.ds(pl.multiple_of(order[p] * HD, HD), HD)
-        for t, ref in enumerate((fk_ref, go_ref)):
-            spot = out_ref.at[seat, :, pl.ds((2 * item + t) * HD, HD)]
-            copies.append(pltpu.make_async_copy(ref.at[:, cols], spot, sems.at[p, t]))
-            copies[-1].start()
-    for copy in copies:
-        copy.wait()
-
-
-def prepare_first(flags, fk, go):
-    return call(
-        prepare_first_kernel,
-        "prepare_first",
-        1,
-        [ANYWHERE] * 2,
-        [block((MEMBERS, ROWS, 4 * HD)), SCALARS],
-        (jax.ShapeDtypeStruct((MEMBERS, ROWS, 4 * HD), BF16), jax.ShapeDtypeStruct((HEADS,), jnp.int32)),
-        [pltpu.SemaphoreType.DMA((2 * MEMBERS, 2))],
-        (0, 2 * 10**6),
-    )(flags, fk, go)
-
-
-def prepare_rest_kernel(order, x_ref, down_ref, fq_ref, fv_ref, up_ref, fk_ref, go_ref, *refs):
-    a_ref, b_ref, c_ref, low_ref, sems = refs
-    copies = []
+        cols = pl.ds(pl.multiple_of(order[first + p] * HD, HD), HD)
+        places = (
+            (fq_ref, q_in.at[p]),
+            (fv_ref, v_in.at[p]),
+            (fk_ref, out_ref.at[seat, :, pl.ds((4 * item + 1) * HD, HD)]),
+            (go_ref, out_ref.at[seat, :, pl.ds((4 * item + 3) * HD, HD)]),
+        )
+        row = [
+            pltpu.make_async_copy(ref.at[:, cols], spot, sems.at[p, t])
+            for t, (ref, spot) in enumerate(places)
+        ]
+        for copy in row:
+            copy.start()
+        copies.append(row)
+    return copies
+
+
+def raise_heads(first, order, low, up_ref, copies, q_in, v_in, out_ref):
     for p in range(2 * MEMBERS):
         item, seat = divmod(p, MEMBERS)
-        cols = pl.ds(pl.multiple_of(order[2 * MEMBERS + p] * HD, HD), HD)
-        for t, ref in ((1, fk_ref), (3, go_ref)):
-            spot = (b_ref, c_ref)[item].at[seat, :, pl.ds(t * HD, HD)]
-            copies.append(pltpu.make_async_copy(ref.at[:, cols], spot, sems.at[p, t // 2]))
-            copies[-1].start()
-    low = dot_t(x_ref[...], down_ref[...]).astype(BF16)
-    low_ref[...] = low
-    for p in range(4 * MEMBERS):
-        item, seat = divmod(p, MEMBERS)
-        cols = pl.ds(pl.multiple_of(order[p] * HD, HD), HD)
+        cols = pl.ds(pl.multiple_of(order[first + p] * HD, HD), HD)
         raised_q = jnp.dot(low[:, :RANK], up_ref[pl.ds(0, RANK), cols], preferred_element_type=F32)
         raised_v = jnp.dot(low[:, RANK:], up_ref[pl.ds(RANK, RANK), cols], preferred_element_type=F32)
-        q = (fq_ref[:, cols].astype(F32) + adapter_scale * raised_q).astype(BF16)
-        v = (fv_ref[:, cols].astype(F32) + adapter_scale * raised_v).astype(BF16)
-        if item < 2:
-            a_ref[seat, :, pl.ds(2 * item * HD, HD)] = q
-            a_ref[seat, :, pl.ds((2 * item + 1) * HD, HD)] = v
-        else:
-            out = (b_ref, c_ref)[item - 2]
-            out[seat, :, pl.ds(0, HD)] = q
-            out[seat, :, pl.ds(2 * HD, HD)] = v
-    for copy in copies:
-        copy.wait()
-
-
-def prepare_rest(order, x, down, fq, fv, up, fk, go):
-    chunk = jax.ShapeDtypeStruct((MEMBERS, ROWS, 4 * HD), BF16)
-    return call(
-        prepare_rest_kernel,
-        "prepare_rest",
+        copies[p][0].wait()
+        copies[p][1].wait()
+        q = (q_in[p].astype(F32) + adapter_scale * raised_q).astype(BF16)
+        v = (v_in[p].astype(F32) + adapter_scale * raised_v).astype(BF16)
+        out_ref[seat, :, pl.ds(4 * item * HD, HD)] = q
+        out_ref[seat, :, pl.ds((4 * item + 2) * HD, HD)] = v
+    for row in copies:
+        row[2].wait()
+        row[3].wait()
+
+
+def prepare_plain_kernel(flags, x_hbm, down_hbm, up_hbm, *refs):
+    frozen, (out_ref, order, low_ref, x_in, down_in, up_in, q_in, v_in, sems, whole_sems) = refs[:4], refs[4:]
+    wholes = [
+        pltpu.make_async_copy(source, spot, whole_sems.at[t])
+        for t, (source, spot) in enumerate(((x_hbm, x_in), (down_hbm, down_in), (up_hbm, up_in)))
+    ]
+    for copy in wholes:
+        copy.start()
+    order_heads(flags, order)
+    copies = fetch_heads(0, order, *frozen, out_ref, q_in, v_in, sems)
+    wholes[0].wait()
+    wholes[1].wait()
+    low = dot_t(x_in[...], down_in[...]).astype(BF16)
+    low_ref[...] = low
+    wholes[2].wait()
+    raise_heads(0, order, low, up_in, copies, q_in, v_in, out_ref)
+
+
+HEAD_SCRATCH = [pltpu.VMEM((2 * MEMBERS, ROWS, HD), BF16)] * 2 + [pltpu.SemaphoreType.DMA((2 * MEMBERS, 4))]
+
+
+def prepare_plain(flags, x, down, up, frozen):
+    return call(
+        prepare_plain_kernel,
+        "prepare_plain",
         1,
-        [block((ROWS, WIDTH)), block((BOTH, WIDTH))]
-        + [block((ROWS, WIDTH))] * 2
-        + [block((BOTH, WIDTH))]
-        + [ANYWHERE] * 2,
-        [block((MEMBERS, ROWS, 4 * HD))] * 3 + [block((ROWS, BOTH))],
-        (chunk,) * 3 + (jax.ShapeDtypeStruct((ROWS, BOTH), BF16),),
-        [pltpu.SemaphoreType.DMA((2 * MEMBERS, 2))],
-        (4 * 10**9, 10 * 10**6),
-    )(order, x, down, fq, fv, up, fk, go)
+        [ANYWHERE] * 7,
+        [block((MEMBERS, ROWS, 8 * HD)), SCALARS, block((ROWS, BOTH))],
+        (
+            jax.ShapeDtypeStruct((MEMBERS, ROWS, 8 * HD), BF16),
+            jax.ShapeDtypeStruct((HEADS,), jnp.int32),
+            jax.ShapeDtypeStruct((ROWS, BOTH), BF16),
+        ),
+        [pltpu.VMEM((ROWS, WIDTH), BF16), pltpu.VMEM((BOTH, WIDTH), BF16), pltpu.VMEM((BOTH, WIDTH), BF16)]
+        + HEAD_SCRATCH
+        + [pltpu.SemaphoreType.DMA((3,))],
+        (10**9, 8 * 10**6),
+    )(flags, x, down, up, *frozen)
+
+
+def prepare_shifted_kernel(order, low_ref, up_ref, *refs):
+    frozen, (out_ref, q_in, v_in, sems) = refs[:4], refs[4:]
+    copies = fetch_heads(2 * MEMBERS, order, *frozen, out_ref, q_in, v_in, sems)
+    raise_heads(2 * MEMBERS, order, low_ref[...], up_ref, copies, q_in, v_in, out_ref)
+
+
+def prepare_shifted(order, low, up, frozen):
+    return call(
+        prepare_shifted_kernel,
+        "prepare_shifted",
+        1,
+        [block((ROWS, BOTH)), block((BOTH, WIDTH))] + [ANYWHERE] * 4,
+        block((MEMBERS, ROWS, 8 * HD)),
+        jax.ShapeDtypeStruct((MEMBERS, ROWS, 8 * HD), BF16),
+        HEAD_SCRATCH,
+        (10**9, 8 * 10**6),
+    )(order, low, up, *frozen)
 
 
 def turn_kernel(spot, x_ref, out_ref):
@@ -249,7 +275,7 @@
 
 
 def attention_item(kind, item, order, spot, members, up, *more):
-    arrays = [array.reshape(GROUP, 4 * HD) for array, _ in members]
+    arrays = [array.reshape(GROUP, 8 * HD) for array, _ in members]
     columns = [pl.BlockSpec((GROUP, HD), lambda i, *s, column=column: (0, column)) for _, column in members]
     seat = SPOT_PLAIN if item < 2 else SPOT_SHIFT
     shapes = {
@@ -434,41 +460,30 @@
     up = adapter_up_maps.reshape(BOTH, WIDTH)
     down = adapter_down_maps.transpose(0, 2, 1).reshape(BOTH, WIDTH)
 
-    sent_a, order = prepare_first(shifted.astype(jnp.int32), frozen_keys[0], output_gradient[0])
-    keys_a = exchange(sent_a, "ulysses", PLAIN_GROUPS)
-    sent_b, sent_c, sent_d, low = prepare_rest(
-        order, tokens, down, frozen_queries[0], frozen_values[0], up, frozen_keys[0], output_gradient[0]
-    )
-
-    sent_b, keys_a, low, tokens = after((sent_b, keys_a, low, tokens))
-    queries_b = exchange(sent_b, "ulysses", PLAIN_GROUPS)
+    frozen = (frozen_queries[0], frozen_keys[0], frozen_values[0], output_gradient[0])
+    sent, order, low = prepare_plain(shifted.astype(jnp.int32), tokens, down, up, frozen)
+    plain = exchange(sent, "ulysses", PLAIN_GROUPS)
+    sent = prepare_shifted(order, low, up, frozen)
     own = jnp.stack([low] + [lax.ppermute(low, "ulysses", y_shift(dy)) for dy in (1, 2, 3)])
-    turned = turn(place, tokens)
+    turned = turn(place, after(tokens, low))
     other = lax.ppermute(turned[1], "dp", CORE_SWAP)
 
-    sent_c, keys_a, queries_b, own, turned, other = after((sent_c, keys_a, queries_b, own, turned, other))
-    arrived_c = exchange(sent_c, "ulysses", SHIFT_GROUPS)
+    sent, plain, own, turned, other = after((sent, plain, own, turned, other))
+    late = exchange(sent, "ulysses", SHIFT_GROUPS)
     later = lax.ppermute(own, "ulysses", z_shift(-1))
     earlier = lax.ppermute(own, "ulysses", z_shift(1))
-    partial, grads_0 = attention_item(
-        "first", 0, order, spot, [(queries_b, 0), (keys_a, 0), (queries_b, 1), (keys_a, 1)], up
-    )
-    mine, theirs, grads_1 = attention_item(
-        "plain", 1, order, spot, [(queries_b, 2), (keys_a, 2), (queries_b, 3), (keys_a, 3)], up, partial
-    )
-
-    sent_d, arrived_c, later, earlier, theirs, turned, other = after(
-        (sent_d, arrived_c, later, earlier, theirs, turned, other)
-    )
-    arrived_d = exchange(sent_d, "ulysses", SHIFT_GROUPS)
-    theirs = lax.ppermute(theirs, "ulysses", PLAIN_SWAP)
     pieces = [jnp.stack([turned[0, dx], other[dx]]) for dx in range(XS)]
     pieces = pieces[:1] + [lax.ppermute(pieces[dx], "dp", x_shift(dx)) for dx in (1, 2, 3)]
-    partial, grads_2 = attention_item("first", 2, order, spot, [(arrived_c, t) for t in range(4)], up)
-
-    arrived_d, theirs, pieces = after((arrived_d, theirs, pieces), partial)
+    partial, grads_0 = attention_item("first", 0, order, spot, [(plain, t) for t in range(4)], up)
+    mine, theirs, grads_1 = attention_item(
+        "plain", 1, order, spot, [(plain, 4 + t) for t in range(4)], up, partial
+    )
+    theirs = lax.ppermute(theirs, "ulysses", PLAIN_SWAP)
+
+    late, theirs, pieces, later, earlier = after((late, theirs, pieces, later, earlier))
+    partial, grads_2 = attention_item("first", 2, order, spot, [(late, t) for t in range(4)], up)
     partial, grads_3 = attention_item(
-        "shifted", 3, order, spot, [(arrived_d, t) for t in range(4)], up, partial, mine, theirs
+        "shifted", 3, order, spot, [(late, 4 + t) for t in range(4)], up, partial, mine, theirs
     )
     summed = exchange(partial.reshape(MEMBERS, ROWS, BOTH), "ulysses", SHIFT_GROUPS)
     ups = up_gradients(spot, own, later, earlier, (grads_0, grads_1, grads_2, grads_3))

time: 163 us -> 164 us (level)
  Pallas kernels: 28.3 us -> 57.3 us
  local copies, waits for them, and re-layouts: 30.6 us -> 6.34 us
  starting transfers between devices: 43.2 us -> 35 us
  blocking collectives: 39.3 us -> 44.9 us
  waiting for transfers between devices: 19.8 us -> 16.5 us
    unnamed x84 -> x20, local copies, waits for them, and re-layouts: 28.7 us -> 2.09 us
    all_to_all x5 -> x3, starting transfers between devices: 31.7 us -> 22 us  [exchange(): lax.all_to_all(member, axis, 0, 0, tiled=True, axis_index_groups=groups)]
    pallas_call x2, Pallas kernels: 6.37 us -> 16 us  [the longest x1 8.75 us: prepare_plain(): call(prepare_plain_kernel, 'prepare_plain', 1, [ANYWHERE] * 7, [block((ME...]
    pallas_call x4, Pallas kernels: 18.1 us -> 26.5 us  [attention_item(): call(body, 'attention_' + kind, 2, columns + [pl.BlockSpec((BOTH, HD), la...]
    ppermute x3, waiting for transfers between devices: 6.05 us -> 0.01 us  [per_device(): lax.ppermute(pieces[dx], 'dp', x_shift(dx))]
    all_to_all x3, blocking collectives: 39.3 us -> 44.9 us  [exchange(): lax.all_to_all(member, axis, 0, 0, tiled=True, axis_index_groups=groups)]
    all_to_all x5 -> x3, waiting for transfers between devices: 5.56 us -> 0.87 us  [exchange(): lax.all_to_all(member, axis, 0, 0, tiled=True, axis_index_groups=groups)]
    ppermute x1, waiting for transfers between devices: 0.01 us -> 3.28 us  [per_device(): theirs = lax.ppermute(theirs, 'ulysses', PLAIN_SWAP)]
  transfers between devices with their start and end apart: 15 -> 13, of which waited for: 4 -> 6; matrix products, arithmetic and copies ran while one was open for 1% -> 4% of each run, Pallas kernels for 12% -> 17%
where the time goes in v3:
time: 164 us; the launch traced here: 162 us
  Pallas kernels  57.3 us (35%)
  blocking collectives  44.9 us (27%)
  starting transfers between devices  35 us (21%)
  waiting for transfers between devices  16.5 us (10%)
  local copies, waits for them, and re-layouts  6.34 us (4%)
    all_to_all x3, blocking collectives, exchange(): lax.all_to_all(member, axis, 0, 0, tiled=True, axis_index_groups=groups)  44.9 us
    pallas_call x4, Pallas kernels, attention_item(): call(body, 'attention_' + kind, 2, columns + [pl.BlockSpec((BOTH, HD), la...  26.5 us
    all_to_all x3, starting transfers between devices, exchange(): lax.all_to_all(member, axis, 0, 0, tiled=True, axis_index_groups=groups)  22 us
    ppermute x3, waiting for transfers between devices, per_device(): lax.ppermute(low, 'ulysses', y_shift(dy))  10.5 us
    pallas_call x1, Pallas kernels, prepare_plain(): call(prepare_plain_kernel, 'prepare_plain', 1, [ANYWHERE] * 7, [block((ME...  8.75 us
    pallas_call x1, Pallas kernels, prepare_shifted(): call(prepare_shifted_kernel, 'prepare_shifted', 1, [block((ROWS, BOTH)),...  7.25 us
    ppermute x3, starting transfers between devices, per_device(): lax.ppermute(pieces[dx], 'dp', x_shift(dx))  5.24 us
    ppermute x3, starting transfers between devices, per_device(): lax.ppermute(low, 'ulysses', y_shift(dy))  4.11 us
  transfers between devices with their start and end apart: 13, of which 6 were waited for; matrix products, arithmetic and copies ran while one was open for 4% of the time, Pallas kernels for 17%

profile of v3, /device:TPU:1, one launch (start us, length us, event | category | flops | bytes accessed | tf_op | source)
XLA Modules:
  0.0 162.4 jit_solution(15090777023217356786)
XLA Ops:
  0.6 8.7 %prepare_plain.1 = (bf16[8,128,1024]{2,1,0:T(8,128)(2,1)}, s32[32]{0:T(128)}, bf16[128,128]{1,0:T(8,128)(2,1)}) custom-call(s32[32]{0:T(128)} %flags.1, bf16[128,4096]{1,0:T(8,128)(2,1)} %bitcast.53, bf16[128,4096]{1,0:T(8,128)(2,1)} %bitcast.52, bf16[128,4096]{1,0:T(8,128)(2,1)} %bitcast.38, bf16[128,4096]{1,0:T(8,128)(2,1)} %bitcast.30, ...), custom_call_target="tpu_custom_call" | custom-call | flops 1000000000 | bytes 8000000 | tf_op jit(solution)/shard_map/prepare_plain/pallas_call | solution.py:160
  9.4 6.4 %all-to-all-start = ((bf16[8,128,1024]{2,1,0:T(8,128)(2,1)}), bf16[8,128,1024]{2,1,0:T(8,128)(2,1)S(1)}, u32[]{:S(2)}, u32[]{:S(2)}) async-start(bf16[8,128,1024]{2,1,0:T(8,128)(2,1)} %get-tuple-element.32), calls=%async_computation | async-start | bytes 4194304 | tf_op jit(solution)/shard_map/all_to_all | solution.py:56
  15.8 2.5 %turn_input.1 = bf16[2,4,512,128]{3,2,1,0:T(8,128)(2,1)} custom-call(s32[1]{0:T(128)} %bitcast.9.spot.place, bf16[128,4096]{1,0:T(8,128)(2,1)} %bitcast.54), custom_call_target="tpu_custom_call" | custom-call | flops 1000000000 | bytes 2000000 | tf_op jit(solution)/shard_map/turn_input/pallas_call | solution.py:209
  18.3 1.9 %slice_bitcast_fusion = bf16[4,512,128]{2,1,0:T(8,128)(2,1)} fusion(bf16[2,4,512,128]{3,2,1,0:T(8,128)(2,1)} %turn_input.1), kind=kLoop, calls=%fused_computation | loop fusion | bytes 1048576 | tf_op jit(solution)/shard_map/squeeze | solution.py:469
  20.2 1.0 collective-permute-start.3
  21.1 3.0 %collective-permute-start.2 = (bf16[128,128]{1,0:T(8,128)(2,1)}, bf16[128,128]{1,0:T(8,128)(2,1)S(1)}, u32[]{:S(2)}, u32[]{:S(2)}) collective-permute-start(bf16[128,128]{1,0:T(8,128)(2,1)} %get-tuple-element.31.low_ref), channel_id=1, source_target_pairs={{0,3},{1,0},{2,1},{3,2},{4,7},{5,4},{6,5},{7,6},{8,11},{9,8},{10,9... | collective-permute-start | bytes 98312 | tf_op jit(solution)/shard_map/ppermute | solution.py:467
  25.2 7.2 %prepare_shifted.1 = bf16[8,128,1024]{2,1,0:T(8,128)(2,1)} custom-call(s32[32]{0:T(128)} %get-tuple-element.30.order.refs_0_, bf16[128,128]{1,0:T(8,128)(2,1)} %get-tuple-element.31.low_ref, bf16[128,4096]{1,0:T(8,128)(2,1)} %bitcast.39, bf16[128,4096]{1,0:T(8,128)(2,1)} %bitcast.31, bf16[128,4096]{1,0:T(8,128)(2,1)} %bitcast.33, ...), custom_call_target="tpu_custom_call" | custom-call | flops 1000000000 | bytes 8000000 | tf_op jit(solution)/shard_map/prepare_shifted/pallas_call | solution.py:185
  32.5 8.3 %collective-permute-done.2 = bf16[128,128]{1,0:T(8,128)(2,1)S(1)} collective-permute-done((bf16[128,128]{1,0:T(8,128)(2,1)}, bf16[128,128]{1,0:T(8,128)(2,1)S(1)}, u32[]{:S(2)}, u32[]{:S(2)}) %collective-permute-start.2) | collective-permute-done | bytes 32800 | tf_op jit(solution)/shard_map/ppermute | solution.py:467
  41.7 1.3 collective-permute-done
  43.8 1.4 copy-done
  45.2 9.3 %all-to-all-start.1 = ((bf16[8,128,1024]{2,1,0:T(8,128)(2,1)}), bf16[8,128,1024]{2,1,0:T(8,128)(2,1)}, u32[]{:S(2)}, u32[]{:S(2)}) async-start(bf16[8,128,1024]{2,1,0:T(8,128)(2,1)} %prepare_shifted.1), calls=%async_computation.1 | async-start | bytes 4194304 | tf_op jit(solution)/shard_map/all_to_all | solution.py:56
  54.5 1.2 dynamic-slice_bitcast_fusion.refs_1_.spot
  55.7 2.7 %collective-permute-start.8 = (bf16[4,128,128]{2,1,0:T(8,128)(2,1)S(1)}, bf16[4,128,128]{2,1,0:T(8,128)(2,1)S(1)}, u32[]{:S(2)}, u32[]{:S(2)}) collective-permute-start(bf16[4,128,128]{2,1,0:T(8,128)(2,1)S(1)} %pad_maximum_fusion.4.own_ref), channel_id=1, source_target_pairs={{0,28},{1,29},{2,30},{3,31},{4,0},{5,1},{6,2},{7,3},{8,4},{9,5},{1... | collective-permute-start | bytes 393224 | tf_op jit(solution)/shard_map/ppermute | solution.py:473
  58.4 1.1 fusion
  59.6 1.3 collective-permute-start.5
  60.9 2.5 %collective-permute-start.6 = (bf16[2,512,128]{2,1,0:T(8,128)(2,1)S(1)}, bf16[2,512,128]{2,1,0:T(8,128)(2,1)S(1)}, u32[]{:S(2)}, u32[]{:S(2)}) collective-permute-start(bf16[2,512,128]{2,1,0:T(8,128)(2,1)S(1)} %pad_maximum_fusion.2), channel_id=1, source_target_pairs={{0,128},{32,160},{64,192},{96,224},{128,0},{160,32},{192,64},{224,... | collective-permute-start | bytes 786440 | tf_op jit(solution)/shard_map/ppermute | solution.py:476
  63.5 1.4 collective-permute-start.7
  64.9 6.5 %attention_first.2 = (f32[1024,128]{1,0:T(8,128)}, bf16[1024,256]{1,0:T(8,128)(2,1)}) custom-call(s32[32]{0:T(128)} %get-tuple-element.30.order.refs_0_, s32[8]{0:T(128)} %dynamic-slice_bitcast_fusion.refs_1_.spot, bf16[1024,1024]{1,0:T(8,128)(2,1)} %bitcast.44, bf16[1024,1024]{1,0:T(8,128)(2,1)} %bitcast.45, bf16[1024,1024]{1,0:T(8,128)(2,1)} %bitcast.46, ...), custom_call_target="tpu_custom_call" | custom-call | flops 4000000000 | bytes 3000000 | tf_op jit(solution)/shard_map/attention_first/pallas_call | solution.py:293
  71.4 6.8 %attention_plain.1 = (f32[512,128]{1,0:T(8,128)}, bf16[512,128]{1,0:T(8,128)(2,1)}, bf16[1024,256]{1,0:T(8,128)(2,1)}) custom-call(s32[32]{0:T(128)} %get-tuple-element.30.order.refs_0_, s32[8]{0:T(128)} %dynamic-slice_bitcast_fusion.refs_1_.spot, bf16[1024,1024]{1,0:T(8,128)(2,1)} %bitcast.48, bf16[1024,1024]{1,0:T(8,128)(2,1)} %bitcast.49, ...), custom_call_target="tpu_custom_call" | custom-call | flops 4000000000 | bytes 3000000 | tf_op jit(solution)/shard_map/attention_plain/pallas_call | solution.py:293
  78.2 1.8 %collective-permute-done.9.earlier_ref = bf16[4,128,128]{2,1,0:T(8,128)(2,1)S(1)} collective-permute-done((bf16[4,128,128]{2,1,0:T(8,128)(2,1)S(1)}, bf16[4,128,128]{2,1,0:T(8,128)(2,1)S(1)}, u32[]{:S(2)}, u32[]{:S(2)}) %collective-permute-start.9) | collective-permute-done | bytes 131104 | tf_op jit(solution)/shard_map/ppermute | solution.py:474
  80.8 3.3 %collective-permute-done.4.refs_9_ = bf16[512,128]{1,0:T(8,128)(2,1)S(1)} collective-permute-done((bf16[512,128]{1,0:T(8,128)(2,1)}, bf16[512,128]{1,0:T(8,128)(2,1)S(1)}, u32[]{:S(2)}, u32[]{:S(2)}) %collective-permute-start.4) | collective-permute-done | bytes 131104 | tf_op jit(solution)/shard_map/ppermute | solution.py:481
  84.1 6.5 %attention_first.3 = (f32[1024,128]{1,0:T(8,128)}, bf16[1024,256]{1,0:T(8,128)(2,1)}) custom-call(s32[32]{0:T(128)} %get-tuple-element.30.order.refs_0_, s32[8]{0:T(128)} %dynamic-slice_bitcast_fusion.refs_1_.spot, bf16[1024,1024]{1,0:T(8,128)(2,1)} %bitcast.20.refs_2_.refs_3_.refs_4_.refs_5_, bf16[1024,1024]{1,0:T(8,128)(2,1)} %bitcast.20.refs_2_.refs_3_.refs_4_.refs_5_, ...), custom_call_target="tpu_custom_call" | custom-call | flops 4000000000 | bytes 3000000 | tf_op jit(solution)/shard_map/attention_first/pallas_call | solution.py:293
  90.7 6.7 %attention_shifted.1 = (bf16[1024,128]{1,0:T(8,128)(2,1)}, bf16[1024,256]{1,0:T(8,128)(2,1)}) custom-call(s32[32]{0:T(128)} %get-tuple-element.30.order.refs_0_, s32[8]{0:T(128)} %dynamic-slice_bitcast_fusion.refs_1_.spot, bf16[1024,1024]{1,0:T(8,128)(2,1)} %bitcast.20.refs_2_.refs_3_.refs_4_.refs_5_, ...), custom_call_target="tpu_custom_call" | custom-call | flops 4000000000 | bytes 3000000 | tf_op jit(solution)/shard_map/attention_shifted/pallas_call | solution.py:293
  97.4 6.3 %all-to-all-start.2 = ((bf16[8,128,128]{2,1,0:T(8,128)(2,1)}), bf16[8,128,128]{2,1,0:T(8,128)(2,1)S(1)}, u32[]{:S(2)}, u32[]{:S(2)}) async-start(bf16[8,128,128]{2,1,0:T(8,128)(2,1)} %bitcast.55), calls=%async_computation.2 | async-start | bytes 524288 | tf_op jit(solution)/shard_map/all_to_all | solution.py:56
  103.7 4.1 %up_gradients.1.ups_ref = bf16[8,64,128]{2,1,0:T(8,128)(2,1)} custom-call(s32[8]{0:T(128)} %dynamic-slice_bitcast_fusion.refs_1_.spot, bf16[4,128,128]{2,1,0:T(8,128)(2,1)} %copy-done.6, bf16[4,128,128]{2,1,0:T(8,128)(2,1)} %copy-done.8, bf16[4,128,128]{2,1,0:T(8,128)(2,1)} %copy-done.7, bf16[1024,256]{1,0:T(8,128)(2,1)} %get-tuple-element.48.refs_0_, ...), custom_call_target="tpu_custom_call" | custom-call | flops 2000000000 | bytes 3000000 | tf_op jit(solution)/shard_map/up_gradients/pallas_call | solution.py:338
  109.3 1.8 %gather_parts.1 = bf16[8,192,128]{2,1,0:T(8,128)(2,1)} custom-call(bf16[8,128,128]{2,1,0:T(8,128)(2,1)} %copy-done.1, bf16[8,64,128]{2,1,0:T(8,128)(2,1)} %up_gradients.1.ups_ref), custom_call_target="tpu_custom_call" | custom-call | flops 10000000 | bytes 1000000 | tf_op jit(solution)/shard_map/gather_parts/pallas_call | solution.py:359
  111.1 17.1 %all_to_all.30.both_ref = bf16[8,192,128]{2,1,0:T(8,128)(2,1)} all-to-all(bf16[8,192,128]{2,1,0:T(8,128)(2,1)} %gather_parts.1), channel_id=1, replica_groups=mesh['dp'=8,'ulysses'=32] {'dp'}, dimensions={0} | all-to-all | bytes 786432 | tf_op jit(solution)/shard_map/all_to_all | solution.py:56
  128.2 3.1 %merge_gradients.1 = bf16[32,32,128]{2,1,0:T(8,128)(2,1)} custom-call(s32[32]{0:T(128)} %get-tuple-element.30.order.refs_0_, s32[8]{0:T(128)} %dynamic-slice_bitcast_fusion.refs_1_.spot, s32[1]{0:T(128)} %bitcast.9.spot.place, bf16[8,192,128]{2,1,0:T(8,128)(2,1)} %all_to_all.30.both_ref, bf16[2,512,128]{2,1,0:T(8,128)(2,1)} %pad_maximum_fusion.refs_0_, ...), custom_call_target="tpu_custom_call" | custom-call | flops 200000000 | bytes 2000000 | tf_op jit(solution)/shard_map/merge_gradients/pallas_call | solution.py:393
  131.3 15.6 %all_to_all.31.in_ref = bf16[32,32,128]{2,1,0:T(8,128)(2,1)} all-to-all(bf16[32,32,128]{2,1,0:T(8,128)(2,1)} %merge_gradients.1), channel_id=1, replica_groups=mesh['dp'=8,'ulysses'=32] {'ulysses'}, dimensions={0} | all-to-all | bytes 524288 | tf_op jit(solution)/shard_map/all_to_all | solution.py:56
  146.9 1.7 %spread_sums.1 = f32[8,32,128]{2,1,0:T(8,128)} custom-call(bf16[32,32,128]{2,1,0:T(8,128)(2,1)} %all_to_all.31.in_ref), custom_call_target="tpu_custom_call" | custom-call | flops 1000000 | bytes 1000000 | tf_op jit(solution)/shard_map/spread_sums/pallas_call | solution.py:413
  148.6 12.3 %all_to_all.32.in_ref = f32[8,32,128]{2,1,0:T(8,128)} all-to-all(f32[8,32,128]{2,1,0:T(8,128)} %spread_sums.1), channel_id=1, replica_groups=mesh['dp'=8,'ulysses'=32] {'dp'}, dimensions={0} | all-to-all | bytes 262144 | tf_op jit(solution)/shard_map/all_to_all | solution.py:56
  160.8 1.6 %finish.1 = (f32[2,64,128]{2,1,0:T(8,128)}, f32[2,64,128]{2,1,0:T(8,128)}) custom-call(f32[8,32,128]{2,1,0:T(8,128)} %all_to_all.32.in_ref), custom_call_target="tpu_custom_call" | custom-call | flops 1000000 | bytes 1000000 | tf_op jit(solution)/shard_map/finish/pallas_call | solution.py:435
  (38 shorter events, 5.3 us)
Async XLA Ops:
  9.4 34.4 %all-to-all-start = ((bf16[8,128,1024]{2,1,0:T(8,128)(2,1)}), bf16[8,128,1024]{2,1,0:T(8,128)(2,1)S(1)}, u32[]{:S(2)}, u32[]{:S(2)}) async-start(bf16[8,128,1024]{2,1,0:T(8,128)(2,1)} %get-tuple-element.32), calls=%async_computation | async-start | bytes 4194304 | tf_op jit(solution)/shard_map/all_to_all | solution.py:56
  20.2 23.6 %collective-permute-start.3 = (bf16[4,512,128]{2,1,0:T(8,128)(2,1)}, bf16[4,512,128]{2,1,0:T(8,128)(2,1)}, u32[]{:S(2)}, u32[]{:S(2)}) collective-permute-start(bf16[4,512,128]{2,1,0:T(8,128)(2,1)} %slice_bitcast_fusion), channel_id=1, source_target_pairs={{0,32},{32,0},{64,96},{96,64},{128,160},{160,128},{192,224},{224,1... | collective-permute-start | bytes 1572872 | tf_op jit(solution)/shard_map/ppermute | solution.py:469
  21.1 19.7 %collective-permute-start.2 = (bf16[128,128]{1,0:T(8,128)(2,1)}, bf16[128,128]{1,0:T(8,128)(2,1)S(1)}, u32[]{:S(2)}, u32[]{:S(2)}) collective-permute-start(bf16[128,128]{1,0:T(8,128)(2,1)} %get-tuple-element.31.low_ref), channel_id=1, source_target_pairs={{0,3},{1,0},{2,1},{3,2},{4,7},{5,4},{6,5},{7,6},{8,11},{9,8},{10,9... | collective-permute-start | bytes 98312 | tf_op jit(solution)/shard_map/ppermute | solution.py:467
  24.1 17.6 %collective-permute-start.1 = (bf16[128,128]{1,0:T(8,128)(2,1)}, bf16[128,128]{1,0:T(8,128)(2,1)S(1)}, u32[]{:S(2)}, u32[]{:S(2)}) collective-permute-start(bf16[128,128]{1,0:T(8,128)(2,1)} %get-tuple-element.31.low_ref), channel_id=1, source_target_pairs={{0,2},{1,3},{2,0},{3,1},{4,6},{5,7},{6,4},{7,5},{8,10},{9,11},{10,... | collective-permute-start | bytes 98312 | tf_op jit(solution)/shard_map/ppermute | solution.py:467
  24.6 18.3 %collective-permute-start = (bf16[128,128]{1,0:T(8,128)(2,1)}, bf16[128,128]{1,0:T(8,128)(2,1)S(1)}, u32[]{:S(2)}, u32[]{:S(2)}) collective-permute-start(bf16[128,128]{1,0:T(8,128)(2,1)} %get-tuple-element.31.low_ref), channel_id=1, source_target_pairs={{0,1},{1,2},{2,3},{3,0},{4,5},{5,6},{6,7},{7,4},{8,9},{9,10},{10,1... | collective-permute-start | bytes 98312 | tf_op jit(solution)/shard_map/ppermute | solution.py:467
  43.8 12.0 %copy-start.6 = (bf16[4,128,128]{2,1,0:T(8,128)(2,1)}, bf16[4,128,128]{2,1,0:T(8,128)(2,1)S(1)}, u32[]{:S(2)}) copy-start(bf16[4,128,128]{2,1,0:T(8,128)(2,1)S(1)} %pad_maximum_fusion.4.own_ref) | copy-start | bytes 393220
  43.8 14.6 %copy-start.2 = (bf16[2,4,512,128]{3,2,1,0:T(8,128)(2,1)S(1)}, bf16[2,4,512,128]{3,2,1,0:T(8,128)(2,1)}, u32[]{:S(2)}) copy-start(bf16[2,4,512,128]{3,2,1,0:T(8,128)(2,1)} %turn_input.1) | copy-start | bytes 3145732
  43.8 1.4 copy-start
  45.2 39.0 %all-to-all-start.1 = ((bf16[8,128,1024]{2,1,0:T(8,128)(2,1)}), bf16[8,128,1024]{2,1,0:T(8,128)(2,1)}, u32[]{:S(2)}, u32[]{:S(2)}) async-start(bf16[8,128,1024]{2,1,0:T(8,128)(2,1)} %prepare_shifted.1), calls=%async_computation.1 | async-start | bytes 4194304 | tf_op jit(solution)/shard_map/all_to_all | solution.py:56
  55.7 24.3 %collective-permute-start.9 = (bf16[4,128,128]{2,1,0:T(8,128)(2,1)S(1)}, bf16[4,128,128]{2,1,0:T(8,128)(2,1)S(1)}, u32[]{:S(2)}, u32[]{:S(2)}) collective-permute-start(bf16[4,128,128]{2,1,0:T(8,128)(2,1)S(1)} %pad_maximum_fusion.4.own_ref), channel_id=1, source_target_pairs={{0,4},{1,5},{2,6},{3,7},{4,8},{5,9},{6,10},{7,11},{8,12},{9,13},{1... | collective-permute-start | bytes 393224 | tf_op jit(solution)/shard_map/ppermute | solution.py:474
  55.7 25.1 %collective-permute-start.8 = (bf16[4,128,128]{2,1,0:T(8,128)(2,1)S(1)}, bf16[4,128,128]{2,1,0:T(8,128)(2,1)S(1)}, u32[]{:S(2)}, u32[]{:S(2)}) collective-permute-start(bf16[4,128,128]{2,1,0:T(8,128)(2,1)S(1)} %pad_maximum_fusion.4.own_ref), channel_id=1, source_target_pairs={{0,28},{1,29},{2,30},{3,31},{4,0},{5,1},{6,2},{7,3},{8,4},{9,5},{1... | collective-permute-start | bytes 393224 | tf_op jit(solution)/shard_map/ppermute | solution.py:473
  59.6 24.5 %collective-permute-start.5 = (bf16[2,512,128]{2,1,0:T(8,128)(2,1)S(1)}, bf16[2,512,128]{2,1,0:T(8,128)(2,1)S(1)}, u32[]{:S(2)}, u32[]{:S(2)}) collective-permute-start(bf16[2,512,128]{2,1,0:T(8,128)(2,1)S(1)} %pad_maximum_fusion.1), channel_id=1, source_target_pairs={{0,64},{32,96},{64,128},{96,160},{128,192},{160,224},{192,0},{224,... | collective-permute-start | bytes 786440 | tf_op jit(solution)/shard_map/ppermute | solution.py:476
  60.9 23.2 %collective-permute-start.6 = (bf16[2,512,128]{2,1,0:T(8,128)(2,1)S(1)}, bf16[2,512,128]{2,1,0:T(8,128)(2,1)S(1)}, u32[]{:S(2)}, u32[]{:S(2)}) collective-permute-start(bf16[2,512,128]{2,1,0:T(8,128)(2,1)S(1)} %pad_maximum_fusion.2), channel_id=1, source_target_pairs={{0,128},{32,160},{64,192},{96,224},{128,0},{160,32},{192,64},{224,... | collective-permute-start | bytes 786440 | tf_op jit(solution)/shard_map/ppermute | solution.py:476
  63.5 20.6 %collective-permute-start.7 = (bf16[2,512,128]{2,1,0:T(8,128)(2,1)S(1)}, bf16[2,512,128]{2,1,0:T(8,128)(2,1)S(1)}, u32[]{:S(2)}, u32[]{:S(2)}) collective-permute-start(bf16[2,512,128]{2,1,0:T(8,128)(2,1)S(1)} %pad_maximum_fusion.3), channel_id=1, source_target_pairs={{0,192},{32,224},{64,0},{96,32},{128,64},{160,96},{192,128},{224,1... | collective-permute-start | bytes 786440 | tf_op jit(solution)/shard_map/ppermute | solution.py:476
  80.1 10.6 %copy-start.7 = (bf16[4,128,128]{2,1,0:T(8,128)(2,1)}, bf16[4,128,128]{2,1,0:T(8,128)(2,1)S(1)}, u32[]{:S(2)}) copy-start(bf16[4,128,128]{2,1,0:T(8,128)(2,1)S(1)} %collective-permute-done.9.earlier_ref) | copy-start | bytes 393220
  80.1 4.0 %collective-permute-start.4 = (bf16[512,128]{1,0:T(8,128)(2,1)}, bf16[512,128]{1,0:T(8,128)(2,1)S(1)}, u32[]{:S(2)}, u32[]{:S(2)}) collective-permute-start(bf16[512,128]{1,0:T(8,128)(2,1)} %get-tuple-element.37), channel_id=1, source_target_pairs={{0,4},{1,5},{2,6},{3,7},{4,0},{5,1},{6,2},{7,3},{8,12},{9,13},{10,... | collective-permute-start | bytes 393224 | tf_op jit(solution)/shard_map/ppermute | solution.py:481
  80.8 9.8 %copy-start.8 = (bf16[4,128,128]{2,1,0:T(8,128)(2,1)}, bf16[4,128,128]{2,1,0:T(8,128)(2,1)S(1)}, u32[]{:S(2)}) copy-start(bf16[4,128,128]{2,1,0:T(8,128)(2,1)S(1)} %collective-permute-done.8.later_ref) | copy-start | bytes 393220
  84.1 6.6 %copy-start.9 = (bf16[512,128]{1,0:T(8,128)(2,1)}, bf16[512,128]{1,0:T(8,128)(2,1)S(1)}, u32[]{:S(2)}) copy-start(bf16[512,128]{1,0:T(8,128)(2,1)S(1)} %collective-permute-done.4.refs_9_) | copy-start | bytes 393220
  84.1 6.6 %copy-start.3 = (bf16[2,512,128]{2,1,0:T(8,128)(2,1)}, bf16[2,512,128]{2,1,0:T(8,128)(2,1)S(1)}, u32[]{:S(2)}) copy-start(bf16[2,512,128]{2,1,0:T(8,128)(2,1)S(1)} %collective-permute-done.5.refs_1_) | copy-start | bytes 786436
  84.1 6.6 %copy-start.4 = (bf16[2,512,128]{2,1,0:T(8,128)(2,1)}, bf16[2,512,128]{2,1,0:T(8,128)(2,1)S(1)}, u32[]{:S(2)}) copy-start(bf16[2,512,128]{2,1,0:T(8,128)(2,1)S(1)} %collective-permute-done.6.refs_2_) | copy-start | bytes 786436
  84.1 6.6 %copy-start.5 = (bf16[2,512,128]{2,1,0:T(8,128)(2,1)}, bf16[2,512,128]{2,1,0:T(8,128)(2,1)S(1)}, u32[]{:S(2)}) copy-start(bf16[2,512,128]{2,1,0:T(8,128)(2,1)S(1)} %collective-permute-done.7.refs_3_) | copy-start | bytes 786436
  97.4 11.2 %all-to-all-start.2 = ((bf16[8,128,128]{2,1,0:T(8,128)(2,1)}), bf16[8,128,128]{2,1,0:T(8,128)(2,1)S(1)}, u32[]{:S(2)}, u32[]{:S(2)}) async-start(bf16[8,128,128]{2,1,0:T(8,128)(2,1)} %bitcast.55), calls=%async_computation.2 | async-start | bytes 524288 | tf_op jit(solution)/shard_map/all_to_all | solution.py:56
  108.6 0.7 copy-start.1

commit v4 on v3

v4 whole, which is shorter than its diff:
```python
import math

import jax
import jax.numpy as jnp
import numpy as np
from jax import lax
from jax.experimental import pallas as pl
from jax.experimental.pallas import tpu as pltpu
from jax.sharding import PartitionSpec as P

HEADS = 32
HD = 128
WIDTH = HEADS * HD
GROUP = 1024
PLANE = 512
RANK = 64
BOTH = 2 * RANK
ROWS = 128
ZS, YS = 8, 4
XS, CS = 4, 2
SLICES = XS * CS
MEMBERS = 8
PIECE = 16
RB = 256
BF16, F32 = jnp.bfloat16, jnp.float32

adapter_scale = 0.5

PLAIN_GROUPS = [[MEMBERS * g + i for i in range(MEMBERS)] for g in range(4)]
SHIFT_GROUPS = [[(MEMBERS * g + 4 + i) % HEADS for i in range(MEMBERS)] for g in range(4)]
PLAIN_SWAP = [(u, u ^ 4) for u in range(HEADS)]
Y_GROUPS = [[YS * z + y for y in range(YS)] for z in range(ZS)]
SHIFT_SWAP = [(u, (((u + 4) % HEADS ^ 4) - 4) % HEADS) for u in range(HEADS)]
CORE_SWAP = [(d, d ^ 1) for d in range(SLICES)]
ANYWHERE = pl.BlockSpec(memory_space=pltpu.HBM)
SCALARS = pl.BlockSpec(memory_space=pltpu.SMEM)

SPOTS = np.array(
    [[u % 4, u % 8, (u + 4) % 8, PLANE * (u // 4 % 2), PLANE * (1 - u // 4 % 2), 0, 0, 0] for u in range(HEADS)],
    np.int32,
)
SPOT_Y, SPOT_PLAIN, SPOT_SHIFT, SPOT_OWN_PLAIN, SPOT_OWN_SHIFT = range(5)


def z_shift(dz):
    return [(z * YS + y, ((z + dz) % ZS) * YS + y) for z in range(ZS) for y in range(YS)]


def y_shift(dy):
    return [(z * YS + y, z * YS + (y + dy) % YS) for z in range(ZS) for y in range(YS)]


def x_shift(dx):
    return [(x * CS + c, ((x + dx) % XS) * CS + c) for x in range(XS) for c in range(CS)]


def exchange(member, axis, groups=None):
    return lax.all_to_all(member, axis, 0, 0, tiled=True, axis_index_groups=groups)


def after(values, *others):
    return lax.optimization_barrier((values, others))[0]


def block(shape):
    return pl.BlockSpec(shape, lambda i, *s: (0,) * len(shape))


def dot_t(a, b):
    return lax.dot_general(a, b, (((1,), (1,)), ((), ())), preferred_element_type=F32)


def dot_0(a, b):
    return lax.dot_general(a, b, (((0,), (0,)), ((), ())), preferred_element_type=F32)


def call(kernel, name, scalars, in_specs, out_specs, out_shape, scratch, cost, vmem=None):
    params = pltpu.CompilerParams(vmem_limit_bytes=vmem and vmem * 2**20)
    return pl.pallas_call(
        kernel,
        name=name,
        out_shape=out_shape,
        grid_spec=pltpu.PrefetchScalarGridSpec(
            num_scalar_prefetch=scalars,
            grid=(1,),
            in_specs=in_specs,
            out_specs=out_specs,
            scratch_shapes=scratch,
        ),
        compiler_params=params,
        cost_estimate=pl.CostEstimate(flops=cost[0], bytes_accessed=cost[1], transcendentals=0),
    )


def order_heads(flags, order):
    def place(h, ones):
        flag = flags[h]
        order[jnp.where(flag > 0, HEADS // 2 + ones, h - ones)] = h
        return ones + jnp.where(flag > 0, 1, 0)

    lax.fori_loop(0, HEADS, place, 0, unroll=True)


def fetch_heads(heads, places, fq_ref, fk_ref, fv_ref, go_ref, up_ref, q_in, v_in, up_in, sems):
    copies = []
    for p, (head, (buffer, entry)) in enumerate(zip(heads, places)):
        cols = pl.ds(pl.multiple_of(head * HD, HD), HD)
        own = pl.ds(p * HD, HD)
        spots = (
            (up_ref, up_in.at[:, own]),
            (fq_ref, q_in.at[:, own]),
            (fv_ref, v_in.at[:, own]),
            (fk_ref, buffer.at[(*entry[:-1], slice(None), pl.ds(entry[-1] + HD, HD))]),
            (go_ref, buffer.at[(*entry[:-1], slice(None), pl.ds(entry[-1] + 3 * HD, HD))]),
        )
        for t, (ref, spot) in enumerate(spots):
            copies.append(pltpu.make_async_copy(ref.at[:, cols], spot, sems.at[p, t]))
            copies[-1].start()
    return copies


def raise_heads(low, copies, places, q_in, v_in, up_in):
    lanes = lax.broadcasted_iota(jnp.int32, (ROWS, BOTH), 1)
    none = jnp.zeros_like(low)
    lows = jnp.concatenate([jnp.where(lanes < RANK, low, none), jnp.where(lanes < RANK, none, low)], axis=0)
    for copy in copies:
        copy.wait()
    raised = jnp.dot(lows, up_in[...], preferred_element_type=F32)
    for p, (buffer, entry) in enumerate(places):
        own = slice(p * HD, (p + 1) * HD)
        q = (q_in[:, own].astype(F32) + adapter_scale * raised[:ROWS, own]).astype(BF16)
        v = (v_in[:, own].astype(F32) + adapter_scale * raised[ROWS:, own]).astype(BF16)
        buffer[(*entry[:-1], slice(None), pl.ds(entry[-1], HD))] = q
        buffer[(*entry[:-1], slice(None), pl.ds(entry[-1] + 2 * HD, HD))] = v


HALF = HEADS // 2
HEAD_SCRATCH = [
    pltpu.VMEM((ROWS, HALF * HD), BF16),
    pltpu.VMEM((ROWS, HALF * HD), BF16),
    pltpu.VMEM((BOTH, HALF * HD), BF16),
    pltpu.SemaphoreType.DMA((HALF, 5)),
]


def prepare_plain_kernel(flags, x_hbm, down_hbm, *refs):
    frozen, (out_ref, order, low_ref, x_in, down_in, whole_sems, q_in, v_in, up_in, sems) = refs[:5], refs[5:]
    wholes = [
        pltpu.make_async_copy(x_hbm, x_in, whole_sems.at[0]),
        pltpu.make_async_copy(down_hbm, down_in, whole_sems.at[1]),
    ]
    for copy in wholes:
        copy.start()
    order_heads(flags, order)
    places = [(out_ref, (p % MEMBERS, p // MEMBERS * 4 * HD)) for p in range(HALF)]
    copies = fetch_heads([order[p] for p in range(HALF)], places, *frozen, q_in, v_in, up_in, sems)
    for copy in wholes:
        copy.wait()
    low = dot_t(x_in[...], down_in[...]).astype(BF16)
    low_ref[...] = low
    raise_heads(low, copies, places, q_in, v_in, up_in)


def prepare_plain(flags, x, down, frozen):
    return call(
        prepare_plain_kernel,
        "prepare_plain",
        1,
        [ANYWHERE] * 7,
        [block((MEMBERS, ROWS, 8 * HD)), SCALARS, block((ROWS, BOTH))],
        (
            jax.ShapeDtypeStruct((MEMBERS, ROWS, 8 * HD), BF16),
            jax.ShapeDtypeStruct((HEADS,), jnp.int32),
            jax.ShapeDtypeStruct((ROWS, BOTH), BF16),
        ),
        [pltpu.VMEM((ROWS, WIDTH), BF16), pltpu.VMEM((BOTH, WIDTH), BF16), pltpu.SemaphoreType.DMA((2,))]
        + HEAD_SCRATCH,
        (10**9, 8 * 10**6),
    )(flags, x, down, *frozen)


def prepare_shifted_kernel(order, spot, low_ref, *refs):
    frozen, outs, scratch = refs[:5], refs[5:9], refs[9:]
    y, own_half = spot[SPOT_Y], spot[SPOT_OWN_SHIFT] // PLANE
    heads, places = [], []
    for item in range(2):
        for other in range(2):
            for dy in range(YS):
                seat = (own_half + other) % 2 * YS + ((y + dy) % YS if item == 0 else dy)
                heads.append(order[HALF + item * MEMBERS + seat])
                places.append((outs[2 * item + other], (dy, 0)))
    copies = fetch_heads(heads, places, *frozen, *scratch)
    raise_heads(low_ref[...], copies, places, *scratch[:3])


def prepare_shifted(order, spot, low, frozen):
    return call(
        prepare_shifted_kernel,
        "prepare_shifted",
        2,
        [block((ROWS, BOTH))] + [ANYWHERE] * 5,
        [block((YS, ROWS, 4 * HD))] * 4,
        (jax.ShapeDtypeStruct((YS, ROWS, 4 * HD), BF16),) * 4,
        HEAD_SCRATCH,
        (10**9, 8 * 10**6),
    )(order, spot, low, *frozen)


def pack_kernel(low_ref, own_ref, other_ref, *out_refs):
    for dy, out_ref in enumerate(out_refs, 1):
        out_ref[:, pl.ds(0, 4 * HD)] = own_ref[dy]
        out_ref[:, pl.ds(4 * HD, 4 * HD)] = other_ref[dy]
        out_ref[:, pl.ds(8 * HD, BOTH)] = low_ref[...]


def pack(low, own, other):
    shape = (ROWS, 8 * HD + BOTH)
    return call(
        pack_kernel,
        "pack_first",
        0,
        [block(low.shape)] + [block(own.shape)] * 2,
        [block(shape)] * 3,
        (jax.ShapeDtypeStruct(shape, BF16),) * 3,
        [],
        (0, 4 * 10**6),
    )(low, own, other)


def turn_kernel(spot, x_ref, kept_ref, other_ref):
    x, core = spot[0] // CS, spot[0] % CS

    def fill(refs):
        for u in range(HEADS):
            turned = x_ref[:, pl.ds(u * HD, HD)].T
            for d in range(SLICES):
                step = (d // CS - x + XS) % XS
                refs[d % CS][step, pl.ds(u * PIECE, PIECE), :] = turned[d * PIECE : (d + 1) * PIECE]

    @pl.when(core == 0)
    def _():
        fill((kept_ref, other_ref))

    @pl.when(core != 0)
    def _():
        fill((other_ref, kept_ref))


def turn(place, x):
    shape = (XS, HEADS * PIECE, ROWS)
    return call(
        turn_kernel,
        "turn_input",
        1,
        [block(x.shape)],
        [block(shape)] * 2,
        (jax.ShapeDtypeStruct(shape, BF16),) * 2,
        [],
        (10**9, 2 * 10**6),
    )(place, x)


def attend(x_ref, up, grads_ref, column, dv_acc):
    factor = 1.0 / math.sqrt(HD)
    bend = factor * math.log2(math.e)
    row_ids = lax.broadcasted_iota(jnp.int32, (RB, RB), 0)
    column_ids = lax.broadcasted_iota(jnp.int32, (RB, RB), 1)
    keep = column_ids <= row_ids
    for i in range(GROUP // RB):
        n = (i + 1) * RB
        rows = pl.ds(i * RB, RB)
        q = x_ref[rows, pl.ds(0, HD)]
        g = x_ref[rows, pl.ds(3 * HD, HD)]
        k = x_ref[pl.ds(0, n), pl.ds(HD, HD)]
        v = x_ref[pl.ds(0, n), pl.ds(2 * HD, HD)]
        scores = dot_t(q, k)
        last = jnp.where(keep, scores[:, i * RB :], -1e30)
        scores = last if i == 0 else jnp.concatenate([scores[:, : i * RB], last], axis=1)
        top = jnp.max(scores, axis=1, keepdims=True)
        weights = jnp.exp2((scores - top) * bend)
        total = jnp.sum(weights, axis=1, keepdims=True)
        attention = (weights * (1.0 / total)).astype(BF16)
        output = jnp.dot(attention, v, preferred_element_type=F32)
        grad_attention = dot_t(g, v)
        center = jnp.sum(g.astype(F32) * output, axis=1, keepdims=True)
        grad_scores = (attention.astype(F32) * (grad_attention - center)).astype(BF16)
        dq = jnp.dot(grad_scores, k, preferred_element_type=F32) * factor
        grads_ref[rows, pl.ds(column, HD)] = dq.astype(BF16)
        dv = dot_0(attention, g)
        if i:
            dv_acc[pl.ds(0, i * RB), :] += dv[: i * RB]
        dv_acc[rows, :] = dv[i * RB :]
    dq = grads_ref[:, pl.ds(column, HD)]
    dv = dv_acc[...].astype(BF16)
    grads_ref[:, pl.ds(column + HD, HD)] = dv
    lanes = lax.broadcasted_iota(jnp.int32, (GROUP, BOTH), 1)
    return jnp.where(lanes < RANK, dot_t(dq, up), dot_t(dv, up))


def attention_plain_kernel(order, spot, arrived, up_a, up_b, mine_ref, theirs_ref, grads_ref, xs, dv_acc, total, sems):
    copies = []
    for item in range(2):
        source = arrived.at[:, pl.ds(item * 4 * HD, 4 * HD)]
        copies.append(pltpu.make_async_copy(source, xs.at[item], sems.at[item]))
        copies[-1].start()
    copies[0].wait()
    total[...] = attend(xs.at[0], up_a[...], grads_ref, 0, dv_acc)
    copies[1].wait()
    total[...] += attend(xs.at[1], up_b[...], grads_ref, 2 * HD, dv_acc)
    own = pl.multiple_of(spot[SPOT_OWN_PLAIN], PLANE)
    mine_ref[...] = total[pl.ds(own, PLANE), :]
    theirs_ref[...] = total[pl.ds(PLANE - own, PLANE), :].astype(BF16)


def up_columns(item):
    seat = SPOT_PLAIN if item < 2 else SPOT_SHIFT
    return pl.BlockSpec((BOTH, HD), lambda i, order, spot: (0, order[item * MEMBERS + spot[seat]]))


def attention_plain(order, spot, arrived, up):
    shapes = [((PLANE, BOTH), F32), ((PLANE, BOTH), BF16), ((GROUP, 4 * HD), BF16)]
    return call(
        attention_plain_kernel,
        "attention_plain",
        2,
        [ANYWHERE, up_columns(0), up_columns(1)],
        [block(shape) for shape, _ in shapes],
        [jax.ShapeDtypeStruct(*shape) for shape in shapes],
        [
            pltpu.VMEM((2, GROUP, 4 * HD), BF16),
            pltpu.VMEM((GROUP, HD), F32),
            pltpu.VMEM((GROUP, BOTH), F32),
            pltpu.SemaphoreType.DMA((2,)),
        ],
        (2 * 10**10, 4 * 10**6),
    )(order, spot, arrived.reshape(GROUP, 8 * HD), up, up)


def attention_shifted_kernel(last, order, spot, *refs):
    y, own = spot[SPOT_Y], spot[SPOT_OWN_SHIFT]
    if last:
        arrived, up, before_hbm, mine_hbm, theirs_hbm, back_ref, grads_hbm, x_in, dv_acc, sems = refs[:10]
        total, before_ref, mine_ref, theirs_ref, grads_ref, more_sems = refs[10:]
        blocks = [[arrived.at[s, half] for half in range(2)] for s in range(YS)]
        sources = range(YS)
    else:
        own_ref, other_ref, *pieces = refs[:5]
        up, back_ref, grads_ref, x_in, dv_acc, sems = refs[5:]
        blocks = [[own_ref.at[0], other_ref.at[0]]]
        for piece in pieces:
            blocks.append([piece.at[:, pl.ds(half * 4 * HD, 4 * HD)] for half in range(2)])
        sources = [(y - dy + YS) % YS for dy in range(YS)]
    copies = []
    for t, source in enumerate(sources):
        for half in range(2):
            start = (own if half == 0 else PLANE - own) + source * ROWS
            rows = pl.ds(pl.multiple_of(start, ROWS), ROWS)
            copies.append(pltpu.make_async_copy(blocks[t][half], x_in.at[rows, :], sems.at[t, half]))
            copies[-1].start()
    if last:
        pairs = ((before_hbm, before_ref), (mine_hbm, mine_ref), (theirs_hbm, theirs_ref))
        others = [pltpu.make_async_copy(*pair, more_sems.at[t]) for t, pair in enumerate(pairs)]
        for copy in others:
            copy.start()
    for copy in copies:
        copy.wait()
    back = attend(x_in, up[...], grads_ref, 0, dv_acc)
    if not last:
        back_ref[...] = back
        return
    save = pltpu.make_async_copy(grads_ref, grads_hbm, more_sems.at[3])
    save.start()
    for copy in others:
        copy.wait()
    total[...] = back + before_ref[...]
    mine_rows = pl.ds(pl.multiple_of(own, PLANE), PLANE)
    total[mine_rows, :] += mine_ref[...] + theirs_ref[...].astype(F32)
    back_ref[...] = total[...].astype(BF16)
    save.wait()


LAST_SCRATCH = [
    pltpu.VMEM((GROUP, BOTH), F32),
    pltpu.VMEM((GROUP, BOTH), F32),
    pltpu.VMEM((PLANE, BOTH), F32),
    pltpu.VMEM((PLANE, BOTH), BF16),
    pltpu.VMEM((GROUP, 2 * HD), BF16),
    pltpu.SemaphoreType.DMA((4,)),
]


def attention_shifted(item, order, spot, arrived, up, *more):
    last = len(more) > 0
    shapes = [((GROUP, BOTH), BF16 if last else F32), ((GROUP, 2 * HD), BF16)]

    def body(*refs):
        attention_shifted_kernel(last, *refs)

    return call(
        body,
        "attention_last" if last else "attention_third",
        2,
        [pl.BlockSpec(memory_space=pl.ANY) if last else ANYWHERE] * len(arrived)
        + [up_columns(item)]
        + [ANYWHERE] * len(more),
        [block(shapes[0][0]), ANYWHERE if last else block(shapes[1][0])],
        [jax.ShapeDtypeStruct(*shape) for shape in shapes],
        [pltpu.VMEM((GROUP, 4 * HD), BF16), pltpu.VMEM((GROUP, HD), F32), pltpu.SemaphoreType.DMA((YS, 2))]
        + LAST_SCRATCH * last,
        (4 * 10**9, 3 * 10**6) if last else (10**6, 10**4),
    )(order, spot, *arrived, up, *more)


def up_gradient_kernel(spot, own_ref, later_ref, earlier_ref, *refs):
    out_ref, low_a, low_b = refs[-3:]
    y = spot[SPOT_Y]

    def fill(low, first, second):
        for half, ref in enumerate((first, second)):
            for s in range(YS):
                low[pl.ds(half * PLANE + s * ROWS, ROWS), :] = ref[(y - s + YS) % YS]

    @pl.when(spot[SPOT_OWN_PLAIN] == 0)
    def _():
        fill(low_a, own_ref, later_ref)
        fill(low_b, earlier_ref, own_ref)

    @pl.when(spot[SPOT_OWN_PLAIN] != 0)
    def _():
        fill(low_a, earlier_ref, own_ref)
        fill(low_b, own_ref, later_ref)

    for item in range(4):
        low = (low_a, low_b)[item // 2][...]
        grads, column = ((refs[0], 0), (refs[0], 2 * HD), (refs[1], 0), (refs[2], 0))[item]
        for m in range(2):
            columns = pl.ds(column + m * HD, HD)
            part = adapter_scale * dot_0(low[:, m * RANK : (m + 1) * RANK], grads[:, columns])
            part = part.astype(BF16)
            for e in range(RANK // PIECE):
                d = m * (RANK // PIECE) + e
                out_ref[d, pl.ds(item * PIECE, PIECE), :] = part[e * PIECE : (e + 1) * PIECE]


def up_gradients(spot, own, later, earlier, grads):
    shape = (SLICES, 4 * PIECE, HD)
    return call(
        up_gradient_kernel,
        "up_gradients",
        1,
        [block((YS, ROWS, BOTH))] * 3 + [block(array.shape) for array in grads],
        block(shape),
        jax.ShapeDtypeStruct(shape, BF16),
        [pltpu.VMEM((GROUP, BOTH), BF16)] * 2,
        (2 * 10**9, 3 * 10**6),
        16,
    )(spot, own, later, earlier, *grads)


def gather_kernel(summed_ref, ups_ref, out_ref):
    back = jnp.sum(summed_ref[...].astype(F32), axis=0).astype(BF16)
    for d in range(SLICES):
        out_ref[d, pl.ds(0, ROWS), :] = back
    out_ref[:, pl.ds(ROWS, 4 * PIECE), :] = ups_ref[...]


def gather_parts(summed, ups):
    shape = (SLICES, ROWS + 4 * PIECE, HD)
    return call(
        gather_kernel,
        "gather_parts",
        0,
        [block(summed.shape), block(ups.shape)],
        block(shape),
        jax.ShapeDtypeStruct(shape, BF16),
        [],
        (10**7, 10**6),
        16,
    )(summed, ups)


def merge_kernel(order, spot, place, both_ref, *refs):
    x_refs, out_ref = refs[:-1], refs[-1]
    x, core = place[0] // CS, place[0] % CS
    total = jnp.zeros((HEADS * PIECE, BOTH), F32)
    for dx in range(XS):
        for other in range(CS):
            s = (x - dx + XS) % XS * CS + (core + other) % CS
            back = both_ref[s, pl.ds(0, ROWS), :]
            total += jnp.dot(x_refs[dx][other], back, preferred_element_type=F32)
    total = (adapter_scale * total).astype(BF16)
    for u in range(HEADS):
        out_ref[u, pl.ds(0, PIECE), :] = total[u * PIECE : (u + 1) * PIECE]
        out_ref[u, pl.ds(PIECE, PIECE), :] = jnp.zeros((PIECE, HD), BF16)
    ups = jnp.sum(both_ref[:, pl.ds(ROWS, 4 * PIECE), :].astype(F32), axis=0).astype(BF16)
    for item in range(4):
        seat = spot[SPOT_PLAIN if item < 2 else SPOT_SHIFT]
        head = order[item * MEMBERS + seat]
        out_ref[head, pl.ds(PIECE, PIECE), :] = ups[item * PIECE : (item + 1) * PIECE]


def merge(order, spot, place, both, pieces):
    shape = (HEADS, 2 * PIECE, HD)
    return call(
        merge_kernel,
        "merge_gradients",
        3,
        [block(both.shape)] + [block(piece.shape) for piece in pieces],
        block(shape),
        jax.ShapeDtypeStruct(shape, BF16),
        [],
        (2 * 10**8, 2 * 10**6),
        16,
    )(order, spot, place, both, *pieces)


def spread_kernel(in_ref, out_ref):
    total = jnp.sum(in_ref[...].astype(F32), axis=0)
    for d in range(SLICES):
        out_ref[d] = total


def spread(both):
    shape = (SLICES, 2 * PIECE, HD)
    return call(
        spread_kernel,
        "spread_sums",
        0,
        [block(both.shape)],
        block(shape),
        jax.ShapeDtypeStruct(shape, F32),
        [],
        (10**6, 10**6),
        16,
    )(both)


def finish_kernel(in_ref, down_ref, up_ref):
    down = in_ref[:, pl.ds(0, PIECE), :].reshape(HD, BOTH).T
    up = in_ref[:, pl.ds(PIECE, PIECE), :].reshape(BOTH, HD)
    for m in range(2):
        down_ref[m] = down[m * RANK : (m + 1) * RANK]
        up_ref[m] = up[m * RANK : (m + 1) * RANK]


def finish(both):
    shape = (2, RANK, HD)
    return call(
        finish_kernel,
        "finish",
        0,
        [block(both.shape)],
        [block(shape)] * 2,
        [jax.ShapeDtypeStruct(shape, F32)] * 2,
        [],
        (10**6, 10**6),
        16,
    )(both)


def per_device(
    normalized_input,
    frozen_queries,
    frozen_keys,
    frozen_values,
    output_gradient,
    adapter_down_maps,
    adapter_up_maps,
    shifted,
):
    tokens = normalized_input[0]
    spot = lax.dynamic_slice(jnp.asarray(SPOTS), (lax.axis_index("ulysses"), 0), (1, 8)).reshape(8)
    place = lax.axis_index("dp").reshape(1)
    up = adapter_up_maps.reshape(BOTH, WIDTH)
    down = adapter_down_maps.transpose(0, 2, 1).reshape(BOTH, WIDTH)

    frozen = (frozen_queries[0], frozen_keys[0], frozen_values[0], output_gradient[0], up)
    sent, order, low = prepare_plain(shifted.astype(jnp.int32), tokens, down, frozen)
    plain = exchange(sent, "ulysses", PLAIN_GROUPS)
    own_c, other_c, own_d, other_d = prepare_shifted(order, spot, low, frozen)
    other_c = lax.ppermute(other_c, "ulysses", SHIFT_SWAP)
    other_d = lax.ppermute(other_d, "ulysses", SHIFT_SWAP)
    kept, other = turn(place, after(tokens, own_c))
    other = lax.ppermute(other, "dp", CORE_SWAP)
    pieces = [jnp.stack([kept[dx], other[dx]]) for dx in range(XS)]
    pieces = pieces[:1] + [lax.ppermute(pieces[dx], "dp", x_shift(dx)) for dx in (1, 2, 3)]

    packed = pack(low, own_c, other_c)
    arrived_c = [lax.ppermute(packed[dy - 1], "ulysses", y_shift(dy)) for dy in (1, 2, 3)]
    sent = jnp.stack([own_d, other_d], axis=1)
    plain, pieces, sent = after((plain, pieces, sent), packed)

    arrived_d = exchange(sent, "ulysses", Y_GROUPS)
    mine, theirs, grads_plain = attention_plain(order, spot, plain, up)
    theirs = lax.ppermute(theirs, "ulysses", PLAIN_SWAP)
    arrived_c = after(arrived_c, grads_plain, sent)
    partial, grads_c = attention_shifted(2, order, spot, [own_c, other_c, *arrived_c], up)
    own = jnp.stack([low] + [array[:, 8 * HD :] for array in arrived_c])
    later = lax.ppermute(own, "ulysses", z_shift(-1))
    earlier = lax.ppermute(own, "ulysses", z_shift(1))

    arrived_d, theirs, later, earlier = after((arrived_d, theirs, later, earlier), partial)
    partial, grads_d = attention_shifted(
        3, order, spot, [arrived_d], up, partial, mine, theirs
    )
    summed = exchange(partial.reshape(MEMBERS, ROWS, BOTH), "ulysses", SHIFT_GROUPS)
    ups = up_gradients(spot, own, later, earlier, (grads_plain, grads_c, grads_d))
    both = exchange(gather_parts(summed, ups), "dp")
    both = exchange(merge(order, spot, place, both, pieces), "ulysses")
    both = exchange(spread(both), "dp")
    grad_down, grad_up = finish(both)
    return (grad_down.transpose(0, 2, 1), grad_up)


def solution(mesh):
    rows = P("dp", "ulysses", None)
    in_specs = (rows, rows, rows, rows, rows, P(), P(), P())
    out_specs = (P(None, "ulysses", None), P(None, None, "ulysses"))
    return jax.shard_map(
        per_device, mesh=mesh, in_specs=in_specs, out_specs=out_specs, check_vma=False
    )
```

time: 164 us -> 159 us (0.970)
  Pallas kernels: 57.3 us -> 47.5 us
  other arithmetic: 1.6 us -> 5.46 us
  blocking collectives: 44.9 us -> 43.1 us
    ppermute x4 -> x6, starting transfers between devices: 5.06 us -> 11.5 us  [the longest x1 5.68 us: per_device(): other_d = lax.ppermute(other_d, 'ulysses', SHIFT_SWAP)]
    all_to_all x3, starting transfers between devices: 22 us -> 17.4 us  [exchange(): lax.all_to_all(member, axis, 0, 0, tiled=True, axis_index_groups=groups)]
    ppermute x4 -> x6, waiting for transfers between devices: 10.5 us -> 14.8 us  [the longest x1 14.8 us: per_device(): other_c = lax.ppermute(other_c, 'ulysses', SHIFT_SWAP)]
    another operation x5 -> x6, other arithmetic: 1.6 us -> 5.46 us  [the longest x4 3.16 us: per_device(): pieces = [jnp.stack([kept[dx], other[dx]]) for dx in range(XS)]]
    ppermute x1, waiting for transfers between devices: 3.28 us -> 0.01 us  [per_device(): theirs = lax.ppermute(theirs, 'ulysses', PLAIN_SWAP)]
    pallas_call x1, Pallas kernels: 4.09 us -> 1.68 us  [up_gradients(): call(up_gradient_kernel, 'up_gradients', 1, [block((YS, ROWS, BOTH))] * 3...]
    pallas_call x1, Pallas kernels: 3.1 us -> 0.98 us  [merge(): call(merge_kernel, 'merge_gradients', 3, [block(both.shape)] + [block(pie...]
    squeeze x1 -> x0, local copies, waits for them, and re-layouts: 1.88 us -> none  [per_device(): other = lax.ppermute(turned[1], 'dp', CORE_SWAP)]
  transfers between devices with their start and end apart: 13 -> 15, of which waited for: 6 -> 2; matrix products, arithmetic and copies ran while one was open for 4% -> 6% of each run, Pallas kernels for 17% -> 19%
where the time goes in v4:
time: 159 us; the launch traced here: 158 us
  Pallas kernels  47.5 us (30%)
  blocking collectives  43.1 us (27%)
  starting transfers between devices  36.5 us (23%)
  waiting for transfers between devices  17 us (11%)
  local copies, waits for them, and re-layouts  7.17 us (5%)
  other arithmetic  5.46 us (3%)
    all_to_all x3, blocking collectives, exchange(): lax.all_to_all(member, axis, 0, 0, tiled=True, axis_index_groups=groups)  43.1 us
    all_to_all x3, starting transfers between devices, exchange(): lax.all_to_all(member, axis, 0, 0, tiled=True, axis_index_groups=groups)  17.4 us
    pallas_call x2, Pallas kernels, attention_shifted(): call(body, 'attention_last' if last else 'attention_third', 2, [pl.BlockS...  15.6 us
    ppermute x1, waiting for transfers between devices, per_device(): other_c = lax.ppermute(other_c, 'ulysses', SHIFT_SWAP)  14.8 us
    pallas_call x1, Pallas kernels, attention_plain(): call(attention_plain_kernel, 'attention_plain', 2, [ANYWHERE, up_columns(...  11.4 us
    pallas_call x1, Pallas kernels, prepare_plain(): call(prepare_plain_kernel, 'prepare_plain', 1, [ANYWHERE] * 7, [block((ME...  6.9 us
    ppermute x1, starting transfers between devices, per_device(): other_d = lax.ppermute(other_d, 'ulysses', SHIFT_SWAP)  5.68 us
    pallas_call x1, Pallas kernels, prepare_shifted(): call(prepare_shifted_kernel, 'prepare_shifted', 2, [block((ROWS, BOTH))]...  5.38 us
  transfers between devices with their start and end apart: 15, of which 2 were waited for; matrix products, arithmetic and copies ran while one was open for 6% of the time, Pallas kernels for 19%

profile of v4, /device:TPU:1, one launch (start us, length us, event | category | flops | bytes accessed | tf_op | source)
XLA Modules:
  0.0 157.6 jit_solution(13010538910440177235)
XLA Ops:
  0.6 6.9 %prepare_plain.1 = (bf16[8,128,1024]{2,1,0:T(8,128)(2,1)}, s32[32]{0:T(128)}, bf16[128,128]{1,0:T(8,128)(2,1)}) custom-call(s32[32]{0:T(128)} %flags.1, bf16[128,4096]{1,0:T(8,128)(2,1)} %bitcast.40, bf16[128,4096]{1,0:T(8,128)(2,1)} %bitcast.39, bf16[128,4096]{1,0:T(8,128)(2,1)} %bitcast.30, bf16[128,4096]{1,0:T(8,128)(2,1)} %bitcast.32, ...), custom_call_target="tpu_custom_call" | custom-call | flops 1000000000 | bytes 8000000 | tf_op jit(solution)/shard_map/prepare_plain/pallas_call | solution.py:165
  7.5 6.4 %all-to-all-start = ((bf16[8,128,1024]{2,1,0:T(8,128)(2,1)}), bf16[8,128,1024]{2,1,0:T(8,128)(2,1)S(1)}, u32[]{:S(2)}, u32[]{:S(2)}) async-start(bf16[8,128,1024]{2,1,0:T(8,128)(2,1)} %get-tuple-element.38), calls=%async_computation | async-start | bytes 4194304 | tf_op jit(solution)/shard_map/all_to_all | solution.py:58
  13.9 1.3 dynamic-slice_bitcast_fusion.spot.refs_1_
  15.2 5.4 %prepare_shifted.1 = (bf16[4,128,512]{2,1,0:T(8,128)(2,1)}, bf16[4,128,512]{2,1,0:T(8,128)(2,1)}, bf16[4,128,512]{2,1,0:T(8,128)(2,1)}, bf16[4,128,512]{2,1,0:T(8,128)(2,1)}) custom-call(s32[32]{0:T(128)} %get-tuple-element.37.order.refs_0_, s32[8]{0:T(128)} %dynamic-slice_bitcast_fusion.spot.refs_1_, bf16[128,128]{1,0:T(8,128)(2,1)} %get-tuple-element.39.low_ref, ...), custom_call_target="tpu_custom_call" | custom-call | flops 1000000000 | bytes 8000000 | tf_op jit(solution)/shard_map/prepare_shifted/pallas_call | solution.py:197
  20.6 2.6 %turn_input.1 = (bf16[4,512,128]{2,1,0:T(8,128)(2,1)}, bf16[4,512,128]{2,1,0:T(8,128)(2,1)}) custom-call(s32[1]{0:T(128)} %bitcast.9.spot.place, bf16[128,4096]{1,0:T(8,128)(2,1)} %bitcast.41), custom_call_target="tpu_custom_call" | custom-call | flops 1000000000 | bytes 2000000 | tf_op jit(solution)/shard_map/turn_input/pallas_call | solution.py:251
  23.1 1.0 collective-permute-start
  24.1 5.7 %collective-permute-start.4 = (bf16[4,128,512]{2,1,0:T(8,128)(2,1)}, bf16[4,128,512]{2,1,0:T(8,128)(2,1)}, u32[]{:S(2)}, u32[]{:S(2)}) collective-permute-start(bf16[4,128,512]{2,1,0:T(8,128)(2,1)} %get-tuple-element.45), channel_id=1, source_target_pairs={{0,28},{1,29},{2,30},{3,31},{4,8},{5,9},{6,10},{7,11},{8,4},{9,5},... | collective-permute-start | bytes 1572872 | tf_op jit(solution)/shard_map/ppermute | solution.py:582
  29.8 1.1 fusion
  32.4 1.2 collective-permute-start.1
  34.4 2.4 %collective-permute-start.2 = (bf16[2,512,128]{2,1,0:T(8,128)(2,1)}, bf16[2,512,128]{2,1,0:T(8,128)(2,1)S(1)}, u32[]{:S(2)}, u32[]{:S(2)}) collective-permute-start(bf16[2,512,128]{2,1,0:T(8,128)(2,1)} %pad_maximum_fusion.3), channel_id=1, source_target_pairs={{0,128},{32,160},{64,192},{96,224},{128,0},{160,32},{192,64},{224,... | collective-permute-start | bytes 786440 | tf_op jit(solution)/shard_map/ppermute | solution.py:586
  37.6 1.2 collective-permute-start.3
  38.7 14.8 %collective-permute-done.5.other_ref.refs_3_ = bf16[4,128,512]{2,1,0:T(8,128)(2,1)S(1)} collective-permute-done((bf16[4,128,512]{2,1,0:T(8,128)(2,1)}, bf16[4,128,512]{2,1,0:T(8,128)(2,1)S(1)}, u32[]{:S(2)}, u32[]{:S(2)}) %collective-permute-start.5) | collective-permute-done | bytes 524320 | tf_op jit(solution)/shard_map/ppermute | solution.py:581
  53.5 0.8 copy-done.6
  54.3 2.2 %pack_first.1 = (bf16[128,1152]{1,0:T(8,128)(2,1)}, bf16[128,1152]{1,0:T(8,128)(2,1)}, bf16[128,1152]{1,0:T(8,128)(2,1)}) custom-call(bf16[128,128]{1,0:T(8,128)(2,1)} %get-tuple-element.39.low_ref, bf16[4,128,512]{2,1,0:T(8,128)(2,1)} %get-tuple-element.40.own_ref.refs_2_, bf16[4,128,512]{2,1,0:T(8,128)(2,1)} %copy-done.6), custom_call_target="tpu_custom_call" | custom-call | bytes 4000000 | tf_op jit(solution)/shard_map/pack_first/pallas_call | solution.py:218
  56.5 1.2 collective-permute-start.7
  57.7 0.9 pad_maximum_fusion.1.refs_0_
  58.6 2.5 %collective-permute-start.8 = (bf16[128,1152]{1,0:T(8,128)(2,1)}, bf16[128,1152]{1,0:T(8,128)(2,1)S(1)}, u32[]{:S(2)}, u32[]{:S(2)}) collective-permute-start(bf16[128,1152]{1,0:T(8,128)(2,1)} %get-tuple-element.48), channel_id=1, source_target_pairs={{0,2},{1,3},{2,0},{3,1},{4,6},{5,7},{6,4},{7,5},{8,10},{9,11},{10,... | collective-permute-start | bytes 884744 | tf_op jit(solution)/shard_map/ppermute | solution.py:589
  61.1 2.3 %pad_maximum_fusion = bf16[4,2,128,512]{3,2,1,0:T(8,128)(2,1)} fusion(bf16[4,1,128,512]{3,2,1,0:T(8,128)(2,1)} %bitcast.11, bf16[4,1,128,512]{3,2,1,0:T(8,128)(2,1)} %bitcast.42), kind=kLoop, calls=%fused_computation | loop fusion | flops 524288 | bytes 2097152 | tf_op jit(solution)/shard_map/stack | solution.py:590
  63.4 1.2 collective-permute-start.9
  64.6 4.5 %all-to-all-start.1 = ((bf16[4,2,128,512]{3,2,1,0:T(8,128)(2,1)}), bf16[4,2,128,512]{3,2,1,0:T(8,128)(2,1)}, u32[]{:S(2)}, u32[]{:S(2)}) async-start(bf16[4,2,128,512]{3,2,1,0:T(8,128)(2,1)} %pad_maximum_fusion), calls=%async_computation.1 | async-start | bytes 2097152 | tf_op jit(solution)/shard_map/all_to_all | solution.py:58
  69.1 11.4 %attention_plain.1 = (f32[512,128]{1,0:T(8,128)}, bf16[512,128]{1,0:T(8,128)(2,1)}, bf16[1024,512]{1,0:T(8,128)(2,1)}) custom-call(s32[32]{0:T(128)} %get-tuple-element.37.order.refs_0_, s32[8]{0:T(128)} %dynamic-slice_bitcast_fusion.spot.refs_1_, bf16[1024,1024]{1,0:T(8,128)(2,1)} %bitcast.38, bf16[128,4096]{1,0:T(8,128)(2,1)} %bitcast.26, ...), custom_call_target="tpu_custom_call" | custom-call | flops 20000000000 | bytes 4000000 | tf_op jit(solution)/shard_map/attention_plain/pallas_call | solution.py:322
  82.2 2.7 %collective-permute-start.10 = (bf16[4,128,128]{2,1,0:T(8,128)(2,1)S(1)}, bf16[4,128,128]{2,1,0:T(8,128)(2,1)S(1)}, u32[]{:S(2)}, u32[]{:S(2)}) collective-permute-start(bf16[4,128,128]{2,1,0:T(8,128)(2,1)S(1)} %pad_maximum_fusion.5.own_ref), channel_id=1, source_target_pairs={{0,28},{1,29},{2,30},{3,31},{4,0},{5,1},{6,2},{7,3},{8,4},{9,5},{1... | collective-permute-start | bytes 393224 | tf_op jit(solution)/shard_map/ppermute | solution.py:599
  84.9 7.4 %attention_third.1 = (f32[1024,128]{1,0:T(8,128)}, bf16[1024,256]{1,0:T(8,128)(2,1)}) custom-call(s32[32]{0:T(128)} %get-tuple-element.37.order.refs_0_, s32[8]{0:T(128)} %dynamic-slice_bitcast_fusion.spot.refs_1_, bf16[4,128,512]{2,1,0:T(8,128)(2,1)} %get-tuple-element.40.own_ref.refs_2_, bf16[4,128,512]{2,1,0:T(8,128)(2,1)} %copy-done.6, ...), custom_call_target="tpu_custom_call" | custom-call | flops 1000000 | bytes 10000 | tf_op jit(solution)/shard_map/attention_third/pallas_call | solution.py:399
  93.0 8.2 %attention_last.1 = (bf16[1024,128]{1,0:T(8,128)(2,1)}, bf16[1024,256]{1,0:T(8,128)(2,1)}) custom-call(s32[32]{0:T(128)} %get-tuple-element.37.order.refs_0_, s32[8]{0:T(128)} %dynamic-slice_bitcast_fusion.spot.refs_1_, bf16[4,2,128,512]{3,2,1,0:T(8,128)(2,1)} %all-to-all-done.1.refs_2_, bf16[128,4096]{1,0:T(8,128)(2,1)} %bitcast.29, ...), custom_call_target="tpu_custom_call" | custom-call | flops 4000000000 | bytes 3000000 | tf_op jit(solution)/shard_map/attention_last/pallas_call | solution.py:399
  101.2 6.5 %all-to-all-start.2 = ((bf16[8,128,128]{2,1,0:T(8,128)(2,1)}), bf16[8,128,128]{2,1,0:T(8,128)(2,1)S(1)}, u32[]{:S(2)}, u32[]{:S(2)}) async-start(bf16[8,128,128]{2,1,0:T(8,128)(2,1)} %bitcast.44), calls=%async_computation.2 | async-start | bytes 524288 | tf_op jit(solution)/shard_map/all_to_all | solution.py:58
  107.8 1.0 copy-done.4
  108.8 1.7 %up_gradients.1.ups_ref = bf16[8,64,128]{2,1,0:T(8,128)(2,1)S(1)} custom-call(s32[8]{0:T(128)S(1)} %copy-done.1, bf16[4,128,128]{2,1,0:T(8,128)(2,1)S(1)} %pad_maximum_fusion.5.own_ref, bf16[4,128,128]{2,1,0:T(8,128)(2,1)S(1)} %collective-permute-done.10.later_ref, bf16[4,128,128]{2,1,0:T(8,128)(2,1)S(1)} %collective-permute-done.11.earlier_ref, ...), custom_call_target="tpu_custom_call" | custom-call | flops 2000000000 | bytes 3000000 | tf_op jit(solution)/shard_map/up_gradients/pallas_call | solution.py:447
  110.5 2.2 %all-to-all-done.2.summed_ref = bf16[8,128,128]{2,1,0:T(8,128)(2,1)S(1)} async-done(((bf16[8,128,128]{2,1,0:T(8,128)(2,1)}), bf16[8,128,128]{2,1,0:T(8,128)(2,1)S(1)}, u32[]{:S(2)}, u32[]{:S(2)}) %all-to-all-start.2) | async-done | bytes 262176 | tf_op jit(solution)/shard_map/all_to_all | solution.py:58
  112.8 15.9 %all_to_all.30.both_ref = bf16[8,192,128]{2,1,0:T(8,128)(2,1)S(1)} all-to-all(bf16[8,192,128]{2,1,0:T(8,128)(2,1)S(1)} %gather_parts.1), channel_id=1, replica_groups=mesh['dp'=8,'ulysses'=32] {'dp'}, dimensions={0} | all-to-all | bytes 786432 | tf_op jit(solution)/shard_map/all_to_all | solution.py:58
  128.6 1.0 merge_gradients.1
  129.6 17.0 %all_to_all.31.in_ref = bf16[32,32,128]{2,1,0:T(8,128)(2,1)S(1)} all-to-all(bf16[32,32,128]{2,1,0:T(8,128)(2,1)S(1)} %merge_gradients.1), channel_id=1, replica_groups=mesh['dp'=8,'ulysses'=32] {'ulysses'}, dimensions={0} | all-to-all | bytes 524288 | tf_op jit(solution)/shard_map/all_to_all | solution.py:58
  146.7 10.2 %all_to_all.32.in_ref = f32[8,32,128]{2,1,0:T(8,128)S(1)} all-to-all(f32[8,32,128]{2,1,0:T(8,128)S(1)} %spread_sums.1), channel_id=1, replica_groups=mesh['dp'=8,'ulysses'=32] {'dp'}, dimensions={0} | all-to-all | bytes 262144 | tf_op jit(solution)/shard_map/all_to_all | solution.py:58
  (44 shorter events, 6.2 us)
Async XLA Ops:
  7.5 57.1 %all-to-all-start = ((bf16[8,128,1024]{2,1,0:T(8,128)(2,1)}), bf16[8,128,1024]{2,1,0:T(8,128)(2,1)S(1)}, u32[]{:S(2)}, u32[]{:S(2)}) async-start(bf16[8,128,1024]{2,1,0:T(8,128)(2,1)} %get-tuple-element.38), calls=%async_computation | async-start | bytes 4194304 | tf_op jit(solution)/shard_map/all_to_all | solution.py:58
  23.1 7.8 %collective-permute-start = (bf16[4,512,128]{2,1,0:T(8,128)(2,1)}, bf16[4,512,128]{2,1,0:T(8,128)(2,1)S(1)}, u32[]{:S(2)}, u32[]{:S(2)}) collective-permute-start(bf16[4,512,128]{2,1,0:T(8,128)(2,1)} %get-tuple-element.43), channel_id=1, source_target_pairs={{0,32},{32,0},{64,96},{96,64},{128,160},{160,128},{192,224},{224,1... | collective-permute-start | bytes 1572872 | tf_op jit(solution)/shard_map/ppermute | solution.py:584
  24.1 34.5 %collective-permute-start.4 = (bf16[4,128,512]{2,1,0:T(8,128)(2,1)}, bf16[4,128,512]{2,1,0:T(8,128)(2,1)}, u32[]{:S(2)}, u32[]{:S(2)}) collective-permute-start(bf16[4,128,512]{2,1,0:T(8,128)(2,1)} %get-tuple-element.45), channel_id=1, source_target_pairs={{0,28},{1,29},{2,30},{3,31},{4,8},{5,9},{6,10},{7,11},{8,4},{9,5},... | collective-permute-start | bytes 1572872 | tf_op jit(solution)/shard_map/ppermute | solution.py:582
  29.8 23.7 %collective-permute-start.5 = (bf16[4,128,512]{2,1,0:T(8,128)(2,1)}, bf16[4,128,512]{2,1,0:T(8,128)(2,1)S(1)}, u32[]{:S(2)}, u32[]{:S(2)}) collective-permute-start(bf16[4,128,512]{2,1,0:T(8,128)(2,1)} %get-tuple-element.46), channel_id=1, source_target_pairs={{0,28},{1,29},{2,30},{3,31},{4,8},{5,9},{6,10},{7,11},{8,4},{9,5},... | collective-permute-start | bytes 1572872 | tf_op jit(solution)/shard_map/ppermute | solution.py:581
  32.4 31.0 %collective-permute-start.1 = (bf16[2,512,128]{2,1,0:T(8,128)(2,1)}, bf16[2,512,128]{2,1,0:T(8,128)(2,1)S(1)}, u32[]{:S(2)}, u32[]{:S(2)}) collective-permute-start(bf16[2,512,128]{2,1,0:T(8,128)(2,1)} %pad_maximum_fusion.2), channel_id=1, source_target_pairs={{0,64},{32,96},{64,128},{96,160},{128,192},{160,224},{192,0},{224,... | collective-permute-start | bytes 786440 | tf_op jit(solution)/shard_map/ppermute | solution.py:586
  34.4 30.2 %collective-permute-start.2 = (bf16[2,512,128]{2,1,0:T(8,128)(2,1)}, bf16[2,512,128]{2,1,0:T(8,128)(2,1)S(1)}, u32[]{:S(2)}, u32[]{:S(2)}) collective-permute-start(bf16[2,512,128]{2,1,0:T(8,128)(2,1)} %pad_maximum_fusion.3), channel_id=1, source_target_pairs={{0,128},{32,160},{64,192},{96,224},{128,0},{160,32},{192,64},{224,... | collective-permute-start | bytes 786440 | tf_op jit(solution)/shard_map/ppermute | solution.py:586
  37.6 27.0 %collective-permute-start.3 = (bf16[2,512,128]{2,1,0:T(8,128)(2,1)}, bf16[2,512,128]{2,1,0:T(8,128)(2,1)S(1)}, u32[]{:S(2)}, u32[]{:S(2)}) collective-permute-start(bf16[2,512,128]{2,1,0:T(8,128)(2,1)} %pad_maximum_fusion.4), channel_id=1, source_target_pairs={{0,192},{32,224},{64,0},{96,32},{128,64},{160,96},{192,128},{224,1... | collective-permute-start | bytes 786440 | tf_op jit(solution)/shard_map/ppermute | solution.py:586
  53.5 0.8 copy-start.6
  56.5 24.0 %collective-permute-start.7 = (bf16[128,1152]{1,0:T(8,128)(2,1)}, bf16[128,1152]{1,0:T(8,128)(2,1)}, u32[]{:S(2)}, u32[]{:S(2)}) collective-permute-start(bf16[128,1152]{1,0:T(8,128)(2,1)} %get-tuple-element.47), channel_id=1, source_target_pairs={{0,1},{1,2},{2,3},{3,0},{4,5},{5,6},{6,7},{7,4},{8,9},{9,10},{10,1... | collective-permute-start | bytes 884744 | tf_op jit(solution)/shard_map/ppermute | solution.py:589
  58.6 21.9 %collective-permute-start.8 = (bf16[128,1152]{1,0:T(8,128)(2,1)}, bf16[128,1152]{1,0:T(8,128)(2,1)S(1)}, u32[]{:S(2)}, u32[]{:S(2)}) collective-permute-start(bf16[128,1152]{1,0:T(8,128)(2,1)} %get-tuple-element.48), channel_id=1, source_target_pairs={{0,2},{1,3},{2,0},{3,1},{4,6},{5,7},{6,4},{7,5},{8,10},{9,11},{10,... | collective-permute-start | bytes 884744 | tf_op jit(solution)/shard_map/ppermute | solution.py:589
  63.4 17.2 %collective-permute-start.9 = (bf16[128,1152]{1,0:T(8,128)(2,1)}, bf16[128,1152]{1,0:T(8,128)(2,1)}, u32[]{:S(2)}, u32[]{:S(2)}) collective-permute-start(bf16[128,1152]{1,0:T(8,128)(2,1)} %get-tuple-element.49), channel_id=1, source_target_pairs={{0,3},{1,0},{2,1},{3,2},{4,7},{5,4},{6,5},{7,6},{8,11},{9,8},{10,9... | collective-permute-start | bytes 884744 | tf_op jit(solution)/shard_map/ppermute | solution.py:589
  64.6 4.5 %copy-start.5 = (bf16[8,128,1024]{2,1,0:T(8,128)(2,1)}, bf16[8,128,1024]{2,1,0:T(8,128)(2,1)S(1)}, u32[]{:S(2)}) copy-start(bf16[8,128,1024]{2,1,0:T(8,128)(2,1)S(1)} %all-to-all-done) | copy-start | bytes 6291460
  64.6 27.7 %all-to-all-start.1 = ((bf16[4,2,128,512]{3,2,1,0:T(8,128)(2,1)}), bf16[4,2,128,512]{3,2,1,0:T(8,128)(2,1)}, u32[]{:S(2)}, u32[]{:S(2)}) async-start(bf16[4,2,128,512]{3,2,1,0:T(8,128)(2,1)} %pad_maximum_fusion), calls=%async_computation.1 | async-start | bytes 2097152 | tf_op jit(solution)/shard_map/all_to_all | solution.py:58
  69.1 13.0 %copy-start.8 = (bf16[128,128]{1,0:T(8,128)(2,1)S(1)}, bf16[128,128]{1,0:T(8,128)(2,1)}, u32[]{:S(2)}) copy-start(bf16[128,128]{1,0:T(8,128)(2,1)} %get-tuple-element.39.low_ref) | copy-start | bytes 98308
  80.5 4.4 %copy-start.7 = (bf16[128,1152]{1,0:T(8,128)(2,1)}, bf16[128,1152]{1,0:T(8,128)(2,1)S(1)}, u32[]{:S(2)}) copy-start(bf16[128,1152]{1,0:T(8,128)(2,1)S(1)} %collective-permute-done.8.refs_5_) | copy-start | bytes 884740
  82.1 10.2 %collective-permute-start.11 = (bf16[4,128,128]{2,1,0:T(8,128)(2,1)S(1)}, bf16[4,128,128]{2,1,0:T(8,128)(2,1)S(1)}, u32[]{:S(2)}, u32[]{:S(2)}) collective-permute-start(bf16[4,128,128]{2,1,0:T(8,128)(2,1)S(1)} %pad_maximum_fusion.5.own_ref), channel_id=1, source_target_pairs={{0,4},{1,5},{2,6},{3,7},{4,8},{5,9},{6,10},{7,11},{8,12},{9,13},{1... | collective-permute-start | bytes 393224 | tf_op jit(solution)/shard_map/ppermute | solution.py:600
  82.2 10.1 %collective-permute-start.10 = (bf16[4,128,128]{2,1,0:T(8,128)(2,1)S(1)}, bf16[4,128,128]{2,1,0:T(8,128)(2,1)S(1)}, u32[]{:S(2)}, u32[]{:S(2)}) collective-permute-start(bf16[4,128,128]{2,1,0:T(8,128)(2,1)S(1)} %pad_maximum_fusion.5.own_ref), channel_id=1, source_target_pairs={{0,28},{1,29},{2,30},{3,31},{4,0},{5,1},{6,2},{7,3},{8,4},{9,5},{1... | collective-permute-start | bytes 393224 | tf_op jit(solution)/shard_map/ppermute | solution.py:599
  84.9 7.4 %collective-permute-start.6 = (bf16[512,128]{1,0:T(8,128)(2,1)}, bf16[512,128]{1,0:T(8,128)(2,1)S(1)}, u32[]{:S(2)}, u32[]{:S(2)}) collective-permute-start(bf16[512,128]{1,0:T(8,128)(2,1)} %get-tuple-element.52), channel_id=1, source_target_pairs={{0,4},{1,5},{2,6},{3,7},{4,0},{5,1},{6,2},{7,3},{8,12},{9,13},{10,... | collective-permute-start | bytes 393224 | tf_op jit(solution)/shard_map/ppermute | solution.py:595
  92.3 0.7 copy-start.9
  93.0 14.8 %copy-start.1 = (s32[8]{0:T(128)S(1)}, s32[8]{0:T(128)}, u32[]{:S(2)}) copy-start(s32[8]{0:T(128)} %dynamic-slice_bitcast_fusion.spot.refs_1_) | copy-start | bytes 100
  93.0 14.8 %copy-start.2 = (bf16[1024,256]{1,0:T(8,128)(2,1)S(1)}, bf16[1024,256]{1,0:T(8,128)(2,1)}, u32[]{:S(2)}) copy-start(bf16[1024,256]{1,0:T(8,128)(2,1)} %get-tuple-element.64.refs_1_) | copy-start | bytes 1572868
  93.0 14.8 %copy-start.3 = (bf16[1024,512]{1,0:T(8,128)(2,1)S(1)}, bf16[1024,512]{1,0:T(8,128)(2,1)}, u32[]{:S(2)}) copy-start(bf16[1024,512]{1,0:T(8,128)(2,1)} %get-tuple-element.53.refs_0_) | copy-start | bytes 3145732
  101.2 11.5 %all-to-all-start.2 = ((bf16[8,128,128]{2,1,0:T(8,128)(2,1)}), bf16[8,128,128]{2,1,0:T(8,128)(2,1)S(1)}, u32[]{:S(2)}, u32[]{:S(2)}) async-start(bf16[8,128,128]{2,1,0:T(8,128)(2,1)} %bitcast.44), calls=%async_computation.2 | async-start | bytes 524288 | tf_op jit(solution)/shard_map/all_to_all | solution.py:58
  107.8 1.0 copy-start.4
  108.8 19.8 %copy-start = (s32[32]{0:T(128)S(1)}, s32[32]{0:T(128)}, u32[]{:S(2)}) copy-start(s32[32]{0:T(128)} %get-tuple-element.37.order.refs_0_) | copy-start | bytes 388

commit v5 on v4

--- a/solution.py
+++ b/solution.py
@@ -2,7 +2,6 @@
 
 import jax
 import jax.numpy as jnp
-import numpy as np
 from jax import lax
 from jax.experimental import pallas as pl
 from jax.experimental.pallas import tpu as pltpu
@@ -35,10 +34,6 @@
 ANYWHERE = pl.BlockSpec(memory_space=pltpu.HBM)
 SCALARS = pl.BlockSpec(memory_space=pltpu.SMEM)
 
-SPOTS = np.array(
-    [[u % 4, u % 8, (u + 4) % 8, PLANE * (u // 4 % 2), PLANE * (1 - u // 4 % 2), 0, 0, 0] for u in range(HEADS)],
-    np.int32,
-)
 SPOT_Y, SPOT_PLAIN, SPOT_SHIFT, SPOT_OWN_PLAIN, SPOT_OWN_SHIFT = range(5)
 
 
@@ -135,16 +130,19 @@
 
 
 HALF = HEADS // 2
-HEAD_SCRATCH = [
-    pltpu.VMEM((ROWS, HALF * HD), BF16),
-    pltpu.VMEM((ROWS, HALF * HD), BF16),
-    pltpu.VMEM((BOTH, HALF * HD), BF16),
-    pltpu.SemaphoreType.DMA((HALF, 5)),
-]
+
+
+def head_scratch(count):
+    return [
+        pltpu.VMEM((ROWS, count * HD), BF16),
+        pltpu.VMEM((ROWS, count * HD), BF16),
+        pltpu.VMEM((BOTH, count * HD), BF16),
+        pltpu.SemaphoreType.DMA((count, 5)),
+    ]
 
 
 def prepare_plain_kernel(flags, x_hbm, down_hbm, *refs):
-    frozen, (out_ref, order, low_ref, x_in, down_in, whole_sems, q_in, v_in, up_in, sems) = refs[:5], refs[5:]
+    frozen, (out_ref, order, spot, low_ref, x_in, down_in, whole_sems, q_in, v_in, up_in, sems) = refs[:5], refs[5:]
     wholes = [
         pltpu.make_async_copy(x_hbm, x_in, whole_sems.at[0]),
         pltpu.make_async_copy(down_hbm, down_in, whole_sems.at[1]),
@@ -152,6 +150,12 @@
     for copy in wholes:
         copy.start()
     order_heads(flags, order)
+    me = lax.axis_index("ulysses")
+    spot[SPOT_Y] = me % YS
+    spot[SPOT_PLAIN] = me % MEMBERS
+    spot[SPOT_SHIFT] = (me + YS) % MEMBERS
+    spot[SPOT_OWN_PLAIN] = me // YS % 2 * PLANE
+    spot[SPOT_OWN_SHIFT] = (1 - me // YS % 2) * PLANE
     places = [(out_ref, (p % MEMBERS, p // MEMBERS * 4 * HD)) for p in range(HALF)]
     copies = fetch_heads([order[p] for p in range(HALF)], places, *frozen, q_in, v_in, up_in, sems)
     for copy in wholes:
@@ -167,41 +171,44 @@
         "prepare_plain",
         1,
         [ANYWHERE] * 7,
-        [block((MEMBERS, ROWS, 8 * HD)), SCALARS, block((ROWS, BOTH))],
+        [block((MEMBERS, ROWS, 8 * HD)), SCALARS, SCALARS, block((ROWS, BOTH))],
         (
             jax.ShapeDtypeStruct((MEMBERS, ROWS, 8 * HD), BF16),
             jax.ShapeDtypeStruct((HEADS,), jnp.int32),
+            jax.ShapeDtypeStruct((MEMBERS,), jnp.int32),
             jax.ShapeDtypeStruct((ROWS, BOTH), BF16),
         ),
         [pltpu.VMEM((ROWS, WIDTH), BF16), pltpu.VMEM((BOTH, WIDTH), BF16), pltpu.SemaphoreType.DMA((2,))]
-        + HEAD_SCRATCH,
+        + head_scratch(HALF),
         (10**9, 8 * 10**6),
     )(flags, x, down, *frozen)
 
 
-def prepare_shifted_kernel(order, spot, low_ref, *refs):
-    frozen, outs, scratch = refs[:5], refs[5:9], refs[9:]
+def prepare_shifted_kernel(item, order, spot, low_ref, *refs):
+    frozen, outs, scratch = refs[:5], refs[5:7], refs[7:]
     y, own_half = spot[SPOT_Y], spot[SPOT_OWN_SHIFT] // PLANE
     heads, places = [], []
-    for item in range(2):
-        for other in range(2):
-            for dy in range(YS):
-                seat = (own_half + other) % 2 * YS + ((y + dy) % YS if item == 0 else dy)
-                heads.append(order[HALF + item * MEMBERS + seat])
-                places.append((outs[2 * item + other], (dy, 0)))
+    for other in range(2):
+        for step in range(YS):
+            seat = (own_half + other) % 2 * YS + ((y + step) % YS if item == 2 else step)
+            heads.append(order[item * MEMBERS + seat])
+            places.append((outs[other], (step, 0)))
     copies = fetch_heads(heads, places, *frozen, *scratch)
     raise_heads(low_ref[...], copies, places, *scratch[:3])
 
 
-def prepare_shifted(order, spot, low, frozen):
-    return call(
-        prepare_shifted_kernel,
-        "prepare_shifted",
+def prepare_shifted(item, order, spot, low, frozen):
+    def body(*refs):
+        prepare_shifted_kernel(item, *refs)
+
+    return call(
+        body,
+        "prepare_third" if item == 2 else "prepare_last",
         2,
         [block((ROWS, BOTH))] + [ANYWHERE] * 5,
-        [block((YS, ROWS, 4 * HD))] * 4,
-        (jax.ShapeDtypeStruct((YS, ROWS, 4 * HD), BF16),) * 4,
-        HEAD_SCRATCH,
+        [block((YS, ROWS, 4 * HD))] * 2,
+        (jax.ShapeDtypeStruct((YS, ROWS, 4 * HD), BF16),) * 2,
+        head_scratch(MEMBERS),
         (10**9, 8 * 10**6),
     )(order, spot, low, *frozen)
 
@@ -227,46 +234,41 @@
     )(low, own, other)
 
 
-def turn_kernel(spot, x_ref, kept_ref, other_ref):
+def turn_kernel(spot, x_ref, *out_refs):
     x, core = spot[0] // CS, spot[0] % CS
-
-    def fill(refs):
-        for u in range(HEADS):
-            turned = x_ref[:, pl.ds(u * HD, HD)].T
-            for d in range(SLICES):
-                step = (d // CS - x + XS) % XS
-                refs[d % CS][step, pl.ds(u * PIECE, PIECE), :] = turned[d * PIECE : (d + 1) * PIECE]
-
-    @pl.when(core == 0)
-    def _():
-        fill((kept_ref, other_ref))
-
-    @pl.when(core != 0)
-    def _():
-        fill((other_ref, kept_ref))
+    *out_refs, stage = out_refs
+    for u in range(HEADS):
+        stage[pl.ds(u * HD, HD), :] = x_ref[:, pl.ds(u * HD, HD)].T
+    for step, out_ref in enumerate(out_refs):
+        for other in range(CS):
+            d = (x + step) % XS * CS + (core + other) % CS
+            for u in range(HEADS):
+                rows = pl.ds(pl.multiple_of(u * HD + d * PIECE, PIECE), PIECE)
+                out_ref[other, pl.ds(u * PIECE, PIECE), :] = stage[rows, :]
 
 
 def turn(place, x):
-    shape = (XS, HEADS * PIECE, ROWS)
+    shape = (CS, HEADS * PIECE, ROWS)
     return call(
         turn_kernel,
         "turn_input",
         1,
         [block(x.shape)],
-        [block(shape)] * 2,
-        (jax.ShapeDtypeStruct(shape, BF16),) * 2,
-        [],
+        [block(shape)] * XS,
+        (jax.ShapeDtypeStruct(shape, BF16),) * XS,
+        [pltpu.VMEM((WIDTH, ROWS), BF16)],
         (10**9, 2 * 10**6),
     )(place, x)
 
 
-def attend(x_ref, up, grads_ref, column, dv_acc):
+def attend(x_ref, up, grads_ref, column, dv_acc, arrive):
     factor = 1.0 / math.sqrt(HD)
     bend = factor * math.log2(math.e)
     row_ids = lax.broadcasted_iota(jnp.int32, (RB, RB), 0)
     column_ids = lax.broadcasted_iota(jnp.int32, (RB, RB), 1)
     keep = column_ids <= row_ids
     for i in range(GROUP // RB):
+        arrive(i)
         n = (i + 1) * RB
         rows = pl.ds(i * RB, RB)
         q = x_ref[rows, pl.ds(0, HD)]
@@ -300,13 +302,15 @@
 def attention_plain_kernel(order, spot, arrived, up_a, up_b, mine_ref, theirs_ref, grads_ref, xs, dv_acc, total, sems):
     copies = []
     for item in range(2):
-        source = arrived.at[:, pl.ds(item * 4 * HD, 4 * HD)]
-        copies.append(pltpu.make_async_copy(source, xs.at[item], sems.at[item]))
-        copies[-1].start()
-    copies[0].wait()
-    total[...] = attend(xs.at[0], up_a[...], grads_ref, 0, dv_acc)
-    copies[1].wait()
-    total[...] += attend(xs.at[1], up_b[...], grads_ref, 2 * HD, dv_acc)
+        for i in range(GROUP // RB):
+            rows = pl.ds(i * RB, RB)
+            source = arrived.at[rows, pl.ds(item * 4 * HD, 4 * HD)]
+            copies.append(pltpu.make_async_copy(source, xs.at[item, rows, :], sems.at[item, i]))
+            copies[-1].start()
+    arrive = lambda i: copies[i].wait()
+    total[...] = attend(xs.at[0], up_a[...], grads_ref, 0, dv_acc, arrive)
+    arrive = lambda i: copies[GROUP // RB + i].wait()
+    total[...] += attend(xs.at[1], up_b[...], grads_ref, 2 * HD, dv_acc, arrive)
     own = pl.multiple_of(spot[SPOT_OWN_PLAIN], PLANE)
     mine_ref[...] = total[pl.ds(own, PLANE), :]
     theirs_ref[...] = total[pl.ds(PLANE - own, PLANE), :].astype(BF16)
@@ -330,7 +334,7 @@
             pltpu.VMEM((2, GROUP, 4 * HD), BF16),
             pltpu.VMEM((GROUP, HD), F32),
             pltpu.VMEM((GROUP, BOTH), F32),
-            pltpu.SemaphoreType.DMA((2,)),
+            pltpu.SemaphoreType.DMA((2, GROUP // RB)),
         ],
         (2 * 10**10, 4 * 10**6),
     )(order, spot, arrived.reshape(GROUP, 8 * HD), up, up)
@@ -344,29 +348,40 @@
         blocks = [[arrived.at[s, half] for half in range(2)] for s in range(YS)]
         sources = range(YS)
     else:
-        own_ref, other_ref, *pieces = refs[:5]
-        up, back_ref, grads_ref, x_in, dv_acc, sems = refs[5:]
+        low_ref, own_ref, other_ref, *pieces = refs[:6]
+        up, back_ref, grads_ref, lows_ref, x_in, dv_acc, sems = refs[6:]
         blocks = [[own_ref.at[0], other_ref.at[0]]]
         for piece in pieces:
             blocks.append([piece.at[:, pl.ds(half * 4 * HD, 4 * HD)] for half in range(2)])
         sources = [(y - dy + YS) % YS for dy in range(YS)]
-    copies = []
     for t, source in enumerate(sources):
         for half in range(2):
-            start = (own if half == 0 else PLANE - own) + source * ROWS
-            rows = pl.ds(pl.multiple_of(start, ROWS), ROWS)
-            copies.append(pltpu.make_async_copy(blocks[t][half], x_in.at[rows, :], sems.at[t, half]))
-            copies[-1].start()
+            at = (own if half == 0 else PLANE - own) // ROWS + source
+            rows = pl.ds(pl.multiple_of(at * ROWS, ROWS), ROWS)
+            pltpu.make_async_copy(blocks[t][half], x_in.at[rows, :], sems.at[at]).start()
+
+    def arrive(i):
+        for at in range(i * RB // ROWS, (i + 1) * RB // ROWS):
+            pltpu.make_async_copy(blocks[0][0], x_in.at[pl.ds(at * ROWS, ROWS), :], sems.at[at]).wait()
+
     if last:
         pairs = ((before_hbm, before_ref), (mine_hbm, mine_ref), (theirs_hbm, theirs_ref))
         others = [pltpu.make_async_copy(*pair, more_sems.at[t]) for t, pair in enumerate(pairs)]
         for copy in others:
             copy.start()
-    for copy in copies:
-        copy.wait()
-    back = attend(x_in, up[...], grads_ref, 0, dv_acc)
+    else:
+        sources = [low_ref] + [piece.at[:, pl.ds(8 * HD, BOTH)] for piece in pieces]
+        others = [
+            pltpu.make_async_copy(source, lows_ref.at[dy], sems.at[MEMBERS + dy])
+            for dy, source in enumerate(sources)
+        ]
+        for copy in others:
+            copy.start()
+    back = attend(x_in, up[...], grads_ref, 0, dv_acc, arrive)
     if not last:
         back_ref[...] = back
+        for copy in others:
+            copy.wait()
         return
     save = pltpu.make_async_copy(grads_ref, grads_hbm, more_sems.at[3])
     save.start()
@@ -392,6 +407,8 @@
 def attention_shifted(item, order, spot, arrived, up, *more):
     last = len(more) > 0
     shapes = [((GROUP, BOTH), BF16 if last else F32), ((GROUP, 2 * HD), BF16)]
+    if not last:
+        shapes.append(((YS, ROWS, BOTH), BF16))
 
     def body(*refs):
         attention_shifted_kernel(last, *refs)
@@ -403,9 +420,9 @@
         [pl.BlockSpec(memory_space=pl.ANY) if last else ANYWHERE] * len(arrived)
         + [up_columns(item)]
         + [ANYWHERE] * len(more),
-        [block(shapes[0][0]), ANYWHERE if last else block(shapes[1][0])],
+        [block(shapes[0][0]), ANYWHERE] if last else [block(shape) for shape, _ in shapes],
         [jax.ShapeDtypeStruct(*shape) for shape in shapes],
-        [pltpu.VMEM((GROUP, 4 * HD), BF16), pltpu.VMEM((GROUP, HD), F32), pltpu.SemaphoreType.DMA((YS, 2))]
+        [pltpu.VMEM((GROUP, 4 * HD), BF16), pltpu.VMEM((GROUP, HD), F32), pltpu.SemaphoreType.DMA((3 * YS,))]
         + LAST_SCRATCH * last,
         (4 * 10**9, 3 * 10**6) if last else (10**6, 10**4),
     )(order, spot, *arrived, up, *more)
@@ -480,14 +497,15 @@
 
 
 def merge_kernel(order, spot, place, both_ref, *refs):
-    x_refs, out_ref = refs[:-1], refs[-1]
+    x_refs, crossed_ref, out_ref = refs[:-2], refs[-2], refs[-1]
     x, core = place[0] // CS, place[0] % CS
     total = jnp.zeros((HEADS * PIECE, BOTH), F32)
     for dx in range(XS):
         for other in range(CS):
             s = (x - dx + XS) % XS * CS + (core + other) % CS
             back = both_ref[s, pl.ds(0, ROWS), :]
-            total += jnp.dot(x_refs[dx][other], back, preferred_element_type=F32)
+            part = x_refs[dx][0] if other == 0 else crossed_ref[dx]
+            total += jnp.dot(part, back, preferred_element_type=F32)
     total = (adapter_scale * total).astype(BF16)
     for u in range(HEADS):
         out_ref[u, pl.ds(0, PIECE), :] = total[u * PIECE : (u + 1) * PIECE]
@@ -499,19 +517,19 @@
         out_ref[head, pl.ds(PIECE, PIECE), :] = ups[item * PIECE : (item + 1) * PIECE]
 
 
-def merge(order, spot, place, both, pieces):
+def merge(order, spot, place, both, pieces, crossed):
     shape = (HEADS, 2 * PIECE, HD)
     return call(
         merge_kernel,
         "merge_gradients",
         3,
-        [block(both.shape)] + [block(piece.shape) for piece in pieces],
+        [block(both.shape)] + [block((1, *piece.shape[1:])) for piece in pieces] + [block(crossed.shape)],
         block(shape),
         jax.ShapeDtypeStruct(shape, BF16),
         [],
         (2 * 10**8, 2 * 10**6),
         16,
-    )(order, spot, place, both, *pieces)
+    )(order, spot, place, both, *pieces, crossed)
 
 
 def spread_kernel(in_ref, out_ref):
@@ -569,44 +587,42 @@
     shifted,
 ):
     tokens = normalized_input[0]
-    spot = lax.dynamic_slice(jnp.asarray(SPOTS), (lax.axis_index("ulysses"), 0), (1, 8)).reshape(8)
     place = lax.axis_index("dp").reshape(1)
     up = adapter_up_maps.reshape(BOTH, WIDTH)
     down = adapter_down_maps.transpose(0, 2, 1).reshape(BOTH, WIDTH)
 
     frozen = (frozen_queries[0], frozen_keys[0], frozen_values[0], output_gradient[0], up)
-    sent, order, low = prepare_plain(shifted.astype(jnp.int32), tokens, down, frozen)
+    sent, order, spot, low = prepare_plain(shifted.astype(jnp.int32), tokens, down, frozen)
     plain = exchange(sent, "ulysses", PLAIN_GROUPS)
-    own_c, other_c, own_d, other_d = prepare_shifted(order, spot, low, frozen)
+    own_c, other_c = prepare_shifted(2, order, spot, low, frozen)
     other_c = lax.ppermute(other_c, "ulysses", SHIFT_SWAP)
+    own_d, other_d = prepare_shifted(3, order, spot, after(low, own_c), frozen)
+    turned = turn(place, after(tokens, own_d))
+    pieces = [turned[0]] + [lax.ppermute(turned[dx], "dp", x_shift(dx)) for dx in (1, 2, 3)]
+    other_d, other_c = after((other_d, other_c), turned)
     other_d = lax.ppermute(other_d, "ulysses", SHIFT_SWAP)
-    kept, other = turn(place, after(tokens, own_c))
-    other = lax.ppermute(other, "dp", CORE_SWAP)
-    pieces = [jnp.stack([kept[dx], other[dx]]) for dx in range(XS)]
-    pieces = pieces[:1] + [lax.ppermute(pieces[dx], "dp", x_shift(dx)) for dx in (1, 2, 3)]
 
     packed = pack(low, own_c, other_c)
     arrived_c = [lax.ppermute(packed[dy - 1], "ulysses", y_shift(dy)) for dy in (1, 2, 3)]
     sent = jnp.stack([own_d, other_d], axis=1)
-    plain, pieces, sent = after((plain, pieces, sent), packed)
+    crossed = jnp.stack([piece[1] for piece in pieces])
+    plain, pieces, sent, crossed = after((plain, pieces, sent, crossed), packed)
 
     arrived_d = exchange(sent, "ulysses", Y_GROUPS)
+    crossed = lax.ppermute(crossed, "dp", CORE_SWAP)
     mine, theirs, grads_plain = attention_plain(order, spot, plain, up)
     theirs = lax.ppermute(theirs, "ulysses", PLAIN_SWAP)
     arrived_c = after(arrived_c, grads_plain, sent)
-    partial, grads_c = attention_shifted(2, order, spot, [own_c, other_c, *arrived_c], up)
-    own = jnp.stack([low] + [array[:, 8 * HD :] for array in arrived_c])
+    partial, grads_c, own = attention_shifted(2, order, spot, [low, own_c, other_c, *arrived_c], up)
     later = lax.ppermute(own, "ulysses", z_shift(-1))
     earlier = lax.ppermute(own, "ulysses", z_shift(1))
 
-    arrived_d, theirs, later, earlier = after((arrived_d, theirs, later, earlier), partial)
-    partial, grads_d = attention_shifted(
-        3, order, spot, [arrived_d], up, partial, mine, theirs
-    )
+    arrived_d, theirs, crossed = after((arrived_d, theirs, crossed), partial)
+    partial, grads_d = attention_shifted(3, order, spot, [arrived_d], up, partial, mine, theirs)
     summed = exchange(partial.reshape(MEMBERS, ROWS, BOTH), "ulysses", SHIFT_GROUPS)
     ups = up_gradients(spot, own, later, earlier, (grads_plain, grads_c, grads_d))
     both = exchange(gather_parts(summed, ups), "dp")
-    both = exchange(merge(order, spot, place, both, pieces), "ulysses")
+    both = exchange(merge(order, spot, place, both, pieces, crossed), "ulysses")
     both = exchange(spread(both), "dp")
     grad_down, grad_up = finish(both)
     return (grad_down.transpose(0, 2, 1), grad_up)

time: 159 us -> 162 us (1.019)
  starting transfers between devices: 36.5 us -> 42.1 us
  Pallas kernels: 47.5 us -> 52.8 us
  blocking collectives: 43.1 us -> 40.7 us
  other arithmetic: 5.46 us -> 3.21 us
  local copies, waits for them, and re-layouts: 7.17 us -> 5.19 us
    ppermute x1, waiting for transfers between devices: 14.8 us -> 4.33 us  [per_device(): other_c = lax.ppermute(other_c, 'ulysses', SHIFT_SWAP)]
    ppermute x4, waiting for transfers between devices: 0.01 us -> 7.59 us  [the longest x3 7.59 us: per_device(): lax.ppermute(turned[dx], 'dp', x_shift(dx))]
    ppermute x1, starting transfers between devices: 0.03 us -> 5.49 us  [per_device(): other_c = lax.ppermute(other_c, 'ulysses', SHIFT_SWAP)]
    ppermute x1, waiting for transfers between devices: 0.01 us -> 3.72 us  [per_device(): earlier = lax.ppermute(own, 'ulysses', z_shift(1))]
    ppermute x4, starting transfers between devices: 5.78 us -> 9.35 us  [the longest x3 4.82 us: per_device(): lax.ppermute(turned[dx], 'dp', x_shift(dx))]
    ppermute x1, starting transfers between devices: 5.68 us -> 2.38 us  [per_device(): other_d = lax.ppermute(other_d, 'ulysses', SHIFT_SWAP)]
    pallas_call x3 -> x4, Pallas kernels: 8.94 us -> 12.1 us  [the longest x2 8.53 us: prepare_shifted(): call(body, 'prepare_third' if item == 2 else 'prepare_last', 2, [block((R...]
    all_to_all x3, blocking collectives: 43.1 us -> 40.7 us  [exchange(): lax.all_to_all(member, axis, 0, 0, tiled=True, axis_index_groups=groups)]
  transfers between devices with their start and end apart: 15 -> 15, of which waited for: 2 -> 5; matrix products, arithmetic and copies ran while one was open for 6% -> 3% of each run, Pallas kernels for 19% -> 22%
where the time goes in v5:
time: 162 us; the launch traced here: 161 us
  Pallas kernels  52.8 us (33%)
  starting transfers between devices  42.1 us (26%)
  blocking collectives  40.7 us (25%)
  waiting for transfers between devices  15.7 us (10%)
  local copies, waits for them, and re-layouts  5.19 us (3%)
  other arithmetic  3.21 us (2%)
    all_to_all x3, blocking collectives, exchange(): lax.all_to_all(member, axis, 0, 0, tiled=True, axis_index_groups=groups)  40.7 us
    all_to_all x3, starting transfers between devices, exchange(): lax.all_to_all(member, axis, 0, 0, tiled=True, axis_index_groups=groups)  17.2 us
    pallas_call x2, Pallas kernels, attention_shifted(): call(body, 'attention_last' if last else 'attention_third', 2, [pl.BlockS...  16.8 us
    pallas_call x1, Pallas kernels, attention_plain(): call(attention_plain_kernel, 'attention_plain', 2, [ANYWHERE, up_columns(...  12.3 us
    pallas_call x2, Pallas kernels, prepare_shifted(): call(body, 'prepare_third' if item == 2 else 'prepare_last', 2, [block((R...  8.53 us
    ppermute x3, waiting for transfers between devices, per_device(): lax.ppermute(turned[dx], 'dp', x_shift(dx))  7.59 us
    pallas_call x1, Pallas kernels, prepare_plain(): call(prepare_plain_kernel, 'prepare_plain', 1, [ANYWHERE] * 7, [block((ME...  6.9 us
    ppermute x1, starting transfers between devices, per_device(): other_c = lax.ppermute(other_c, 'ulysses', SHIFT_SWAP)  5.49 us
  transfers between devices with their start and end apart: 15, of which 5 were waited for; matrix products, arithmetic and copies ran while one was open for 3% of the time, Pallas kernels for 22%

profile of v5, /device:TPU:1, one launch (start us, length us, event | category | flops | bytes accessed | tf_op | source)
XLA Modules:
  0.0 160.6 jit_solution(14117851976305186587)
XLA Ops:
  0.6 6.9 %prepare_plain.1 = (bf16[8,128,1024]{2,1,0:T(8,128)(2,1)}, s32[32]{0:T(128)}, s32[8]{0:T(128)}, bf16[128,128]{1,0:T(8,128)(2,1)}) custom-call(s32[32]{0:T(128)} %flags.1, bf16[128,4096]{1,0:T(8,128)(2,1)} %bitcast.36, bf16[128,4096]{1,0:T(8,128)(2,1)} %bitcast.35, bf16[128,4096]{1,0:T(8,128)(2,1)} %bitcast.22, bf16[128,4096]{1,0:T(8,128)(2,1)} %bitcast.25, ...), custom_call_target="tpu_custom_call" | custom-call | flops 1000000000 | bytes 8000000 | tf_op jit(solution)/shard_map/prepare_plain/pallas_call | solution.py:169
  7.5 6.4 %all-to-all-start = ((bf16[8,128,1024]{2,1,0:T(8,128)(2,1)}), bf16[8,128,1024]{2,1,0:T(8,128)(2,1)S(1)}, u32[]{:S(2)}, u32[]{:S(2)}) async-start(bf16[8,128,1024]{2,1,0:T(8,128)(2,1)} %get-tuple-element.46), calls=%async_computation | async-start | bytes 4194304 | tf_op jit(solution)/shard_map/all_to_all | solution.py:53
  13.9 4.3 %prepare_third.1 = (bf16[4,128,512]{2,1,0:T(8,128)(2,1)}, bf16[4,128,512]{2,1,0:T(8,128)(2,1)}) custom-call(s32[32]{0:T(128)} %get-tuple-element.44.refs_0_.order, s32[8]{0:T(128)} %get-tuple-element.45.refs_1_.spot, bf16[128,128]{1,0:T(8,128)(2,1)} %get-tuple-element.49.refs_2_.low_ref, bf16[128,4096]{1,0:T(8,128)(2,1)} %bitcast.23, ...), custom_call_target="tpu_custom_call" | custom-call | flops 1000000000 | bytes 8000000 | tf_op jit(solution)/shard_map/prepare_third/pallas_call | solution.py:204
  18.2 5.5 %collective-permute-start.3 = (bf16[4,128,512]{2,1,0:T(8,128)(2,1)}, bf16[4,128,512]{2,1,0:T(8,128)(2,1)S(1)}, u32[]{:S(2)}, u32[]{:S(2)}) collective-permute-start(bf16[4,128,512]{2,1,0:T(8,128)(2,1)} %get-tuple-element.57), channel_id=1, source_target_pairs={{0,28},{1,29},{2,30},{3,31},{4,8},{5,9},{6,10},{7,11},{8,4},{9,5},... | collective-permute-start | bytes 1572872 | tf_op jit(solution)/shard_map/ppermute | solution.py:598
  23.7 4.3 %prepare_last.1 = (bf16[4,128,512]{2,1,0:T(8,128)(2,1)}, bf16[4,128,512]{2,1,0:T(8,128)(2,1)}) custom-call(s32[32]{0:T(128)} %get-tuple-element.44.refs_0_.order, s32[8]{0:T(128)} %get-tuple-element.45.refs_1_.spot, bf16[128,128]{1,0:T(8,128)(2,1)} %get-tuple-element.49.refs_2_.low_ref, bf16[128,4096]{1,0:T(8,128)(2,1)} %bitcast.24, ...), custom_call_target="tpu_custom_call" | custom-call | flops 1000000000 | bytes 8000000 | tf_op jit(solution)/shard_map/prepare_last/pallas_call | solution.py:204
  28.0 2.6 %turn_input.1 = (bf16[2,512,128]{2,1,0:T(8,128)(2,1)}, bf16[2,512,128]{2,1,0:T(8,128)(2,1)}, bf16[2,512,128]{2,1,0:T(8,128)(2,1)}, bf16[2,512,128]{2,1,0:T(8,128)(2,1)}) custom-call(s32[1]{0:T(128)} %bitcast.8.spot.place, bf16[128,4096]{1,0:T(8,128)(2,1)} %bitcast.37), custom_call_target="tpu_custom_call" | custom-call | flops 1000000000 | bytes 2000000 | tf_op jit(solution)/shard_map/turn_input/pallas_call | solution.py:252
  30.6 4.3 %collective-permute-done.3.other_ref.refs_4_ = bf16[4,128,512]{2,1,0:T(8,128)(2,1)S(1)} collective-permute-done((bf16[4,128,512]{2,1,0:T(8,128)(2,1)}, bf16[4,128,512]{2,1,0:T(8,128)(2,1)S(1)}, u32[]{:S(2)}, u32[]{:S(2)}) %collective-permute-start.3) | collective-permute-done | bytes 524320 | tf_op jit(solution)/shard_map/ppermute | solution.py:598
  34.9 2.4 %collective-permute-start.4 = (bf16[4,128,512]{2,1,0:T(8,128)(2,1)}, bf16[4,128,512]{2,1,0:T(8,128)(2,1)}, u32[]{:S(2)}, u32[]{:S(2)}) collective-permute-start(bf16[4,128,512]{2,1,0:T(8,128)(2,1)} %get-tuple-element.58), channel_id=1, source_target_pairs={{0,28},{1,29},{2,30},{3,31},{4,8},{5,9},{6,10},{7,11},{8,4},{9,5},... | collective-permute-start | bytes 1572872 | tf_op jit(solution)/shard_map/ppermute | solution.py:603
  37.3 1.2 collective-permute-start
  38.5 2.5 %collective-permute-start.1 = (bf16[2,512,128]{2,1,0:T(8,128)(2,1)}, bf16[2,512,128]{2,1,0:T(8,128)(2,1)S(1)}, u32[]{:S(2)}, u32[]{:S(2)}) collective-permute-start(bf16[2,512,128]{2,1,0:T(8,128)(2,1)} %get-tuple-element.54), channel_id=1, source_target_pairs={{0,128},{32,160},{64,192},{96,224},{128,0},{160,32},{192,64},{224,... | collective-permute-start | bytes 786440 | tf_op jit(solution)/shard_map/ppermute | solution.py:601
  40.9 1.2 collective-permute-start.2
  43.0 1.3 collective-permute-done.refs_1_
  44.3 6.0 %collective-permute-done.1.refs_2_ = bf16[2,512,128]{2,1,0:T(8,128)(2,1)S(1)} collective-permute-done((bf16[2,512,128]{2,1,0:T(8,128)(2,1)}, bf16[2,512,128]{2,1,0:T(8,128)(2,1)S(1)}, u32[]{:S(2)}, u32[]{:S(2)}) %collective-permute-start.1) | collective-permute-done | bytes 262176 | tf_op jit(solution)/shard_map/ppermute | solution.py:601
  51.5 2.2 %pack_first.1 = (bf16[128,1152]{1,0:T(8,128)(2,1)}, bf16[128,1152]{1,0:T(8,128)(2,1)}, bf16[128,1152]{1,0:T(8,128)(2,1)}) custom-call(bf16[128,128]{1,0:T(8,128)(2,1)} %get-tuple-element.49.refs_2_.low_ref, bf16[4,128,512]{2,1,0:T(8,128)(2,1)} %get-tuple-element.48.own_ref.refs_3_, bf16[4,128,512]{2,1,0:T(8,128)(2,1)} %copy-done.8), custom_call_target="tpu_custom_call" | custom-call | bytes 4000000 | tf_op jit(solution)/shard_map/pack_first/pallas_call | solution.py:225
  53.7 1.2 collective-permute-start.7
  54.9 2.4 %collective-permute-start.8 = (bf16[128,1152]{1,0:T(8,128)(2,1)}, bf16[128,1152]{1,0:T(8,128)(2,1)}, u32[]{:S(2)}, u32[]{:S(2)}) collective-permute-start(bf16[128,1152]{1,0:T(8,128)(2,1)} %get-tuple-element.61), channel_id=1, source_target_pairs={{0,2},{1,3},{2,0},{3,1},{4,6},{5,7},{6,4},{7,5},{8,10},{9,11},{10,... | collective-permute-start | bytes 884744 | tf_op jit(solution)/shard_map/ppermute | solution.py:606
  57.3 1.2 collective-permute-start.9
  58.5 2.3 %pad_maximum_fusion = bf16[4,2,128,512]{3,2,1,0:T(8,128)(2,1)} fusion(bf16[4,1,128,512]{3,2,1,0:T(8,128)(2,1)} %bitcast.10, bf16[4,1,128,512]{3,2,1,0:T(8,128)(2,1)} %bitcast.38), kind=kLoop, calls=%fused_computation | loop fusion | flops 524288 | bytes 2097152 | tf_op jit(solution)/shard_map/stack | solution.py:607
  60.8 1.4 copy-done.7
  62.2 4.3 %all-to-all-start.1 = ((bf16[4,2,128,512]{3,2,1,0:T(8,128)(2,1)}), bf16[4,2,128,512]{3,2,1,0:T(8,128)(2,1)}, u32[]{:S(2)}, u32[]{:S(2)}) async-start(bf16[4,2,128,512]{3,2,1,0:T(8,128)(2,1)} %pad_maximum_fusion), calls=%async_computation.1 | async-start | bytes 2097152 | tf_op jit(solution)/shard_map/all_to_all | solution.py:53
  66.5 4.5 %collective-permute-start.6 = (bf16[4,512,128]{2,1,0:T(8,128)(2,1)S(1)}, bf16[4,512,128]{2,1,0:T(8,128)(2,1)S(1)}, u32[]{:S(2)}, u32[]{:S(2)}) collective-permute-start(bf16[4,512,128]{2,1,0:T(8,128)(2,1)S(1)} %copy-done.9), channel_id=1, source_target_pairs={{0,32},{32,0},{64,96},{96,64},{128,160},{160,128},{192,224},{224,1... | collective-permute-start | bytes 1572872 | tf_op jit(solution)/shard_map/ppermute | solution.py:612
  71.0 12.3 %attention_plain.1 = (f32[512,128]{1,0:T(8,128)}, bf16[512,128]{1,0:T(8,128)(2,1)}, bf16[1024,512]{1,0:T(8,128)(2,1)}) custom-call(s32[32]{0:T(128)} %get-tuple-element.44.refs_0_.order, s32[8]{0:T(128)} %get-tuple-element.45.refs_1_.spot, bf16[1024,1024]{1,0:T(8,128)(2,1)} %bitcast.34, bf16[128,4096]{1,0:T(8,128)(2,1)} %bitcast.18, bf16[128,4096]{1,0:T(8,128)(2,1)} %bitcast.19), custom_call_target="tpu_custom_call" | custom-call | flops 20000000000 | bytes 4000000 | tf_op jit(solution)/shard_map/attention_plain/pallas_call | solution.py:326
  83.6 8.2 %attention_third.1 = (f32[1024,128]{1,0:T(8,128)}, bf16[1024,256]{1,0:T(8,128)(2,1)}, bf16[4,128,128]{2,1,0:T(8,128)(2,1)}) custom-call(s32[32]{0:T(128)} %get-tuple-element.44.refs_0_.order, s32[8]{0:T(128)} %get-tuple-element.45.refs_1_.spot, bf16[128,128]{1,0:T(8,128)(2,1)} %get-tuple-element.49.refs_2_.low_ref, ...), custom_call_target="tpu_custom_call" | custom-call | flops 1000000 | bytes 10000 | tf_op jit(solution)/shard_map/attention_third/pallas_call | solution.py:416
  92.5 8.6 %attention_last.1 = (bf16[1024,128]{1,0:T(8,128)(2,1)}, bf16[1024,256]{1,0:T(8,128)(2,1)}) custom-call(s32[32]{0:T(128)} %get-tuple-element.44.refs_0_.order, s32[8]{0:T(128)} %get-tuple-element.45.refs_1_.spot, bf16[4,2,128,512]{3,2,1,0:T(8,128)(2,1)} %all-to-all-done.1.refs_2_, bf16[128,4096]{1,0:T(8,128)(2,1)} %bitcast.21, ...), custom_call_target="tpu_custom_call" | custom-call | flops 4000000000 | bytes 3000000 | tf_op jit(solution)/shard_map/attention_last/pallas_call | solution.py:416
  101.1 6.5 %all-to-all-start.2 = ((bf16[8,128,128]{2,1,0:T(8,128)(2,1)}), bf16[8,128,128]{2,1,0:T(8,128)(2,1)S(1)}, u32[]{:S(2)}, u32[]{:S(2)}) async-start(bf16[8,128,128]{2,1,0:T(8,128)(2,1)} %bitcast.39), calls=%async_computation.2 | async-start | bytes 524288 | tf_op jit(solution)/shard_map/all_to_all | solution.py:53
  107.7 2.7 %collective-permute-start.10 = (bf16[4,128,128]{2,1,0:T(8,128)(2,1)S(1)}, bf16[4,128,128]{2,1,0:T(8,128)(2,1)S(1)}, u32[]{:S(2)}, u32[]{:S(2)}) collective-permute-start(bf16[4,128,128]{2,1,0:T(8,128)(2,1)S(1)} %copy-done.4), channel_id=1, source_target_pairs={{0,28},{1,29},{2,30},{3,31},{4,0},{5,1},{6,2},{7,3},{8,4},{9,5},{1... | collective-permute-start | bytes 393224 | tf_op jit(solution)/shard_map/ppermute | solution.py:617
  110.4 3.7 %collective-permute-done.11.earlier_ref = bf16[4,128,128]{2,1,0:T(8,128)(2,1)S(1)} collective-permute-done((bf16[4,128,128]{2,1,0:T(8,128)(2,1)S(1)}, bf16[4,128,128]{2,1,0:T(8,128)(2,1)S(1)}, u32[]{:S(2)}, u32[]{:S(2)}) %collective-permute-start.11) | collective-permute-done | bytes 131104 | tf_op jit(solution)/shard_map/ppermute | solution.py:618
  114.1 1.2 copy-done.5
  116.4 1.7 %up_gradients.1.ups_ref = bf16[8,64,128]{2,1,0:T(8,128)(2,1)S(1)} custom-call(s32[8]{0:T(128)S(1)} %copy-done.2, bf16[4,128,128]{2,1,0:T(8,128)(2,1)S(1)} %copy-done.4, bf16[4,128,128]{2,1,0:T(8,128)(2,1)S(1)} %collective-permute-done.10.later_ref, bf16[4,128,128]{2,1,0:T(8,128)(2,1)S(1)} %collective-permute-done.11.earlier_ref, ...), custom_call_target="tpu_custom_call" | custom-call | flops 2000000000 | bytes 3000000 | tf_op jit(solution)/shard_map/up_gradients/pallas_call | solution.py:464
  118.1 12.8 %all_to_all.30.both_ref = bf16[8,192,128]{2,1,0:T(8,128)(2,1)S(1)} all-to-all(bf16[8,192,128]{2,1,0:T(8,128)(2,1)S(1)} %gather_parts.1), channel_id=1, replica_groups=mesh['dp'=8,'ulysses'=32] {'dp'}, dimensions={0} | all-to-all | bytes 786432 | tf_op jit(solution)/shard_map/all_to_all | solution.py:53
  131.9 17.6 %all_to_all.31.in_ref = bf16[32,32,128]{2,1,0:T(8,128)(2,1)S(1)} all-to-all(bf16[32,32,128]{2,1,0:T(8,128)(2,1)S(1)} %merge_gradients.1), channel_id=1, replica_groups=mesh['dp'=8,'ulysses'=32] {'ulysses'}, dimensions={0} | all-to-all | bytes 524288 | tf_op jit(solution)/shard_map/all_to_all | solution.py:53
  149.6 10.2 %all_to_all.32.in_ref = f32[8,32,128]{2,1,0:T(8,128)S(1)} all-to-all(f32[8,32,128]{2,1,0:T(8,128)S(1)} %spread_sums.1), channel_id=1, replica_groups=mesh['dp'=8,'ulysses'=32] {'dp'}, dimensions={0} | all-to-all | bytes 262144 | tf_op jit(solution)/shard_map/all_to_all | solution.py:53
  (42 shorter events, 5.9 us)
Async XLA Ops:
  7.5 53.3 %all-to-all-start = ((bf16[8,128,1024]{2,1,0:T(8,128)(2,1)}), bf16[8,128,1024]{2,1,0:T(8,128)(2,1)S(1)}, u32[]{:S(2)}, u32[]{:S(2)}) async-start(bf16[8,128,1024]{2,1,0:T(8,128)(2,1)} %get-tuple-element.46), calls=%async_computation | async-start | bytes 4194304 | tf_op jit(solution)/shard_map/all_to_all | solution.py:53
  18.2 16.7 %collective-permute-start.3 = (bf16[4,128,512]{2,1,0:T(8,128)(2,1)}, bf16[4,128,512]{2,1,0:T(8,128)(2,1)S(1)}, u32[]{:S(2)}, u32[]{:S(2)}) collective-permute-start(bf16[4,128,512]{2,1,0:T(8,128)(2,1)} %get-tuple-element.57), channel_id=1, source_target_pairs={{0,28},{1,29},{2,30},{3,31},{4,8},{5,9},{6,10},{7,11},{8,4},{9,5},... | collective-permute-start | bytes 1572872 | tf_op jit(solution)/shard_map/ppermute | solution.py:598
  34.9 16.6 %copy-start.8 = (bf16[4,128,512]{2,1,0:T(8,128)(2,1)}, bf16[4,128,512]{2,1,0:T(8,128)(2,1)S(1)}, u32[]{:S(2)}) copy-start(bf16[4,128,512]{2,1,0:T(8,128)(2,1)S(1)} %collective-permute-done.3.other_ref.refs_4_) | copy-start | bytes 1572868
  34.9 23.6 %collective-permute-start.4 = (bf16[4,128,512]{2,1,0:T(8,128)(2,1)}, bf16[4,128,512]{2,1,0:T(8,128)(2,1)}, u32[]{:S(2)}, u32[]{:S(2)}) collective-permute-start(bf16[4,128,512]{2,1,0:T(8,128)(2,1)} %get-tuple-element.58), channel_id=1, source_target_pairs={{0,28},{1,29},{2,30},{3,31},{4,8},{5,9},{6,10},{7,11},{8,4},{9,5},... | collective-permute-start | bytes 1572872 | tf_op jit(solution)/shard_map/ppermute | solution.py:603
  37.3 7.0 %collective-permute-start = (bf16[2,512,128]{2,1,0:T(8,128)(2,1)}, bf16[2,512,128]{2,1,0:T(8,128)(2,1)S(1)}, u32[]{:S(2)}, u32[]{:S(2)}) collective-permute-start(bf16[2,512,128]{2,1,0:T(8,128)(2,1)} %get-tuple-element.53), channel_id=1, source_target_pairs={{0,64},{32,96},{64,128},{96,160},{128,192},{160,224},{192,0},{224,... | collective-permute-start | bytes 786440 | tf_op jit(solution)/shard_map/ppermute | solution.py:601
  38.5 11.9 %collective-permute-start.1 = (bf16[2,512,128]{2,1,0:T(8,128)(2,1)}, bf16[2,512,128]{2,1,0:T(8,128)(2,1)S(1)}, u32[]{:S(2)}, u32[]{:S(2)}) collective-permute-start(bf16[2,512,128]{2,1,0:T(8,128)(2,1)} %get-tuple-element.54), channel_id=1, source_target_pairs={{0,128},{32,160},{64,192},{96,224},{128,0},{160,32},{192,64},{224,... | collective-permute-start | bytes 786440 | tf_op jit(solution)/shard_map/ppermute | solution.py:601
  40.9 9.7 %collective-permute-start.2 = (bf16[2,512,128]{2,1,0:T(8,128)(2,1)}, bf16[2,512,128]{2,1,0:T(8,128)(2,1)S(1)}, u32[]{:S(2)}, u32[]{:S(2)}) collective-permute-start(bf16[2,512,128]{2,1,0:T(8,128)(2,1)} %get-tuple-element.55), channel_id=1, source_target_pairs={{0,192},{32,224},{64,0},{96,32},{128,64},{160,96},{192,128},{224,1... | collective-permute-start | bytes 786440 | tf_op jit(solution)/shard_map/ppermute | solution.py:601
  53.7 29.9 %collective-permute-start.7 = (bf16[128,1152]{1,0:T(8,128)(2,1)}, bf16[128,1152]{1,0:T(8,128)(2,1)}, u32[]{:S(2)}, u32[]{:S(2)}) collective-permute-start(bf16[128,1152]{1,0:T(8,128)(2,1)} %get-tuple-element.60), channel_id=1, source_target_pairs={{0,1},{1,2},{2,3},{3,0},{4,5},{5,6},{6,7},{7,4},{8,9},{9,10},{10,1... | collective-permute-start | bytes 884744 | tf_op jit(solution)/shard_map/ppermute | solution.py:606
  54.9 28.7 %collective-permute-start.8 = (bf16[128,1152]{1,0:T(8,128)(2,1)}, bf16[128,1152]{1,0:T(8,128)(2,1)}, u32[]{:S(2)}, u32[]{:S(2)}) collective-permute-start(bf16[128,1152]{1,0:T(8,128)(2,1)} %get-tuple-element.61), channel_id=1, source_target_pairs={{0,2},{1,3},{2,0},{3,1},{4,6},{5,7},{6,4},{7,5},{8,10},{9,11},{10,... | collective-permute-start | bytes 884744 | tf_op jit(solution)/shard_map/ppermute | solution.py:606
  57.3 26.3 %collective-permute-start.9 = (bf16[128,1152]{1,0:T(8,128)(2,1)}, bf16[128,1152]{1,0:T(8,128)(2,1)}, u32[]{:S(2)}, u32[]{:S(2)}) collective-permute-start(bf16[128,1152]{1,0:T(8,128)(2,1)} %get-tuple-element.62), channel_id=1, source_target_pairs={{0,3},{1,0},{2,1},{3,2},{4,7},{5,4},{6,5},{7,6},{8,11},{9,8},{10,9... | collective-permute-start | bytes 884744 | tf_op jit(solution)/shard_map/ppermute | solution.py:606
  58.5 8.0 %copy-start.9 = (bf16[4,512,128]{2,1,0:T(8,128)(2,1)S(1)}, bf16[4,512,128]{2,1,0:T(8,128)(2,1)}, u32[]{:S(2)}) copy-start(bf16[4,512,128]{2,1,0:T(8,128)(2,1)} %pad_maximum_fusion.1) | copy-start | bytes 1572868
  60.8 1.4 copy-start.7
  62.2 29.7 %all-to-all-start.1 = ((bf16[4,2,128,512]{3,2,1,0:T(8,128)(2,1)}), bf16[4,2,128,512]{3,2,1,0:T(8,128)(2,1)}, u32[]{:S(2)}, u32[]{:S(2)}) async-start(bf16[4,2,128,512]{3,2,1,0:T(8,128)(2,1)} %pad_maximum_fusion), calls=%async_computation.1 | async-start | bytes 2097152 | tf_op jit(solution)/shard_map/all_to_all | solution.py:53
  66.5 25.4 %collective-permute-start.6 = (bf16[4,512,128]{2,1,0:T(8,128)(2,1)S(1)}, bf16[4,512,128]{2,1,0:T(8,128)(2,1)S(1)}, u32[]{:S(2)}, u32[]{:S(2)}) collective-permute-start(bf16[4,512,128]{2,1,0:T(8,128)(2,1)S(1)} %copy-done.9), channel_id=1, source_target_pairs={{0,32},{32,0},{64,96},{96,64},{128,160},{160,128},{192,224},{224,1... | collective-permute-start | bytes 1572872 | tf_op jit(solution)/shard_map/ppermute | solution.py:612
  83.3 8.6 %collective-permute-start.5 = (bf16[512,128]{1,0:T(8,128)(2,1)}, bf16[512,128]{1,0:T(8,128)(2,1)S(1)}, u32[]{:S(2)}, u32[]{:S(2)}) collective-permute-start(bf16[512,128]{1,0:T(8,128)(2,1)} %get-tuple-element.65), channel_id=1, source_target_pairs={{0,4},{1,5},{2,6},{3,7},{4,0},{5,1},{6,2},{7,3},{8,12},{9,13},{10,... | collective-permute-start | bytes 393224 | tf_op jit(solution)/shard_map/ppermute | solution.py:614
  91.9 0.6 copy-start.10
  92.5 15.2 %copy-start.4 = (bf16[4,128,128]{2,1,0:T(8,128)(2,1)S(1)}, bf16[4,128,128]{2,1,0:T(8,128)(2,1)}, u32[]{:S(2)}) copy-start(bf16[4,128,128]{2,1,0:T(8,128)(2,1)} %get-tuple-element.76.own_ref) | copy-start | bytes 393220
  92.5 21.6 %copy-start.2 = (s32[8]{0:T(128)S(1)}, s32[8]{0:T(128)}, u32[]{:S(2)}) copy-start(s32[8]{0:T(128)} %get-tuple-element.45.refs_1_.spot) | copy-start | bytes 100
  92.5 21.6 %copy-start.3 = (bf16[1024,256]{1,0:T(8,128)(2,1)S(1)}, bf16[1024,256]{1,0:T(8,128)(2,1)}, u32[]{:S(2)}) copy-start(bf16[1024,256]{1,0:T(8,128)(2,1)} %get-tuple-element.77.refs_1_) | copy-start | bytes 1572868
  101.1 16.9 %all-to-all-start.2 = ((bf16[8,128,128]{2,1,0:T(8,128)(2,1)}), bf16[8,128,128]{2,1,0:T(8,128)(2,1)S(1)}, u32[]{:S(2)}, u32[]{:S(2)}) async-start(bf16[8,128,128]{2,1,0:T(8,128)(2,1)} %bitcast.39), calls=%async_computation.2 | async-start | bytes 524288 | tf_op jit(solution)/shard_map/all_to_all | solution.py:53
  107.7 6.4 %collective-permute-start.11 = (bf16[4,128,128]{2,1,0:T(8,128)(2,1)S(1)}, bf16[4,128,128]{2,1,0:T(8,128)(2,1)S(1)}, u32[]{:S(2)}, u32[]{:S(2)}) collective-permute-start(bf16[4,128,128]{2,1,0:T(8,128)(2,1)S(1)} %copy-done.4), channel_id=1, source_target_pairs={{0,4},{1,5},{2,6},{3,7},{4,8},{5,9},{6,10},{7,11},{8,12},{9,13},{1... | collective-permute-start | bytes 393224 | tf_op jit(solution)/shard_map/ppermute | solution.py:618
  107.7 6.4 %collective-permute-start.10 = (bf16[4,128,128]{2,1,0:T(8,128)(2,1)S(1)}, bf16[4,128,128]{2,1,0:T(8,128)(2,1)S(1)}, u32[]{:S(2)}, u32[]{:S(2)}) collective-permute-start(bf16[4,128,128]{2,1,0:T(8,128)(2,1)S(1)} %copy-done.4), channel_id=1, source_target_pairs={{0,28},{1,29},{2,30},{3,31},{4,0},{5,1},{6,2},{7,3},{8,4},{9,5},{1... | collective-permute-start | bytes 393224 | tf_op jit(solution)/shard_map/ppermute | solution.py:617
  114.1 1.2 copy-start.5
  115.3 1.0 copy-start.6
  116.4 14.6 %copy-start = (bf16[2,512,128]{2,1,0:T(8,128)(2,1)S(1)}, bf16[2,512,128]{2,1,0:T(8,128)(2,1)}, u32[]{:S(2)}) copy-start(bf16[2,512,128]{2,1,0:T(8,128)(2,1)} %get-tuple-element.79.refs_0_) | copy-start | bytes 786436
  116.4 14.6 %copy-start.1 = (s32[32]{0:T(128)S(1)}, s32[32]{0:T(128)}, u32[]{:S(2)}) copy-start(s32[32]{0:T(128)} %get-tuple-element.44.refs_0_.order) | copy-start | bytes 388

commit v6 on v5

--- a/solution.py
+++ b/solution.py
@@ -28,7 +28,6 @@
 PLAIN_GROUPS = [[MEMBERS * g + i for i in range(MEMBERS)] for g in range(4)]
 SHIFT_GROUPS = [[(MEMBERS * g + 4 + i) % HEADS for i in range(MEMBERS)] for g in range(4)]
 PLAIN_SWAP = [(u, u ^ 4) for u in range(HEADS)]
-Y_GROUPS = [[YS * z + y for y in range(YS)] for z in range(ZS)]
 SHIFT_SWAP = [(u, (((u + 4) % HEADS ^ 4) - 4) % HEADS) for u in range(HEADS)]
 CORE_SWAP = [(d, d ^ 1) for d in range(SLICES)]
 ANYWHERE = pl.BlockSpec(memory_space=pltpu.HBM)
@@ -184,30 +183,36 @@
     )(flags, x, down, *frozen)
 
 
-def prepare_shifted_kernel(item, order, spot, low_ref, *refs):
+def prepare_third_kernel(order, spot, low_ref, *refs):
     frozen, outs, scratch = refs[:5], refs[5:7], refs[7:]
     y, own_half = spot[SPOT_Y], spot[SPOT_OWN_SHIFT] // PLANE
     heads, places = [], []
     for other in range(2):
-        for step in range(YS):
-            seat = (own_half + other) % 2 * YS + ((y + step) % YS if item == 2 else step)
-            heads.append(order[item * MEMBERS + seat])
-            places.append((outs[other], (step, 0)))
+        for dy in range(YS):
+            seat = (own_half + other) % 2 * YS + (y + dy) % YS
+            heads.append(order[2 * MEMBERS + seat])
+            places.append((outs[other], (dy, 0)))
     copies = fetch_heads(heads, places, *frozen, *scratch)
     raise_heads(low_ref[...], copies, places, *scratch[:3])
 
 
+def prepare_last_kernel(order, spot, low_ref, *refs):
+    frozen, out_ref, scratch = refs[:5], refs[5], refs[6:]
+    heads = [order[3 * MEMBERS + seat] for seat in range(MEMBERS)]
+    places = [(out_ref, (seat, 0)) for seat in range(MEMBERS)]
+    copies = fetch_heads(heads, places, *frozen, *scratch)
+    raise_heads(low_ref[...], copies, places, *scratch[:3])
+
+
 def prepare_shifted(item, order, spot, low, frozen):
-    def body(*refs):
-        prepare_shifted_kernel(item, *refs)
-
-    return call(
-        body,
+    shapes = [(YS, ROWS, 4 * HD)] * 2 if item == 2 else [(MEMBERS, ROWS, 4 * HD)]
+    return call(
+        prepare_third_kernel if item == 2 else prepare_last_kernel,
         "prepare_third" if item == 2 else "prepare_last",
         2,
         [block((ROWS, BOTH))] + [ANYWHERE] * 5,
-        [block((YS, ROWS, 4 * HD))] * 2,
-        (jax.ShapeDtypeStruct((YS, ROWS, 4 * HD), BF16),) * 2,
+        [block(shape) for shape in shapes],
+        [jax.ShapeDtypeStruct(shape, BF16) for shape in shapes],
         head_scratch(MEMBERS),
         (10**9, 8 * 10**6),
     )(order, spot, low, *frozen)
@@ -261,14 +266,13 @@
     )(place, x)
 
 
-def attend(x_ref, up, grads_ref, column, dv_acc, arrive):
+def attend(x_ref, up, grads_ref, column, dv_acc):
     factor = 1.0 / math.sqrt(HD)
     bend = factor * math.log2(math.e)
     row_ids = lax.broadcasted_iota(jnp.int32, (RB, RB), 0)
     column_ids = lax.broadcasted_iota(jnp.int32, (RB, RB), 1)
     keep = column_ids <= row_ids
     for i in range(GROUP // RB):
-        arrive(i)
         n = (i + 1) * RB
         rows = pl.ds(i * RB, RB)
         q = x_ref[rows, pl.ds(0, HD)]
@@ -282,18 +286,17 @@
         weights = jnp.exp2((scores - top) * bend)
         total = jnp.sum(weights, axis=1, keepdims=True)
         attention = (weights * (1.0 / total)).astype(BF16)
-        output = jnp.dot(attention, v, preferred_element_type=F32)
         grad_attention = dot_t(g, v)
-        center = jnp.sum(g.astype(F32) * output, axis=1, keepdims=True)
+        center = jnp.sum(attention.astype(F32) * grad_attention, axis=1, keepdims=True)
         grad_scores = (attention.astype(F32) * (grad_attention - center)).astype(BF16)
         dq = jnp.dot(grad_scores, k, preferred_element_type=F32) * factor
         grads_ref[rows, pl.ds(column, HD)] = dq.astype(BF16)
-        dv = dot_0(attention, g)
+        dv = dot_0(g, attention)
         if i:
-            dv_acc[pl.ds(0, i * RB), :] += dv[: i * RB]
-        dv_acc[rows, :] = dv[i * RB :]
+            dv_acc[:, pl.ds(0, i * RB)] += dv[:, : i * RB]
+        dv_acc[:, rows] = dv[:, i * RB :]
     dq = grads_ref[:, pl.ds(column, HD)]
-    dv = dv_acc[...].astype(BF16)
+    dv = dv_acc[...].T.astype(BF16)
     grads_ref[:, pl.ds(column + HD, HD)] = dv
     lanes = lax.broadcasted_iota(jnp.int32, (GROUP, BOTH), 1)
     return jnp.where(lanes < RANK, dot_t(dq, up), dot_t(dv, up))
@@ -302,15 +305,13 @@
 def attention_plain_kernel(order, spot, arrived, up_a, up_b, mine_ref, theirs_ref, grads_ref, xs, dv_acc, total, sems):
     copies = []
     for item in range(2):
-        for i in range(GROUP // RB):
-            rows = pl.ds(i * RB, RB)
-            source = arrived.at[rows, pl.ds(item * 4 * HD, 4 * HD)]
-            copies.append(pltpu.make_async_copy(source, xs.at[item, rows, :], sems.at[item, i]))
-            copies[-1].start()
-    arrive = lambda i: copies[i].wait()
-    total[...] = attend(xs.at[0], up_a[...], grads_ref, 0, dv_acc, arrive)
-    arrive = lambda i: copies[GROUP // RB + i].wait()
-    total[...] += attend(xs.at[1], up_b[...], grads_ref, 2 * HD, dv_acc, arrive)
+        source = arrived.at[:, pl.ds(item * 4 * HD, 4 * HD)]
+        copies.append(pltpu.make_async_copy(source, xs.at[item], sems.at[item]))
+        copies[-1].start()
+    copies[0].wait()
+    total[...] = attend(xs.at[0], up_a[...], grads_ref, 0, dv_acc)
+    copies[1].wait()
+    total[...] += attend(xs.at[1], up_b[...], grads_ref, 2 * HD, dv_acc)
     own = pl.multiple_of(spot[SPOT_OWN_PLAIN], PLANE)
     mine_ref[...] = total[pl.ds(own, PLANE), :]
     theirs_ref[...] = total[pl.ds(PLANE - own, PLANE), :].astype(BF16)
@@ -332,9 +333,9 @@
         [jax.ShapeDtypeStruct(*shape) for shape in shapes],
         [
             pltpu.VMEM((2, GROUP, 4 * HD), BF16),
-            pltpu.VMEM((GROUP, HD), F32),
+            pltpu.VMEM((HD, GROUP), F32),
             pltpu.VMEM((GROUP, BOTH), F32),
-            pltpu.SemaphoreType.DMA((2, GROUP // RB)),
+            pltpu.SemaphoreType.DMA((2,)),
         ],
         (2 * 10**10, 4 * 10**6),
     )(order, spot, arrived.reshape(GROUP, 8 * HD), up, up)
@@ -345,25 +346,19 @@
     if last:
         arrived, up, before_hbm, mine_hbm, theirs_hbm, back_ref, grads_hbm, x_in, dv_acc, sems = refs[:10]
         total, before_ref, mine_ref, theirs_ref, grads_ref, more_sems = refs[10:]
-        blocks = [[arrived.at[s, half] for half in range(2)] for s in range(YS)]
-        sources = range(YS)
+        pltpu.make_async_copy(arrived, x_in, sems.at[0]).start()
     else:
         low_ref, own_ref, other_ref, *pieces = refs[:6]
         up, back_ref, grads_ref, lows_ref, x_in, dv_acc, sems = refs[6:]
-        blocks = [[own_ref.at[0], other_ref.at[0]]]
-        for piece in pieces:
-            blocks.append([piece.at[:, pl.ds(half * 4 * HD, 4 * HD)] for half in range(2)])
-        sources = [(y - dy + YS) % YS for dy in range(YS)]
-    for t, source in enumerate(sources):
-        for half in range(2):
-            at = (own if half == 0 else PLANE - own) // ROWS + source
-            rows = pl.ds(pl.multiple_of(at * ROWS, ROWS), ROWS)
-            pltpu.make_async_copy(blocks[t][half], x_in.at[rows, :], sems.at[at]).start()
-
-    def arrive(i):
-        for at in range(i * RB // ROWS, (i + 1) * RB // ROWS):
-            pltpu.make_async_copy(blocks[0][0], x_in.at[pl.ds(at * ROWS, ROWS), :], sems.at[at]).wait()
-
+        for dy in range(YS):
+            for half in range(2):
+                at = (own if half == 0 else PLANE - own) // ROWS + (y - dy + YS) % YS
+                rows = pl.ds(pl.multiple_of(at * ROWS, ROWS), ROWS)
+                if dy == 0:
+                    source = (own_ref, other_ref)[half].at[0]
+                else:
+                    source = pieces[dy - 1].at[:, pl.ds(half * 4 * HD, 4 * HD)]
+                pltpu.make_async_copy(source, x_in.at[rows, :], sems.at[2 * dy + half]).start()
     if last:
         pairs = ((before_hbm, before_ref), (mine_hbm, mine_ref), (theirs_hbm, theirs_ref))
         others = [pltpu.make_async_copy(*pair, more_sems.at[t]) for t, pair in enumerate(pairs)]
@@ -377,7 +372,12 @@
         ]
         for copy in others:
             copy.start()
-    back = attend(x_in, up[...], grads_ref, 0, dv_acc, arrive)
+    if last:
+        pltpu.make_async_copy(arrived, x_in, sems.at[0]).wait()
+    else:
+        for t in range(MEMBERS):
+            pltpu.make_async_copy(own_ref.at[0], x_in.at[pl.ds(t * ROWS, ROWS), :], sems.at[t]).wait()
+    back = attend(x_in, up[...], grads_ref, 0, dv_acc)
     if not last:
         back_ref[...] = back
         for copy in others:
@@ -422,7 +422,7 @@
         + [ANYWHERE] * len(more),
         [block(shapes[0][0]), ANYWHERE] if last else [block(shape) for shape, _ in shapes],
         [jax.ShapeDtypeStruct(*shape) for shape in shapes],
-        [pltpu.VMEM((GROUP, 4 * HD), BF16), pltpu.VMEM((GROUP, HD), F32), pltpu.SemaphoreType.DMA((3 * YS,))]
+        [pltpu.VMEM((GROUP, 4 * HD), BF16), pltpu.VMEM((HD, GROUP), F32), pltpu.SemaphoreType.DMA((3 * YS,))]
         + LAST_SCRATCH * last,
         (4 * 10**9, 3 * 10**6) if last else (10**6, 10**4),
     )(order, spot, *arrived, up, *more)
@@ -596,20 +596,16 @@
     plain = exchange(sent, "ulysses", PLAIN_GROUPS)
     own_c, other_c = prepare_shifted(2, order, spot, low, frozen)
     other_c = lax.ppermute(other_c, "ulysses", SHIFT_SWAP)
-    own_d, other_d = prepare_shifted(3, order, spot, after(low, own_c), frozen)
-    turned = turn(place, after(tokens, own_d))
+    turned = turn(place, after(tokens, own_c))
     pieces = [turned[0]] + [lax.ppermute(turned[dx], "dp", x_shift(dx)) for dx in (1, 2, 3)]
-    other_d, other_c = after((other_d, other_c), turned)
-    other_d = lax.ppermute(other_d, "ulysses", SHIFT_SWAP)
-
-    packed = pack(low, own_c, other_c)
+    (sent,) = prepare_shifted(3, order, spot, after(low, turned), frozen)
+
+    packed = pack(after(low, pieces, sent), own_c, other_c)
     arrived_c = [lax.ppermute(packed[dy - 1], "ulysses", y_shift(dy)) for dy in (1, 2, 3)]
-    sent = jnp.stack([own_d, other_d], axis=1)
-    crossed = jnp.stack([piece[1] for piece in pieces])
-    plain, pieces, sent, crossed = after((plain, pieces, sent, crossed), packed)
-
-    arrived_d = exchange(sent, "ulysses", Y_GROUPS)
-    crossed = lax.ppermute(crossed, "dp", CORE_SWAP)
+    plain, pieces, sent = after((plain, pieces, sent), packed)
+
+    arrived_d = exchange(sent, "ulysses", SHIFT_GROUPS).reshape(GROUP, 4 * HD)
+    crossed = lax.ppermute(jnp.stack([piece[1] for piece in pieces]), "dp", CORE_SWAP)
     mine, theirs, grads_plain = attention_plain(order, spot, plain, up)
     theirs = lax.ppermute(theirs, "ulysses", PLAIN_SWAP)
     arrived_c = after(arrived_c, grads_plain, sent)
@@ -617,7 +613,7 @@
     later = lax.ppermute(own, "ulysses", z_shift(-1))
     earlier = lax.ppermute(own, "ulysses", z_shift(1))
 
-    arrived_d, theirs, crossed = after((arrived_d, theirs, crossed), partial)
+    arrived_d, theirs, crossed, later, earlier = after((arrived_d, theirs, crossed, later, earlier), partial)
     partial, grads_d = attention_shifted(3, order, spot, [arrived_d], up, partial, mine, theirs)
     summed = exchange(partial.reshape(MEMBERS, ROWS, BOTH), "ulysses", SHIFT_GROUPS)
     ups = up_gradients(spot, own, later, earlier, (grads_plain, grads_c, grads_d))

time: 162 us -> 146 us (0.901)
  waiting for transfers between devices: 15.7 us -> 8.98 us
  Pallas kernels: 52.8 us -> 48.5 us
  starting transfers between devices: 42.1 us -> 38.7 us
  other arithmetic: 3.21 us -> 0.07 us
  blocking collectives: 40.7 us -> 43.2 us
    ppermute x1, waiting for transfers between devices: 4.33 us -> 0.01 us  [per_device(): other_c = lax.ppermute(other_c, 'ulysses', SHIFT_SWAP)]
    another operation x2 -> x1, other arithmetic: 3.21 us -> 0.07 us  [per_device(): jnp.stack([piece[1] for piece in pieces])]
    ppermute x2 -> x1, starting transfers between devices: 6.91 us -> 4 us  [per_device(): lax.ppermute(jnp.stack([piece[1] for piece in pieces]), 'dp', CORE_SWAP)]
    all_to_all x3, blocking collectives: 40.7 us -> 43.2 us  [exchange(): lax.all_to_all(member, axis, 0, 0, tiled=True, axis_index_groups=groups)]
    ppermute x3, waiting for transfers between devices: 7.59 us -> 5.19 us  [per_device(): lax.ppermute(turned[dx], 'dp', x_shift(dx))]
    pallas_call x1, Pallas kernels: 12.3 us -> 10.1 us  [attention_plain(): call(attention_plain_kernel, 'attention_plain', 2, [ANYWHERE, up_columns(...]
    pallas_call x2, Pallas kernels: 16.8 us -> 14.6 us  [attention_shifted(): call(body, 'attention_last' if last else 'attention_third', 2, [pl.BlockS...]
    unnamed x22 -> x20, local copies, waits for them, and re-layouts: 4.25 us -> 4.06 us
  transfers between devices with their start and end apart: 15 -> 14, of which waited for: 5 -> 5; matrix products, arithmetic and copies ran while one was open for 3% -> 0% of each run, Pallas kernels for 22% -> 22%
where the time goes in v6:
time: 146 us; the launch traced here: 144 us
  Pallas kernels  48.5 us (33%)
  blocking collectives  43.2 us (30%)
  starting transfers between devices  38.7 us (27%)
  waiting for transfers between devices  8.98 us (6%)
  local copies, waits for them, and re-layouts  4.1 us (3%)
    all_to_all x3, blocking collectives, exchange(): lax.all_to_all(member, axis, 0, 0, tiled=True, axis_index_groups=groups)  43.2 us
    all_to_all x3, starting transfers between devices, exchange(): lax.all_to_all(member, axis, 0, 0, tiled=True, axis_index_groups=groups)  16.8 us
    pallas_call x2, Pallas kernels, attention_shifted(): call(body, 'attention_last' if last else 'attention_third', 2, [pl.BlockS...  14.6 us
    pallas_call x1, Pallas kernels, attention_plain(): call(attention_plain_kernel, 'attention_plain', 2, [ANYWHERE, up_columns(...  10.1 us
    pallas_call x2, Pallas kernels, prepare_shifted(): call(prepare_third_kernel if item == 2 else prepare_last_kernel, 'prepare...  8.67 us
    pallas_call x1, Pallas kernels, prepare_plain(): call(prepare_plain_kernel, 'prepare_plain', 1, [ANYWHERE] * 7, [block((ME...  6.88 us
    ppermute x1, starting transfers between devices, per_device(): other_c = lax.ppermute(other_c, 'ulysses', SHIFT_SWAP)  5.49 us
    ppermute x3, waiting for transfers between devices, per_device(): lax.ppermute(turned[dx], 'dp', x_shift(dx))  5.19 us
  transfers between devices with their start and end apart: 14, of which 5 were waited for; matrix products, arithmetic and copies ran while one was open for 0% of the time, Pallas kernels for 22%

profile of v6, /device:TPU:1, one launch (start us, length us, event | category | flops | bytes accessed | tf_op | source)
XLA Modules:
  0.0 144.4 jit_solution(16864270301058321054)
XLA Ops:
  0.6 6.9 %prepare_plain.1 = (bf16[8,128,1024]{2,1,0:T(8,128)(2,1)}, s32[32]{0:T(128)}, s32[8]{0:T(128)}, bf16[128,128]{1,0:T(8,128)(2,1)}) custom-call(s32[32]{0:T(128)} %flags.1, bf16[128,4096]{1,0:T(8,128)(2,1)} %bitcast.35, bf16[128,4096]{1,0:T(8,128)(2,1)} %bitcast.34, bf16[128,4096]{1,0:T(8,128)(2,1)} %bitcast.21, bf16[128,4096]{1,0:T(8,128)(2,1)} %bitcast.24, ...), custom_call_target="tpu_custom_call" | custom-call | flops 1000000000 | bytes 8000000 | tf_op jit(solution)/shard_map/prepare_plain/pallas_call | solution.py:168
  7.5 6.4 %all-to-all-start = ((bf16[8,128,1024]{2,1,0:T(8,128)(2,1)}), bf16[8,128,1024]{2,1,0:T(8,128)(2,1)}, u32[]{:S(2)}, u32[]{:S(2)}) async-start(bf16[8,128,1024]{2,1,0:T(8,128)(2,1)} %get-tuple-element.44), calls=%async_computation | async-start | bytes 4194304 | tf_op jit(solution)/shard_map/all_to_all | solution.py:52
  13.9 4.3 %prepare_third.1 = (bf16[4,128,512]{2,1,0:T(8,128)(2,1)}, bf16[4,128,512]{2,1,0:T(8,128)(2,1)}) custom-call(s32[32]{0:T(128)} %get-tuple-element.42.order.refs_0_, s32[8]{0:T(128)} %get-tuple-element.43.spot.refs_1_, bf16[128,128]{1,0:T(8,128)(2,1)} %get-tuple-element.53.low_ref.refs_2_, bf16[128,4096]{1,0:T(8,128)(2,1)} %bitcast.22, ...), custom_call_target="tpu_custom_call" | custom-call | flops 1000000000 | bytes 8000000 | tf_op jit(solution)/shard_map/prepare_third/pallas_call | solution.py:209
  18.2 5.5 %collective-permute-start.3 = (bf16[4,128,512]{2,1,0:T(8,128)(2,1)}, bf16[4,128,512]{2,1,0:T(8,128)(2,1)S(1)}, u32[]{:S(2)}, u32[]{:S(2)}) collective-permute-start(bf16[4,128,512]{2,1,0:T(8,128)(2,1)} %get-tuple-element.54), channel_id=1, source_target_pairs={{0,28},{1,29},{2,30},{3,31},{4,8},{5,9},{6,10},{7,11},{8,4},{9,5},... | collective-permute-start | bytes 1572872 | tf_op jit(solution)/shard_map/ppermute | solution.py:598
  23.7 2.6 %turn_input.1 = (bf16[2,512,128]{2,1,0:T(8,128)(2,1)}, bf16[2,512,128]{2,1,0:T(8,128)(2,1)}, bf16[2,512,128]{2,1,0:T(8,128)(2,1)}, bf16[2,512,128]{2,1,0:T(8,128)(2,1)}) custom-call(s32[1]{0:T(128)} %bitcast.8.spot.place, bf16[128,4096]{1,0:T(8,128)(2,1)} %bitcast.36), custom_call_target="tpu_custom_call" | custom-call | flops 1000000000 | bytes 2000000 | tf_op jit(solution)/shard_map/turn_input/pallas_call | solution.py:257
  26.2 1.2 collective-permute-start
  27.4 2.5 %collective-permute-start.1 = (bf16[2,512,128]{2,1,0:T(8,128)(2,1)}, bf16[2,512,128]{2,1,0:T(8,128)(2,1)S(1)}, u32[]{:S(2)}, u32[]{:S(2)}) collective-permute-start(bf16[2,512,128]{2,1,0:T(8,128)(2,1)} %get-tuple-element.50), channel_id=1, source_target_pairs={{0,128},{32,160},{64,192},{96,224},{128,0},{160,32},{192,64},{224,... | collective-permute-start | bytes 786440 | tf_op jit(solution)/shard_map/ppermute | solution.py:600
  29.9 1.2 collective-permute-start.2
  31.1 4.4 %prepare_last.1 = bf16[8,128,512]{2,1,0:T(8,128)(2,1)} custom-call(s32[32]{0:T(128)} %get-tuple-element.42.order.refs_0_, s32[8]{0:T(128)} %get-tuple-element.43.spot.refs_1_, bf16[128,128]{1,0:T(8,128)(2,1)} %get-tuple-element.53.low_ref.refs_2_, bf16[128,4096]{1,0:T(8,128)(2,1)} %bitcast.23, bf16[128,4096]{1,0:T(8,128)(2,1)} %bitcast.26, ...), custom_call_target="tpu_custom_call" | custom-call | flops 1000000000 | bytes 8000000 | tf_op jit(solution)/shard_map/prepare_last/pallas_call | solution.py:209
  35.5 5.1 %collective-permute-done.1.refs_2_ = bf16[2,512,128]{2,1,0:T(8,128)(2,1)S(1)} collective-permute-done((bf16[2,512,128]{2,1,0:T(8,128)(2,1)}, bf16[2,512,128]{2,1,0:T(8,128)(2,1)S(1)}, u32[]{:S(2)}, u32[]{:S(2)}) %collective-permute-start.1) | collective-permute-done | bytes 262176 | tf_op jit(solution)/shard_map/ppermute | solution.py:600
  41.5 2.2 %pack_first.1 = (bf16[128,1152]{1,0:T(8,128)(2,1)}, bf16[128,1152]{1,0:T(8,128)(2,1)}, bf16[128,1152]{1,0:T(8,128)(2,1)}) custom-call(bf16[128,128]{1,0:T(8,128)(2,1)} %get-tuple-element.53.low_ref.refs_2_, bf16[4,128,512]{2,1,0:T(8,128)(2,1)} %get-tuple-element.46.own_ref.refs_3_, bf16[4,128,512]{2,1,0:T(8,128)(2,1)} %copy-done.7), custom_call_target="tpu_custom_call" | custom-call | bytes 4000000 | tf_op jit(solution)/shard_map/pack_first/pallas_call | solution.py:230
  43.7 1.2 collective-permute-start.6
  44.8 2.4 %collective-permute-start.7 = (bf16[128,1152]{1,0:T(8,128)(2,1)}, bf16[128,1152]{1,0:T(8,128)(2,1)}, u32[]{:S(2)}, u32[]{:S(2)}) collective-permute-start(bf16[128,1152]{1,0:T(8,128)(2,1)} %get-tuple-element.56), channel_id=1, source_target_pairs={{0,2},{1,3},{2,0},{3,1},{4,6},{5,7},{6,4},{7,5},{8,10},{9,11},{10,... | collective-permute-start | bytes 884744 | tf_op jit(solution)/shard_map/ppermute | solution.py:604
  47.2 1.2 collective-permute-start.8
  48.4 4.0 %all-to-all-start.1 = ((bf16[8,128,512]{2,1,0:T(8,128)(2,1)}), bf16[8,128,512]{2,1,0:T(8,128)(2,1)S(1)}, u32[]{:S(2)}, u32[]{:S(2)}) async-start(bf16[8,128,512]{2,1,0:T(8,128)(2,1)} %prepare_last.1), calls=%async_computation.1 | async-start | bytes 2097152 | tf_op jit(solution)/shard_map/all_to_all | solution.py:52
  52.5 4.0 %collective-permute-start.5 = (bf16[4,512,128]{2,1,0:T(8,128)(2,1)S(1)}, bf16[4,512,128]{2,1,0:T(8,128)(2,1)S(1)}, u32[]{:S(2)}, u32[]{:S(2)}) collective-permute-start(bf16[4,512,128]{2,1,0:T(8,128)(2,1)S(1)} %pad_maximum_fusion), channel_id=1, source_target_pairs={{0,32},{32,0},{64,96},{96,64},{128,160},{160,128},{192,224},{224,1... | collective-permute-start | bytes 1572872 | tf_op jit(solution)/shard_map/ppermute | solution.py:608
  56.5 10.1 %attention_plain.1 = (f32[512,128]{1,0:T(8,128)}, bf16[512,128]{1,0:T(8,128)(2,1)}, bf16[1024,512]{1,0:T(8,128)(2,1)}) custom-call(s32[32]{0:T(128)} %get-tuple-element.42.order.refs_0_, s32[8]{0:T(128)} %get-tuple-element.43.spot.refs_1_, bf16[1024,1024]{1,0:T(8,128)(2,1)} %bitcast.10.arrived, bf16[128,4096]{1,0:T(8,128)(2,1)} %bitcast.17, ...), custom_call_target="tpu_custom_call" | custom-call | flops 20000000000 | bytes 4000000 | tf_op jit(solution)/shard_map/attention_plain/pallas_call | solution.py:327
  66.8 7.0 %attention_third.1 = (f32[1024,128]{1,0:T(8,128)}, bf16[1024,256]{1,0:T(8,128)(2,1)}, bf16[4,128,128]{2,1,0:T(8,128)(2,1)}) custom-call(s32[32]{0:T(128)} %get-tuple-element.42.order.refs_0_, s32[8]{0:T(128)} %get-tuple-element.43.spot.refs_1_, bf16[128,128]{1,0:T(8,128)(2,1)} %get-tuple-element.53.low_ref.refs_2_, ...), custom_call_target="tpu_custom_call" | custom-call | flops 1000000 | bytes 10000 | tf_op jit(solution)/shard_map/attention_third/pallas_call | solution.py:416
  73.7 1.5 %collective-permute-start.10 = (bf16[4,128,128]{2,1,0:T(8,128)(2,1)}, bf16[4,128,128]{2,1,0:T(8,128)(2,1)S(1)}, u32[]{:S(2)}, u32[]{:S(2)}) collective-permute-start(bf16[4,128,128]{2,1,0:T(8,128)(2,1)} %get-tuple-element.69.own_ref), channel_id=1, source_target_pairs={{0,4},{1,5},{2,6},{3,7},{4,8},{5,9},{6,10},{7,11},{8,12},{9,13},{1... | collective-permute-start | bytes 393224 | tf_op jit(solution)/shard_map/ppermute | solution.py:614
  75.2 1.2 collective-permute-start.9
  76.5 2.6 %collective-permute-done.10.earlier_ref = bf16[4,128,128]{2,1,0:T(8,128)(2,1)S(1)} collective-permute-done((bf16[4,128,128]{2,1,0:T(8,128)(2,1)}, bf16[4,128,128]{2,1,0:T(8,128)(2,1)S(1)}, u32[]{:S(2)}, u32[]{:S(2)}) %collective-permute-start.10) | collective-permute-done | bytes 131104 | tf_op jit(solution)/shard_map/ppermute | solution.py:614
  79.3 1.0 copy-done.8
  80.3 7.7 %attention_last.1 = (bf16[1024,128]{1,0:T(8,128)(2,1)}, bf16[1024,256]{1,0:T(8,128)(2,1)}) custom-call(s32[32]{0:T(128)} %get-tuple-element.42.order.refs_0_, s32[8]{0:T(128)} %get-tuple-element.43.spot.refs_1_, bf16[1024,512]{1,0:T(8,128)(2,1)} %bitcast.33, bf16[128,4096]{1,0:T(8,128)(2,1)} %bitcast.20, f32[1024,128]{1,0:T(8,128)} %get-tuple-element.70.refs_4_, ...), custom_call_target="tpu_custom_call" | custom-call | flops 4000000000 | bytes 3000000 | tf_op jit(solution)/shard_map/attention_last/pallas_call | solution.py:416
  87.9 6.4 %all-to-all-start.2 = ((bf16[8,128,128]{2,1,0:T(8,128)(2,1)}), bf16[8,128,128]{2,1,0:T(8,128)(2,1)S(1)}, u32[]{:S(2)}, u32[]{:S(2)}) async-start(bf16[8,128,128]{2,1,0:T(8,128)(2,1)} %bitcast.37), calls=%async_computation.2 | async-start | bytes 524288 | tf_op jit(solution)/shard_map/all_to_all | solution.py:52
  94.4 1.2 copy-done.5
  95.6 1.0 copy-done.6
  96.7 1.7 %up_gradients.1.ups_ref = bf16[8,64,128]{2,1,0:T(8,128)(2,1)S(1)} custom-call(s32[8]{0:T(128)S(1)} %copy-done.2, bf16[4,128,128]{2,1,0:T(8,128)(2,1)S(1)} %copy-done.4, bf16[4,128,128]{2,1,0:T(8,128)(2,1)S(1)} %collective-permute-done.9.later_ref, bf16[4,128,128]{2,1,0:T(8,128)(2,1)S(1)} %collective-permute-done.10.earlier_ref, ...), custom_call_target="tpu_custom_call" | custom-call | flops 2000000000 | bytes 3000000 | tf_op jit(solution)/shard_map/up_gradients/pallas_call | solution.py:464
  98.3 1.0 all-to-all-done.2.summed_ref
  99.4 17.8 %all_to_all.30.both_ref = bf16[8,192,128]{2,1,0:T(8,128)(2,1)S(1)} all-to-all(bf16[8,192,128]{2,1,0:T(8,128)(2,1)S(1)} %gather_parts.1), channel_id=1, replica_groups=mesh['dp'=8,'ulysses'=32] {'dp'}, dimensions={0} | all-to-all | bytes 786432 | tf_op jit(solution)/shard_map/all_to_all | solution.py:52
  117.2 1.0 merge_gradients.1
  118.2 15.2 %all_to_all.31.in_ref = bf16[32,32,128]{2,1,0:T(8,128)(2,1)S(1)} all-to-all(bf16[32,32,128]{2,1,0:T(8,128)(2,1)S(1)} %merge_gradients.1), channel_id=1, replica_groups=mesh['dp'=8,'ulysses'=32] {'ulysses'}, dimensions={0} | all-to-all | bytes 524288 | tf_op jit(solution)/shard_map/all_to_all | solution.py:52
  133.4 10.2 %all_to_all.32.in_ref = f32[8,32,128]{2,1,0:T(8,128)S(1)} all-to-all(f32[8,32,128]{2,1,0:T(8,128)S(1)} %spread_sums.1), channel_id=1, replica_groups=mesh['dp'=8,'ulysses'=32] {'dp'}, dimensions={0} | all-to-all | bytes 262144 | tf_op jit(solution)/shard_map/all_to_all | solution.py:52
  (37 shorter events, 2.2 us)
Async XLA Ops:
  7.5 40.9 %all-to-all-start = ((bf16[8,128,1024]{2,1,0:T(8,128)(2,1)}), bf16[8,128,1024]{2,1,0:T(8,128)(2,1)}, u32[]{:S(2)}, u32[]{:S(2)}) async-start(bf16[8,128,1024]{2,1,0:T(8,128)(2,1)} %get-tuple-element.44), calls=%async_computation | async-start | bytes 4194304 | tf_op jit(solution)/shard_map/all_to_all | solution.py:52
  18.2 22.5 %collective-permute-start.3 = (bf16[4,128,512]{2,1,0:T(8,128)(2,1)}, bf16[4,128,512]{2,1,0:T(8,128)(2,1)S(1)}, u32[]{:S(2)}, u32[]{:S(2)}) collective-permute-start(bf16[4,128,512]{2,1,0:T(8,128)(2,1)} %get-tuple-element.54), channel_id=1, source_target_pairs={{0,28},{1,29},{2,30},{3,31},{4,8},{5,9},{6,10},{7,11},{8,4},{9,5},... | collective-permute-start | bytes 1572872 | tf_op jit(solution)/shard_map/ppermute | solution.py:598
  26.2 9.2 %collective-permute-start = (bf16[2,512,128]{2,1,0:T(8,128)(2,1)}, bf16[2,512,128]{2,1,0:T(8,128)(2,1)S(1)}, u32[]{:S(2)}, u32[]{:S(2)}) collective-permute-start(bf16[2,512,128]{2,1,0:T(8,128)(2,1)} %get-tuple-element.49), channel_id=1, source_target_pairs={{0,64},{32,96},{64,128},{96,160},{128,192},{160,224},{192,0},{224,... | collective-permute-start | bytes 786440 | tf_op jit(solution)/shard_map/ppermute | solution.py:600
  27.4 13.1 %collective-permute-start.1 = (bf16[2,512,128]{2,1,0:T(8,128)(2,1)}, bf16[2,512,128]{2,1,0:T(8,128)(2,1)S(1)}, u32[]{:S(2)}, u32[]{:S(2)}) collective-permute-start(bf16[2,512,128]{2,1,0:T(8,128)(2,1)} %get-tuple-element.50), channel_id=1, source_target_pairs={{0,128},{32,160},{64,192},{96,224},{128,0},{160,32},{192,64},{224,... | collective-permute-start | bytes 786440 | tf_op jit(solution)/shard_map/ppermute | solution.py:600
  29.9 10.8 %collective-permute-start.2 = (bf16[2,512,128]{2,1,0:T(8,128)(2,1)}, bf16[2,512,128]{2,1,0:T(8,128)(2,1)S(1)}, u32[]{:S(2)}, u32[]{:S(2)}) collective-permute-start(bf16[2,512,128]{2,1,0:T(8,128)(2,1)} %get-tuple-element.51), channel_id=1, source_target_pairs={{0,192},{32,224},{64,0},{96,32},{128,64},{160,96},{192,128},{224,1... | collective-permute-start | bytes 786440 | tf_op jit(solution)/shard_map/ppermute | solution.py:600
  35.4 16.9 %copy-start = (bf16[2,512,128]{2,1,0:T(8,128)(2,1)S(1)}, bf16[2,512,128]{2,1,0:T(8,128)(2,1)}, u32[]{:S(2)}) copy-start(bf16[2,512,128]{2,1,0:T(8,128)(2,1)} %get-tuple-element.61.refs_0_) | copy-start | bytes 786436
  40.7 0.8 copy-start.7
  43.7 23.1 %collective-permute-start.6 = (bf16[128,1152]{1,0:T(8,128)(2,1)}, bf16[128,1152]{1,0:T(8,128)(2,1)}, u32[]{:S(2)}, u32[]{:S(2)}) collective-permute-start(bf16[128,1152]{1,0:T(8,128)(2,1)} %get-tuple-element.55), channel_id=1, source_target_pairs={{0,1},{1,2},{2,3},{3,0},{4,5},{5,6},{6,7},{7,4},{8,9},{9,10},{10,1... | collective-permute-start | bytes 884744 | tf_op jit(solution)/shard_map/ppermute | solution.py:604
  44.8 21.9 %collective-permute-start.7 = (bf16[128,1152]{1,0:T(8,128)(2,1)}, bf16[128,1152]{1,0:T(8,128)(2,1)}, u32[]{:S(2)}, u32[]{:S(2)}) collective-permute-start(bf16[128,1152]{1,0:T(8,128)(2,1)} %get-tuple-element.56), channel_id=1, source_target_pairs={{0,2},{1,3},{2,0},{3,1},{4,6},{5,7},{6,4},{7,5},{8,10},{9,11},{10,... | collective-permute-start | bytes 884744 | tf_op jit(solution)/shard_map/ppermute | solution.py:604
  47.2 19.5 %collective-permute-start.8 = (bf16[128,1152]{1,0:T(8,128)(2,1)}, bf16[128,1152]{1,0:T(8,128)(2,1)}, u32[]{:S(2)}, u32[]{:S(2)}) collective-permute-start(bf16[128,1152]{1,0:T(8,128)(2,1)} %get-tuple-element.57), channel_id=1, source_target_pairs={{0,3},{1,0},{2,1},{3,2},{4,7},{5,4},{6,5},{7,6},{8,11},{9,8},{10,9... | collective-permute-start | bytes 884744 | tf_op jit(solution)/shard_map/ppermute | solution.py:604
  48.4 30.8 %all-to-all-start.1 = ((bf16[8,128,512]{2,1,0:T(8,128)(2,1)}), bf16[8,128,512]{2,1,0:T(8,128)(2,1)S(1)}, u32[]{:S(2)}, u32[]{:S(2)}) async-start(bf16[8,128,512]{2,1,0:T(8,128)(2,1)} %prepare_last.1), calls=%async_computation.1 | async-start | bytes 2097152 | tf_op jit(solution)/shard_map/all_to_all | solution.py:52
  52.5 26.7 %collective-permute-start.5 = (bf16[4,512,128]{2,1,0:T(8,128)(2,1)S(1)}, bf16[4,512,128]{2,1,0:T(8,128)(2,1)S(1)}, u32[]{:S(2)}, u32[]{:S(2)}) collective-permute-start(bf16[4,512,128]{2,1,0:T(8,128)(2,1)S(1)} %pad_maximum_fusion), channel_id=1, source_target_pairs={{0,32},{32,0},{64,96},{96,64},{128,160},{160,128},{192,224},{224,1... | collective-permute-start | bytes 1572872 | tf_op jit(solution)/shard_map/ppermute | solution.py:608
  66.6 9.9 %collective-permute-start.4 = (bf16[512,128]{1,0:T(8,128)(2,1)}, bf16[512,128]{1,0:T(8,128)(2,1)S(1)}, u32[]{:S(2)}, u32[]{:S(2)}) collective-permute-start(bf16[512,128]{1,0:T(8,128)(2,1)} %get-tuple-element.60), channel_id=1, source_target_pairs={{0,4},{1,5},{2,6},{3,7},{4,0},{5,1},{6,2},{7,3},{8,12},{9,13},{10,... | collective-permute-start | bytes 393224 | tf_op jit(solution)/shard_map/ppermute | solution.py:610
  73.7 5.3 %collective-permute-start.10 = (bf16[4,128,128]{2,1,0:T(8,128)(2,1)}, bf16[4,128,128]{2,1,0:T(8,128)(2,1)S(1)}, u32[]{:S(2)}, u32[]{:S(2)}) collective-permute-start(bf16[4,128,128]{2,1,0:T(8,128)(2,1)} %get-tuple-element.69.own_ref), channel_id=1, source_target_pairs={{0,4},{1,5},{2,6},{3,7},{4,8},{5,9},{6,10},{7,11},{8,12},{9,13},{1... | collective-permute-start | bytes 393224 | tf_op jit(solution)/shard_map/ppermute | solution.py:614
  75.2 4.0 %collective-permute-start.9 = (bf16[4,128,128]{2,1,0:T(8,128)(2,1)}, bf16[4,128,128]{2,1,0:T(8,128)(2,1)S(1)}, u32[]{:S(2)}, u32[]{:S(2)}) collective-permute-start(bf16[4,128,128]{2,1,0:T(8,128)(2,1)} %get-tuple-element.69.own_ref), channel_id=1, source_target_pairs={{0,28},{1,29},{2,30},{3,31},{4,0},{5,1},{6,2},{7,3},{8,4},{9,5},{1... | collective-permute-start | bytes 393224 | tf_op jit(solution)/shard_map/ppermute | solution.py:613
  76.5 2.8 %copy-start.9 = (bf16[512,128]{1,0:T(8,128)(2,1)}, bf16[512,128]{1,0:T(8,128)(2,1)S(1)}, u32[]{:S(2)}) copy-start(bf16[512,128]{1,0:T(8,128)(2,1)S(1)} %collective-permute-done.4.refs_6_) | copy-start | bytes 393220
  79.3 1.0 copy-start.8
  80.3 14.1 %copy-start.2 = (s32[8]{0:T(128)S(1)}, s32[8]{0:T(128)}, u32[]{:S(2)}) copy-start(s32[8]{0:T(128)} %get-tuple-element.43.spot.refs_1_) | copy-start | bytes 100
  80.3 14.1 %copy-start.3 = (bf16[1024,256]{1,0:T(8,128)(2,1)S(1)}, bf16[1024,256]{1,0:T(8,128)(2,1)}, u32[]{:S(2)}) copy-start(bf16[1024,256]{1,0:T(8,128)(2,1)} %get-tuple-element.77.refs_1_) | copy-start | bytes 1572868
  80.3 14.1 %copy-start.4 = (bf16[4,128,128]{2,1,0:T(8,128)(2,1)S(1)}, bf16[4,128,128]{2,1,0:T(8,128)(2,1)}, u32[]{:S(2)}) copy-start(bf16[4,128,128]{2,1,0:T(8,128)(2,1)} %get-tuple-element.69.own_ref) | copy-start | bytes 393220
  87.9 11.4 %all-to-all-start.2 = ((bf16[8,128,128]{2,1,0:T(8,128)(2,1)}), bf16[8,128,128]{2,1,0:T(8,128)(2,1)S(1)}, u32[]{:S(2)}, u32[]{:S(2)}) async-start(bf16[8,128,128]{2,1,0:T(8,128)(2,1)} %bitcast.37), calls=%async_computation.2 | async-start | bytes 524288 | tf_op jit(solution)/shard_map/all_to_all | solution.py:52
  94.4 1.2 copy-start.5
  95.6 1.0 copy-start.6
  96.7 20.5 %copy-start.1 = (s32[32]{0:T(128)S(1)}, s32[32]{0:T(128)}, u32[]{:S(2)}) copy-start(s32[32]{0:T(128)} %get-tuple-element.42.order.refs_0_) | copy-start | bytes 388

commit v7 on v6

--- a/solution.py
+++ b/solution.py
@@ -34,10 +34,6 @@
 SCALARS = pl.BlockSpec(memory_space=pltpu.SMEM)
 
 SPOT_Y, SPOT_PLAIN, SPOT_SHIFT, SPOT_OWN_PLAIN, SPOT_OWN_SHIFT = range(5)
-
-
-def z_shift(dz):
-    return [(z * YS + y, ((z + dz) % ZS) * YS + y) for z in range(ZS) for y in range(YS)]
 
 
 def y_shift(dy):
@@ -161,6 +157,8 @@
         copy.wait()
     low = dot_t(x_in[...], down_in[...]).astype(BF16)
     low_ref[...] = low
+    for seat in range(MEMBERS):
+        out_ref[seat, :, pl.ds(8 * HD, BOTH)] = low
     raise_heads(low, copies, places, q_in, v_in, up_in)
 
 
@@ -170,9 +168,9 @@
         "prepare_plain",
         1,
         [ANYWHERE] * 7,
-        [block((MEMBERS, ROWS, 8 * HD)), SCALARS, SCALARS, block((ROWS, BOTH))],
+        [block((MEMBERS, ROWS, 8 * HD + BOTH)), SCALARS, SCALARS, block((ROWS, BOTH))],
         (
-            jax.ShapeDtypeStruct((MEMBERS, ROWS, 8 * HD), BF16),
+            jax.ShapeDtypeStruct((MEMBERS, ROWS, 8 * HD + BOTH), BF16),
             jax.ShapeDtypeStruct((HEADS,), jnp.int32),
             jax.ShapeDtypeStruct((MEMBERS,), jnp.int32),
             jax.ShapeDtypeStruct((ROWS, BOTH), BF16),
@@ -200,12 +198,14 @@
     frozen, out_ref, scratch = refs[:5], refs[5], refs[6:]
     heads = [order[3 * MEMBERS + seat] for seat in range(MEMBERS)]
     places = [(out_ref, (seat, 0)) for seat in range(MEMBERS)]
+    for seat in range(MEMBERS):
+        out_ref[seat, :, pl.ds(4 * HD, BOTH)] = low_ref[...]
     copies = fetch_heads(heads, places, *frozen, *scratch)
     raise_heads(low_ref[...], copies, places, *scratch[:3])
 
 
 def prepare_shifted(item, order, spot, low, frozen):
-    shapes = [(YS, ROWS, 4 * HD)] * 2 if item == 2 else [(MEMBERS, ROWS, 4 * HD)]
+    shapes = [(YS, ROWS, 4 * HD)] * 2 if item == 2 else [(MEMBERS, ROWS, 4 * HD + BOTH)]
     return call(
         prepare_third_kernel if item == 2 else prepare_last_kernel,
         "prepare_third" if item == 2 else "prepare_last",
@@ -218,25 +218,24 @@
     )(order, spot, low, *frozen)
 
 
-def pack_kernel(low_ref, own_ref, other_ref, *out_refs):
+def pack_kernel(own_ref, other_ref, *out_refs):
     for dy, out_ref in enumerate(out_refs, 1):
         out_ref[:, pl.ds(0, 4 * HD)] = own_ref[dy]
         out_ref[:, pl.ds(4 * HD, 4 * HD)] = other_ref[dy]
-        out_ref[:, pl.ds(8 * HD, BOTH)] = low_ref[...]
-
-
-def pack(low, own, other):
-    shape = (ROWS, 8 * HD + BOTH)
+
+
+def pack(own, other):
+    shape = (ROWS, 8 * HD)
     return call(
         pack_kernel,
-        "pack_first",
+        "pack_third",
         0,
-        [block(low.shape)] + [block(own.shape)] * 2,
+        [block(own.shape)] * 2,
         [block(shape)] * 3,
         (jax.ShapeDtypeStruct(shape, BF16),) * 3,
         [],
         (0, 4 * 10**6),
-    )(low, own, other)
+    )(own, other)
 
 
 def turn_kernel(spot, x_ref, *out_refs):
@@ -338,18 +337,15 @@
             pltpu.SemaphoreType.DMA((2,)),
         ],
         (2 * 10**10, 4 * 10**6),
-    )(order, spot, arrived.reshape(GROUP, 8 * HD), up, up)
+    )(order, spot, arrived, up, up)
 
 
 def attention_shifted_kernel(last, order, spot, *refs):
     y, own = spot[SPOT_Y], spot[SPOT_OWN_SHIFT]
     if last:
-        arrived, up, before_hbm, mine_hbm, theirs_hbm, back_ref, grads_hbm, x_in, dv_acc, sems = refs[:10]
-        total, before_ref, mine_ref, theirs_ref, grads_ref, more_sems = refs[10:]
-        pltpu.make_async_copy(arrived, x_in, sems.at[0]).start()
-    else:
-        low_ref, own_ref, other_ref, *pieces = refs[:6]
-        up, back_ref, grads_ref, lows_ref, x_in, dv_acc, sems = refs[6:]
+        own_ref, other_ref, *pieces = refs[:5]
+        up, before_hbm, mine_hbm, theirs_hbm, back_ref, grads_hbm, x_in, dv_acc, sems = refs[5:14]
+        total, before_ref, mine_ref, theirs_ref, grads_ref, more_sems = refs[14:]
         for dy in range(YS):
             for half in range(2):
                 at = (own if half == 0 else PLANE - own) // ROWS + (y - dy + YS) % YS
@@ -359,29 +355,22 @@
                 else:
                     source = pieces[dy - 1].at[:, pl.ds(half * 4 * HD, 4 * HD)]
                 pltpu.make_async_copy(source, x_in.at[rows, :], sems.at[2 * dy + half]).start()
+    else:
+        arrived, up, back_ref, grads_ref, x_in, dv_acc, sems = refs
+        pltpu.make_async_copy(arrived.at[:, pl.ds(0, 4 * HD)], x_in, sems.at[0]).start()
     if last:
         pairs = ((before_hbm, before_ref), (mine_hbm, mine_ref), (theirs_hbm, theirs_ref))
         others = [pltpu.make_async_copy(*pair, more_sems.at[t]) for t, pair in enumerate(pairs)]
         for copy in others:
             copy.start()
-    else:
-        sources = [low_ref] + [piece.at[:, pl.ds(8 * HD, BOTH)] for piece in pieces]
-        others = [
-            pltpu.make_async_copy(source, lows_ref.at[dy], sems.at[MEMBERS + dy])
-            for dy, source in enumerate(sources)
-        ]
-        for copy in others:
-            copy.start()
     if last:
-        pltpu.make_async_copy(arrived, x_in, sems.at[0]).wait()
-    else:
         for t in range(MEMBERS):
             pltpu.make_async_copy(own_ref.at[0], x_in.at[pl.ds(t * ROWS, ROWS), :], sems.at[t]).wait()
+    else:
+        pltpu.make_async_copy(arrived.at[:, pl.ds(0, 4 * HD)], x_in, sems.at[0]).wait()
     back = attend(x_in, up[...], grads_ref, 0, dv_acc)
     if not last:
         back_ref[...] = back
-        for copy in others:
-            copy.wait()
         return
     save = pltpu.make_async_copy(grads_ref, grads_hbm, more_sems.at[3])
     save.start()
@@ -407,8 +396,6 @@
 def attention_shifted(item, order, spot, arrived, up, *more):
     last = len(more) > 0
     shapes = [((GROUP, BOTH), BF16 if last else F32), ((GROUP, 2 * HD), BF16)]
-    if not last:
-        shapes.append(((YS, ROWS, BOTH), BF16))
 
     def body(*refs):
         attention_shifted_kernel(last, *refs)
@@ -422,31 +409,14 @@
         + [ANYWHERE] * len(more),
         [block(shapes[0][0]), ANYWHERE] if last else [block(shape) for shape, _ in shapes],
         [jax.ShapeDtypeStruct(*shape) for shape in shapes],
-        [pltpu.VMEM((GROUP, 4 * HD), BF16), pltpu.VMEM((HD, GROUP), F32), pltpu.SemaphoreType.DMA((3 * YS,))]
+        [pltpu.VMEM((GROUP, 4 * HD), BF16), pltpu.VMEM((HD, GROUP), F32), pltpu.SemaphoreType.DMA((2 * YS,))]
         + LAST_SCRATCH * last,
         (4 * 10**9, 3 * 10**6) if last else (10**6, 10**4),
     )(order, spot, *arrived, up, *more)
 
 
-def up_gradient_kernel(spot, own_ref, later_ref, earlier_ref, *refs):
-    out_ref, low_a, low_b = refs[-3:]
-    y = spot[SPOT_Y]
-
-    def fill(low, first, second):
-        for half, ref in enumerate((first, second)):
-            for s in range(YS):
-                low[pl.ds(half * PLANE + s * ROWS, ROWS), :] = ref[(y - s + YS) % YS]
-
-    @pl.when(spot[SPOT_OWN_PLAIN] == 0)
-    def _():
-        fill(low_a, own_ref, later_ref)
-        fill(low_b, earlier_ref, own_ref)
-
-    @pl.when(spot[SPOT_OWN_PLAIN] != 0)
-    def _():
-        fill(low_a, earlier_ref, own_ref)
-        fill(low_b, own_ref, later_ref)
-
+def up_gradient_kernel(low_a, low_b, *refs):
+    out_ref = refs[-1]
     for item in range(4):
         low = (low_a, low_b)[item // 2][...]
         grads, column = ((refs[0], 0), (refs[0], 2 * HD), (refs[1], 0), (refs[2], 0))[item]
@@ -459,19 +429,19 @@
                 out_ref[d, pl.ds(item * PIECE, PIECE), :] = part[e * PIECE : (e + 1) * PIECE]
 
 
-def up_gradients(spot, own, later, earlier, grads):
+def up_gradients(plain, late, grads):
     shape = (SLICES, 4 * PIECE, HD)
+    lows = [pl.BlockSpec((GROUP, BOTH), lambda i, column=column: (0, column)) for column in (8, 4)]
     return call(
         up_gradient_kernel,
         "up_gradients",
-        1,
-        [block((YS, ROWS, BOTH))] * 3 + [block(array.shape) for array in grads],
+        0,
+        lows + [block(array.shape) for array in grads],
         block(shape),
         jax.ShapeDtypeStruct(shape, BF16),
-        [pltpu.VMEM((GROUP, BOTH), BF16)] * 2,
+        [],
         (2 * 10**9, 3 * 10**6),
-        16,
-    )(spot, own, later, earlier, *grads)
+    )(plain, late, *grads)
 
 
 def gather_kernel(summed_ref, ups_ref, out_ref):
@@ -497,14 +467,14 @@
 
 
 def merge_kernel(order, spot, place, both_ref, *refs):
-    x_refs, crossed_ref, out_ref = refs[:-2], refs[-2], refs[-1]
+    x_refs, crossed_refs, out_ref = refs[:XS], refs[XS:-1], refs[-1]
     x, core = place[0] // CS, place[0] % CS
     total = jnp.zeros((HEADS * PIECE, BOTH), F32)
     for dx in range(XS):
         for other in range(CS):
             s = (x - dx + XS) % XS * CS + (core + other) % CS
             back = both_ref[s, pl.ds(0, ROWS), :]
-            part = x_refs[dx][0] if other == 0 else crossed_ref[dx]
+            part = (x_refs, crossed_refs)[other][dx][0]
             total += jnp.dot(part, back, preferred_element_type=F32)
     total = (adapter_scale * total).astype(BF16)
     for u in range(HEADS):
@@ -523,13 +493,18 @@
         merge_kernel,
         "merge_gradients",
         3,
-        [block(both.shape)] + [block((1, *piece.shape[1:])) for piece in pieces] + [block(crossed.shape)],
+        [block(both.shape)]
+        + [
+            pl.BlockSpec((1, *piece.shape[1:]), lambda i, *s, half=half: (half, 0, 0))
+            for half in range(2)
+            for piece in (pieces, crossed)[half]
+        ],
         block(shape),
         jax.ShapeDtypeStruct(shape, BF16),
         [],
         (2 * 10**8, 2 * 10**6),
         16,
-    )(order, spot, place, both, *pieces, crossed)
+    )(order, spot, place, both, *pieces, *crossed)
 
 
 def spread_kernel(in_ref, out_ref):
@@ -593,30 +568,28 @@
 
     frozen = (frozen_queries[0], frozen_keys[0], frozen_values[0], output_gradient[0], up)
     sent, order, spot, low = prepare_plain(shifted.astype(jnp.int32), tokens, down, frozen)
-    plain = exchange(sent, "ulysses", PLAIN_GROUPS)
+    plain = exchange(sent, "ulysses", PLAIN_GROUPS).reshape(GROUP, 8 * HD + BOTH)
     own_c, other_c = prepare_shifted(2, order, spot, low, frozen)
     other_c = lax.ppermute(other_c, "ulysses", SHIFT_SWAP)
     turned = turn(place, after(tokens, own_c))
     pieces = [turned[0]] + [lax.ppermute(turned[dx], "dp", x_shift(dx)) for dx in (1, 2, 3)]
     (sent,) = prepare_shifted(3, order, spot, after(low, turned), frozen)
 
-    packed = pack(after(low, pieces, sent), own_c, other_c)
+    packed = pack(after(own_c, pieces, sent), other_c)
+    plain, pieces, sent, packed = after((plain, pieces, sent, packed))
+    arrived_d = exchange(sent, "ulysses", SHIFT_GROUPS).reshape(GROUP, 4 * HD + BOTH)
     arrived_c = [lax.ppermute(packed[dy - 1], "ulysses", y_shift(dy)) for dy in (1, 2, 3)]
-    plain, pieces, sent = after((plain, pieces, sent), packed)
-
-    arrived_d = exchange(sent, "ulysses", SHIFT_GROUPS).reshape(GROUP, 4 * HD)
-    crossed = lax.ppermute(jnp.stack([piece[1] for piece in pieces]), "dp", CORE_SWAP)
     mine, theirs, grads_plain = attention_plain(order, spot, plain, up)
     theirs = lax.ppermute(theirs, "ulysses", PLAIN_SWAP)
-    arrived_c = after(arrived_c, grads_plain, sent)
-    partial, grads_c, own = attention_shifted(2, order, spot, [low, own_c, other_c, *arrived_c], up)
-    later = lax.ppermute(own, "ulysses", z_shift(-1))
-    earlier = lax.ppermute(own, "ulysses", z_shift(1))
-
-    arrived_d, theirs, crossed, later, earlier = after((arrived_d, theirs, crossed, later, earlier), partial)
-    partial, grads_d = attention_shifted(3, order, spot, [arrived_d], up, partial, mine, theirs)
+    arrived_d = after(arrived_d, grads_plain)
+    partial, grads_d = attention_shifted(3, order, spot, [arrived_d], up)
+
+    arrived_c, theirs = after((arrived_c, theirs), partial)
+    partial, grads_c = attention_shifted(2, order, spot, [own_c, other_c, *arrived_c], up, partial, mine, theirs)
+    crossed = [lax.ppermute(piece, "dp", CORE_SWAP) for piece in after(pieces, partial)]
     summed = exchange(partial.reshape(MEMBERS, ROWS, BOTH), "ulysses", SHIFT_GROUPS)
-    ups = up_gradients(spot, own, later, earlier, (grads_plain, grads_c, grads_d))
+    ups = up_gradients(plain, arrived_d, (grads_plain, grads_c, grads_d))
+
     both = exchange(gather_parts(summed, ups), "dp")
     both = exchange(merge(order, spot, place, both, pieces, crossed), "ulysses")
     both = exchange(spread(both), "dp")

time: 146 us -> 147 us (level)
  blocking collectives: 43.2 us -> 27.3 us
  waiting for transfers between devices: 8.98 us -> 19.2 us
  starting transfers between devices: 38.7 us -> 43.2 us
  Pallas kernels: 48.5 us -> 50.7 us
    all_to_all x3 -> x2, blocking collectives: 43.2 us -> 27.3 us  [exchange(): lax.all_to_all(member, axis, 0, 0, tiled=True, axis_index_groups=groups)]
    all_to_all x3 -> x4, starting transfers between devices: 16.8 us -> 27 us  [exchange(): lax.all_to_all(member, axis, 0, 0, tiled=True, axis_index_groups=groups)]
    all_to_all x3 -> x4, waiting for transfers between devices: 0.99 us -> 9.47 us  [exchange(): lax.all_to_all(member, axis, 0, 0, tiled=True, axis_index_groups=groups)]
    ppermute x3 -> x4, starting transfers between devices: 6.75 us -> 1.02 us  [per_device(): lax.ppermute(piece, 'dp', CORE_SWAP)]
    ppermute x3, waiting for transfers between devices: 0.01 us -> 2.89 us  [per_device(): lax.ppermute(packed[dy - 1], 'ulysses', y_shift(dy))]
    pallas_call x3, Pallas kernels: 4.86 us -> 6.55 us  [the longest x1 3.46 us: up_gradients(): call(up_gradient_kernel, 'up_gradients', 0, lows + [block(array.shape) fo...]
    unnamed x20 -> x22, local copies, waits for them, and re-layouts: 4.06 us -> 4.23 us
  transfers between devices with their start and end apart: 14 -> 16, of which waited for: 5 -> 11; matrix products, arithmetic and copies ran while one was open for 0% -> 0% of each run, Pallas kernels for 22% -> 23%
where the time goes in v7:
time: 147 us; the launch traced here: 145 us
  Pallas kernels  50.7 us (34%)
  starting transfers between devices  43.2 us (29%)
  blocking collectives  27.3 us (19%)
  waiting for transfers between devices  19.2 us (13%)
  local copies, waits for them, and re-layouts  4.23 us (3%)
    all_to_all x2, blocking collectives, exchange(): lax.all_to_all(member, axis, 0, 0, tiled=True, axis_index_groups=groups)  27.3 us
    all_to_all x4, starting transfers between devices, exchange(): lax.all_to_all(member, axis, 0, 0, tiled=True, axis_index_groups=groups)  27 us
    pallas_call x2, Pallas kernels, attention_shifted(): call(body, 'attention_last' if last else 'attention_third', 2, [pl.BlockS...  14.2 us
    pallas_call x1, Pallas kernels, attention_plain(): call(attention_plain_kernel, 'attention_plain', 2, [ANYWHERE, up_columns(...  10.1 us
    all_to_all x4, waiting for transfers between devices, exchange(): lax.all_to_all(member, axis, 0, 0, tiled=True, axis_index_groups=groups)  9.47 us
    pallas_call x2, Pallas kernels, prepare_shifted(): call(prepare_third_kernel if item == 2 else prepare_last_kernel, 'prepare...  8.71 us
    pallas_call x1, Pallas kernels, prepare_plain(): call(prepare_plain_kernel, 'prepare_plain', 1, [ANYWHERE] * 7, [block((ME...  6.98 us
    ppermute x1, starting transfers between devices, per_device(): other_c = lax.ppermute(other_c, 'ulysses', SHIFT_SWAP)  5.48 us
  transfers between devices with their start and end apart: 16, of which 11 were waited for; matrix products, arithmetic and copies ran while one was open for 0% of the time, Pallas kernels for 23%

profile of v7, /device:TPU:1, one launch (start us, length us, event | category | flops | bytes accessed | tf_op | source)
XLA Modules:
  0.0 145.3 jit_solution(6262222798436645966)
XLA Ops:
  0.6 7.0 %prepare_plain.1 = (bf16[8,128,1152]{2,1,0:T(8,128)(2,1)}, s32[32]{0:T(128)}, s32[8]{0:T(128)}, bf16[128,128]{1,0:T(8,128)(2,1)}) custom-call(s32[32]{0:T(128)} %flags.1, bf16[128,4096]{1,0:T(8,128)(2,1)} %bitcast.38, bf16[128,4096]{1,0:T(8,128)(2,1)} %bitcast.37, bf16[128,4096]{1,0:T(8,128)(2,1)} %bitcast.21, bf16[128,4096]{1,0:T(8,128)(2,1)} %bitcast.24, ...), custom_call_target="tpu_custom_call" | custom-call | flops 1000000000 | bytes 8000000 | tf_op jit(solution)/shard_map/prepare_plain/pallas_call | solution.py:166
  7.6 6.4 %all-to-all-start = ((bf16[8,128,1152]{2,1,0:T(8,128)(2,1)}), bf16[8,128,1152]{2,1,0:T(8,128)(2,1)S(1)}, u32[]{:S(2)}, u32[]{:S(2)}) async-start(bf16[8,128,1152]{2,1,0:T(8,128)(2,1)} %get-tuple-element.50), calls=%async_computation | async-start | bytes 4718592 | tf_op jit(solution)/shard_map/all_to_all | solution.py:48
  14.0 4.3 %prepare_third.1 = (bf16[4,128,512]{2,1,0:T(8,128)(2,1)}, bf16[4,128,512]{2,1,0:T(8,128)(2,1)}) custom-call(s32[32]{0:T(128)} %get-tuple-element.45.order.refs_0_, s32[8]{0:T(128)} %get-tuple-element.46.spot.refs_1_, bf16[128,128]{1,0:T(8,128)(2,1)} %get-tuple-element.56.low_ref, bf16[128,4096]{1,0:T(8,128)(2,1)} %bitcast.22, bf16[128,4096]{1,0:T(8,128)(2,1)} %bitcast.25, ...), custom_call_target="tpu_custom_call" | custom-call | flops 1000000000 | bytes 8000000 | tf_op jit(solution)/shard_map/prepare_third/pallas_call | solution.py:209
  18.3 5.5 %collective-permute-start = (bf16[4,128,512]{2,1,0:T(8,128)(2,1)}, bf16[4,128,512]{2,1,0:T(8,128)(2,1)}, u32[]{:S(2)}, u32[]{:S(2)}) collective-permute-start(bf16[4,128,512]{2,1,0:T(8,128)(2,1)} %get-tuple-element.49), channel_id=1, source_target_pairs={{0,28},{1,29},{2,30},{3,31},{4,8},{5,9},{6,10},{7,11},{8,4},{9,5},... | collective-permute-start | bytes 1572872 | tf_op jit(solution)/shard_map/ppermute | solution.py:573
  23.8 2.6 %turn_input.1 = (bf16[2,512,128]{2,1,0:T(8,128)(2,1)}, bf16[2,512,128]{2,1,0:T(8,128)(2,1)}, bf16[2,512,128]{2,1,0:T(8,128)(2,1)}, bf16[2,512,128]{2,1,0:T(8,128)(2,1)}) custom-call(s32[1]{0:T(128)} %bitcast.8.spot.place, bf16[128,4096]{1,0:T(8,128)(2,1)} %bitcast.39), custom_call_target="tpu_custom_call" | custom-call | flops 1000000000 | bytes 2000000 | tf_op jit(solution)/shard_map/turn_input/pallas_call | solution.py:256
  26.4 1.2 collective-permute-start.1
  27.6 2.5 %collective-permute-start.2 = (bf16[2,512,128]{2,1,0:T(8,128)(2,1)}, bf16[2,512,128]{2,1,0:T(8,128)(2,1)S(1)}, u32[]{:S(2)}, u32[]{:S(2)}) collective-permute-start(bf16[2,512,128]{2,1,0:T(8,128)(2,1)} %get-tuple-element.54), channel_id=1, source_target_pairs={{0,128},{32,160},{64,192},{96,224},{128,0},{160,32},{192,64},{224,... | collective-permute-start | bytes 786440 | tf_op jit(solution)/shard_map/ppermute | solution.py:575
  30.0 1.2 collective-permute-start.3
  31.2 4.4 %prepare_last.1 = bf16[8,128,640]{2,1,0:T(8,128)(2,1)} custom-call(s32[32]{0:T(128)} %get-tuple-element.45.order.refs_0_, s32[8]{0:T(128)} %get-tuple-element.46.spot.refs_1_, bf16[128,128]{1,0:T(8,128)(2,1)} %get-tuple-element.56.low_ref, bf16[128,4096]{1,0:T(8,128)(2,1)} %bitcast.23, bf16[128,4096]{1,0:T(8,128)(2,1)} %bitcast.26, ...), custom_call_target="tpu_custom_call" | custom-call | flops 1000000000 | bytes 8000000 | tf_op jit(solution)/shard_map/prepare_last/pallas_call | solution.py:209
  35.6 5.0 %collective-permute-done.2.refs_2_ = bf16[2,512,128]{2,1,0:T(8,128)(2,1)S(1)} collective-permute-done((bf16[2,512,128]{2,1,0:T(8,128)(2,1)}, bf16[2,512,128]{2,1,0:T(8,128)(2,1)S(1)}, u32[]{:S(2)}, u32[]{:S(2)}) %collective-permute-start.2) | collective-permute-done | bytes 262176 | tf_op jit(solution)/shard_map/ppermute | solution.py:575
  40.8 2.1 %pack_third.1 = (bf16[128,1024]{1,0:T(8,128)(2,1)}, bf16[128,1024]{1,0:T(8,128)(2,1)}, bf16[128,1024]{1,0:T(8,128)(2,1)}) custom-call(bf16[4,128,512]{2,1,0:T(8,128)(2,1)} %get-tuple-element.57.own_ref.refs_2_, bf16[4,128,512]{2,1,0:T(8,128)(2,1)} %collective-permute-done.other_ref.refs_3_), custom_call_target="tpu_custom_call" | custom-call | bytes 4000000 | tf_op jit(solution)/shard_map/pack_third/pallas_call | solution.py:229
  43.0 1.4 copy-done.5
  44.4 8.6 %all-to-all-start.1 = ((bf16[8,128,640]{2,1,0:T(8,128)(2,1)}), bf16[8,128,640]{2,1,0:T(8,128)(2,1)S(1)}, u32[]{:S(2)}, u32[]{:S(2)}) async-start(bf16[8,128,640]{2,1,0:T(8,128)(2,1)} %prepare_last.1), calls=%async_computation.1 | async-start | bytes 2621440 | tf_op jit(solution)/shard_map/all_to_all | solution.py:48
  53.0 1.2 collective-permute-start.4
  54.2 2.4 %collective-permute-start.5 = (bf16[128,1024]{1,0:T(8,128)(2,1)}, bf16[128,1024]{1,0:T(8,128)(2,1)S(1)}, u32[]{:S(2)}, u32[]{:S(2)}) collective-permute-start(bf16[128,1024]{1,0:T(8,128)(2,1)} %get-tuple-element.62), channel_id=1, source_target_pairs={{0,2},{1,3},{2,0},{3,1},{4,6},{5,7},{6,4},{7,5},{8,10},{9,11},{10,... | collective-permute-start | bytes 786440 | tf_op jit(solution)/shard_map/ppermute | solution.py:581
  56.6 1.2 collective-permute-start.6
  57.8 10.1 %attention_plain.1 = (f32[512,128]{1,0:T(8,128)}, bf16[512,128]{1,0:T(8,128)(2,1)}, bf16[1024,512]{1,0:T(8,128)(2,1)}) custom-call(s32[32]{0:T(128)} %get-tuple-element.45.order.refs_0_, s32[8]{0:T(128)} %get-tuple-element.46.spot.refs_1_, bf16[1024,1152]{1,0:T(8,128)(2,1)} %bitcast.35, bf16[128,4096]{1,0:T(8,128)(2,1)} %bitcast.17, bf16[128,4096]{1,0:T(8,128)(2,1)} %bitcast.18), custom_call_target="tpu_custom_call" | custom-call | flops 20000000000 | bytes 4000000 | tf_op jit(solution)/shard_map/attention_plain/pallas_call | solution.py:326
  68.0 2.5 %all-to-all-done.1 = bf16[8,128,640]{2,1,0:T(8,128)(2,1)S(1)} async-done(((bf16[8,128,640]{2,1,0:T(8,128)(2,1)}), bf16[8,128,640]{2,1,0:T(8,128)(2,1)S(1)}, u32[]{:S(2)}, u32[]{:S(2)}) %all-to-all-start.1) | async-done | bytes 1310752 | tf_op jit(solution)/shard_map/all_to_all | solution.py:48
  70.5 1.1 copy-done.4
  71.6 6.7 %attention_third.1 = (f32[1024,128]{1,0:T(8,128)}, bf16[1024,256]{1,0:T(8,128)(2,1)}) custom-call(s32[32]{0:T(128)} %get-tuple-element.45.order.refs_0_, s32[8]{0:T(128)} %get-tuple-element.46.spot.refs_1_, bf16[1024,640]{1,0:T(8,128)(2,1)} %bitcast.33, bf16[128,4096]{1,0:T(8,128)(2,1)} %bitcast.19), custom_call_target="tpu_custom_call" | custom-call | flops 1000000 | bytes 10000 | tf_op jit(solution)/shard_map/attention_third/pallas_call | solution.py:403
  78.3 2.9 %collective-permute-done.5.refs_5_ = bf16[128,1024]{1,0:T(8,128)(2,1)S(1)} collective-permute-done((bf16[128,1024]{1,0:T(8,128)(2,1)}, bf16[128,1024]{1,0:T(8,128)(2,1)S(1)}, u32[]{:S(2)}, u32[]{:S(2)}) %collective-permute-start.5) | collective-permute-done | bytes 262176 | tf_op jit(solution)/shard_map/ppermute | solution.py:581
  82.0 7.5 %attention_last.1 = (bf16[1024,128]{1,0:T(8,128)(2,1)}, bf16[1024,256]{1,0:T(8,128)(2,1)}) custom-call(s32[32]{0:T(128)} %get-tuple-element.45.order.refs_0_, s32[8]{0:T(128)} %get-tuple-element.46.spot.refs_1_, bf16[4,128,512]{2,1,0:T(8,128)(2,1)} %get-tuple-element.57.own_ref.refs_2_, bf16[4,128,512]{2,1,0:T(8,128)(2,1)} %collective-permute-done.other_ref.refs_3_, ...), custom_call_target="tpu_custom_call" | custom-call | flops 4000000000 | bytes 3000000 | tf_op jit(solution)/shard_map/attention_last/pallas_call | solution.py:403
  89.5 5.6 %all-to-all-start.2 = ((bf16[8,128,128]{2,1,0:T(8,128)(2,1)}), bf16[8,128,128]{2,1,0:T(8,128)(2,1)S(1)}, u32[]{:S(2)}, u32[]{:S(2)}) async-start(bf16[8,128,128]{2,1,0:T(8,128)(2,1)} %bitcast.40), calls=%async_computation.2 | async-start | bytes 524288 | tf_op jit(solution)/shard_map/all_to_all | solution.py:48
  95.1 3.5 %up_gradients.1.ups_ref = bf16[8,64,128]{2,1,0:T(8,128)(2,1)} custom-call(bf16[1024,1152]{1,0:T(8,128)(2,1)} %bitcast.36, bf16[1024,640]{1,0:T(8,128)(2,1)} %bitcast.34, bf16[1024,512]{1,0:T(8,128)(2,1)} %get-tuple-element.67.refs_0_, bf16[1024,256]{1,0:T(8,128)(2,1)} %get-tuple-element.76.refs_1_, bf16[1024,256]{1,0:T(8,128)(2,1)} %get-tuple-element.77.refs_2_), custom_call_target="tpu_custom_call" | custom-call | flops 2000000000 | bytes 3000000 | tf_op jit(solution)/shard_map/up_gradients/pallas_call | solution.py:435
  98.6 1.5 %all-to-all-done.2.summed_ref = bf16[8,128,128]{2,1,0:T(8,128)(2,1)S(1)} async-done(((bf16[8,128,128]{2,1,0:T(8,128)(2,1)}), bf16[8,128,128]{2,1,0:T(8,128)(2,1)S(1)}, u32[]{:S(2)}, u32[]{:S(2)}) %all-to-all-start.2) | async-done | bytes 262176 | tf_op jit(solution)/shard_map/all_to_all | solution.py:48
  100.1 0.9 copy-done.1
  101.0 0.8 gather_parts.1
  101.8 6.4 %all-to-all-start.3 = ((bf16[8,192,128]{2,1,0:T(8,128)(2,1)}), bf16[8,192,128]{2,1,0:T(8,128)(2,1)S(1)}, u32[]{:S(2)}, u32[]{:S(2)}) async-start(bf16[8,192,128]{2,1,0:T(8,128)(2,1)} %gather_parts.1), calls=%async_computation.3 | async-start | bytes 786432 | tf_op jit(solution)/shard_map/all_to_all | solution.py:48
  110.9 5.4 %all-to-all-done.3.both_ref = bf16[8,192,128]{2,1,0:T(8,128)(2,1)S(1)} async-done(((bf16[8,192,128]{2,1,0:T(8,128)(2,1)}), bf16[8,192,128]{2,1,0:T(8,128)(2,1)S(1)}, u32[]{:S(2)}, u32[]{:S(2)}) %all-to-all-start.3) | async-done | bytes 393248 | tf_op jit(solution)/shard_map/all_to_all | solution.py:48
  116.3 1.0 merge_gradients.1
  117.3 17.0 %all_to_all.30.in_ref = bf16[32,32,128]{2,1,0:T(8,128)(2,1)S(1)} all-to-all(bf16[32,32,128]{2,1,0:T(8,128)(2,1)S(1)} %merge_gradients.1), channel_id=1, replica_groups=mesh['dp'=8,'ulysses'=32] {'ulysses'}, dimensions={0} | all-to-all | bytes 524288 | tf_op jit(solution)/shard_map/all_to_all | solution.py:48
  134.3 10.2 %all_to_all.31.in_ref = f32[8,32,128]{2,1,0:T(8,128)S(1)} all-to-all(f32[8,32,128]{2,1,0:T(8,128)S(1)} %spread_sums.1), channel_id=1, replica_groups=mesh['dp'=8,'ulysses'=32] {'dp'}, dimensions={0} | all-to-all | bytes 262144 | tf_op jit(solution)/shard_map/all_to_all | solution.py:48
  (37 shorter events, 4.6 us)
Async XLA Ops:
  7.6 35.3 %all-to-all-start = ((bf16[8,128,1152]{2,1,0:T(8,128)(2,1)}), bf16[8,128,1152]{2,1,0:T(8,128)(2,1)S(1)}, u32[]{:S(2)}, u32[]{:S(2)}) async-start(bf16[8,128,1152]{2,1,0:T(8,128)(2,1)} %get-tuple-element.50), calls=%async_computation | async-start | bytes 4718592 | tf_op jit(solution)/shard_map/all_to_all | solution.py:48
  18.3 22.5 %collective-permute-start = (bf16[4,128,512]{2,1,0:T(8,128)(2,1)}, bf16[4,128,512]{2,1,0:T(8,128)(2,1)}, u32[]{:S(2)}, u32[]{:S(2)}) collective-permute-start(bf16[4,128,512]{2,1,0:T(8,128)(2,1)} %get-tuple-element.49), channel_id=1, source_target_pairs={{0,28},{1,29},{2,30},{3,31},{4,8},{5,9},{6,10},{7,11},{8,4},{9,5},... | collective-permute-start | bytes 1572872 | tf_op jit(solution)/shard_map/ppermute | solution.py:573
  26.4 9.3 %collective-permute-start.1 = (bf16[2,512,128]{2,1,0:T(8,128)(2,1)}, bf16[2,512,128]{2,1,0:T(8,128)(2,1)S(1)}, u32[]{:S(2)}, u32[]{:S(2)}) collective-permute-start(bf16[2,512,128]{2,1,0:T(8,128)(2,1)} %get-tuple-element.53), channel_id=1, source_target_pairs={{0,64},{32,96},{64,128},{96,160},{128,192},{160,224},{192,0},{224,... | collective-permute-start | bytes 786440 | tf_op jit(solution)/shard_map/ppermute | solution.py:575
  27.6 13.1 %collective-permute-start.2 = (bf16[2,512,128]{2,1,0:T(8,128)(2,1)}, bf16[2,512,128]{2,1,0:T(8,128)(2,1)S(1)}, u32[]{:S(2)}, u32[]{:S(2)}) collective-permute-start(bf16[2,512,128]{2,1,0:T(8,128)(2,1)} %get-tuple-element.54), channel_id=1, source_target_pairs={{0,128},{32,160},{64,192},{96,224},{128,0},{160,32},{192,64},{224,... | collective-permute-start | bytes 786440 | tf_op jit(solution)/shard_map/ppermute | solution.py:575
  30.0 10.8 %collective-permute-start.3 = (bf16[2,512,128]{2,1,0:T(8,128)(2,1)}, bf16[2,512,128]{2,1,0:T(8,128)(2,1)S(1)}, u32[]{:S(2)}, u32[]{:S(2)}) collective-permute-start(bf16[2,512,128]{2,1,0:T(8,128)(2,1)} %get-tuple-element.55), channel_id=1, source_target_pairs={{0,192},{32,224},{64,0},{96,32},{128,64},{160,96},{192,128},{224,1... | collective-permute-start | bytes 786440 | tf_op jit(solution)/shard_map/ppermute | solution.py:575
  42.9 13.7 %copy-start.6 = (bf16[128,1024]{1,0:T(8,128)(2,1)S(1)}, bf16[128,1024]{1,0:T(8,128)(2,1)}, u32[]{:S(2)}) copy-start(bf16[128,1024]{1,0:T(8,128)(2,1)} %get-tuple-element.63) | copy-start | bytes 786436
  43.0 1.4 copy-start.5
  44.4 26.1 %all-to-all-start.1 = ((bf16[8,128,640]{2,1,0:T(8,128)(2,1)}), bf16[8,128,640]{2,1,0:T(8,128)(2,1)S(1)}, u32[]{:S(2)}, u32[]{:S(2)}) async-start(bf16[8,128,640]{2,1,0:T(8,128)(2,1)} %prepare_last.1), calls=%async_computation.1 | async-start | bytes 2621440 | tf_op jit(solution)/shard_map/all_to_all | solution.py:48
  53.0 25.3 %collective-permute-start.4 = (bf16[128,1024]{1,0:T(8,128)(2,1)}, bf16[128,1024]{1,0:T(8,128)(2,1)S(1)}, u32[]{:S(2)}, u32[]{:S(2)}) collective-permute-start(bf16[128,1024]{1,0:T(8,128)(2,1)} %get-tuple-element.61), channel_id=1, source_target_pairs={{0,1},{1,2},{2,3},{3,0},{4,5},{5,6},{6,7},{7,4},{8,9},{9,10},{10,1... | collective-permute-start | bytes 786440 | tf_op jit(solution)/shard_map/ppermute | solution.py:581
  54.2 27.0 %collective-permute-start.5 = (bf16[128,1024]{1,0:T(8,128)(2,1)}, bf16[128,1024]{1,0:T(8,128)(2,1)S(1)}, u32[]{:S(2)}, u32[]{:S(2)}) collective-permute-start(bf16[128,1024]{1,0:T(8,128)(2,1)} %get-tuple-element.62), channel_id=1, source_target_pairs={{0,2},{1,3},{2,0},{3,1},{4,6},{5,7},{6,4},{7,5},{8,10},{9,11},{10,... | collective-permute-start | bytes 786440 | tf_op jit(solution)/shard_map/ppermute | solution.py:581
  56.6 24.6 %collective-permute-start.6 = (bf16[128,1024]{1,0:T(8,128)(2,1)S(1)}, bf16[128,1024]{1,0:T(8,128)(2,1)S(1)}, u32[]{:S(2)}, u32[]{:S(2)}) collective-permute-start(bf16[128,1024]{1,0:T(8,128)(2,1)S(1)} %copy-done.6), channel_id=1, source_target_pairs={{0,3},{1,0},{2,1},{3,2},{4,7},{5,4},{6,5},{7,6},{8,11},{9,8},{10,9... | collective-permute-start | bytes 786440 | tf_op jit(solution)/shard_map/ppermute | solution.py:581
  67.9 10.4 %collective-permute-start.7 = (bf16[512,128]{1,0:T(8,128)(2,1)}, bf16[512,128]{1,0:T(8,128)(2,1)S(1)}, u32[]{:S(2)}, u32[]{:S(2)}) collective-permute-start(bf16[512,128]{1,0:T(8,128)(2,1)} %get-tuple-element.65), channel_id=1, source_target_pairs={{0,4},{1,5},{2,6},{3,7},{4,0},{5,1},{6,2},{7,3},{8,12},{9,13},{10,... | collective-permute-start | bytes 393224 | tf_op jit(solution)/shard_map/ppermute | solution.py:583
  70.5 1.1 copy-start.4
  78.3 2.9 %copy-start.10 = (bf16[512,128]{1,0:T(8,128)(2,1)}, bf16[512,128]{1,0:T(8,128)(2,1)S(1)}, u32[]{:S(2)}) copy-start(bf16[512,128]{1,0:T(8,128)(2,1)S(1)} %collective-permute-done.7.refs_10_) | copy-start | bytes 393220
  78.3 2.9 %copy-start.7 = (bf16[128,1024]{1,0:T(8,128)(2,1)}, bf16[128,1024]{1,0:T(8,128)(2,1)S(1)}, u32[]{:S(2)}) copy-start(bf16[128,1024]{1,0:T(8,128)(2,1)S(1)} %collective-permute-done.4.refs_4_) | copy-start | bytes 786436
  81.2 0.7 copy-start.8
  81.2 0.8 copy-start.9
  89.5 10.6 %all-to-all-start.2 = ((bf16[8,128,128]{2,1,0:T(8,128)(2,1)}), bf16[8,128,128]{2,1,0:T(8,128)(2,1)S(1)}, u32[]{:S(2)}, u32[]{:S(2)}) async-start(bf16[8,128,128]{2,1,0:T(8,128)(2,1)} %bitcast.40), calls=%async_computation.2 | async-start | bytes 524288 | tf_op jit(solution)/shard_map/all_to_all | solution.py:48
  95.1 13.1 %copy-start = (bf16[2,512,128]{2,1,0:T(8,128)(2,1)S(1)}, bf16[2,512,128]{2,1,0:T(8,128)(2,1)}, u32[]{:S(2)}) copy-start(bf16[2,512,128]{2,1,0:T(8,128)(2,1)} %get-tuple-element.82.refs_0_) | copy-start | bytes 786436
  95.1 21.1 %copy-start.2 = (s32[32]{0:T(128)S(1)}, s32[32]{0:T(128)}, u32[]{:S(2)}) copy-start(s32[32]{0:T(128)} %get-tuple-element.45.order.refs_0_) | copy-start | bytes 388
  95.1 21.1 %copy-start.3 = (s32[8]{0:T(128)S(1)}, s32[8]{0:T(128)}, u32[]{:S(2)}) copy-start(s32[8]{0:T(128)} %get-tuple-element.46.spot.refs_1_) | copy-start | bytes 100
  100.1 0.9 copy-start.1
  101.8 14.5 %all-to-all-start.3 = ((bf16[8,192,128]{2,1,0:T(8,128)(2,1)}), bf16[8,192,128]{2,1,0:T(8,128)(2,1)S(1)}, u32[]{:S(2)}, u32[]{:S(2)}) async-start(bf16[8,192,128]{2,1,0:T(8,128)(2,1)} %gather_parts.1), calls=%async_computation.3 | async-start | bytes 786432 | tf_op jit(solution)/shard_map/all_to_all | solution.py:48
  108.2 1.5 %collective-permute-start.8 = (bf16[2,512,128]{2,1,0:T(8,128)(2,1)S(1)}, bf16[2,512,128]{2,1,0:T(8,128)(2,1)S(1)}, u32[]{:S(2)}, u32[]{:S(2)}) collective-permute-start(bf16[2,512,128]{2,1,0:T(8,128)(2,1)S(1)} %copy-done), channel_id=1, source_target_pairs={{0,32},{32,0},{64,96},{96,64},{128,160},{160,128},{192,224},{224,1... | collective-permute-start | bytes 786440 | tf_op jit(solution)/shard_map/ppermute | solution.py:589
  108.3 1.8 %collective-permute-start.9 = (bf16[2,512,128]{2,1,0:T(8,128)(2,1)S(1)}, bf16[2,512,128]{2,1,0:T(8,128)(2,1)S(1)}, u32[]{:S(2)}, u32[]{:S(2)}) collective-permute-start(bf16[2,512,128]{2,1,0:T(8,128)(2,1)S(1)} %collective-permute-done.1.refs_1_), channel_id=1, source_target_pairs={{0,32},{32,0},{64,96},{96,64},{128,160},{160,128},{192,224},{224,1... | collective-permute-start | bytes 786440 | tf_op jit(solution)/shard_map/ppermute | solution.py:589
  108.7 1.8 %collective-permute-start.10 = (bf16[2,512,128]{2,1,0:T(8,128)(2,1)S(1)}, bf16[2,512,128]{2,1,0:T(8,128)(2,1)S(1)}, u32[]{:S(2)}, u32[]{:S(2)}) collective-permute-start(bf16[2,512,128]{2,1,0:T(8,128)(2,1)S(1)} %collective-permute-done.2.refs_2_), channel_id=1, source_target_pairs={{0,32},{32,0},{64,96},{96,64},{128,160},{160,128},{192,224},{224,1... | collective-permute-start | bytes 786440 | tf_op jit(solution)/shard_map/ppermute | solution.py:589
  108.8 2.1 %collective-permute-start.11 = (bf16[2,512,128]{2,1,0:T(8,128)(2,1)S(1)}, bf16[2,512,128]{2,1,0:T(8,128)(2,1)S(1)}, u32[]{:S(2)}, u32[]{:S(2)}) collective-permute-start(bf16[2,512,128]{2,1,0:T(8,128)(2,1)S(1)} %collective-permute-done.3.refs_3_), channel_id=1, source_target_pairs={{0,32},{32,0},{64,96},{96,64},{128,160},{160,128},{192,224},{224,1... | collective-permute-start | bytes 786440 | tf_op jit(solution)/shard_map/ppermute | solution.py:589

commit v8 on v7

--- a/solution.py
+++ b/solution.py
@@ -343,9 +343,12 @@
 def attention_shifted_kernel(last, order, spot, *refs):
     y, own = spot[SPOT_Y], spot[SPOT_OWN_SHIFT]
     if last:
+        arrived, up, before_hbm, mine_hbm, theirs_hbm, back_ref, grads_hbm, x_in, dv_acc, sems = refs[:10]
+        total, before_ref, mine_ref, theirs_ref, grads_ref, more_sems = refs[10:]
+        pltpu.make_async_copy(arrived.at[:, pl.ds(0, 4 * HD)], x_in, sems.at[0]).start()
+    else:
         own_ref, other_ref, *pieces = refs[:5]
-        up, before_hbm, mine_hbm, theirs_hbm, back_ref, grads_hbm, x_in, dv_acc, sems = refs[5:14]
-        total, before_ref, mine_ref, theirs_ref, grads_ref, more_sems = refs[14:]
+        up, back_ref, grads_ref, x_in, dv_acc, sems = refs[5:]
         for dy in range(YS):
             for half in range(2):
                 at = (own if half == 0 else PLANE - own) // ROWS + (y - dy + YS) % YS
@@ -355,19 +358,16 @@
                 else:
                     source = pieces[dy - 1].at[:, pl.ds(half * 4 * HD, 4 * HD)]
                 pltpu.make_async_copy(source, x_in.at[rows, :], sems.at[2 * dy + half]).start()
-    else:
-        arrived, up, back_ref, grads_ref, x_in, dv_acc, sems = refs
-        pltpu.make_async_copy(arrived.at[:, pl.ds(0, 4 * HD)], x_in, sems.at[0]).start()
     if last:
         pairs = ((before_hbm, before_ref), (mine_hbm, mine_ref), (theirs_hbm, theirs_ref))
         others = [pltpu.make_async_copy(*pair, more_sems.at[t]) for t, pair in enumerate(pairs)]
         for copy in others:
             copy.start()
     if last:
+        pltpu.make_async_copy(arrived.at[:, pl.ds(0, 4 * HD)], x_in, sems.at[0]).wait()
+    else:
         for t in range(MEMBERS):
             pltpu.make_async_copy(own_ref.at[0], x_in.at[pl.ds(t * ROWS, ROWS), :], sems.at[t]).wait()
-    else:
-        pltpu.make_async_copy(arrived.at[:, pl.ds(0, 4 * HD)], x_in, sems.at[0]).wait()
     back = attend(x_in, up[...], grads_ref, 0, dv_acc)
     if not last:
         back_ref[...] = back
@@ -411,7 +411,7 @@
         [jax.ShapeDtypeStruct(*shape) for shape in shapes],
         [pltpu.VMEM((GROUP, 4 * HD), BF16), pltpu.VMEM((HD, GROUP), F32), pltpu.SemaphoreType.DMA((2 * YS,))]
         + LAST_SCRATCH * last,
-        (4 * 10**9, 3 * 10**6) if last else (10**6, 10**4),
+        (4 * 10**9, 3 * 10**6) if last else (10**10, 10**4),
     )(order, spot, *arrived, up, *more)
 
 
@@ -467,14 +467,14 @@
 
 
 def merge_kernel(order, spot, place, both_ref, *refs):
-    x_refs, crossed_refs, out_ref = refs[:XS], refs[XS:-1], refs[-1]
+    x_refs, crossed_ref, out_ref = refs[:-2], refs[-2], refs[-1]
     x, core = place[0] // CS, place[0] % CS
     total = jnp.zeros((HEADS * PIECE, BOTH), F32)
     for dx in range(XS):
         for other in range(CS):
             s = (x - dx + XS) % XS * CS + (core + other) % CS
             back = both_ref[s, pl.ds(0, ROWS), :]
-            part = (x_refs, crossed_refs)[other][dx][0]
+            part = x_refs[dx][0] if other == 0 else crossed_ref[dx]
             total += jnp.dot(part, back, preferred_element_type=F32)
     total = (adapter_scale * total).astype(BF16)
     for u in range(HEADS):
@@ -493,18 +493,13 @@
         merge_kernel,
         "merge_gradients",
         3,
-        [block(both.shape)]
-        + [
-            pl.BlockSpec((1, *piece.shape[1:]), lambda i, *s, half=half: (half, 0, 0))
-            for half in range(2)
-            for piece in (pieces, crossed)[half]
-        ],
+        [block(both.shape)] + [block((1, *piece.shape[1:])) for piece in pieces] + [block(crossed.shape)],
         block(shape),
         jax.ShapeDtypeStruct(shape, BF16),
         [],
         (2 * 10**8, 2 * 10**6),
         16,
-    )(order, spot, place, both, *pieces, *crossed)
+    )(order, spot, place, both, *pieces, crossed)
 
 
 def spread_kernel(in_ref, out_ref):
@@ -575,18 +570,19 @@
     pieces = [turned[0]] + [lax.ppermute(turned[dx], "dp", x_shift(dx)) for dx in (1, 2, 3)]
     (sent,) = prepare_shifted(3, order, spot, after(low, turned), frozen)
 
-    packed = pack(after(own_c, pieces, sent), other_c)
-    plain, pieces, sent, packed = after((plain, pieces, sent, packed))
+    packed = pack(after(own_c, pieces[0], sent), other_c)
+    arrived_c = [lax.ppermute(packed[dy - 1], "ulysses", y_shift(dy)) for dy in (1, 2, 3)]
+    plain, pieces, sent = after((plain, pieces, sent), packed)
+
     arrived_d = exchange(sent, "ulysses", SHIFT_GROUPS).reshape(GROUP, 4 * HD + BOTH)
-    arrived_c = [lax.ppermute(packed[dy - 1], "ulysses", y_shift(dy)) for dy in (1, 2, 3)]
+    crossed = lax.ppermute(jnp.stack([piece[1] for piece in pieces]), "dp", CORE_SWAP)
     mine, theirs, grads_plain = attention_plain(order, spot, plain, up)
     theirs = lax.ppermute(theirs, "ulysses", PLAIN_SWAP)
-    arrived_d = after(arrived_d, grads_plain)
-    partial, grads_d = attention_shifted(3, order, spot, [arrived_d], up)
-
-    arrived_c, theirs = after((arrived_c, theirs), partial)
-    partial, grads_c = attention_shifted(2, order, spot, [own_c, other_c, *arrived_c], up, partial, mine, theirs)
-    crossed = [lax.ppermute(piece, "dp", CORE_SWAP) for piece in after(pieces, partial)]
+    arrived_c = after(arrived_c, grads_plain, sent)
+    partial, grads_c = attention_shifted(2, order, spot, [own_c, other_c, *arrived_c], up)
+
+    arrived_d, theirs, crossed = after((arrived_d, theirs, crossed), partial)
+    partial, grads_d = attention_shifted(3, order, spot, [arrived_d], up, partial, mine, theirs)
     summed = exchange(partial.reshape(MEMBERS, ROWS, BOTH), "ulysses", SHIFT_GROUPS)
     ups = up_gradients(plain, arrived_d, (grads_plain, grads_c, grads_d))
 

time: 147 us -> 136 us (0.925)
  waiting for transfers between devices: 19.2 us -> 2.1 us
  blocking collectives: 27.3 us -> 40.6 us
  starting transfers between devices: 43.2 us -> 39.9 us
  local copies, waits for them, and re-layouts: 4.23 us -> 1.59 us
    all_to_all x2 -> x3, blocking collectives: 27.3 us -> 40.6 us  [exchange(): lax.all_to_all(member, axis, 0, 0, tiled=True, axis_index_groups=groups)]
    all_to_all x4 -> x3, waiting for transfers between devices: 9.47 us -> 2.08 us  [exchange(): lax.all_to_all(member, axis, 0, 0, tiled=True, axis_index_groups=groups)]
    ppermute x3, waiting for transfers between devices: 5.15 us -> 0.01 us  [per_device(): lax.ppermute(turned[dx], 'dp', x_shift(dx))]
    all_to_all x4 -> x3, starting transfers between devices: 27 us -> 23.2 us  [exchange(): lax.all_to_all(member, axis, 0, 0, tiled=True, axis_index_groups=groups)]
    ppermute x3, waiting for transfers between devices: 2.89 us -> 0.01 us  [per_device(): lax.ppermute(packed[dy - 1], 'ulysses', y_shift(dy))]
    unnamed x22 -> x12, local copies, waits for them, and re-layouts: 4.23 us -> 1.55 us
    ppermute x4 -> x1, waiting for transfers between devices: 1.64 us -> 0.01 us  [per_device(): lax.ppermute(jnp.stack([piece[1] for piece in pieces]), 'dp', CORE_SWAP)]
  transfers between devices with their start and end apart: 16 -> 12, of which waited for: 11 -> 2; matrix products, arithmetic and copies ran while one was open for 0% -> 0% of each run, Pallas kernels for 23% -> 25%
where the time goes in v8:
time: 136 us; the launch traced here: 135 us
  Pallas kernels  50.1 us (37%)
  blocking collectives  40.6 us (30%)
  starting transfers between devices  39.9 us (29%)
  waiting for transfers between devices  2.1 us (2%)
  local copies, waits for them, and re-layouts  1.59 us (1%)
    all_to_all x3, blocking collectives, exchange(): lax.all_to_all(member, axis, 0, 0, tiled=True, axis_index_groups=groups)  40.6 us
    all_to_all x3, starting transfers between devices, exchange(): lax.all_to_all(member, axis, 0, 0, tiled=True, axis_index_groups=groups)  23.2 us
    pallas_call x2, Pallas kernels, attention_shifted(): call(body, 'attention_last' if last else 'attention_third', 2, [pl.BlockS...  14.3 us
    pallas_call x1, Pallas kernels, attention_plain(): call(attention_plain_kernel, 'attention_plain', 2, [ANYWHERE, up_columns(...  10.2 us
    pallas_call x2, Pallas kernels, prepare_shifted(): call(prepare_third_kernel if item == 2 else prepare_last_kernel, 'prepare...  8.66 us
    pallas_call x1, Pallas kernels, prepare_plain(): call(prepare_plain_kernel, 'prepare_plain', 1, [ANYWHERE] * 7, [block((ME...  6.99 us
    ppermute x1, starting transfers between devices, per_device(): other_c = lax.ppermute(other_c, 'ulysses', SHIFT_SWAP)  5.49 us
    ppermute x3, starting transfers between devices, per_device(): lax.ppermute(turned[dx], 'dp', x_shift(dx))  4.81 us
  transfers between devices with their start and end apart: 12, of which 2 were waited for; matrix products, arithmetic and copies ran while one was open for 0% of the time, Pallas kernels for 25%

profile of v8, /device:TPU:1, one launch (start us, length us, event | category | flops | bytes accessed | tf_op | source)
XLA Modules:
  0.0 135.2 jit_solution(16229283528540098621)
XLA Ops:
  0.6 7.0 %prepare_plain.1 = (bf16[8,128,1152]{2,1,0:T(8,128)(2,1)}, s32[32]{0:T(128)}, s32[8]{0:T(128)}, bf16[128,128]{1,0:T(8,128)(2,1)}) custom-call(s32[32]{0:T(128)} %flags.1, bf16[128,4096]{1,0:T(8,128)(2,1)} %bitcast.36, bf16[128,4096]{1,0:T(8,128)(2,1)} %bitcast.35, bf16[128,4096]{1,0:T(8,128)(2,1)} %bitcast.14, bf16[128,4096]{1,0:T(8,128)(2,1)} %bitcast.17, ...), custom_call_target="tpu_custom_call" | custom-call | flops 1000000000 | bytes 8000000 | tf_op jit(solution)/shard_map/prepare_plain/pallas_call | solution.py:166
  7.6 6.4 %all-to-all-start = ((bf16[8,128,1152]{2,1,0:T(8,128)(2,1)}), bf16[8,128,1152]{2,1,0:T(8,128)(2,1)S(1)}, u32[]{:S(2)}, u32[]{:S(2)}) async-start(bf16[8,128,1152]{2,1,0:T(8,128)(2,1)} %get-tuple-element.41), calls=%async_computation | async-start | bytes 4718592 | tf_op jit(solution)/shard_map/all_to_all | solution.py:48
  14.0 4.2 %prepare_third.1 = (bf16[4,128,512]{2,1,0:T(8,128)(2,1)}, bf16[4,128,512]{2,1,0:T(8,128)(2,1)}) custom-call(s32[32]{0:T(128)} %get-tuple-element.39.order.refs_0_, s32[8]{0:T(128)} %get-tuple-element.40.spot.refs_1_, bf16[128,128]{1,0:T(8,128)(2,1)} %get-tuple-element.49.low_ref, bf16[128,4096]{1,0:T(8,128)(2,1)} %bitcast.15, bf16[128,4096]{1,0:T(8,128)(2,1)} %bitcast.18, ...), custom_call_target="tpu_custom_call" | custom-call | flops 1000000000 | bytes 8000000 | tf_op jit(solution)/shard_map/prepare_third/pallas_call | solution.py:209
  18.3 5.5 %collective-permute-start.3 = (bf16[4,128,512]{2,1,0:T(8,128)(2,1)}, bf16[4,128,512]{2,1,0:T(8,128)(2,1)}, u32[]{:S(2)}, u32[]{:S(2)}) collective-permute-start(bf16[4,128,512]{2,1,0:T(8,128)(2,1)} %get-tuple-element.51), channel_id=1, source_target_pairs={{0,28},{1,29},{2,30},{3,31},{4,8},{5,9},{6,10},{7,11},{8,4},{9,5},... | collective-permute-start | bytes 1572872 | tf_op jit(solution)/shard_map/ppermute | solution.py:568
  23.8 2.6 %turn_input.1 = (bf16[2,512,128]{2,1,0:T(8,128)(2,1)}, bf16[2,512,128]{2,1,0:T(8,128)(2,1)}, bf16[2,512,128]{2,1,0:T(8,128)(2,1)}, bf16[2,512,128]{2,1,0:T(8,128)(2,1)}) custom-call(s32[1]{0:T(128)} %bitcast.8.spot.place, bf16[128,4096]{1,0:T(8,128)(2,1)} %bitcast.37), custom_call_target="tpu_custom_call" | custom-call | flops 1000000000 | bytes 2000000 | tf_op jit(solution)/shard_map/turn_input/pallas_call | solution.py:256
  26.3 1.2 collective-permute-start
  27.5 2.4 %collective-permute-start.1 = (bf16[2,512,128]{2,1,0:T(8,128)(2,1)}, bf16[2,512,128]{2,1,0:T(8,128)(2,1)S(1)}, u32[]{:S(2)}, u32[]{:S(2)}) collective-permute-start(bf16[2,512,128]{2,1,0:T(8,128)(2,1)} %get-tuple-element.47), channel_id=1, source_target_pairs={{0,128},{32,160},{64,192},{96,224},{128,0},{160,32},{192,64},{224,... | collective-permute-start | bytes 786440 | tf_op jit(solution)/shard_map/ppermute | solution.py:570
  30.0 1.2 collective-permute-start.2
  31.1 4.4 %prepare_last.1 = bf16[8,128,640]{2,1,0:T(8,128)(2,1)} custom-call(s32[32]{0:T(128)} %get-tuple-element.39.order.refs_0_, s32[8]{0:T(128)} %get-tuple-element.40.spot.refs_1_, bf16[128,128]{1,0:T(8,128)(2,1)} %get-tuple-element.49.low_ref, bf16[128,4096]{1,0:T(8,128)(2,1)} %bitcast.16, bf16[128,4096]{1,0:T(8,128)(2,1)} %bitcast.19, ...), custom_call_target="tpu_custom_call" | custom-call | flops 1000000000 | bytes 8000000 | tf_op jit(solution)/shard_map/prepare_last/pallas_call | solution.py:209
  35.6 2.1 %pack_third.1 = (bf16[128,1024]{1,0:T(8,128)(2,1)}, bf16[128,1024]{1,0:T(8,128)(2,1)}, bf16[128,1024]{1,0:T(8,128)(2,1)}) custom-call(bf16[4,128,512]{2,1,0:T(8,128)(2,1)} %get-tuple-element.50.own_ref.refs_2_, bf16[4,128,512]{2,1,0:T(8,128)(2,1)} %collective-permute-done.3.other_ref.refs_3_), custom_call_target="tpu_custom_call" | custom-call | bytes 4000000 | tf_op jit(solution)/shard_map/pack_third/pallas_call | solution.py:229
  37.7 1.2 collective-permute-start.6
  38.9 2.4 %collective-permute-start.7 = (bf16[128,1024]{1,0:T(8,128)(2,1)}, bf16[128,1024]{1,0:T(8,128)(2,1)}, u32[]{:S(2)}, u32[]{:S(2)}) collective-permute-start(bf16[128,1024]{1,0:T(8,128)(2,1)} %get-tuple-element.53), channel_id=1, source_target_pairs={{0,2},{1,3},{2,0},{3,1},{4,6},{5,7},{6,4},{7,5},{8,10},{9,11},{10,... | collective-permute-start | bytes 786440 | tf_op jit(solution)/shard_map/ppermute | solution.py:574
  41.3 1.2 collective-permute-start.8
  42.5 0.5 all-to-all-done
  43.0 9.3 %all-to-all-start.1 = ((bf16[8,128,640]{2,1,0:T(8,128)(2,1)}), bf16[8,128,640]{2,1,0:T(8,128)(2,1)}, u32[]{:S(2)}, u32[]{:S(2)}) async-start(bf16[8,128,640]{2,1,0:T(8,128)(2,1)} %prepare_last.1), calls=%async_computation.1 | async-start | bytes 2621440 | tf_op jit(solution)/shard_map/all_to_all | solution.py:48
  52.3 10.2 %attention_plain.1 = (f32[512,128]{1,0:T(8,128)}, bf16[512,128]{1,0:T(8,128)(2,1)}, bf16[1024,512]{1,0:T(8,128)(2,1)}) custom-call(s32[32]{0:T(128)} %get-tuple-element.39.order.refs_0_, s32[8]{0:T(128)} %get-tuple-element.40.spot.refs_1_, bf16[1024,1152]{1,0:T(8,128)(2,1)} %bitcast.33, bf16[128,4096]{1,0:T(8,128)(2,1)} %bitcast.29, bf16[128,4096]{1,0:T(8,128)(2,1)} %bitcast.30), custom_call_target="tpu_custom_call" | custom-call | flops 20000000000 | bytes 4000000 | tf_op jit(solution)/shard_map/attention_plain/pallas_call | solution.py:326
  62.6 0.1 pad_maximum_fusion
  62.7 1.6 %collective-permute-start.5 = (bf16[4,512,128]{2,1,0:T(8,128)(2,1)S(1)}, bf16[4,512,128]{2,1,0:T(8,128)(2,1)S(1)}, u32[]{:S(2)}, u32[]{:S(2)}) collective-permute-start(bf16[4,512,128]{2,1,0:T(8,128)(2,1)S(1)} %pad_maximum_fusion), channel_id=1, source_target_pairs={{0,32},{32,0},{64,96},{96,64},{128,160},{160,128},{192,224},{224,1... | collective-permute-start | bytes 1572872 | tf_op jit(solution)/shard_map/ppermute | solution.py:578
  64.3 0.0 collective-permute-start.4
  64.3 6.8 %attention_third.1 = (f32[1024,128]{1,0:T(8,128)}, bf16[1024,256]{1,0:T(8,128)(2,1)}) custom-call(s32[32]{0:T(128)} %get-tuple-element.39.order.refs_0_, s32[8]{0:T(128)} %get-tuple-element.40.spot.refs_1_, bf16[4,128,512]{2,1,0:T(8,128)(2,1)} %get-tuple-element.50.own_ref.refs_2_, bf16[4,128,512]{2,1,0:T(8,128)(2,1)} %collective-permute-done.3.other_ref.refs_3_, ...), custom_call_target="tpu_custom_call" | custom-call | flops 10000000000 | bytes 10000 | tf_op jit(solution)/shard_map/attention_third/pallas_call | solution.py:403
  71.2 0.6 copy-done.5
  71.8 7.5 %attention_last.1 = (bf16[1024,128]{1,0:T(8,128)(2,1)}, bf16[1024,256]{1,0:T(8,128)(2,1)}) custom-call(s32[32]{0:T(128)} %get-tuple-element.39.order.refs_0_, s32[8]{0:T(128)} %get-tuple-element.40.spot.refs_1_, bf16[1024,640]{1,0:T(8,128)(2,1)} %bitcast.10.refs_2_.low_b, bf16[128,4096]{1,0:T(8,128)(2,1)} %bitcast.32, ...), custom_call_target="tpu_custom_call" | custom-call | flops 4000000000 | bytes 3000000 | tf_op jit(solution)/shard_map/attention_last/pallas_call | solution.py:403
  79.3 7.5 %all-to-all-start.2 = ((bf16[8,128,128]{2,1,0:T(8,128)(2,1)}), bf16[8,128,128]{2,1,0:T(8,128)(2,1)S(1)}, u32[]{:S(2)}, u32[]{:S(2)}) async-start(bf16[8,128,128]{2,1,0:T(8,128)(2,1)} %bitcast.38), calls=%async_computation.2 | async-start | bytes 524288 | tf_op jit(solution)/shard_map/all_to_all | solution.py:48
  86.8 3.4 %up_gradients.1.ups_ref = bf16[8,64,128]{2,1,0:T(8,128)(2,1)} custom-call(bf16[1024,1152]{1,0:T(8,128)(2,1)} %bitcast.34, bf16[1024,640]{1,0:T(8,128)(2,1)} %bitcast.10.refs_2_.low_b, bf16[1024,512]{1,0:T(8,128)(2,1)} %get-tuple-element.62.refs_0_, bf16[1024,256]{1,0:T(8,128)(2,1)} %get-tuple-element.71.refs_1_, bf16[1024,256]{1,0:T(8,128)(2,1)} %get-tuple-element.72.refs_2_), custom_call_target="tpu_custom_call" | custom-call | flops 2000000000 | bytes 3000000 | tf_op jit(solution)/shard_map/up_gradients/pallas_call | solution.py:435
  90.3 1.6 %all-to-all-done.2.summed_ref = bf16[8,128,128]{2,1,0:T(8,128)(2,1)S(1)} async-done(((bf16[8,128,128]{2,1,0:T(8,128)(2,1)}), bf16[8,128,128]{2,1,0:T(8,128)(2,1)S(1)}, u32[]{:S(2)}, u32[]{:S(2)}) %all-to-all-start.2) | async-done | bytes 262176 | tf_op jit(solution)/shard_map/all_to_all | solution.py:48
  91.9 0.9 copy-done.1
  92.8 14.2 %all_to_all.30.both_ref = bf16[8,192,128]{2,1,0:T(8,128)(2,1)S(1)} all-to-all(bf16[8,192,128]{2,1,0:T(8,128)(2,1)S(1)} %gather_parts.1), channel_id=1, replica_groups=mesh['dp'=8,'ulysses'=32] {'dp'}, dimensions={0} | all-to-all | bytes 786432 | tf_op jit(solution)/shard_map/all_to_all | solution.py:48
  107.0 1.0 merge_gradients.1
  108.0 16.1 %all_to_all.31.in_ref = bf16[32,32,128]{2,1,0:T(8,128)(2,1)S(1)} all-to-all(bf16[32,32,128]{2,1,0:T(8,128)(2,1)S(1)} %merge_gradients.1), channel_id=1, replica_groups=mesh['dp'=8,'ulysses'=32] {'ulysses'}, dimensions={0} | all-to-all | bytes 524288 | tf_op jit(solution)/shard_map/all_to_all | solution.py:48
  124.2 0.1 spread_sums.1
  124.2 10.2 %all_to_all.32.in_ref = f32[8,32,128]{2,1,0:T(8,128)S(1)} all-to-all(f32[8,32,128]{2,1,0:T(8,128)S(1)} %spread_sums.1), channel_id=1, replica_groups=mesh['dp'=8,'ulysses'=32] {'dp'}, dimensions={0} | all-to-all | bytes 262144 | tf_op jit(solution)/shard_map/all_to_all | solution.py:48
  134.5 0.7 finish.1
  (25 shorter events, 0.1 us)
Async XLA Ops:
  7.6 35.3 %all-to-all-start = ((bf16[8,128,1152]{2,1,0:T(8,128)(2,1)}), bf16[8,128,1152]{2,1,0:T(8,128)(2,1)S(1)}, u32[]{:S(2)}, u32[]{:S(2)}) async-start(bf16[8,128,1152]{2,1,0:T(8,128)(2,1)} %get-tuple-element.41), calls=%async_computation | async-start | bytes 4718592 | tf_op jit(solution)/shard_map/all_to_all | solution.py:48
  18.3 17.3 %collective-permute-start.3 = (bf16[4,128,512]{2,1,0:T(8,128)(2,1)}, bf16[4,128,512]{2,1,0:T(8,128)(2,1)}, u32[]{:S(2)}, u32[]{:S(2)}) collective-permute-start(bf16[4,128,512]{2,1,0:T(8,128)(2,1)} %get-tuple-element.51), channel_id=1, source_target_pairs={{0,28},{1,29},{2,30},{3,31},{4,8},{5,9},{6,10},{7,11},{8,4},{9,5},... | collective-permute-start | bytes 1572872 | tf_op jit(solution)/shard_map/ppermute | solution.py:568
  26.3 15.0 %collective-permute-start = (bf16[2,512,128]{2,1,0:T(8,128)(2,1)}, bf16[2,512,128]{2,1,0:T(8,128)(2,1)S(1)}, u32[]{:S(2)}, u32[]{:S(2)}) collective-permute-start(bf16[2,512,128]{2,1,0:T(8,128)(2,1)} %get-tuple-element.46), channel_id=1, source_target_pairs={{0,64},{32,96},{64,128},{96,160},{128,192},{160,224},{192,0},{224,... | collective-permute-start | bytes 786440 | tf_op jit(solution)/shard_map/ppermute | solution.py:570
  27.5 14.9 %collective-permute-start.1 = (bf16[2,512,128]{2,1,0:T(8,128)(2,1)}, bf16[2,512,128]{2,1,0:T(8,128)(2,1)S(1)}, u32[]{:S(2)}, u32[]{:S(2)}) collective-permute-start(bf16[2,512,128]{2,1,0:T(8,128)(2,1)} %get-tuple-element.47), channel_id=1, source_target_pairs={{0,128},{32,160},{64,192},{96,224},{128,0},{160,32},{192,64},{224,... | collective-permute-start | bytes 786440 | tf_op jit(solution)/shard_map/ppermute | solution.py:570
  30.0 12.5 %collective-permute-start.2 = (bf16[2,512,128]{2,1,0:T(8,128)(2,1)}, bf16[2,512,128]{2,1,0:T(8,128)(2,1)S(1)}, u32[]{:S(2)}, u32[]{:S(2)}) collective-permute-start(bf16[2,512,128]{2,1,0:T(8,128)(2,1)} %get-tuple-element.48), channel_id=1, source_target_pairs={{0,192},{32,224},{64,0},{96,32},{128,64},{160,96},{192,128},{224,1... | collective-permute-start | bytes 786440 | tf_op jit(solution)/shard_map/ppermute | solution.py:570
  37.7 24.8 %collective-permute-start.6 = (bf16[128,1024]{1,0:T(8,128)(2,1)}, bf16[128,1024]{1,0:T(8,128)(2,1)}, u32[]{:S(2)}, u32[]{:S(2)}) collective-permute-start(bf16[128,1024]{1,0:T(8,128)(2,1)} %get-tuple-element.52), channel_id=1, source_target_pairs={{0,1},{1,2},{2,3},{3,0},{4,5},{5,6},{6,7},{7,4},{8,9},{9,10},{10,1... | collective-permute-start | bytes 786440 | tf_op jit(solution)/shard_map/ppermute | solution.py:574
  38.9 23.6 %collective-permute-start.7 = (bf16[128,1024]{1,0:T(8,128)(2,1)}, bf16[128,1024]{1,0:T(8,128)(2,1)}, u32[]{:S(2)}, u32[]{:S(2)}) collective-permute-start(bf16[128,1024]{1,0:T(8,128)(2,1)} %get-tuple-element.53), channel_id=1, source_target_pairs={{0,2},{1,3},{2,0},{3,1},{4,6},{5,7},{6,4},{7,5},{8,10},{9,11},{10,... | collective-permute-start | bytes 786440 | tf_op jit(solution)/shard_map/ppermute | solution.py:574
  41.3 21.2 %collective-permute-start.8 = (bf16[128,1024]{1,0:T(8,128)(2,1)}, bf16[128,1024]{1,0:T(8,128)(2,1)}, u32[]{:S(2)}, u32[]{:S(2)}) collective-permute-start(bf16[128,1024]{1,0:T(8,128)(2,1)} %get-tuple-element.54), channel_id=1, source_target_pairs={{0,3},{1,0},{2,1},{3,2},{4,7},{5,4},{6,5},{7,6},{8,11},{9,8},{10,9... | collective-permute-start | bytes 786440 | tf_op jit(solution)/shard_map/ppermute | solution.py:574
  43.0 9.3 %copy-start.4 = (bf16[8,128,1152]{2,1,0:T(8,128)(2,1)}, bf16[8,128,1152]{2,1,0:T(8,128)(2,1)S(1)}, u32[]{:S(2)}) copy-start(bf16[8,128,1152]{2,1,0:T(8,128)(2,1)S(1)} %all-to-all-done) | copy-start | bytes 7077892
  43.0 28.2 %all-to-all-start.1 = ((bf16[8,128,640]{2,1,0:T(8,128)(2,1)}), bf16[8,128,640]{2,1,0:T(8,128)(2,1)}, u32[]{:S(2)}, u32[]{:S(2)}) async-start(bf16[8,128,640]{2,1,0:T(8,128)(2,1)} %prepare_last.1), calls=%async_computation.1 | async-start | bytes 2621440 | tf_op jit(solution)/shard_map/all_to_all | solution.py:48
  52.3 10.3 %copy-start = (bf16[2,512,128]{2,1,0:T(8,128)(2,1)S(1)}, bf16[2,512,128]{2,1,0:T(8,128)(2,1)}, u32[]{:S(2)}) copy-start(bf16[2,512,128]{2,1,0:T(8,128)(2,1)} %get-tuple-element.58.refs_0_) | copy-start | bytes 786436
  62.7 8.5 %collective-permute-start.5 = (bf16[4,512,128]{2,1,0:T(8,128)(2,1)S(1)}, bf16[4,512,128]{2,1,0:T(8,128)(2,1)S(1)}, u32[]{:S(2)}, u32[]{:S(2)}) collective-permute-start(bf16[4,512,128]{2,1,0:T(8,128)(2,1)S(1)} %pad_maximum_fusion), channel_id=1, source_target_pairs={{0,32},{32,0},{64,96},{96,64},{128,160},{160,128},{192,224},{224,1... | collective-permute-start | bytes 1572872 | tf_op jit(solution)/shard_map/ppermute | solution.py:578
  64.3 6.8 %collective-permute-start.4 = (bf16[512,128]{1,0:T(8,128)(2,1)}, bf16[512,128]{1,0:T(8,128)(2,1)S(1)}, u32[]{:S(2)}, u32[]{:S(2)}) collective-permute-start(bf16[512,128]{1,0:T(8,128)(2,1)} %get-tuple-element.57), channel_id=1, source_target_pairs={{0,4},{1,5},{2,6},{3,7},{4,0},{5,1},{6,2},{7,3},{8,12},{9,13},{10,... | collective-permute-start | bytes 393224 | tf_op jit(solution)/shard_map/ppermute | solution.py:580
  71.1 0.7 copy-start.5
  79.3 12.5 %all-to-all-start.2 = ((bf16[8,128,128]{2,1,0:T(8,128)(2,1)}), bf16[8,128,128]{2,1,0:T(8,128)(2,1)S(1)}, u32[]{:S(2)}, u32[]{:S(2)}) async-start(bf16[8,128,128]{2,1,0:T(8,128)(2,1)} %bitcast.38), calls=%async_computation.2 | async-start | bytes 524288 | tf_op jit(solution)/shard_map/all_to_all | solution.py:48
  86.8 20.2 %copy-start.2 = (s32[32]{0:T(128)S(1)}, s32[32]{0:T(128)}, u32[]{:S(2)}) copy-start(s32[32]{0:T(128)} %get-tuple-element.39.order.refs_0_) | copy-start | bytes 388
  86.8 20.2 %copy-start.3 = (s32[8]{0:T(128)S(1)}, s32[8]{0:T(128)}, u32[]{:S(2)}) copy-start(s32[8]{0:T(128)} %get-tuple-element.40.spot.refs_1_) | copy-start | bytes 100
  91.9 0.9 copy-start.1

commit v9 on v8

--- a/solution.py
+++ b/solution.py
@@ -109,19 +109,22 @@
     return copies
 
 
-def raise_heads(low, copies, places, q_in, v_in, up_in):
+def raise_heads(low, copies, places, q_in, v_in, up_in, turns=None, done=None):
     lanes = lax.broadcasted_iota(jnp.int32, (ROWS, BOTH), 1)
     none = jnp.zeros_like(low)
     lows = jnp.concatenate([jnp.where(lanes < RANK, low, none), jnp.where(lanes < RANK, none, low)], axis=0)
     for copy in copies:
         copy.wait()
     raised = jnp.dot(lows, up_in[...], preferred_element_type=F32)
-    for p, (buffer, entry) in enumerate(places):
+    for t, p in enumerate(turns or range(len(places))):
+        buffer, entry = places[p]
         own = slice(p * HD, (p + 1) * HD)
         q = (q_in[:, own].astype(F32) + adapter_scale * raised[:ROWS, own]).astype(BF16)
         v = (v_in[:, own].astype(F32) + adapter_scale * raised[ROWS:, own]).astype(BF16)
         buffer[(*entry[:-1], slice(None), pl.ds(entry[-1], HD))] = q
         buffer[(*entry[:-1], slice(None), pl.ds(entry[-1] + 2 * HD, HD))] = v
+        if done is not None:
+            done(t)
 
 
 HALF = HEADS // 2
@@ -137,7 +140,8 @@
 
 
 def prepare_plain_kernel(flags, x_hbm, down_hbm, *refs):
-    frozen, (out_ref, order, spot, low_ref, x_in, down_in, whole_sems, q_in, v_in, up_in, sems) = refs[:5], refs[5:]
+    frozen, (out_hbm, order, spot, low_ref, out_ref, out_sems, *refs) = refs[:5], refs[5:]
+    x_in, down_in, whole_sems, q_in, v_in, up_in, sems = refs
     wholes = [
         pltpu.make_async_copy(x_hbm, x_in, whole_sems.at[0]),
         pltpu.make_async_copy(down_hbm, down_in, whole_sems.at[1]),
@@ -159,7 +163,19 @@
     low_ref[...] = low
     for seat in range(MEMBERS):
         out_ref[seat, :, pl.ds(8 * HD, BOTH)] = low
-    raise_heads(low, copies, places, q_in, v_in, up_in)
+    sends = [
+        pltpu.make_async_copy(out_ref.at[seat], out_hbm.at[seat], out_sems.at[seat]) for seat in range(MEMBERS)
+    ]
+
+    def done(t):
+        if t % 2 == 1 and t > 1:
+            sends[t // 2 - 1].start()
+
+    turns = [seat + half * MEMBERS for seat in range(MEMBERS) for half in range(2)]
+    raise_heads(low, copies, places, q_in, v_in, up_in, turns, done)
+    sends[-1].start()
+    for send in sends:
+        send.wait()
 
 
 def prepare_plain(flags, x, down, frozen):
@@ -168,14 +184,15 @@
         "prepare_plain",
         1,
         [ANYWHERE] * 7,
-        [block((MEMBERS, ROWS, 8 * HD + BOTH)), SCALARS, SCALARS, block((ROWS, BOTH))],
+        [ANYWHERE, SCALARS, SCALARS, block((ROWS, BOTH))],
         (
             jax.ShapeDtypeStruct((MEMBERS, ROWS, 8 * HD + BOTH), BF16),
             jax.ShapeDtypeStruct((HEADS,), jnp.int32),
             jax.ShapeDtypeStruct((MEMBERS,), jnp.int32),
             jax.ShapeDtypeStruct((ROWS, BOTH), BF16),
         ),
-        [pltpu.VMEM((ROWS, WIDTH), BF16), pltpu.VMEM((BOTH, WIDTH), BF16), pltpu.SemaphoreType.DMA((2,))]
+        [pltpu.VMEM((MEMBERS, ROWS, 8 * HD + BOTH), BF16), pltpu.SemaphoreType.DMA((MEMBERS,))]
+        + [pltpu.VMEM((ROWS, WIDTH), BF16), pltpu.VMEM((BOTH, WIDTH), BF16), pltpu.SemaphoreType.DMA((2,))]
         + head_scratch(HALF),
         (10**9, 8 * 10**6),
     )(flags, x, down, *frozen)
@@ -265,7 +282,7 @@
     )(place, x)
 
 
-def attend(x_ref, up, grads_ref, column, dv_acc):
+def attend(x_ref, up_of, grads_ref, column, dv_acc):
     factor = 1.0 / math.sqrt(HD)
     bend = factor * math.log2(math.e)
     row_ids = lax.broadcasted_iota(jnp.int32, (RB, RB), 0)
@@ -298,27 +315,37 @@
     dv = dv_acc[...].T.astype(BF16)
     grads_ref[:, pl.ds(column + HD, HD)] = dv
     lanes = lax.broadcasted_iota(jnp.int32, (GROUP, BOTH), 1)
+    up = up_of()
     return jnp.where(lanes < RANK, dot_t(dq, up), dot_t(dv, up))
 
 
-def attention_plain_kernel(order, spot, arrived, up_a, up_b, mine_ref, theirs_ref, grads_ref, xs, dv_acc, total, sems):
+def attention_plain_kernel(order, spot, arrived, up_hbm, mine_ref, theirs_ref, grads_ref, xs, dv_acc, total, sems, *ups):
+    up_in, up_sems = ups
     copies = []
     for item in range(2):
         source = arrived.at[:, pl.ds(item * 4 * HD, 4 * HD)]
         copies.append(pltpu.make_async_copy(source, xs.at[item], sems.at[item]))
         copies[-1].start()
+    up_of = [fetch_up(item, order, spot, up_hbm, up_in.at[item], up_sems.at[item]) for item in range(2)]
     copies[0].wait()
-    total[...] = attend(xs.at[0], up_a[...], grads_ref, 0, dv_acc)
+    total[...] = attend(xs.at[0], up_of[0], grads_ref, 0, dv_acc)
     copies[1].wait()
-    total[...] += attend(xs.at[1], up_b[...], grads_ref, 2 * HD, dv_acc)
+    total[...] += attend(xs.at[1], up_of[1], grads_ref, 2 * HD, dv_acc)
     own = pl.multiple_of(spot[SPOT_OWN_PLAIN], PLANE)
     mine_ref[...] = total[pl.ds(own, PLANE), :]
     theirs_ref[...] = total[pl.ds(PLANE - own, PLANE), :].astype(BF16)
 
 
-def up_columns(item):
-    seat = SPOT_PLAIN if item < 2 else SPOT_SHIFT
-    return pl.BlockSpec((BOTH, HD), lambda i, order, spot: (0, order[item * MEMBERS + spot[seat]]))
+def fetch_up(item, order, spot, up_hbm, up_in, sem):
+    head = order[item * MEMBERS + spot[SPOT_PLAIN if item < 2 else SPOT_SHIFT]]
+    copy = pltpu.make_async_copy(up_hbm.at[:, pl.ds(pl.multiple_of(head * HD, HD), HD)], up_in, sem)
+    copy.start()
+
+    def wait_up():
+        copy.wait()
+        return up_in[...]
+
+    return wait_up
 
 
 def attention_plain(order, spot, arrived, up):
@@ -327,7 +354,7 @@
         attention_plain_kernel,
         "attention_plain",
         2,
-        [ANYWHERE, up_columns(0), up_columns(1)],
+        [ANYWHERE] * 2,
         [block(shape) for shape, _ in shapes],
         [jax.ShapeDtypeStruct(*shape) for shape in shapes],
         [
@@ -335,20 +362,22 @@
             pltpu.VMEM((HD, GROUP), F32),
             pltpu.VMEM((GROUP, BOTH), F32),
             pltpu.SemaphoreType.DMA((2,)),
+            pltpu.VMEM((2, BOTH, HD), BF16),
+            pltpu.SemaphoreType.DMA((2,)),
         ],
         (2 * 10**10, 4 * 10**6),
-    )(order, spot, arrived, up, up)
+    )(order, spot, arrived, up)
 
 
 def attention_shifted_kernel(last, order, spot, *refs):
     y, own = spot[SPOT_Y], spot[SPOT_OWN_SHIFT]
     if last:
-        arrived, up, before_hbm, mine_hbm, theirs_hbm, back_ref, grads_hbm, x_in, dv_acc, sems = refs[:10]
-        total, before_ref, mine_ref, theirs_ref, grads_ref, more_sems = refs[10:]
+        arrived, up, before_hbm, mine_hbm, theirs_hbm, back_ref, grads_hbm, x_in, dv_acc, sems, *refs = refs
+        up_in, up_sem, total, before_ref, mine_ref, theirs_ref, grads_ref, more_sems = refs
         pltpu.make_async_copy(arrived.at[:, pl.ds(0, 4 * HD)], x_in, sems.at[0]).start()
     else:
         own_ref, other_ref, *pieces = refs[:5]
-        up, back_ref, grads_ref, x_in, dv_acc, sems = refs[5:]
+        up, back_ref, grads_ref, x_in, dv_acc, sems, up_in, up_sem = refs[5:]
         for dy in range(YS):
             for half in range(2):
                 at = (own if half == 0 else PLANE - own) // ROWS + (y - dy + YS) % YS
@@ -358,6 +387,7 @@
                 else:
                     source = pieces[dy - 1].at[:, pl.ds(half * 4 * HD, 4 * HD)]
                 pltpu.make_async_copy(source, x_in.at[rows, :], sems.at[2 * dy + half]).start()
+    up_of = fetch_up(3 if last else 2, order, spot, up, up_in, up_sem)
     if last:
         pairs = ((before_hbm, before_ref), (mine_hbm, mine_ref), (theirs_hbm, theirs_ref))
         others = [pltpu.make_async_copy(*pair, more_sems.at[t]) for t, pair in enumerate(pairs)]
@@ -368,7 +398,7 @@
     else:
         for t in range(MEMBERS):
             pltpu.make_async_copy(own_ref.at[0], x_in.at[pl.ds(t * ROWS, ROWS), :], sems.at[t]).wait()
-    back = attend(x_in, up[...], grads_ref, 0, dv_acc)
+    back = attend(x_in, up_of, grads_ref, 0, dv_acc)
     if not last:
         back_ref[...] = back
         return
@@ -393,7 +423,7 @@
 ]
 
 
-def attention_shifted(item, order, spot, arrived, up, *more):
+def attention_shifted(order, spot, arrived, up, *more):
     last = len(more) > 0
     shapes = [((GROUP, BOTH), BF16 if last else F32), ((GROUP, 2 * HD), BF16)]
 
@@ -405,11 +435,11 @@
         "attention_last" if last else "attention_third",
         2,
         [pl.BlockSpec(memory_space=pl.ANY) if last else ANYWHERE] * len(arrived)
-        + [up_columns(item)]
-        + [ANYWHERE] * len(more),
+        + [ANYWHERE] * (1 + len(more)),
         [block(shapes[0][0]), ANYWHERE] if last else [block(shape) for shape, _ in shapes],
         [jax.ShapeDtypeStruct(*shape) for shape in shapes],
         [pltpu.VMEM((GROUP, 4 * HD), BF16), pltpu.VMEM((HD, GROUP), F32), pltpu.SemaphoreType.DMA((2 * YS,))]
+        + [pltpu.VMEM((BOTH, HD), BF16), pltpu.SemaphoreType.DMA]
         + LAST_SCRATCH * last,
         (4 * 10**9, 3 * 10**6) if last else (10**10, 10**4),
     )(order, spot, *arrived, up, *more)
@@ -579,10 +609,10 @@
     mine, theirs, grads_plain = attention_plain(order, spot, plain, up)
     theirs = lax.ppermute(theirs, "ulysses", PLAIN_SWAP)
     arrived_c = after(arrived_c, grads_plain, sent)
-    partial, grads_c = attention_shifted(2, order, spot, [own_c, other_c, *arrived_c], up)
+    partial, grads_c = attention_shifted(order, spot, [own_c, other_c, *arrived_c], up)
 
     arrived_d, theirs, crossed = after((arrived_d, theirs, crossed), partial)
-    partial, grads_d = attention_shifted(3, order, spot, [arrived_d], up, partial, mine, theirs)
+    partial, grads_d = attention_shifted(order, spot, [arrived_d], up, partial, mine, theirs)
     summed = exchange(partial.reshape(MEMBERS, ROWS, BOTH), "ulysses", SHIFT_GROUPS)
     ups = up_gradients(plain, arrived_d, (grads_plain, grads_c, grads_d))
 

time: 136 us -> 135 us (level)
  transfers between devices with their start and end apart: 12 -> 12, of which waited for: 2 -> 2; matrix products, arithmetic and copies ran while one was open for 0% -> 0% of each run, Pallas kernels for 25% -> 24%
where the time goes in v9:
time: 135 us; the launch traced here: 134 us
  Pallas kernels  49 us (36%)
  blocking collectives  40.6 us (30%)
  starting transfers between devices  40.2 us (30%)
  waiting for transfers between devices  2.11 us (2%)
  local copies, waits for them, and re-layouts  1.59 us (1%)
    all_to_all x3, blocking collectives, exchange(): lax.all_to_all(member, axis, 0, 0, tiled=True, axis_index_groups=groups)  40.6 us
    all_to_all x3, starting transfers between devices, exchange(): lax.all_to_all(member, axis, 0, 0, tiled=True, axis_index_groups=groups)  23.5 us
    pallas_call x2, Pallas kernels, attention_shifted(): call(body, 'attention_last' if last else 'attention_third', 2, [pl.BlockS...  13 us
    pallas_call x1, Pallas kernels, attention_plain(): call(attention_plain_kernel, 'attention_plain', 2, [ANYWHERE] * 2, [block...  9.91 us
    pallas_call x2, Pallas kernels, prepare_shifted(): call(prepare_third_kernel if item == 2 else prepare_last_kernel, 'prepare...  8.66 us
    pallas_call x1, Pallas kernels, prepare_plain(): call(prepare_plain_kernel, 'prepare_plain', 1, [ANYWHERE] * 7, [ANYWHERE,...  7.47 us
    ppermute x1, starting transfers between devices, per_device(): other_c = lax.ppermute(other_c, 'ulysses', SHIFT_SWAP)  5.48 us
    ppermute x3, starting transfers between devices, per_device(): lax.ppermute(turned[dx], 'dp', x_shift(dx))  4.82 us
  transfers between devices with their start and end apart: 12, of which 2 were waited for; matrix products, arithmetic and copies ran while one was open for 0% of the time, Pallas kernels for 24%

profile of v9, /device:TPU:1, one launch (start us, length us, event | category | flops | bytes accessed | tf_op | source)
XLA Modules:
  0.0 134.4 jit_solution(1977020830678179742)
XLA Ops:
  0.6 7.5 %prepare_plain.1 = (bf16[8,128,1152]{2,1,0:T(8,128)(2,1)}, s32[32]{0:T(128)}, s32[8]{0:T(128)}, bf16[128,128]{1,0:T(8,128)(2,1)}) custom-call(s32[32]{0:T(128)} %flags.1, bf16[128,4096]{1,0:T(8,128)(2,1)} %bitcast.35, bf16[128,4096]{1,0:T(8,128)(2,1)} %bitcast.34, bf16[128,4096]{1,0:T(8,128)(2,1)} %bitcast.14, bf16[128,4096]{1,0:T(8,128)(2,1)} %bitcast.17, ...), custom_call_target="tpu_custom_call" | custom-call | flops 1000000000 | bytes 8000000 | tf_op jit(solution)/shard_map/prepare_plain/pallas_call | solution.py:182
  8.1 6.4 %all-to-all-start = ((bf16[8,128,1152]{2,1,0:T(8,128)(2,1)}), bf16[8,128,1152]{2,1,0:T(8,128)(2,1)S(1)}, u32[]{:S(2)}, u32[]{:S(2)}) async-start(bf16[8,128,1152]{2,1,0:T(8,128)(2,1)} %get-tuple-element.41), calls=%async_computation | async-start | bytes 4718592 | tf_op jit(solution)/shard_map/all_to_all | solution.py:48
  14.5 4.2 %prepare_third.1 = (bf16[4,128,512]{2,1,0:T(8,128)(2,1)}, bf16[4,128,512]{2,1,0:T(8,128)(2,1)}) custom-call(s32[32]{0:T(128)} %get-tuple-element.39.order.refs_0_, s32[8]{0:T(128)} %get-tuple-element.40.spot.refs_1_, bf16[128,128]{1,0:T(8,128)(2,1)} %get-tuple-element.49.low_ref, bf16[128,4096]{1,0:T(8,128)(2,1)} %bitcast.15, bf16[128,4096]{1,0:T(8,128)(2,1)} %bitcast.18, ...), custom_call_target="tpu_custom_call" | custom-call | flops 1000000000 | bytes 8000000 | tf_op jit(solution)/shard_map/prepare_third/pallas_call | solution.py:226
  18.7 5.5 %collective-permute-start.3 = (bf16[4,128,512]{2,1,0:T(8,128)(2,1)}, bf16[4,128,512]{2,1,0:T(8,128)(2,1)}, u32[]{:S(2)}, u32[]{:S(2)}) collective-permute-start(bf16[4,128,512]{2,1,0:T(8,128)(2,1)} %get-tuple-element.51), channel_id=1, source_target_pairs={{0,28},{1,29},{2,30},{3,31},{4,8},{5,9},{6,10},{7,11},{8,4},{9,5},... | collective-permute-start | bytes 1572872 | tf_op jit(solution)/shard_map/ppermute | solution.py:598
  24.2 2.6 %turn_input.1 = (bf16[2,512,128]{2,1,0:T(8,128)(2,1)}, bf16[2,512,128]{2,1,0:T(8,128)(2,1)}, bf16[2,512,128]{2,1,0:T(8,128)(2,1)}, bf16[2,512,128]{2,1,0:T(8,128)(2,1)}) custom-call(s32[1]{0:T(128)} %bitcast.8.spot.place, bf16[128,4096]{1,0:T(8,128)(2,1)} %bitcast.36), custom_call_target="tpu_custom_call" | custom-call | flops 1000000000 | bytes 2000000 | tf_op jit(solution)/shard_map/turn_input/pallas_call | solution.py:273
  26.8 1.2 collective-permute-start
  28.0 2.4 %collective-permute-start.1 = (bf16[2,512,128]{2,1,0:T(8,128)(2,1)}, bf16[2,512,128]{2,1,0:T(8,128)(2,1)S(1)}, u32[]{:S(2)}, u32[]{:S(2)}) collective-permute-start(bf16[2,512,128]{2,1,0:T(8,128)(2,1)} %get-tuple-element.47), channel_id=1, source_target_pairs={{0,128},{32,160},{64,192},{96,224},{128,0},{160,32},{192,64},{224,... | collective-permute-start | bytes 786440 | tf_op jit(solution)/shard_map/ppermute | solution.py:600
  30.5 1.2 collective-permute-start.2
  31.6 4.4 %prepare_last.1 = bf16[8,128,640]{2,1,0:T(8,128)(2,1)} custom-call(s32[32]{0:T(128)} %get-tuple-element.39.order.refs_0_, s32[8]{0:T(128)} %get-tuple-element.40.spot.refs_1_, bf16[128,128]{1,0:T(8,128)(2,1)} %get-tuple-element.49.low_ref, bf16[128,4096]{1,0:T(8,128)(2,1)} %bitcast.16, bf16[128,4096]{1,0:T(8,128)(2,1)} %bitcast.19, ...), custom_call_target="tpu_custom_call" | custom-call | flops 1000000000 | bytes 8000000 | tf_op jit(solution)/shard_map/prepare_last/pallas_call | solution.py:226
  36.1 2.1 %pack_third.1 = (bf16[128,1024]{1,0:T(8,128)(2,1)}, bf16[128,1024]{1,0:T(8,128)(2,1)}, bf16[128,1024]{1,0:T(8,128)(2,1)}) custom-call(bf16[4,128,512]{2,1,0:T(8,128)(2,1)} %get-tuple-element.50.own_ref.refs_2_, bf16[4,128,512]{2,1,0:T(8,128)(2,1)} %collective-permute-done.3.other_ref.refs_3_), custom_call_target="tpu_custom_call" | custom-call | bytes 4000000 | tf_op jit(solution)/shard_map/pack_third/pallas_call | solution.py:246
  38.2 1.2 collective-permute-start.6
  39.4 2.4 %collective-permute-start.7 = (bf16[128,1024]{1,0:T(8,128)(2,1)}, bf16[128,1024]{1,0:T(8,128)(2,1)}, u32[]{:S(2)}, u32[]{:S(2)}) collective-permute-start(bf16[128,1024]{1,0:T(8,128)(2,1)} %get-tuple-element.53), channel_id=1, source_target_pairs={{0,2},{1,3},{2,0},{3,1},{4,6},{5,7},{6,4},{7,5},{8,10},{9,11},{10,... | collective-permute-start | bytes 786440 | tf_op jit(solution)/shard_map/ppermute | solution.py:604
  41.8 1.2 collective-permute-start.8
  43.0 0.5 all-to-all-done
  43.5 9.3 %all-to-all-start.1 = ((bf16[8,128,640]{2,1,0:T(8,128)(2,1)}), bf16[8,128,640]{2,1,0:T(8,128)(2,1)}, u32[]{:S(2)}, u32[]{:S(2)}) async-start(bf16[8,128,640]{2,1,0:T(8,128)(2,1)} %prepare_last.1), calls=%async_computation.1 | async-start | bytes 2621440 | tf_op jit(solution)/shard_map/all_to_all | solution.py:48
  52.7 9.9 %attention_plain.1 = (f32[512,128]{1,0:T(8,128)}, bf16[512,128]{1,0:T(8,128)(2,1)}, bf16[1024,512]{1,0:T(8,128)(2,1)}) custom-call(s32[32]{0:T(128)} %get-tuple-element.39.order.refs_0_, s32[8]{0:T(128)} %get-tuple-element.40.spot.refs_1_, bf16[1024,1152]{1,0:T(8,128)(2,1)} %bitcast.32, bf16[128,4096]{1,0:T(8,128)(2,1)} %bitcast.29), custom_call_target="tpu_custom_call" | custom-call | flops 20000000000 | bytes 4000000 | tf_op jit(solution)/shard_map/attention_plain/pallas_call | solution.py:353
  62.8 0.1 pad_maximum_fusion
  62.9 1.7 %collective-permute-start.5 = (bf16[4,512,128]{2,1,0:T(8,128)(2,1)S(1)}, bf16[4,512,128]{2,1,0:T(8,128)(2,1)S(1)}, u32[]{:S(2)}, u32[]{:S(2)}) collective-permute-start(bf16[4,512,128]{2,1,0:T(8,128)(2,1)S(1)} %pad_maximum_fusion), channel_id=1, source_target_pairs={{0,32},{32,0},{64,96},{96,64},{128,160},{160,128},{192,224},{224,1... | collective-permute-start | bytes 1572872 | tf_op jit(solution)/shard_map/ppermute | solution.py:608
  64.5 0.0 collective-permute-start.4
  64.5 6.2 %attention_third.1 = (f32[1024,128]{1,0:T(8,128)}, bf16[1024,256]{1,0:T(8,128)(2,1)}) custom-call(s32[32]{0:T(128)} %get-tuple-element.39.order.refs_0_, s32[8]{0:T(128)} %get-tuple-element.40.spot.refs_1_, bf16[4,128,512]{2,1,0:T(8,128)(2,1)} %get-tuple-element.50.own_ref.refs_2_, bf16[4,128,512]{2,1,0:T(8,128)(2,1)} %collective-permute-done.3.other_ref.refs_3_, ...), custom_call_target="tpu_custom_call" | custom-call | flops 10000000000 | bytes 10000 | tf_op jit(solution)/shard_map/attention_third/pallas_call | solution.py:433
  70.8 0.6 copy-done.5
  71.4 6.8 %attention_last.1 = (bf16[1024,128]{1,0:T(8,128)(2,1)}, bf16[1024,256]{1,0:T(8,128)(2,1)}) custom-call(s32[32]{0:T(128)} %get-tuple-element.39.order.refs_0_, s32[8]{0:T(128)} %get-tuple-element.40.spot.refs_1_, bf16[1024,640]{1,0:T(8,128)(2,1)} %bitcast.10.refs_2_.low_b, bf16[128,4096]{1,0:T(8,128)(2,1)} %bitcast.31, ...), custom_call_target="tpu_custom_call" | custom-call | flops 4000000000 | bytes 3000000 | tf_op jit(solution)/shard_map/attention_last/pallas_call | solution.py:433
  78.2 7.8 %all-to-all-start.2 = ((bf16[8,128,128]{2,1,0:T(8,128)(2,1)}), bf16[8,128,128]{2,1,0:T(8,128)(2,1)S(1)}, u32[]{:S(2)}, u32[]{:S(2)}) async-start(bf16[8,128,128]{2,1,0:T(8,128)(2,1)} %bitcast.37), calls=%async_computation.2 | async-start | bytes 524288 | tf_op jit(solution)/shard_map/all_to_all | solution.py:48
  86.1 3.4 %up_gradients.1.ups_ref = bf16[8,64,128]{2,1,0:T(8,128)(2,1)} custom-call(bf16[1024,1152]{1,0:T(8,128)(2,1)} %bitcast.33, bf16[1024,640]{1,0:T(8,128)(2,1)} %bitcast.10.refs_2_.low_b, bf16[1024,512]{1,0:T(8,128)(2,1)} %get-tuple-element.62.refs_0_, bf16[1024,256]{1,0:T(8,128)(2,1)} %get-tuple-element.71.refs_1_, bf16[1024,256]{1,0:T(8,128)(2,1)} %get-tuple-element.72.refs_2_), custom_call_target="tpu_custom_call" | custom-call | flops 2000000000 | bytes 3000000 | tf_op jit(solution)/shard_map/up_gradients/pallas_call | solution.py:465
  89.5 1.6 %all-to-all-done.2.summed_ref = bf16[8,128,128]{2,1,0:T(8,128)(2,1)S(1)} async-done(((bf16[8,128,128]{2,1,0:T(8,128)(2,1)}), bf16[8,128,128]{2,1,0:T(8,128)(2,1)S(1)}, u32[]{:S(2)}, u32[]{:S(2)}) %all-to-all-start.2) | async-done | bytes 262176 | tf_op jit(solution)/shard_map/all_to_all | solution.py:48
  91.1 0.9 copy-done.1
  92.0 14.2 %all_to_all.30.both_ref = bf16[8,192,128]{2,1,0:T(8,128)(2,1)S(1)} all-to-all(bf16[8,192,128]{2,1,0:T(8,128)(2,1)S(1)} %gather_parts.1), channel_id=1, replica_groups=mesh['dp'=8,'ulysses'=32] {'dp'}, dimensions={0} | all-to-all | bytes 786432 | tf_op jit(solution)/shard_map/all_to_all | solution.py:48
  106.2 1.0 merge_gradients.1
  107.2 16.2 %all_to_all.31.in_ref = bf16[32,32,128]{2,1,0:T(8,128)(2,1)S(1)} all-to-all(bf16[32,32,128]{2,1,0:T(8,128)(2,1)S(1)} %merge_gradients.1), channel_id=1, replica_groups=mesh['dp'=8,'ulysses'=32] {'ulysses'}, dimensions={0} | all-to-all | bytes 524288 | tf_op jit(solution)/shard_map/all_to_all | solution.py:48
  123.4 0.1 spread_sums.1
  123.5 10.2 %all_to_all.32.in_ref = f32[8,32,128]{2,1,0:T(8,128)S(1)} all-to-all(f32[8,32,128]{2,1,0:T(8,128)S(1)} %spread_sums.1), channel_id=1, replica_groups=mesh['dp'=8,'ulysses'=32] {'dp'}, dimensions={0} | all-to-all | bytes 262144 | tf_op jit(solution)/shard_map/all_to_all | solution.py:48
  133.7 0.7 finish.1
  (25 shorter events, 0.1 us)
Async XLA Ops:
  8.1 35.3 %all-to-all-start = ((bf16[8,128,1152]{2,1,0:T(8,128)(2,1)}), bf16[8,128,1152]{2,1,0:T(8,128)(2,1)S(1)}, u32[]{:S(2)}, u32[]{:S(2)}) async-start(bf16[8,128,1152]{2,1,0:T(8,128)(2,1)} %get-tuple-element.41), calls=%async_computation | async-start | bytes 4718592 | tf_op jit(solution)/shard_map/all_to_all | solution.py:48
  18.7 17.3 %collective-permute-start.3 = (bf16[4,128,512]{2,1,0:T(8,128)(2,1)}, bf16[4,128,512]{2,1,0:T(8,128)(2,1)}, u32[]{:S(2)}, u32[]{:S(2)}) collective-permute-start(bf16[4,128,512]{2,1,0:T(8,128)(2,1)} %get-tuple-element.51), channel_id=1, source_target_pairs={{0,28},{1,29},{2,30},{3,31},{4,8},{5,9},{6,10},{7,11},{8,4},{9,5},... | collective-permute-start | bytes 1572872 | tf_op jit(solution)/shard_map/ppermute | solution.py:598
  26.8 15.0 %collective-permute-start = (bf16[2,512,128]{2,1,0:T(8,128)(2,1)}, bf16[2,512,128]{2,1,0:T(8,128)(2,1)S(1)}, u32[]{:S(2)}, u32[]{:S(2)}) collective-permute-start(bf16[2,512,128]{2,1,0:T(8,128)(2,1)} %get-tuple-element.46), channel_id=1, source_target_pairs={{0,64},{32,96},{64,128},{96,160},{128,192},{160,224},{192,0},{224,... | collective-permute-start | bytes 786440 | tf_op jit(solution)/shard_map/ppermute | solution.py:600
  28.0 14.9 %collective-permute-start.1 = (bf16[2,512,128]{2,1,0:T(8,128)(2,1)}, bf16[2,512,128]{2,1,0:T(8,128)(2,1)S(1)}, u32[]{:S(2)}, u32[]{:S(2)}) collective-permute-start(bf16[2,512,128]{2,1,0:T(8,128)(2,1)} %get-tuple-element.47), channel_id=1, source_target_pairs={{0,128},{32,160},{64,192},{96,224},{128,0},{160,32},{192,64},{224,... | collective-permute-start | bytes 786440 | tf_op jit(solution)/shard_map/ppermute | solution.py:600
  30.5 12.5 %collective-permute-start.2 = (bf16[2,512,128]{2,1,0:T(8,128)(2,1)}, bf16[2,512,128]{2,1,0:T(8,128)(2,1)S(1)}, u32[]{:S(2)}, u32[]{:S(2)}) collective-permute-start(bf16[2,512,128]{2,1,0:T(8,128)(2,1)} %get-tuple-element.48), channel_id=1, source_target_pairs={{0,192},{32,224},{64,0},{96,32},{128,64},{160,96},{192,128},{224,1... | collective-permute-start | bytes 786440 | tf_op jit(solution)/shard_map/ppermute | solution.py:600
  38.2 24.5 %collective-permute-start.6 = (bf16[128,1024]{1,0:T(8,128)(2,1)}, bf16[128,1024]{1,0:T(8,128)(2,1)}, u32[]{:S(2)}, u32[]{:S(2)}) collective-permute-start(bf16[128,1024]{1,0:T(8,128)(2,1)} %get-tuple-element.52), channel_id=1, source_target_pairs={{0,1},{1,2},{2,3},{3,0},{4,5},{5,6},{6,7},{7,4},{8,9},{9,10},{10,1... | collective-permute-start | bytes 786440 | tf_op jit(solution)/shard_map/ppermute | solution.py:604
  39.4 23.3 %collective-permute-start.7 = (bf16[128,1024]{1,0:T(8,128)(2,1)}, bf16[128,1024]{1,0:T(8,128)(2,1)}, u32[]{:S(2)}, u32[]{:S(2)}) collective-permute-start(bf16[128,1024]{1,0:T(8,128)(2,1)} %get-tuple-element.53), channel_id=1, source_target_pairs={{0,2},{1,3},{2,0},{3,1},{4,6},{5,7},{6,4},{7,5},{8,10},{9,11},{10,... | collective-permute-start | bytes 786440 | tf_op jit(solution)/shard_map/ppermute | solution.py:604
  41.8 20.9 %collective-permute-start.8 = (bf16[128,1024]{1,0:T(8,128)(2,1)}, bf16[128,1024]{1,0:T(8,128)(2,1)}, u32[]{:S(2)}, u32[]{:S(2)}) collective-permute-start(bf16[128,1024]{1,0:T(8,128)(2,1)} %get-tuple-element.54), channel_id=1, source_target_pairs={{0,3},{1,0},{2,1},{3,2},{4,7},{5,4},{6,5},{7,6},{8,11},{9,8},{10,9... | collective-permute-start | bytes 786440 | tf_op jit(solution)/shard_map/ppermute | solution.py:604
  43.5 9.3 %copy-start.4 = (bf16[8,128,1152]{2,1,0:T(8,128)(2,1)}, bf16[8,128,1152]{2,1,0:T(8,128)(2,1)S(1)}, u32[]{:S(2)}) copy-start(bf16[8,128,1152]{2,1,0:T(8,128)(2,1)S(1)} %all-to-all-done) | copy-start | bytes 7077892
  43.5 27.3 %all-to-all-start.1 = ((bf16[8,128,640]{2,1,0:T(8,128)(2,1)}), bf16[8,128,640]{2,1,0:T(8,128)(2,1)}, u32[]{:S(2)}, u32[]{:S(2)}) async-start(bf16[8,128,640]{2,1,0:T(8,128)(2,1)} %prepare_last.1), calls=%async_computation.1 | async-start | bytes 2621440 | tf_op jit(solution)/shard_map/all_to_all | solution.py:48
  52.7 10.0 %copy-start = (bf16[2,512,128]{2,1,0:T(8,128)(2,1)S(1)}, bf16[2,512,128]{2,1,0:T(8,128)(2,1)}, u32[]{:S(2)}) copy-start(bf16[2,512,128]{2,1,0:T(8,128)(2,1)} %get-tuple-element.58.refs_0_) | copy-start | bytes 786436
  62.9 7.9 %collective-permute-start.5 = (bf16[4,512,128]{2,1,0:T(8,128)(2,1)S(1)}, bf16[4,512,128]{2,1,0:T(8,128)(2,1)S(1)}, u32[]{:S(2)}, u32[]{:S(2)}) collective-permute-start(bf16[4,512,128]{2,1,0:T(8,128)(2,1)S(1)} %pad_maximum_fusion), channel_id=1, source_target_pairs={{0,32},{32,0},{64,96},{96,64},{128,160},{160,128},{192,224},{224,1... | collective-permute-start | bytes 1572872 | tf_op jit(solution)/shard_map/ppermute | solution.py:608
  64.5 6.2 %collective-permute-start.4 = (bf16[512,128]{1,0:T(8,128)(2,1)}, bf16[512,128]{1,0:T(8,128)(2,1)S(1)}, u32[]{:S(2)}, u32[]{:S(2)}) collective-permute-start(bf16[512,128]{1,0:T(8,128)(2,1)} %get-tuple-element.57), channel_id=1, source_target_pairs={{0,4},{1,5},{2,6},{3,7},{4,0},{5,1},{6,2},{7,3},{8,12},{9,13},{10,... | collective-permute-start | bytes 393224 | tf_op jit(solution)/shard_map/ppermute | solution.py:610
  70.8 0.7 copy-start.5
  78.2 12.8 %all-to-all-start.2 = ((bf16[8,128,128]{2,1,0:T(8,128)(2,1)}), bf16[8,128,128]{2,1,0:T(8,128)(2,1)S(1)}, u32[]{:S(2)}, u32[]{:S(2)}) async-start(bf16[8,128,128]{2,1,0:T(8,128)(2,1)} %bitcast.37), calls=%async_computation.2 | async-start | bytes 524288 | tf_op jit(solution)/shard_map/all_to_all | solution.py:48
  86.1 20.2 %copy-start.2 = (s32[32]{0:T(128)S(1)}, s32[32]{0:T(128)}, u32[]{:S(2)}) copy-start(s32[32]{0:T(128)} %get-tuple-element.39.order.refs_0_) | copy-start | bytes 388
  86.1 20.2 %copy-start.3 = (s32[8]{0:T(128)S(1)}, s32[8]{0:T(128)}, u32[]{:S(2)}) copy-start(s32[8]{0:T(128)} %get-tuple-element.40.spot.refs_1_) | copy-start | bytes 100
  91.1 0.9 copy-start.1

commit v10 on v9

--- a/solution.py
+++ b/solution.py
@@ -109,22 +109,19 @@
     return copies
 
 
-def raise_heads(low, copies, places, q_in, v_in, up_in, turns=None, done=None):
+def raise_heads(low, copies, places, q_in, v_in, up_in):
     lanes = lax.broadcasted_iota(jnp.int32, (ROWS, BOTH), 1)
     none = jnp.zeros_like(low)
     lows = jnp.concatenate([jnp.where(lanes < RANK, low, none), jnp.where(lanes < RANK, none, low)], axis=0)
     for copy in copies:
         copy.wait()
     raised = jnp.dot(lows, up_in[...], preferred_element_type=F32)
-    for t, p in enumerate(turns or range(len(places))):
-        buffer, entry = places[p]
+    for p, (buffer, entry) in enumerate(places):
         own = slice(p * HD, (p + 1) * HD)
         q = (q_in[:, own].astype(F32) + adapter_scale * raised[:ROWS, own]).astype(BF16)
         v = (v_in[:, own].astype(F32) + adapter_scale * raised[ROWS:, own]).astype(BF16)
         buffer[(*entry[:-1], slice(None), pl.ds(entry[-1], HD))] = q
         buffer[(*entry[:-1], slice(None), pl.ds(entry[-1] + 2 * HD, HD))] = v
-        if done is not None:
-            done(t)
 
 
 HALF = HEADS // 2
@@ -140,8 +137,7 @@
 
 
 def prepare_plain_kernel(flags, x_hbm, down_hbm, *refs):
-    frozen, (out_hbm, order, spot, low_ref, out_ref, out_sems, *refs) = refs[:5], refs[5:]
-    x_in, down_in, whole_sems, q_in, v_in, up_in, sems = refs
+    frozen, (out_ref, order, spot, low_ref, x_in, down_in, whole_sems, q_in, v_in, up_in, sems) = refs[:5], refs[5:]
     wholes = [
         pltpu.make_async_copy(x_hbm, x_in, whole_sems.at[0]),
         pltpu.make_async_copy(down_hbm, down_in, whole_sems.at[1]),
@@ -163,19 +159,7 @@
     low_ref[...] = low
     for seat in range(MEMBERS):
         out_ref[seat, :, pl.ds(8 * HD, BOTH)] = low
-    sends = [
-        pltpu.make_async_copy(out_ref.at[seat], out_hbm.at[seat], out_sems.at[seat]) for seat in range(MEMBERS)
-    ]
-
-    def done(t):
-        if t % 2 == 1 and t > 1:
-            sends[t // 2 - 1].start()
-
-    turns = [seat + half * MEMBERS for seat in range(MEMBERS) for half in range(2)]
-    raise_heads(low, copies, places, q_in, v_in, up_in, turns, done)
-    sends[-1].start()
-    for send in sends:
-        send.wait()
+    raise_heads(low, copies, places, q_in, v_in, up_in)
 
 
 def prepare_plain(flags, x, down, frozen):
@@ -184,15 +168,14 @@
         "prepare_plain",
         1,
         [ANYWHERE] * 7,
-        [ANYWHERE, SCALARS, SCALARS, block((ROWS, BOTH))],
+        [block((MEMBERS, ROWS, 8 * HD + BOTH)), SCALARS, SCALARS, block((ROWS, BOTH))],
         (
             jax.ShapeDtypeStruct((MEMBERS, ROWS, 8 * HD + BOTH), BF16),
             jax.ShapeDtypeStruct((HEADS,), jnp.int32),
             jax.ShapeDtypeStruct((MEMBERS,), jnp.int32),
             jax.ShapeDtypeStruct((ROWS, BOTH), BF16),
         ),
-        [pltpu.VMEM((MEMBERS, ROWS, 8 * HD + BOTH), BF16), pltpu.SemaphoreType.DMA((MEMBERS,))]
-        + [pltpu.VMEM((ROWS, WIDTH), BF16), pltpu.VMEM((BOTH, WIDTH), BF16), pltpu.SemaphoreType.DMA((2,))]
+        [pltpu.VMEM((ROWS, WIDTH), BF16), pltpu.VMEM((BOTH, WIDTH), BF16), pltpu.SemaphoreType.DMA((2,))]
         + head_scratch(HALF),
         (10**9, 8 * 10**6),
     )(flags, x, down, *frozen)

time: 135 us -> 135 us (level)
  transfers between devices with their start and end apart: 12 -> 12, of which waited for: 2 -> 2; matrix products, arithmetic and copies ran while one was open for 0% -> 0% of each run, Pallas kernels for 24% -> 25%
where the time goes in v10:
time: 135 us; the launch traced here: 134 us
  Pallas kernels  48.5 us (36%)
  blocking collectives  40.6 us (30%)
  starting transfers between devices  40.2 us (30%)
  waiting for transfers between devices  2.1 us (2%)
  local copies, waits for them, and re-layouts  1.59 us (1%)
    all_to_all x3, blocking collectives, exchange(): lax.all_to_all(member, axis, 0, 0, tiled=True, axis_index_groups=groups)  40.6 us
    all_to_all x3, starting transfers between devices, exchange(): lax.all_to_all(member, axis, 0, 0, tiled=True, axis_index_groups=groups)  23.5 us
    pallas_call x2, Pallas kernels, attention_shifted(): call(body, 'attention_last' if last else 'attention_third', 2, [pl.BlockS...  13 us
    pallas_call x1, Pallas kernels, attention_plain(): call(attention_plain_kernel, 'attention_plain', 2, [ANYWHERE] * 2, [block...  9.91 us
    pallas_call x2, Pallas kernels, prepare_shifted(): call(prepare_third_kernel if item == 2 else prepare_last_kernel, 'prepare...  8.66 us
    pallas_call x1, Pallas kernels, prepare_plain(): call(prepare_plain_kernel, 'prepare_plain', 1, [ANYWHERE] * 7, [block((ME...  6.99 us
    ppermute x1, starting transfers between devices, per_device(): other_c = lax.ppermute(other_c, 'ulysses', SHIFT_SWAP)  5.49 us
    ppermute x3, starting transfers between devices, per_device(): lax.ppermute(turned[dx], 'dp', x_shift(dx))  4.81 us
  transfers between devices with their start and end apart: 12, of which 2 were waited for; matrix products, arithmetic and copies ran while one was open for 0% of the time, Pallas kernels for 25%

profile of v10, /device:TPU:1, one launch (start us, length us, event | category | flops | bytes accessed | tf_op | source)
XLA Modules:
  0.0 133.9 jit_solution(10654755978325719639)
XLA Ops:
  0.6 7.0 %prepare_plain.1 = (bf16[8,128,1152]{2,1,0:T(8,128)(2,1)}, s32[32]{0:T(128)}, s32[8]{0:T(128)}, bf16[128,128]{1,0:T(8,128)(2,1)}) custom-call(s32[32]{0:T(128)} %flags.1, bf16[128,4096]{1,0:T(8,128)(2,1)} %bitcast.35, bf16[128,4096]{1,0:T(8,128)(2,1)} %bitcast.34, bf16[128,4096]{1,0:T(8,128)(2,1)} %bitcast.14, bf16[128,4096]{1,0:T(8,128)(2,1)} %bitcast.17, ...), custom_call_target="tpu_custom_call" | custom-call | flops 1000000000 | bytes 8000000 | tf_op jit(solution)/shard_map/prepare_plain/pallas_call | solution.py:166
  7.6 6.4 %all-to-all-start = ((bf16[8,128,1152]{2,1,0:T(8,128)(2,1)}), bf16[8,128,1152]{2,1,0:T(8,128)(2,1)S(1)}, u32[]{:S(2)}, u32[]{:S(2)}) async-start(bf16[8,128,1152]{2,1,0:T(8,128)(2,1)} %get-tuple-element.41), calls=%async_computation | async-start | bytes 4718592 | tf_op jit(solution)/shard_map/all_to_all | solution.py:48
  14.0 4.2 %prepare_third.1 = (bf16[4,128,512]{2,1,0:T(8,128)(2,1)}, bf16[4,128,512]{2,1,0:T(8,128)(2,1)}) custom-call(s32[32]{0:T(128)} %get-tuple-element.39.order.refs_0_, s32[8]{0:T(128)} %get-tuple-element.40.spot.refs_1_, bf16[128,128]{1,0:T(8,128)(2,1)} %get-tuple-element.49.low_ref, bf16[128,4096]{1,0:T(8,128)(2,1)} %bitcast.15, bf16[128,4096]{1,0:T(8,128)(2,1)} %bitcast.18, ...), custom_call_target="tpu_custom_call" | custom-call | flops 1000000000 | bytes 8000000 | tf_op jit(solution)/shard_map/prepare_third/pallas_call | solution.py:209
  18.3 5.5 %collective-permute-start.3 = (bf16[4,128,512]{2,1,0:T(8,128)(2,1)}, bf16[4,128,512]{2,1,0:T(8,128)(2,1)}, u32[]{:S(2)}, u32[]{:S(2)}) collective-permute-start(bf16[4,128,512]{2,1,0:T(8,128)(2,1)} %get-tuple-element.51), channel_id=1, source_target_pairs={{0,28},{1,29},{2,30},{3,31},{4,8},{5,9},{6,10},{7,11},{8,4},{9,5},... | collective-permute-start | bytes 1572872 | tf_op jit(solution)/shard_map/ppermute | solution.py:581
  23.8 2.6 %turn_input.1 = (bf16[2,512,128]{2,1,0:T(8,128)(2,1)}, bf16[2,512,128]{2,1,0:T(8,128)(2,1)}, bf16[2,512,128]{2,1,0:T(8,128)(2,1)}, bf16[2,512,128]{2,1,0:T(8,128)(2,1)}) custom-call(s32[1]{0:T(128)} %bitcast.8.spot.place, bf16[128,4096]{1,0:T(8,128)(2,1)} %bitcast.36), custom_call_target="tpu_custom_call" | custom-call | flops 1000000000 | bytes 2000000 | tf_op jit(solution)/shard_map/turn_input/pallas_call | solution.py:256
  26.3 1.2 collective-permute-start
  27.5 2.4 %collective-permute-start.1 = (bf16[2,512,128]{2,1,0:T(8,128)(2,1)}, bf16[2,512,128]{2,1,0:T(8,128)(2,1)S(1)}, u32[]{:S(2)}, u32[]{:S(2)}) collective-permute-start(bf16[2,512,128]{2,1,0:T(8,128)(2,1)} %get-tuple-element.47), channel_id=1, source_target_pairs={{0,128},{32,160},{64,192},{96,224},{128,0},{160,32},{192,64},{224,... | collective-permute-start | bytes 786440 | tf_op jit(solution)/shard_map/ppermute | solution.py:583
  30.0 1.2 collective-permute-start.2
  31.1 4.4 %prepare_last.1 = bf16[8,128,640]{2,1,0:T(8,128)(2,1)} custom-call(s32[32]{0:T(128)} %get-tuple-element.39.order.refs_0_, s32[8]{0:T(128)} %get-tuple-element.40.spot.refs_1_, bf16[128,128]{1,0:T(8,128)(2,1)} %get-tuple-element.49.low_ref, bf16[128,4096]{1,0:T(8,128)(2,1)} %bitcast.16, bf16[128,4096]{1,0:T(8,128)(2,1)} %bitcast.19, ...), custom_call_target="tpu_custom_call" | custom-call | flops 1000000000 | bytes 8000000 | tf_op jit(solution)/shard_map/prepare_last/pallas_call | solution.py:209
  35.6 2.1 %pack_third.1 = (bf16[128,1024]{1,0:T(8,128)(2,1)}, bf16[128,1024]{1,0:T(8,128)(2,1)}, bf16[128,1024]{1,0:T(8,128)(2,1)}) custom-call(bf16[4,128,512]{2,1,0:T(8,128)(2,1)} %get-tuple-element.50.own_ref.refs_2_, bf16[4,128,512]{2,1,0:T(8,128)(2,1)} %collective-permute-done.3.other_ref.refs_3_), custom_call_target="tpu_custom_call" | custom-call | bytes 4000000 | tf_op jit(solution)/shard_map/pack_third/pallas_call | solution.py:229
  37.7 1.2 collective-permute-start.6
  38.9 2.4 %collective-permute-start.7 = (bf16[128,1024]{1,0:T(8,128)(2,1)}, bf16[128,1024]{1,0:T(8,128)(2,1)}, u32[]{:S(2)}, u32[]{:S(2)}) collective-permute-start(bf16[128,1024]{1,0:T(8,128)(2,1)} %get-tuple-element.53), channel_id=1, source_target_pairs={{0,2},{1,3},{2,0},{3,1},{4,6},{5,7},{6,4},{7,5},{8,10},{9,11},{10,... | collective-permute-start | bytes 786440 | tf_op jit(solution)/shard_map/ppermute | solution.py:587
  41.3 1.2 collective-permute-start.8
  42.5 0.5 all-to-all-done
  43.0 9.3 %all-to-all-start.1 = ((bf16[8,128,640]{2,1,0:T(8,128)(2,1)}), bf16[8,128,640]{2,1,0:T(8,128)(2,1)}, u32[]{:S(2)}, u32[]{:S(2)}) async-start(bf16[8,128,640]{2,1,0:T(8,128)(2,1)} %prepare_last.1), calls=%async_computation.1 | async-start | bytes 2621440 | tf_op jit(solution)/shard_map/all_to_all | solution.py:48
  52.3 9.9 %attention_plain.1 = (f32[512,128]{1,0:T(8,128)}, bf16[512,128]{1,0:T(8,128)(2,1)}, bf16[1024,512]{1,0:T(8,128)(2,1)}) custom-call(s32[32]{0:T(128)} %get-tuple-element.39.order.refs_0_, s32[8]{0:T(128)} %get-tuple-element.40.spot.refs_1_, bf16[1024,1152]{1,0:T(8,128)(2,1)} %bitcast.32, bf16[128,4096]{1,0:T(8,128)(2,1)} %bitcast.29), custom_call_target="tpu_custom_call" | custom-call | flops 20000000000 | bytes 4000000 | tf_op jit(solution)/shard_map/attention_plain/pallas_call | solution.py:336
  62.3 0.1 pad_maximum_fusion
  62.4 1.7 %collective-permute-start.5 = (bf16[4,512,128]{2,1,0:T(8,128)(2,1)S(1)}, bf16[4,512,128]{2,1,0:T(8,128)(2,1)S(1)}, u32[]{:S(2)}, u32[]{:S(2)}) collective-permute-start(bf16[4,512,128]{2,1,0:T(8,128)(2,1)S(1)} %pad_maximum_fusion), channel_id=1, source_target_pairs={{0,32},{32,0},{64,96},{96,64},{128,160},{160,128},{192,224},{224,1... | collective-permute-start | bytes 1572872 | tf_op jit(solution)/shard_map/ppermute | solution.py:591
  64.0 0.0 collective-permute-start.4
  64.0 6.2 %attention_third.1 = (f32[1024,128]{1,0:T(8,128)}, bf16[1024,256]{1,0:T(8,128)(2,1)}) custom-call(s32[32]{0:T(128)} %get-tuple-element.39.order.refs_0_, s32[8]{0:T(128)} %get-tuple-element.40.spot.refs_1_, bf16[4,128,512]{2,1,0:T(8,128)(2,1)} %get-tuple-element.50.own_ref.refs_2_, bf16[4,128,512]{2,1,0:T(8,128)(2,1)} %collective-permute-done.3.other_ref.refs_3_, ...), custom_call_target="tpu_custom_call" | custom-call | flops 10000000000 | bytes 10000 | tf_op jit(solution)/shard_map/attention_third/pallas_call | solution.py:416
  70.3 0.6 copy-done.5
  70.9 6.8 %attention_last.1 = (bf16[1024,128]{1,0:T(8,128)(2,1)}, bf16[1024,256]{1,0:T(8,128)(2,1)}) custom-call(s32[32]{0:T(128)} %get-tuple-element.39.order.refs_0_, s32[8]{0:T(128)} %get-tuple-element.40.spot.refs_1_, bf16[1024,640]{1,0:T(8,128)(2,1)} %bitcast.10.refs_2_.low_b, bf16[128,4096]{1,0:T(8,128)(2,1)} %bitcast.31, ...), custom_call_target="tpu_custom_call" | custom-call | flops 4000000000 | bytes 3000000 | tf_op jit(solution)/shard_map/attention_last/pallas_call | solution.py:416
  77.7 7.8 %all-to-all-start.2 = ((bf16[8,128,128]{2,1,0:T(8,128)(2,1)}), bf16[8,128,128]{2,1,0:T(8,128)(2,1)S(1)}, u32[]{:S(2)}, u32[]{:S(2)}) async-start(bf16[8,128,128]{2,1,0:T(8,128)(2,1)} %bitcast.37), calls=%async_computation.2 | async-start | bytes 524288 | tf_op jit(solution)/shard_map/all_to_all | solution.py:48
  85.6 3.4 %up_gradients.1.ups_ref = bf16[8,64,128]{2,1,0:T(8,128)(2,1)} custom-call(bf16[1024,1152]{1,0:T(8,128)(2,1)} %bitcast.33, bf16[1024,640]{1,0:T(8,128)(2,1)} %bitcast.10.refs_2_.low_b, bf16[1024,512]{1,0:T(8,128)(2,1)} %get-tuple-element.62.refs_0_, bf16[1024,256]{1,0:T(8,128)(2,1)} %get-tuple-element.71.refs_1_, bf16[1024,256]{1,0:T(8,128)(2,1)} %get-tuple-element.72.refs_2_), custom_call_target="tpu_custom_call" | custom-call | flops 2000000000 | bytes 3000000 | tf_op jit(solution)/shard_map/up_gradients/pallas_call | solution.py:448
  89.0 1.6 %all-to-all-done.2.summed_ref = bf16[8,128,128]{2,1,0:T(8,128)(2,1)S(1)} async-done(((bf16[8,128,128]{2,1,0:T(8,128)(2,1)}), bf16[8,128,128]{2,1,0:T(8,128)(2,1)S(1)}, u32[]{:S(2)}, u32[]{:S(2)}) %all-to-all-start.2) | async-done | bytes 262176 | tf_op jit(solution)/shard_map/all_to_all | solution.py:48
  90.6 0.9 copy-done.1
  91.5 14.2 %all_to_all.30.both_ref = bf16[8,192,128]{2,1,0:T(8,128)(2,1)S(1)} all-to-all(bf16[8,192,128]{2,1,0:T(8,128)(2,1)S(1)} %gather_parts.1), channel_id=1, replica_groups=mesh['dp'=8,'ulysses'=32] {'dp'}, dimensions={0} | all-to-all | bytes 786432 | tf_op jit(solution)/shard_map/all_to_all | solution.py:48
  105.8 1.0 merge_gradients.1
  106.8 16.1 %all_to_all.31.in_ref = bf16[32,32,128]{2,1,0:T(8,128)(2,1)S(1)} all-to-all(bf16[32,32,128]{2,1,0:T(8,128)(2,1)S(1)} %merge_gradients.1), channel_id=1, replica_groups=mesh['dp'=8,'ulysses'=32] {'ulysses'}, dimensions={0} | all-to-all | bytes 524288 | tf_op jit(solution)/shard_map/all_to_all | solution.py:48
  122.9 0.1 spread_sums.1
  123.0 10.2 %all_to_all.32.in_ref = f32[8,32,128]{2,1,0:T(8,128)S(1)} all-to-all(f32[8,32,128]{2,1,0:T(8,128)S(1)} %spread_sums.1), channel_id=1, replica_groups=mesh['dp'=8,'ulysses'=32] {'dp'}, dimensions={0} | all-to-all | bytes 262144 | tf_op jit(solution)/shard_map/all_to_all | solution.py:48
  133.2 0.7 finish.1
  (25 shorter events, 0.1 us)
Async XLA Ops:
  7.6 35.3 %all-to-all-start = ((bf16[8,128,1152]{2,1,0:T(8,128)(2,1)}), bf16[8,128,1152]{2,1,0:T(8,128)(2,1)S(1)}, u32[]{:S(2)}, u32[]{:S(2)}) async-start(bf16[8,128,1152]{2,1,0:T(8,128)(2,1)} %get-tuple-element.41), calls=%async_computation | async-start | bytes 4718592 | tf_op jit(solution)/shard_map/all_to_all | solution.py:48
  18.3 17.3 %collective-permute-start.3 = (bf16[4,128,512]{2,1,0:T(8,128)(2,1)}, bf16[4,128,512]{2,1,0:T(8,128)(2,1)}, u32[]{:S(2)}, u32[]{:S(2)}) collective-permute-start(bf16[4,128,512]{2,1,0:T(8,128)(2,1)} %get-tuple-element.51), channel_id=1, source_target_pairs={{0,28},{1,29},{2,30},{3,31},{4,8},{5,9},{6,10},{7,11},{8,4},{9,5},... | collective-permute-start | bytes 1572872 | tf_op jit(solution)/shard_map/ppermute | solution.py:581
  26.3 15.0 %collective-permute-start = (bf16[2,512,128]{2,1,0:T(8,128)(2,1)}, bf16[2,512,128]{2,1,0:T(8,128)(2,1)S(1)}, u32[]{:S(2)}, u32[]{:S(2)}) collective-permute-start(bf16[2,512,128]{2,1,0:T(8,128)(2,1)} %get-tuple-element.46), channel_id=1, source_target_pairs={{0,64},{32,96},{64,128},{96,160},{128,192},{160,224},{192,0},{224,... | collective-permute-start | bytes 786440 | tf_op jit(solution)/shard_map/ppermute | solution.py:583
  27.5 14.9 %collective-permute-start.1 = (bf16[2,512,128]{2,1,0:T(8,128)(2,1)}, bf16[2,512,128]{2,1,0:T(8,128)(2,1)S(1)}, u32[]{:S(2)}, u32[]{:S(2)}) collective-permute-start(bf16[2,512,128]{2,1,0:T(8,128)(2,1)} %get-tuple-element.47), channel_id=1, source_target_pairs={{0,128},{32,160},{64,192},{96,224},{128,0},{160,32},{192,64},{224,... | collective-permute-start | bytes 786440 | tf_op jit(solution)/shard_map/ppermute | solution.py:583
  30.0 12.5 %collective-permute-start.2 = (bf16[2,512,128]{2,1,0:T(8,128)(2,1)}, bf16[2,512,128]{2,1,0:T(8,128)(2,1)S(1)}, u32[]{:S(2)}, u32[]{:S(2)}) collective-permute-start(bf16[2,512,128]{2,1,0:T(8,128)(2,1)} %get-tuple-element.48), channel_id=1, source_target_pairs={{0,192},{32,224},{64,0},{96,32},{128,64},{160,96},{192,128},{224,1... | collective-permute-start | bytes 786440 | tf_op jit(solution)/shard_map/ppermute | solution.py:583
  37.7 24.5 %collective-permute-start.6 = (bf16[128,1024]{1,0:T(8,128)(2,1)}, bf16[128,1024]{1,0:T(8,128)(2,1)}, u32[]{:S(2)}, u32[]{:S(2)}) collective-permute-start(bf16[128,1024]{1,0:T(8,128)(2,1)} %get-tuple-element.52), channel_id=1, source_target_pairs={{0,1},{1,2},{2,3},{3,0},{4,5},{5,6},{6,7},{7,4},{8,9},{9,10},{10,1... | collective-permute-start | bytes 786440 | tf_op jit(solution)/shard_map/ppermute | solution.py:587
  38.9 23.3 %collective-permute-start.7 = (bf16[128,1024]{1,0:T(8,128)(2,1)}, bf16[128,1024]{1,0:T(8,128)(2,1)}, u32[]{:S(2)}, u32[]{:S(2)}) collective-permute-start(bf16[128,1024]{1,0:T(8,128)(2,1)} %get-tuple-element.53), channel_id=1, source_target_pairs={{0,2},{1,3},{2,0},{3,1},{4,6},{5,7},{6,4},{7,5},{8,10},{9,11},{10,... | collective-permute-start | bytes 786440 | tf_op jit(solution)/shard_map/ppermute | solution.py:587
  41.3 20.9 %collective-permute-start.8 = (bf16[128,1024]{1,0:T(8,128)(2,1)}, bf16[128,1024]{1,0:T(8,128)(2,1)}, u32[]{:S(2)}, u32[]{:S(2)}) collective-permute-start(bf16[128,1024]{1,0:T(8,128)(2,1)} %get-tuple-element.54), channel_id=1, source_target_pairs={{0,3},{1,0},{2,1},{3,2},{4,7},{5,4},{6,5},{7,6},{8,11},{9,8},{10,9... | collective-permute-start | bytes 786440 | tf_op jit(solution)/shard_map/ppermute | solution.py:587
  43.0 9.3 %copy-start.4 = (bf16[8,128,1152]{2,1,0:T(8,128)(2,1)}, bf16[8,128,1152]{2,1,0:T(8,128)(2,1)S(1)}, u32[]{:S(2)}) copy-start(bf16[8,128,1152]{2,1,0:T(8,128)(2,1)S(1)} %all-to-all-done) | copy-start | bytes 7077892
  43.0 27.3 %all-to-all-start.1 = ((bf16[8,128,640]{2,1,0:T(8,128)(2,1)}), bf16[8,128,640]{2,1,0:T(8,128)(2,1)}, u32[]{:S(2)}, u32[]{:S(2)}) async-start(bf16[8,128,640]{2,1,0:T(8,128)(2,1)} %prepare_last.1), calls=%async_computation.1 | async-start | bytes 2621440 | tf_op jit(solution)/shard_map/all_to_all | solution.py:48
  52.3 10.0 %copy-start = (bf16[2,512,128]{2,1,0:T(8,128)(2,1)S(1)}, bf16[2,512,128]{2,1,0:T(8,128)(2,1)}, u32[]{:S(2)}) copy-start(bf16[2,512,128]{2,1,0:T(8,128)(2,1)} %get-tuple-element.58.refs_0_) | copy-start | bytes 786436
  62.4 7.9 %collective-permute-start.5 = (bf16[4,512,128]{2,1,0:T(8,128)(2,1)S(1)}, bf16[4,512,128]{2,1,0:T(8,128)(2,1)S(1)}, u32[]{:S(2)}, u32[]{:S(2)}) collective-permute-start(bf16[4,512,128]{2,1,0:T(8,128)(2,1)S(1)} %pad_maximum_fusion), channel_id=1, source_target_pairs={{0,32},{32,0},{64,96},{96,64},{128,160},{160,128},{192,224},{224,1... | collective-permute-start | bytes 1572872 | tf_op jit(solution)/shard_map/ppermute | solution.py:591
  64.0 6.2 %collective-permute-start.4 = (bf16[512,128]{1,0:T(8,128)(2,1)}, bf16[512,128]{1,0:T(8,128)(2,1)S(1)}, u32[]{:S(2)}, u32[]{:S(2)}) collective-permute-start(bf16[512,128]{1,0:T(8,128)(2,1)} %get-tuple-element.57), channel_id=1, source_target_pairs={{0,4},{1,5},{2,6},{3,7},{4,0},{5,1},{6,2},{7,3},{8,12},{9,13},{10,... | collective-permute-start | bytes 393224 | tf_op jit(solution)/shard_map/ppermute | solution.py:593
  70.3 0.7 copy-start.5
  77.7 12.8 %all-to-all-start.2 = ((bf16[8,128,128]{2,1,0:T(8,128)(2,1)}), bf16[8,128,128]{2,1,0:T(8,128)(2,1)S(1)}, u32[]{:S(2)}, u32[]{:S(2)}) async-start(bf16[8,128,128]{2,1,0:T(8,128)(2,1)} %bitcast.37), calls=%async_computation.2 | async-start | bytes 524288 | tf_op jit(solution)/shard_map/all_to_all | solution.py:48
  85.6 20.2 %copy-start.2 = (s32[32]{0:T(128)S(1)}, s32[32]{0:T(128)}, u32[]{:S(2)}) copy-start(s32[32]{0:T(128)} %get-tuple-element.39.order.refs_0_) | copy-start | bytes 388
  85.6 20.2 %copy-start.3 = (s32[8]{0:T(128)S(1)}, s32[8]{0:T(128)}, u32[]{:S(2)}) copy-start(s32[8]{0:T(128)} %get-tuple-element.40.spot.refs_1_) | copy-start | bytes 100
  90.6 0.9 copy-start.1

commit v11 on v10

--- a/solution.py
+++ b/solution.py
@@ -480,14 +480,14 @@
 
 
 def merge_kernel(order, spot, place, both_ref, *refs):
-    x_refs, crossed_ref, out_ref = refs[:-2], refs[-2], refs[-1]
+    x_refs, crossed_refs, out_ref = refs[:XS], refs[XS:-1], refs[-1]
     x, core = place[0] // CS, place[0] % CS
     total = jnp.zeros((HEADS * PIECE, BOTH), F32)
     for dx in range(XS):
         for other in range(CS):
             s = (x - dx + XS) % XS * CS + (core + other) % CS
             back = both_ref[s, pl.ds(0, ROWS), :]
-            part = x_refs[dx][0] if other == 0 else crossed_ref[dx]
+            part = (x_refs, crossed_refs)[other][dx][0]
             total += jnp.dot(part, back, preferred_element_type=F32)
     total = (adapter_scale * total).astype(BF16)
     for u in range(HEADS):
@@ -506,13 +506,18 @@
         merge_kernel,
         "merge_gradients",
         3,
-        [block(both.shape)] + [block((1, *piece.shape[1:])) for piece in pieces] + [block(crossed.shape)],
+        [block(both.shape)]
+        + [
+            pl.BlockSpec((1, *piece.shape[1:]), lambda i, *s, half=half: (half, 0, 0))
+            for half in range(2)
+            for piece in (pieces, crossed)[half]
+        ],
         block(shape),
         jax.ShapeDtypeStruct(shape, BF16),
         [],
         (2 * 10**8, 2 * 10**6),
         16,
-    )(order, spot, place, both, *pieces, crossed)
+    )(order, spot, place, both, *pieces, *crossed)
 
 
 def spread_kernel(in_ref, out_ref):
@@ -588,14 +593,14 @@
     plain, pieces, sent = after((plain, pieces, sent), packed)
 
     arrived_d = exchange(sent, "ulysses", SHIFT_GROUPS).reshape(GROUP, 4 * HD + BOTH)
-    crossed = lax.ppermute(jnp.stack([piece[1] for piece in pieces]), "dp", CORE_SWAP)
     mine, theirs, grads_plain = attention_plain(order, spot, plain, up)
     theirs = lax.ppermute(theirs, "ulysses", PLAIN_SWAP)
     arrived_c = after(arrived_c, grads_plain, sent)
     partial, grads_c = attention_shifted(order, spot, [own_c, other_c, *arrived_c], up)
 
-    arrived_d, theirs, crossed = after((arrived_d, theirs, crossed), partial)
+    arrived_d, theirs = after((arrived_d, theirs), partial)
     partial, grads_d = attention_shifted(order, spot, [arrived_d], up, partial, mine, theirs)
+    crossed = [lax.ppermute(piece, "dp", CORE_SWAP) for piece in after(pieces, partial)]
     summed = exchange(partial.reshape(MEMBERS, ROWS, BOTH), "ulysses", SHIFT_GROUPS)
     ups = up_gradients(plain, arrived_d, (grads_plain, grads_c, grads_d))
 

time: 135 us -> 135 us (level)
  blocking collectives: 40.6 us -> 26.6 us
  waiting for transfers between devices: 2.1 us -> 9.82 us
  starting transfers between devices: 40.2 us -> 46.3 us
    all_to_all x3 -> x2, blocking collectives: 40.6 us -> 26.6 us  [exchange(): lax.all_to_all(member, axis, 0, 0, tiled=True, axis_index_groups=groups)]
    all_to_all x3 -> x4, starting transfers between devices: 23.5 us -> 30.1 us  [exchange(): lax.all_to_all(member, axis, 0, 0, tiled=True, axis_index_groups=groups)]
    all_to_all x3 -> x4, waiting for transfers between devices: 2.07 us -> 8.17 us  [exchange(): lax.all_to_all(member, axis, 0, 0, tiled=True, axis_index_groups=groups)]
    ppermute x1 -> x4, waiting for transfers between devices: 0.01 us -> 1.63 us  [per_device(): lax.ppermute(piece, 'dp', CORE_SWAP)]
  transfers between devices with their start and end apart: 12 -> 16, of which waited for: 2 -> 8; matrix products, arithmetic and copies ran while one was open for 0% -> 0% of each run, Pallas kernels for 25% -> 24%
where the time goes in v11:
time: 135 us; the launch traced here: 134 us
  Pallas kernels  49.2 us (36%)
  starting transfers between devices  46.3 us (34%)
  blocking collectives  26.6 us (20%)
  waiting for transfers between devices  9.82 us (7%)
  local copies, waits for them, and re-layouts  1.5 us (1%)
    all_to_all x4, starting transfers between devices, exchange(): lax.all_to_all(member, axis, 0, 0, tiled=True, axis_index_groups=groups)  30.1 us
    all_to_all x2, blocking collectives, exchange(): lax.all_to_all(member, axis, 0, 0, tiled=True, axis_index_groups=groups)  26.6 us
    pallas_call x2, Pallas kernels, attention_shifted(): call(body, 'attention_last' if last else 'attention_third', 2, [pl.BlockS...  13 us
    pallas_call x1, Pallas kernels, attention_plain(): call(attention_plain_kernel, 'attention_plain', 2, [ANYWHERE] * 2, [block...  9.79 us
    pallas_call x2, Pallas kernels, prepare_shifted(): call(prepare_third_kernel if item == 2 else prepare_last_kernel, 'prepare...  8.68 us
    all_to_all x4, waiting for transfers between devices, exchange(): lax.all_to_all(member, axis, 0, 0, tiled=True, axis_index_groups=groups)  8.17 us
    pallas_call x1, Pallas kernels, prepare_plain(): call(prepare_plain_kernel, 'prepare_plain', 1, [ANYWHERE] * 7, [block((ME...  6.98 us
    ppermute x1, starting transfers between devices, per_device(): other_c = lax.ppermute(other_c, 'ulysses', SHIFT_SWAP)  5.48 us
  transfers between devices with their start and end apart: 16, of which 8 were waited for; matrix products, arithmetic and copies ran while one was open for 0% of the time, Pallas kernels for 24%

profile of v11, /device:TPU:1, one launch (start us, length us, event | category | flops | bytes accessed | tf_op | source)
XLA Modules:
  0.0 134.2 jit_solution(3840818142289131315)
XLA Ops:
  0.6 7.0 %prepare_plain.1 = (bf16[8,128,1152]{2,1,0:T(8,128)(2,1)}, s32[32]{0:T(128)}, s32[8]{0:T(128)}, bf16[128,128]{1,0:T(8,128)(2,1)}) custom-call(s32[32]{0:T(128)} %flags.1, bf16[128,4096]{1,0:T(8,128)(2,1)} %bitcast.35, bf16[128,4096]{1,0:T(8,128)(2,1)} %bitcast.34, bf16[128,4096]{1,0:T(8,128)(2,1)} %bitcast.14, bf16[128,4096]{1,0:T(8,128)(2,1)} %bitcast.17, ...), custom_call_target="tpu_custom_call" | custom-call | flops 1000000000 | bytes 8000000 | tf_op jit(solution)/shard_map/prepare_plain/pallas_call | solution.py:166
  7.6 6.4 %all-to-all-start = ((bf16[8,128,1152]{2,1,0:T(8,128)(2,1)}), bf16[8,128,1152]{2,1,0:T(8,128)(2,1)S(1)}, u32[]{:S(2)}, u32[]{:S(2)}) async-start(bf16[8,128,1152]{2,1,0:T(8,128)(2,1)} %get-tuple-element.44), calls=%async_computation | async-start | bytes 4718592 | tf_op jit(solution)/shard_map/all_to_all | solution.py:48
  14.0 4.2 %prepare_third.1 = (bf16[4,128,512]{2,1,0:T(8,128)(2,1)}, bf16[4,128,512]{2,1,0:T(8,128)(2,1)}) custom-call(s32[32]{0:T(128)} %get-tuple-element.42.order.refs_0_, s32[8]{0:T(128)} %get-tuple-element.43.spot.refs_1_, bf16[128,128]{1,0:T(8,128)(2,1)} %get-tuple-element.52.low_ref, bf16[128,4096]{1,0:T(8,128)(2,1)} %bitcast.15, bf16[128,4096]{1,0:T(8,128)(2,1)} %bitcast.18, ...), custom_call_target="tpu_custom_call" | custom-call | flops 1000000000 | bytes 8000000 | tf_op jit(solution)/shard_map/prepare_third/pallas_call | solution.py:209
  18.3 5.5 %collective-permute-start.3 = (bf16[4,128,512]{2,1,0:T(8,128)(2,1)}, bf16[4,128,512]{2,1,0:T(8,128)(2,1)}, u32[]{:S(2)}, u32[]{:S(2)}) collective-permute-start(bf16[4,128,512]{2,1,0:T(8,128)(2,1)} %get-tuple-element.54), channel_id=1, source_target_pairs={{0,28},{1,29},{2,30},{3,31},{4,8},{5,9},{6,10},{7,11},{8,4},{9,5},... | collective-permute-start | bytes 1572872 | tf_op jit(solution)/shard_map/ppermute | solution.py:586
  23.7 2.6 %turn_input.1 = (bf16[2,512,128]{2,1,0:T(8,128)(2,1)}, bf16[2,512,128]{2,1,0:T(8,128)(2,1)}, bf16[2,512,128]{2,1,0:T(8,128)(2,1)}, bf16[2,512,128]{2,1,0:T(8,128)(2,1)}) custom-call(s32[1]{0:T(128)} %bitcast.8.spot.place, bf16[128,4096]{1,0:T(8,128)(2,1)} %bitcast.36), custom_call_target="tpu_custom_call" | custom-call | flops 1000000000 | bytes 2000000 | tf_op jit(solution)/shard_map/turn_input/pallas_call | solution.py:256
  26.4 1.2 collective-permute-start
  27.6 2.4 %collective-permute-start.1 = (bf16[2,512,128]{2,1,0:T(8,128)(2,1)}, bf16[2,512,128]{2,1,0:T(8,128)(2,1)S(1)}, u32[]{:S(2)}, u32[]{:S(2)}) collective-permute-start(bf16[2,512,128]{2,1,0:T(8,128)(2,1)} %get-tuple-element.50), channel_id=1, source_target_pairs={{0,128},{32,160},{64,192},{96,224},{128,0},{160,32},{192,64},{224,... | collective-permute-start | bytes 786440 | tf_op jit(solution)/shard_map/ppermute | solution.py:588
  30.0 1.2 collective-permute-start.2
  31.2 4.4 %prepare_last.1 = bf16[8,128,640]{2,1,0:T(8,128)(2,1)} custom-call(s32[32]{0:T(128)} %get-tuple-element.42.order.refs_0_, s32[8]{0:T(128)} %get-tuple-element.43.spot.refs_1_, bf16[128,128]{1,0:T(8,128)(2,1)} %get-tuple-element.52.low_ref, bf16[128,4096]{1,0:T(8,128)(2,1)} %bitcast.16, bf16[128,4096]{1,0:T(8,128)(2,1)} %bitcast.19, ...), custom_call_target="tpu_custom_call" | custom-call | flops 1000000000 | bytes 8000000 | tf_op jit(solution)/shard_map/prepare_last/pallas_call | solution.py:209
  35.6 2.1 %pack_third.1 = (bf16[128,1024]{1,0:T(8,128)(2,1)}, bf16[128,1024]{1,0:T(8,128)(2,1)}, bf16[128,1024]{1,0:T(8,128)(2,1)}) custom-call(bf16[4,128,512]{2,1,0:T(8,128)(2,1)} %get-tuple-element.53.own_ref.refs_2_, bf16[4,128,512]{2,1,0:T(8,128)(2,1)} %collective-permute-done.3.other_ref.refs_3_), custom_call_target="tpu_custom_call" | custom-call | bytes 4000000 | tf_op jit(solution)/shard_map/pack_third/pallas_call | solution.py:229
  37.8 1.2 collective-permute-start.5
  38.9 2.4 %collective-permute-start.6 = (bf16[128,1024]{1,0:T(8,128)(2,1)}, bf16[128,1024]{1,0:T(8,128)(2,1)}, u32[]{:S(2)}, u32[]{:S(2)}) collective-permute-start(bf16[128,1024]{1,0:T(8,128)(2,1)} %get-tuple-element.56), channel_id=1, source_target_pairs={{0,2},{1,3},{2,0},{3,1},{4,6},{5,7},{6,4},{7,5},{8,10},{9,11},{10,... | collective-permute-start | bytes 786440 | tf_op jit(solution)/shard_map/ppermute | solution.py:592
  41.3 1.2 collective-permute-start.7
  43.0 9.3 %all-to-all-start.1 = ((bf16[8,128,640]{2,1,0:T(8,128)(2,1)}), bf16[8,128,640]{2,1,0:T(8,128)(2,1)}, u32[]{:S(2)}, u32[]{:S(2)}) async-start(bf16[8,128,640]{2,1,0:T(8,128)(2,1)} %prepare_last.1), calls=%async_computation.1 | async-start | bytes 2621440 | tf_op jit(solution)/shard_map/all_to_all | solution.py:48
  52.2 9.8 %attention_plain.1 = (f32[512,128]{1,0:T(8,128)}, bf16[512,128]{1,0:T(8,128)(2,1)}, bf16[1024,512]{1,0:T(8,128)(2,1)}) custom-call(s32[32]{0:T(128)} %get-tuple-element.42.order.refs_0_, s32[8]{0:T(128)} %get-tuple-element.43.spot.refs_1_, bf16[1024,1152]{1,0:T(8,128)(2,1)} %bitcast.32, bf16[128,4096]{1,0:T(8,128)(2,1)} %bitcast.29), custom_call_target="tpu_custom_call" | custom-call | flops 20000000000 | bytes 4000000 | tf_op jit(solution)/shard_map/attention_plain/pallas_call | solution.py:336
  62.2 0.6 copy-done.5
  62.8 6.2 %attention_third.1 = (f32[1024,128]{1,0:T(8,128)}, bf16[1024,256]{1,0:T(8,128)(2,1)}) custom-call(s32[32]{0:T(128)} %get-tuple-element.42.order.refs_0_, s32[8]{0:T(128)} %get-tuple-element.43.spot.refs_1_, bf16[4,128,512]{2,1,0:T(8,128)(2,1)} %get-tuple-element.53.own_ref.refs_2_, bf16[4,128,512]{2,1,0:T(8,128)(2,1)} %collective-permute-done.3.other_ref.refs_3_, ...), custom_call_target="tpu_custom_call" | custom-call | flops 10000000000 | bytes 10000 | tf_op jit(solution)/shard_map/attention_third/pallas_call | solution.py:416
  69.0 0.8 all-to-all-done.1
  69.8 6.8 %attention_last.1 = (bf16[1024,128]{1,0:T(8,128)(2,1)}, bf16[1024,256]{1,0:T(8,128)(2,1)}) custom-call(s32[32]{0:T(128)} %get-tuple-element.42.order.refs_0_, s32[8]{0:T(128)} %get-tuple-element.43.spot.refs_1_, bf16[1024,640]{1,0:T(8,128)(2,1)} %bitcast.10.refs_2_.low_b, bf16[128,4096]{1,0:T(8,128)(2,1)} %bitcast.31, ...), custom_call_target="tpu_custom_call" | custom-call | flops 4000000000 | bytes 3000000 | tf_op jit(solution)/shard_map/attention_last/pallas_call | solution.py:416
  76.6 7.7 %all-to-all-start.2 = ((bf16[8,128,128]{2,1,0:T(8,128)(2,1)}), bf16[8,128,128]{2,1,0:T(8,128)(2,1)S(1)}, u32[]{:S(2)}, u32[]{:S(2)}) async-start(bf16[8,128,128]{2,1,0:T(8,128)(2,1)} %bitcast.37), calls=%async_computation.2 | async-start | bytes 524288 | tf_op jit(solution)/shard_map/all_to_all | solution.py:48
  84.3 3.4 %up_gradients.1.ups_ref = bf16[8,64,128]{2,1,0:T(8,128)(2,1)} custom-call(bf16[1024,1152]{1,0:T(8,128)(2,1)} %bitcast.33, bf16[1024,640]{1,0:T(8,128)(2,1)} %bitcast.10.refs_2_.low_b, bf16[1024,512]{1,0:T(8,128)(2,1)} %get-tuple-element.61.refs_0_, bf16[1024,256]{1,0:T(8,128)(2,1)} %get-tuple-element.70.refs_1_, bf16[1024,256]{1,0:T(8,128)(2,1)} %get-tuple-element.71.refs_2_), custom_call_target="tpu_custom_call" | custom-call | flops 2000000000 | bytes 3000000 | tf_op jit(solution)/shard_map/up_gradients/pallas_call | solution.py:448
  87.8 1.5 %all-to-all-done.2.summed_ref = bf16[8,128,128]{2,1,0:T(8,128)(2,1)S(1)} async-done(((bf16[8,128,128]{2,1,0:T(8,128)(2,1)}), bf16[8,128,128]{2,1,0:T(8,128)(2,1)S(1)}, u32[]{:S(2)}, u32[]{:S(2)}) %all-to-all-start.2) | async-done | bytes 262176 | tf_op jit(solution)/shard_map/all_to_all | solution.py:48
  89.3 0.9 copy-done.1
  90.2 0.8 gather_parts.1
  91.0 6.7 %all-to-all-start.3 = ((bf16[8,192,128]{2,1,0:T(8,128)(2,1)}), bf16[8,192,128]{2,1,0:T(8,128)(2,1)S(1)}, u32[]{:S(2)}, u32[]{:S(2)}) async-start(bf16[8,192,128]{2,1,0:T(8,128)(2,1)} %gather_parts.1), calls=%async_computation.3 | async-start | bytes 786432 | tf_op jit(solution)/shard_map/all_to_all | solution.py:48
  97.7 0.5 collective-permute-start.11
  98.8 0.5 collective-permute-done.10.refs_6_
  100.4 5.4 %all-to-all-done.3.both_ref = bf16[8,192,128]{2,1,0:T(8,128)(2,1)S(1)} async-done(((bf16[8,192,128]{2,1,0:T(8,128)(2,1)}), bf16[8,192,128]{2,1,0:T(8,128)(2,1)S(1)}, u32[]{:S(2)}, u32[]{:S(2)}) %all-to-all-start.3) | async-done | bytes 393248 | tf_op jit(solution)/shard_map/all_to_all | solution.py:48
  105.8 1.0 merge_gradients.1
  106.8 16.4 %all_to_all.30.in_ref = bf16[32,32,128]{2,1,0:T(8,128)(2,1)S(1)} all-to-all(bf16[32,32,128]{2,1,0:T(8,128)(2,1)S(1)} %merge_gradients.1), channel_id=1, replica_groups=mesh['dp'=8,'ulysses'=32] {'ulysses'}, dimensions={0} | all-to-all | bytes 524288 | tf_op jit(solution)/shard_map/all_to_all | solution.py:48
  123.3 10.2 %all_to_all.31.in_ref = f32[8,32,128]{2,1,0:T(8,128)S(1)} all-to-all(f32[8,32,128]{2,1,0:T(8,128)S(1)} %spread_sums.1), channel_id=1, replica_groups=mesh['dp'=8,'ulysses'=32] {'dp'}, dimensions={0} | all-to-all | bytes 262144 | tf_op jit(solution)/shard_map/all_to_all | solution.py:48
  133.5 0.7 finish.1
  (29 shorter events, 2.3 us)
Async XLA Ops:
  7.6 35.3 %all-to-all-start = ((bf16[8,128,1152]{2,1,0:T(8,128)(2,1)}), bf16[8,128,1152]{2,1,0:T(8,128)(2,1)S(1)}, u32[]{:S(2)}, u32[]{:S(2)}) async-start(bf16[8,128,1152]{2,1,0:T(8,128)(2,1)} %get-tuple-element.44), calls=%async_computation | async-start | bytes 4718592 | tf_op jit(solution)/shard_map/all_to_all | solution.py:48
  18.3 17.4 %collective-permute-start.3 = (bf16[4,128,512]{2,1,0:T(8,128)(2,1)}, bf16[4,128,512]{2,1,0:T(8,128)(2,1)}, u32[]{:S(2)}, u32[]{:S(2)}) collective-permute-start(bf16[4,128,512]{2,1,0:T(8,128)(2,1)} %get-tuple-element.54), channel_id=1, source_target_pairs={{0,28},{1,29},{2,30},{3,31},{4,8},{5,9},{6,10},{7,11},{8,4},{9,5},... | collective-permute-start | bytes 1572872 | tf_op jit(solution)/shard_map/ppermute | solution.py:586
  26.4 15.0 %collective-permute-start = (bf16[2,512,128]{2,1,0:T(8,128)(2,1)}, bf16[2,512,128]{2,1,0:T(8,128)(2,1)S(1)}, u32[]{:S(2)}, u32[]{:S(2)}) collective-permute-start(bf16[2,512,128]{2,1,0:T(8,128)(2,1)} %get-tuple-element.49), channel_id=1, source_target_pairs={{0,64},{32,96},{64,128},{96,160},{128,192},{160,224},{192,0},{224,... | collective-permute-start | bytes 786440 | tf_op jit(solution)/shard_map/ppermute | solution.py:588
  27.6 14.9 %collective-permute-start.1 = (bf16[2,512,128]{2,1,0:T(8,128)(2,1)}, bf16[2,512,128]{2,1,0:T(8,128)(2,1)S(1)}, u32[]{:S(2)}, u32[]{:S(2)}) collective-permute-start(bf16[2,512,128]{2,1,0:T(8,128)(2,1)} %get-tuple-element.50), channel_id=1, source_target_pairs={{0,128},{32,160},{64,192},{96,224},{128,0},{160,32},{192,64},{224,... | collective-permute-start | bytes 786440 | tf_op jit(solution)/shard_map/ppermute | solution.py:588
  30.0 12.5 %collective-permute-start.2 = (bf16[2,512,128]{2,1,0:T(8,128)(2,1)}, bf16[2,512,128]{2,1,0:T(8,128)(2,1)S(1)}, u32[]{:S(2)}, u32[]{:S(2)}) collective-permute-start(bf16[2,512,128]{2,1,0:T(8,128)(2,1)} %get-tuple-element.51), channel_id=1, source_target_pairs={{0,192},{32,224},{64,0},{96,32},{128,64},{160,96},{192,128},{224,1... | collective-permute-start | bytes 786440 | tf_op jit(solution)/shard_map/ppermute | solution.py:588
  37.8 24.3 %collective-permute-start.5 = (bf16[128,1024]{1,0:T(8,128)(2,1)}, bf16[128,1024]{1,0:T(8,128)(2,1)S(1)}, u32[]{:S(2)}, u32[]{:S(2)}) collective-permute-start(bf16[128,1024]{1,0:T(8,128)(2,1)} %get-tuple-element.55), channel_id=1, source_target_pairs={{0,1},{1,2},{2,3},{3,0},{4,5},{5,6},{6,7},{7,4},{8,9},{9,10},{10,1... | collective-permute-start | bytes 786440 | tf_op jit(solution)/shard_map/ppermute | solution.py:592
  38.9 23.1 %collective-permute-start.6 = (bf16[128,1024]{1,0:T(8,128)(2,1)}, bf16[128,1024]{1,0:T(8,128)(2,1)}, u32[]{:S(2)}, u32[]{:S(2)}) collective-permute-start(bf16[128,1024]{1,0:T(8,128)(2,1)} %get-tuple-element.56), channel_id=1, source_target_pairs={{0,2},{1,3},{2,0},{3,1},{4,6},{5,7},{6,4},{7,5},{8,10},{9,11},{10,... | collective-permute-start | bytes 786440 | tf_op jit(solution)/shard_map/ppermute | solution.py:592
  41.3 20.7 %collective-permute-start.7 = (bf16[128,1024]{1,0:T(8,128)(2,1)}, bf16[128,1024]{1,0:T(8,128)(2,1)}, u32[]{:S(2)}, u32[]{:S(2)}) collective-permute-start(bf16[128,1024]{1,0:T(8,128)(2,1)} %get-tuple-element.57), channel_id=1, source_target_pairs={{0,3},{1,0},{2,1},{3,2},{4,7},{5,4},{6,5},{7,6},{8,11},{9,8},{10,9... | collective-permute-start | bytes 786440 | tf_op jit(solution)/shard_map/ppermute | solution.py:592
  43.0 9.3 %copy-start.4 = (bf16[8,128,1152]{2,1,0:T(8,128)(2,1)}, bf16[8,128,1152]{2,1,0:T(8,128)(2,1)S(1)}, u32[]{:S(2)}) copy-start(bf16[8,128,1152]{2,1,0:T(8,128)(2,1)S(1)} %all-to-all-done) | copy-start | bytes 7077892
  43.0 26.8 %all-to-all-start.1 = ((bf16[8,128,640]{2,1,0:T(8,128)(2,1)}), bf16[8,128,640]{2,1,0:T(8,128)(2,1)}, u32[]{:S(2)}, u32[]{:S(2)}) async-start(bf16[8,128,640]{2,1,0:T(8,128)(2,1)} %prepare_last.1), calls=%async_computation.1 | async-start | bytes 2621440 | tf_op jit(solution)/shard_map/all_to_all | solution.py:48
  62.1 0.7 copy-start.5
  62.1 6.9 %collective-permute-start.4 = (bf16[512,128]{1,0:T(8,128)(2,1)}, bf16[512,128]{1,0:T(8,128)(2,1)S(1)}, u32[]{:S(2)}, u32[]{:S(2)}) collective-permute-start(bf16[512,128]{1,0:T(8,128)(2,1)} %get-tuple-element.60), channel_id=1, source_target_pairs={{0,4},{1,5},{2,6},{3,7},{4,0},{5,1},{6,2},{7,3},{8,12},{9,13},{10,... | collective-permute-start | bytes 393224 | tf_op jit(solution)/shard_map/ppermute | solution.py:597
  69.0 0.8 copy-start.6
  76.6 12.7 %all-to-all-start.2 = ((bf16[8,128,128]{2,1,0:T(8,128)(2,1)}), bf16[8,128,128]{2,1,0:T(8,128)(2,1)S(1)}, u32[]{:S(2)}, u32[]{:S(2)}) async-start(bf16[8,128,128]{2,1,0:T(8,128)(2,1)} %bitcast.37), calls=%async_computation.2 | async-start | bytes 524288 | tf_op jit(solution)/shard_map/all_to_all | solution.py:48
  84.3 13.9 %copy-start = (bf16[2,512,128]{2,1,0:T(8,128)(2,1)S(1)}, bf16[2,512,128]{2,1,0:T(8,128)(2,1)}, u32[]{:S(2)}) copy-start(bf16[2,512,128]{2,1,0:T(8,128)(2,1)} %get-tuple-element.76.refs_0_) | copy-start | bytes 786436
  84.3 21.5 %copy-start.2 = (s32[32]{0:T(128)S(1)}, s32[32]{0:T(128)}, u32[]{:S(2)}) copy-start(s32[32]{0:T(128)} %get-tuple-element.42.order.refs_0_) | copy-start | bytes 388
  84.3 21.5 %copy-start.3 = (s32[8]{0:T(128)S(1)}, s32[8]{0:T(128)}, u32[]{:S(2)}) copy-start(s32[8]{0:T(128)} %get-tuple-element.43.spot.refs_1_) | copy-start | bytes 100
  89.3 0.9 copy-start.1
  91.0 14.8 %all-to-all-start.3 = ((bf16[8,192,128]{2,1,0:T(8,128)(2,1)}), bf16[8,192,128]{2,1,0:T(8,128)(2,1)S(1)}, u32[]{:S(2)}, u32[]{:S(2)}) async-start(bf16[8,192,128]{2,1,0:T(8,128)(2,1)} %gather_parts.1), calls=%async_computation.3 | async-start | bytes 786432 | tf_op jit(solution)/shard_map/all_to_all | solution.py:48
  97.7 1.5 %collective-permute-start.10 = (bf16[2,512,128]{2,1,0:T(8,128)(2,1)S(1)}, bf16[2,512,128]{2,1,0:T(8,128)(2,1)S(1)}, u32[]{:S(2)}, u32[]{:S(2)}) collective-permute-start(bf16[2,512,128]{2,1,0:T(8,128)(2,1)S(1)} %collective-permute-done.1.refs_2_), channel_id=1, source_target_pairs={{0,32},{32,0},{64,96},{96,64},{128,160},{160,128},{192,224},{224,1... | collective-permute-start | bytes 786440 | tf_op jit(solution)/shard_map/ppermute | solution.py:603
  97.7 1.9 %collective-permute-start.11 = (bf16[2,512,128]{2,1,0:T(8,128)(2,1)S(1)}, bf16[2,512,128]{2,1,0:T(8,128)(2,1)S(1)}, u32[]{:S(2)}, u32[]{:S(2)}) collective-permute-start(bf16[2,512,128]{2,1,0:T(8,128)(2,1)S(1)} %collective-permute-done.2.refs_3_), channel_id=1, source_target_pairs={{0,32},{32,0},{64,96},{96,64},{128,160},{160,128},{192,224},{224,1... | collective-permute-start | bytes 786440 | tf_op jit(solution)/shard_map/ppermute | solution.py:603
  98.2 1.8 %collective-permute-start.8 = (bf16[2,512,128]{2,1,0:T(8,128)(2,1)S(1)}, bf16[2,512,128]{2,1,0:T(8,128)(2,1)S(1)}, u32[]{:S(2)}, u32[]{:S(2)}) collective-permute-start(bf16[2,512,128]{2,1,0:T(8,128)(2,1)S(1)} %copy-done), channel_id=1, source_target_pairs={{0,32},{32,0},{64,96},{96,64},{128,160},{160,128},{192,224},{224,1... | collective-permute-start | bytes 786440 | tf_op jit(solution)/shard_map/ppermute | solution.py:603
  98.3 2.1 %collective-permute-start.9 = (bf16[2,512,128]{2,1,0:T(8,128)(2,1)S(1)}, bf16[2,512,128]{2,1,0:T(8,128)(2,1)S(1)}, u32[]{:S(2)}, u32[]{:S(2)}) collective-permute-start(bf16[2,512,128]{2,1,0:T(8,128)(2,1)S(1)} %collective-permute-done.refs_1_), channel_id=1, source_target_pairs={{0,32},{32,0},{64,96},{96,64},{128,160},{160,128},{192,224},{224,1... | collective-permute-start | bytes 786440 | tf_op jit(solution)/shard_map/ppermute | solution.py:603

commit v12 on v10

--- a/solution.py
+++ b/solution.py
@@ -113,15 +113,19 @@
     lanes = lax.broadcasted_iota(jnp.int32, (ROWS, BOTH), 1)
     none = jnp.zeros_like(low)
     lows = jnp.concatenate([jnp.where(lanes < RANK, low, none), jnp.where(lanes < RANK, none, low)], axis=0)
-    for copy in copies:
+    for copy in copies[0::5]:
         copy.wait()
     raised = jnp.dot(lows, up_in[...], preferred_element_type=F32)
+    for copy in copies[1::5] + copies[2::5]:
+        copy.wait()
     for p, (buffer, entry) in enumerate(places):
         own = slice(p * HD, (p + 1) * HD)
         q = (q_in[:, own].astype(F32) + adapter_scale * raised[:ROWS, own]).astype(BF16)
         v = (v_in[:, own].astype(F32) + adapter_scale * raised[ROWS:, own]).astype(BF16)
         buffer[(*entry[:-1], slice(None), pl.ds(entry[-1], HD))] = q
         buffer[(*entry[:-1], slice(None), pl.ds(entry[-1] + 2 * HD, HD))] = v
+    for copy in copies[3::5] + copies[4::5]:
+        copy.wait()
 
 
 HALF = HEADS // 2

time: 135 us -> 135 us (level)
  no operation moved by 1% of the time
where the time goes in v12:
time: 135 us; the launch traced here: 134 us
  Pallas kernels  49.1 us (36%)
  blocking collectives  40.6 us (30%)
  starting transfers between devices  40.2 us (30%)
  waiting for transfers between devices  1.75 us (1%)
  local copies, waits for them, and re-layouts  1.59 us (1%)
    all_to_all x3, blocking collectives, exchange(): lax.all_to_all(member, axis, 0, 0, tiled=True, axis_index_groups=groups)  40.6 us
    all_to_all x3, starting transfers between devices, exchange(): lax.all_to_all(member, axis, 0, 0, tiled=True, axis_index_groups=groups)  23.5 us
    pallas_call x2, Pallas kernels, attention_shifted(): call(body, 'attention_last' if last else 'attention_third', 2, [pl.BlockS...  13 us
    pallas_call x1, Pallas kernels, attention_plain(): call(attention_plain_kernel, 'attention_plain', 2, [ANYWHERE] * 2, [block...  9.91 us
    pallas_call x2, Pallas kernels, prepare_shifted(): call(prepare_third_kernel if item == 2 else prepare_last_kernel, 'prepare...  9.01 us
    pallas_call x1, Pallas kernels, prepare_plain(): call(prepare_plain_kernel, 'prepare_plain', 1, [ANYWHERE] * 7, [block((ME...  7.27 us
    ppermute x1, starting transfers between devices, per_device(): other_c = lax.ppermute(other_c, 'ulysses', SHIFT_SWAP)  5.49 us
    ppermute x3, starting transfers between devices, per_device(): lax.ppermute(turned[dx], 'dp', x_shift(dx))  4.81 us
  transfers between devices with their start and end apart: 12, of which 2 were waited for; matrix products, arithmetic and copies ran while one was open for 0% of the time, Pallas kernels for 25%

profile of v12, /device:TPU:1, one launch (start us, length us, event | category | flops | bytes accessed | tf_op | source)
XLA Modules:
  0.0 134.2 jit_solution(1303681098068513022)
XLA Ops:
  0.6 7.3 %prepare_plain.1 = (bf16[8,128,1152]{2,1,0:T(8,128)(2,1)}, s32[32]{0:T(128)}, s32[8]{0:T(128)}, bf16[128,128]{1,0:T(8,128)(2,1)}) custom-call(s32[32]{0:T(128)} %flags.1, bf16[128,4096]{1,0:T(8,128)(2,1)} %bitcast.35, bf16[128,4096]{1,0:T(8,128)(2,1)} %bitcast.34, bf16[128,4096]{1,0:T(8,128)(2,1)} %bitcast.14, bf16[128,4096]{1,0:T(8,128)(2,1)} %bitcast.17, ...), custom_call_target="tpu_custom_call" | custom-call | flops 1000000000 | bytes 8000000 | tf_op jit(solution)/shard_map/prepare_plain/pallas_call | solution.py:170
  7.9 6.4 %all-to-all-start = ((bf16[8,128,1152]{2,1,0:T(8,128)(2,1)}), bf16[8,128,1152]{2,1,0:T(8,128)(2,1)S(1)}, u32[]{:S(2)}, u32[]{:S(2)}) async-start(bf16[8,128,1152]{2,1,0:T(8,128)(2,1)} %get-tuple-element.41), calls=%async_computation | async-start | bytes 4718592 | tf_op jit(solution)/shard_map/all_to_all | solution.py:48
  14.3 4.4 %prepare_third.1 = (bf16[4,128,512]{2,1,0:T(8,128)(2,1)}, bf16[4,128,512]{2,1,0:T(8,128)(2,1)}) custom-call(s32[32]{0:T(128)} %get-tuple-element.39.order.refs_0_, s32[8]{0:T(128)} %get-tuple-element.40.spot.refs_1_, bf16[128,128]{1,0:T(8,128)(2,1)} %get-tuple-element.49.low_ref, bf16[128,4096]{1,0:T(8,128)(2,1)} %bitcast.15, bf16[128,4096]{1,0:T(8,128)(2,1)} %bitcast.18, ...), custom_call_target="tpu_custom_call" | custom-call | flops 1000000000 | bytes 8000000 | tf_op jit(solution)/shard_map/prepare_third/pallas_call | solution.py:213
  18.7 5.5 %collective-permute-start.3 = (bf16[4,128,512]{2,1,0:T(8,128)(2,1)}, bf16[4,128,512]{2,1,0:T(8,128)(2,1)}, u32[]{:S(2)}, u32[]{:S(2)}) collective-permute-start(bf16[4,128,512]{2,1,0:T(8,128)(2,1)} %get-tuple-element.51), channel_id=1, source_target_pairs={{0,28},{1,29},{2,30},{3,31},{4,8},{5,9},{6,10},{7,11},{8,4},{9,5},... | collective-permute-start | bytes 1572872 | tf_op jit(solution)/shard_map/ppermute | solution.py:585
  24.2 2.6 %turn_input.1 = (bf16[2,512,128]{2,1,0:T(8,128)(2,1)}, bf16[2,512,128]{2,1,0:T(8,128)(2,1)}, bf16[2,512,128]{2,1,0:T(8,128)(2,1)}, bf16[2,512,128]{2,1,0:T(8,128)(2,1)}) custom-call(s32[1]{0:T(128)} %bitcast.8.spot.place, bf16[128,4096]{1,0:T(8,128)(2,1)} %bitcast.36), custom_call_target="tpu_custom_call" | custom-call | flops 1000000000 | bytes 2000000 | tf_op jit(solution)/shard_map/turn_input/pallas_call | solution.py:260
  26.8 1.2 collective-permute-start
  28.0 2.5 %collective-permute-start.1 = (bf16[2,512,128]{2,1,0:T(8,128)(2,1)}, bf16[2,512,128]{2,1,0:T(8,128)(2,1)S(1)}, u32[]{:S(2)}, u32[]{:S(2)}) collective-permute-start(bf16[2,512,128]{2,1,0:T(8,128)(2,1)} %get-tuple-element.47), channel_id=1, source_target_pairs={{0,128},{32,160},{64,192},{96,224},{128,0},{160,32},{192,64},{224,... | collective-permute-start | bytes 786440 | tf_op jit(solution)/shard_map/ppermute | solution.py:587
  30.5 1.1 collective-permute-start.2
  31.6 4.6 %prepare_last.1 = bf16[8,128,640]{2,1,0:T(8,128)(2,1)} custom-call(s32[32]{0:T(128)} %get-tuple-element.39.order.refs_0_, s32[8]{0:T(128)} %get-tuple-element.40.spot.refs_1_, bf16[128,128]{1,0:T(8,128)(2,1)} %get-tuple-element.49.low_ref, bf16[128,4096]{1,0:T(8,128)(2,1)} %bitcast.16, bf16[128,4096]{1,0:T(8,128)(2,1)} %bitcast.19, ...), custom_call_target="tpu_custom_call" | custom-call | flops 1000000000 | bytes 8000000 | tf_op jit(solution)/shard_map/prepare_last/pallas_call | solution.py:213
  36.2 2.1 %pack_third.1 = (bf16[128,1024]{1,0:T(8,128)(2,1)}, bf16[128,1024]{1,0:T(8,128)(2,1)}, bf16[128,1024]{1,0:T(8,128)(2,1)}) custom-call(bf16[4,128,512]{2,1,0:T(8,128)(2,1)} %get-tuple-element.50.own_ref.refs_2_, bf16[4,128,512]{2,1,0:T(8,128)(2,1)} %collective-permute-done.3.other_ref.refs_3_), custom_call_target="tpu_custom_call" | custom-call | bytes 4000000 | tf_op jit(solution)/shard_map/pack_third/pallas_call | solution.py:233
  38.3 1.2 collective-permute-start.6
  39.5 2.4 %collective-permute-start.7 = (bf16[128,1024]{1,0:T(8,128)(2,1)}, bf16[128,1024]{1,0:T(8,128)(2,1)}, u32[]{:S(2)}, u32[]{:S(2)}) collective-permute-start(bf16[128,1024]{1,0:T(8,128)(2,1)} %get-tuple-element.53), channel_id=1, source_target_pairs={{0,2},{1,3},{2,0},{3,1},{4,6},{5,7},{6,4},{7,5},{8,10},{9,11},{10,... | collective-permute-start | bytes 786440 | tf_op jit(solution)/shard_map/ppermute | solution.py:591
  41.9 1.2 collective-permute-start.8
  43.1 0.1 all-to-all-done
  43.2 9.3 %all-to-all-start.1 = ((bf16[8,128,640]{2,1,0:T(8,128)(2,1)}), bf16[8,128,640]{2,1,0:T(8,128)(2,1)}, u32[]{:S(2)}, u32[]{:S(2)}) async-start(bf16[8,128,640]{2,1,0:T(8,128)(2,1)} %prepare_last.1), calls=%async_computation.1 | async-start | bytes 2621440 | tf_op jit(solution)/shard_map/all_to_all | solution.py:48
  52.5 9.9 %attention_plain.1 = (f32[512,128]{1,0:T(8,128)}, bf16[512,128]{1,0:T(8,128)(2,1)}, bf16[1024,512]{1,0:T(8,128)(2,1)}) custom-call(s32[32]{0:T(128)} %get-tuple-element.39.order.refs_0_, s32[8]{0:T(128)} %get-tuple-element.40.spot.refs_1_, bf16[1024,1152]{1,0:T(8,128)(2,1)} %bitcast.32, bf16[128,4096]{1,0:T(8,128)(2,1)} %bitcast.29), custom_call_target="tpu_custom_call" | custom-call | flops 20000000000 | bytes 4000000 | tf_op jit(solution)/shard_map/attention_plain/pallas_call | solution.py:340
  62.6 0.1 pad_maximum_fusion
  62.6 1.7 %collective-permute-start.5 = (bf16[4,512,128]{2,1,0:T(8,128)(2,1)S(1)}, bf16[4,512,128]{2,1,0:T(8,128)(2,1)S(1)}, u32[]{:S(2)}, u32[]{:S(2)}) collective-permute-start(bf16[4,512,128]{2,1,0:T(8,128)(2,1)S(1)} %pad_maximum_fusion), channel_id=1, source_target_pairs={{0,32},{32,0},{64,96},{96,64},{128,160},{160,128},{192,224},{224,1... | collective-permute-start | bytes 1572872 | tf_op jit(solution)/shard_map/ppermute | solution.py:595
  64.3 0.0 collective-permute-start.4
  64.3 6.2 %attention_third.1 = (f32[1024,128]{1,0:T(8,128)}, bf16[1024,256]{1,0:T(8,128)(2,1)}) custom-call(s32[32]{0:T(128)} %get-tuple-element.39.order.refs_0_, s32[8]{0:T(128)} %get-tuple-element.40.spot.refs_1_, bf16[4,128,512]{2,1,0:T(8,128)(2,1)} %get-tuple-element.50.own_ref.refs_2_, bf16[4,128,512]{2,1,0:T(8,128)(2,1)} %collective-permute-done.3.other_ref.refs_3_, ...), custom_call_target="tpu_custom_call" | custom-call | flops 10000000000 | bytes 10000 | tf_op jit(solution)/shard_map/attention_third/pallas_call | solution.py:420
  70.6 0.6 copy-done.5
  71.2 6.8 %attention_last.1 = (bf16[1024,128]{1,0:T(8,128)(2,1)}, bf16[1024,256]{1,0:T(8,128)(2,1)}) custom-call(s32[32]{0:T(128)} %get-tuple-element.39.order.refs_0_, s32[8]{0:T(128)} %get-tuple-element.40.spot.refs_1_, bf16[1024,640]{1,0:T(8,128)(2,1)} %bitcast.10.refs_2_.low_b, bf16[128,4096]{1,0:T(8,128)(2,1)} %bitcast.31, ...), custom_call_target="tpu_custom_call" | custom-call | flops 4000000000 | bytes 3000000 | tf_op jit(solution)/shard_map/attention_last/pallas_call | solution.py:420
  78.0 7.8 %all-to-all-start.2 = ((bf16[8,128,128]{2,1,0:T(8,128)(2,1)}), bf16[8,128,128]{2,1,0:T(8,128)(2,1)S(1)}, u32[]{:S(2)}, u32[]{:S(2)}) async-start(bf16[8,128,128]{2,1,0:T(8,128)(2,1)} %bitcast.37), calls=%async_computation.2 | async-start | bytes 524288 | tf_op jit(solution)/shard_map/all_to_all | solution.py:48
  85.8 3.4 %up_gradients.1.ups_ref = bf16[8,64,128]{2,1,0:T(8,128)(2,1)} custom-call(bf16[1024,1152]{1,0:T(8,128)(2,1)} %bitcast.33, bf16[1024,640]{1,0:T(8,128)(2,1)} %bitcast.10.refs_2_.low_b, bf16[1024,512]{1,0:T(8,128)(2,1)} %get-tuple-element.62.refs_0_, bf16[1024,256]{1,0:T(8,128)(2,1)} %get-tuple-element.71.refs_1_, bf16[1024,256]{1,0:T(8,128)(2,1)} %get-tuple-element.72.refs_2_), custom_call_target="tpu_custom_call" | custom-call | flops 2000000000 | bytes 3000000 | tf_op jit(solution)/shard_map/up_gradients/pallas_call | solution.py:452
  89.3 1.6 %all-to-all-done.2.summed_ref = bf16[8,128,128]{2,1,0:T(8,128)(2,1)S(1)} async-done(((bf16[8,128,128]{2,1,0:T(8,128)(2,1)}), bf16[8,128,128]{2,1,0:T(8,128)(2,1)S(1)}, u32[]{:S(2)}, u32[]{:S(2)}) %all-to-all-start.2) | async-done | bytes 262176 | tf_op jit(solution)/shard_map/all_to_all | solution.py:48
  90.9 0.9 copy-done.1
  91.8 14.2 %all_to_all.30.both_ref = bf16[8,192,128]{2,1,0:T(8,128)(2,1)S(1)} all-to-all(bf16[8,192,128]{2,1,0:T(8,128)(2,1)S(1)} %gather_parts.1), channel_id=1, replica_groups=mesh['dp'=8,'ulysses'=32] {'dp'}, dimensions={0} | all-to-all | bytes 786432 | tf_op jit(solution)/shard_map/all_to_all | solution.py:48
  106.0 1.0 merge_gradients.1
  107.0 16.2 %all_to_all.31.in_ref = bf16[32,32,128]{2,1,0:T(8,128)(2,1)S(1)} all-to-all(bf16[32,32,128]{2,1,0:T(8,128)(2,1)S(1)} %merge_gradients.1), channel_id=1, replica_groups=mesh['dp'=8,'ulysses'=32] {'ulysses'}, dimensions={0} | all-to-all | bytes 524288 | tf_op jit(solution)/shard_map/all_to_all | solution.py:48
  123.2 0.1 spread_sums.1
  123.3 10.2 %all_to_all.32.in_ref = f32[8,32,128]{2,1,0:T(8,128)S(1)} all-to-all(f32[8,32,128]{2,1,0:T(8,128)S(1)} %spread_sums.1), channel_id=1, replica_groups=mesh['dp'=8,'ulysses'=32] {'dp'}, dimensions={0} | all-to-all | bytes 262144 | tf_op jit(solution)/shard_map/all_to_all | solution.py:48
  133.5 0.7 finish.1
  (25 shorter events, 0.1 us)
Async XLA Ops:
  7.9 35.3 %all-to-all-start = ((bf16[8,128,1152]{2,1,0:T(8,128)(2,1)}), bf16[8,128,1152]{2,1,0:T(8,128)(2,1)S(1)}, u32[]{:S(2)}, u32[]{:S(2)}) async-start(bf16[8,128,1152]{2,1,0:T(8,128)(2,1)} %get-tuple-element.41), calls=%async_computation | async-start | bytes 4718592 | tf_op jit(solution)/shard_map/all_to_all | solution.py:48
  18.7 17.4 %collective-permute-start.3 = (bf16[4,128,512]{2,1,0:T(8,128)(2,1)}, bf16[4,128,512]{2,1,0:T(8,128)(2,1)}, u32[]{:S(2)}, u32[]{:S(2)}) collective-permute-start(bf16[4,128,512]{2,1,0:T(8,128)(2,1)} %get-tuple-element.51), channel_id=1, source_target_pairs={{0,28},{1,29},{2,30},{3,31},{4,8},{5,9},{6,10},{7,11},{8,4},{9,5},... | collective-permute-start | bytes 1572872 | tf_op jit(solution)/shard_map/ppermute | solution.py:585
  26.8 15.1 %collective-permute-start = (bf16[2,512,128]{2,1,0:T(8,128)(2,1)}, bf16[2,512,128]{2,1,0:T(8,128)(2,1)S(1)}, u32[]{:S(2)}, u32[]{:S(2)}) collective-permute-start(bf16[2,512,128]{2,1,0:T(8,128)(2,1)} %get-tuple-element.46), channel_id=1, source_target_pairs={{0,64},{32,96},{64,128},{96,160},{128,192},{160,224},{192,0},{224,... | collective-permute-start | bytes 786440 | tf_op jit(solution)/shard_map/ppermute | solution.py:587
  28.0 15.1 %collective-permute-start.1 = (bf16[2,512,128]{2,1,0:T(8,128)(2,1)}, bf16[2,512,128]{2,1,0:T(8,128)(2,1)S(1)}, u32[]{:S(2)}, u32[]{:S(2)}) collective-permute-start(bf16[2,512,128]{2,1,0:T(8,128)(2,1)} %get-tuple-element.47), channel_id=1, source_target_pairs={{0,128},{32,160},{64,192},{96,224},{128,0},{160,32},{192,64},{224,... | collective-permute-start | bytes 786440 | tf_op jit(solution)/shard_map/ppermute | solution.py:587
  30.5 12.6 %collective-permute-start.2 = (bf16[2,512,128]{2,1,0:T(8,128)(2,1)}, bf16[2,512,128]{2,1,0:T(8,128)(2,1)S(1)}, u32[]{:S(2)}, u32[]{:S(2)}) collective-permute-start(bf16[2,512,128]{2,1,0:T(8,128)(2,1)} %get-tuple-element.48), channel_id=1, source_target_pairs={{0,192},{32,224},{64,0},{96,32},{128,64},{160,96},{192,128},{224,1... | collective-permute-start | bytes 786440 | tf_op jit(solution)/shard_map/ppermute | solution.py:587
  38.3 24.1 %collective-permute-start.6 = (bf16[128,1024]{1,0:T(8,128)(2,1)}, bf16[128,1024]{1,0:T(8,128)(2,1)}, u32[]{:S(2)}, u32[]{:S(2)}) collective-permute-start(bf16[128,1024]{1,0:T(8,128)(2,1)} %get-tuple-element.52), channel_id=1, source_target_pairs={{0,1},{1,2},{2,3},{3,0},{4,5},{5,6},{6,7},{7,4},{8,9},{9,10},{10,1... | collective-permute-start | bytes 786440 | tf_op jit(solution)/shard_map/ppermute | solution.py:591
  39.5 22.9 %collective-permute-start.7 = (bf16[128,1024]{1,0:T(8,128)(2,1)}, bf16[128,1024]{1,0:T(8,128)(2,1)}, u32[]{:S(2)}, u32[]{:S(2)}) collective-permute-start(bf16[128,1024]{1,0:T(8,128)(2,1)} %get-tuple-element.53), channel_id=1, source_target_pairs={{0,2},{1,3},{2,0},{3,1},{4,6},{5,7},{6,4},{7,5},{8,10},{9,11},{10,... | collective-permute-start | bytes 786440 | tf_op jit(solution)/shard_map/ppermute | solution.py:591
  41.9 20.6 %collective-permute-start.8 = (bf16[128,1024]{1,0:T(8,128)(2,1)}, bf16[128,1024]{1,0:T(8,128)(2,1)}, u32[]{:S(2)}, u32[]{:S(2)}) collective-permute-start(bf16[128,1024]{1,0:T(8,128)(2,1)} %get-tuple-element.54), channel_id=1, source_target_pairs={{0,3},{1,0},{2,1},{3,2},{4,7},{5,4},{6,5},{7,6},{8,11},{9,8},{10,9... | collective-permute-start | bytes 786440 | tf_op jit(solution)/shard_map/ppermute | solution.py:591
  43.2 9.3 %copy-start.4 = (bf16[8,128,1152]{2,1,0:T(8,128)(2,1)}, bf16[8,128,1152]{2,1,0:T(8,128)(2,1)S(1)}, u32[]{:S(2)}) copy-start(bf16[8,128,1152]{2,1,0:T(8,128)(2,1)S(1)} %all-to-all-done) | copy-start | bytes 7077892
  43.2 27.3 %all-to-all-start.1 = ((bf16[8,128,640]{2,1,0:T(8,128)(2,1)}), bf16[8,128,640]{2,1,0:T(8,128)(2,1)}, u32[]{:S(2)}, u32[]{:S(2)}) async-start(bf16[8,128,640]{2,1,0:T(8,128)(2,1)} %prepare_last.1), calls=%async_computation.1 | async-start | bytes 2621440 | tf_op jit(solution)/shard_map/all_to_all | solution.py:48
  52.5 10.0 %copy-start = (bf16[2,512,128]{2,1,0:T(8,128)(2,1)S(1)}, bf16[2,512,128]{2,1,0:T(8,128)(2,1)}, u32[]{:S(2)}) copy-start(bf16[2,512,128]{2,1,0:T(8,128)(2,1)} %get-tuple-element.58.refs_0_) | copy-start | bytes 786436
  62.6 7.9 %collective-permute-start.5 = (bf16[4,512,128]{2,1,0:T(8,128)(2,1)S(1)}, bf16[4,512,128]{2,1,0:T(8,128)(2,1)S(1)}, u32[]{:S(2)}, u32[]{:S(2)}) collective-permute-start(bf16[4,512,128]{2,1,0:T(8,128)(2,1)S(1)} %pad_maximum_fusion), channel_id=1, source_target_pairs={{0,32},{32,0},{64,96},{96,64},{128,160},{160,128},{192,224},{224,1... | collective-permute-start | bytes 1572872 | tf_op jit(solution)/shard_map/ppermute | solution.py:595
  64.3 6.2 %collective-permute-start.4 = (bf16[512,128]{1,0:T(8,128)(2,1)}, bf16[512,128]{1,0:T(8,128)(2,1)S(1)}, u32[]{:S(2)}, u32[]{:S(2)}) collective-permute-start(bf16[512,128]{1,0:T(8,128)(2,1)} %get-tuple-element.57), channel_id=1, source_target_pairs={{0,4},{1,5},{2,6},{3,7},{4,0},{5,1},{6,2},{7,3},{8,12},{9,13},{10,... | collective-permute-start | bytes 393224 | tf_op jit(solution)/shard_map/ppermute | solution.py:597
  70.6 0.7 copy-start.5
  78.0 12.8 %all-to-all-start.2 = ((bf16[8,128,128]{2,1,0:T(8,128)(2,1)}), bf16[8,128,128]{2,1,0:T(8,128)(2,1)S(1)}, u32[]{:S(2)}, u32[]{:S(2)}) async-start(bf16[8,128,128]{2,1,0:T(8,128)(2,1)} %bitcast.37), calls=%async_computation.2 | async-start | bytes 524288 | tf_op jit(solution)/shard_map/all_to_all | solution.py:48
  85.8 20.2 %copy-start.2 = (s32[32]{0:T(128)S(1)}, s32[32]{0:T(128)}, u32[]{:S(2)}) copy-start(s32[32]{0:T(128)} %get-tuple-element.39.order.refs_0_) | copy-start | bytes 388
  85.8 20.2 %copy-start.3 = (s32[8]{0:T(128)S(1)}, s32[8]{0:T(128)}, u32[]{:S(2)}) copy-start(s32[8]{0:T(128)} %get-tuple-element.40.spot.refs_1_) | copy-start | bytes 100
  90.9 0.9 copy-start.1
